TPU v7x, 256 devices: a whole 4x4x8 slice. The times are simulated.
256 devices in a mesh: epoch: 16 (over z, y_lo), col: 16 (over x, y_hi, core).
Axes of the slice: x: 4, y: 4 (y_hi: 2, y_lo: 2; y = y_hi * 2 + y_lo), z: 8, core: 2. Of those that a mesh axis runs over, the one named last changes fastest.
Arguments:
- partials: bfloat16 [4096, 8192], P('epoch', 'col'), may hold values from -6 to 6
- gaps: int32 [4096], P('epoch'), may hold values 0 or 1
- arc_start: int32 [1], replicated, may hold values from 1024 to 3071
- taps: bfloat16 [241], replicated, may hold values from -0.375 to 0.375
Outputs:
- normal_matrix: float32 [8192, 8192], P('col', 'epoch')
All inputs are finite; a program needn't handle non-finite values. No bound on the sum of `gaps` on one device may be relied on, other than what follows from the above.
Results may differ from a plain program's by a relative error of at most 0.0026.
Values may be sent and summed in bfloat16 or wider, within the bound.
No kernel may reach another device: no remote copies, remote signals or barrier semaphores. Data moves between devices by JAX's collectives and lax.ppermute only.
A program may use at most 64 MiB of HBM per device.

v0:
```python
import jax
import jax.numpy as jnp
from jax import lax
from jax.sharding import PartitionSpec as P


def shifted(block, axis, distance):
    devices = range(lax.axis_size(axis))
    route = [(i - distance, i) for i in devices if i - distance in devices]
    return lax.ppermute(block, axis, route)


def filter_table(first, rows, halo, taps, boundary):
    width = rows + halo
    padded_taps = jnp.concatenate([taps[::-1], jnp.zeros((rows,), taps.dtype)], axis=0)
    values = jnp.tile(padded_taps, rows)[: rows * width].reshape(rows, width)
    later = jnp.arange(rows, dtype=jnp.int32)
    source = jnp.arange(width, dtype=jnp.int32)
    lag = later[:, None] + halo - source[None, :]
    arc_later = first + later >= boundary
    arc_source = first - halo + source >= boundary
    keep = (lag >= 0) & (lag <= halo) & (arc_later[:, None] == arc_source[None, :])
    return jnp.where(keep, values, jnp.zeros_like(values))


def on_device(partials, gaps, arc_start, taps):
    rows = partials.shape[0]
    halo = taps.shape[0] - 1
    masked = partials * gaps[:, None].astype(jnp.bfloat16)
    earlier = shifted(masked[rows - halo :], "epoch", 1)
    first = lax.axis_index("epoch") * rows
    table = filter_table(first, rows, halo, taps, arc_start[0])
    stacked = jnp.concatenate([earlier, masked], axis=0)
    white = jnp.dot(table, stacked, preferred_element_type=jnp.float32).astype(jnp.bfloat16)
    scale_factor = (rows * lax.axis_size("epoch")) ** (-0.5)
    contract = (((0,), (0,)), ((), ()))
    widened = lax.all_gather(white, "col", axis=1, tiled=True)
    right_cols = lax.all_to_all(widened, "epoch", split_axis=1, concat_axis=0, tiled=True)
    left_cols = lax.all_gather(white, "epoch", axis=0, tiled=True)
    gram = lax.dot_general(left_cols, right_cols, contract, preferred_element_type=jnp.float32)
    return gram * scale_factor


def solution(mesh):
    in_specs = (P("epoch", "col"), P("epoch"), P(), P())
    out_specs = P("col", "epoch")
    return jax.shard_map(
        on_device, mesh=mesh, in_specs=in_specs, out_specs=out_specs, check_vma=False
    )
```

profile of v0, /device:TPU:1, one launch (start us, length us, event | category | flops | bytes accessed | tf_op | source)
XLA Modules:
  0.0 271.6 jit_solution(847331416391286945)
XLA Ops:
  6.5 0.0 all-gather.5.cloned.1.call-start
  6.5 0.7 convert_element_type.7
  7.2 1.0 broadcast_multiply_fusion
  8.3 4.0 %collective-permute-start = (bf16[240,512]{1,0:T(8,128)(2,1)S(1)}, bf16[240,512]{1,0:T(8,128)(2,1)S(1)}, u32[]{:S(2)}, u32[]{:S(2)}) collective-permute-start(bf16[240,512]{1,0:T(8,128)(2,1)S(1)} %slice.9), channel_id=1, source_target_pairs={{0,16},{16,32},{32,48},{48,64},{64,80},{80,96},{96,112},{112,128},... | collective-permute-start | bytes 737288 | tf_op jit(solution)/shard_map/ppermute | solution.py:10
  13.0 0.7 reverse
  13.8 0.1 slice.10
  13.9 0.5 tile.10
  14.4 0.5 reshape.24
  14.9 2.0 collective-permute-done
  16.9 1.1 convolution_convert_fusion
  18.0 0.0 all-gather.5.cloned.1.call-update
  18.1 0.0 all-gather.3.cloned.1.call-start
  18.1 0.7 all-gather.3.cloned.1.call-update
  18.8 70.9 %all-gather.5.cloned.1.call-done = bf16[256,8192]{1,0:T(8,128)(2,1)} async-done(((bf16[256,512]{1,0:T(8,128)(2,1)}), bf16[256,8192]{1,0:T(8,128)(2,1)}) %all-gather.5.cloned.1.call-update) | async-done | bytes 4194320 | tf_op jit(solution)/shard_map/all_gather | solution.py:37
  89.7 4.6 %copy.8 = bf16[32,16,8,512]{3,2,0,1:T(8,128)(2,1)} copy(bf16[32,16,8,512]{3,2,1,0:T(8,128)(2,1)} %bitcast.14) | data formatting | bytes 8388608 | tf_op jit(solution)/shard_map/all_to_all | solution.py:38
  94.3 6.9 %all-to-all-start = ((bf16[256,16,512]{2,0,1:T(8,128)(2,1)}), bf16[256,16,512]{2,0,1:T(8,128)(2,1)}, u32[]{:S(2)}, u32[]{:S(2)}) async-start(bf16[256,16,512]{2,0,1:T(8,128)(2,1)} %bitcast.13), calls=%async_computation | async-start | bytes 8388608 | tf_op jit(solution)/shard_map/all_to_all | solution.py:38
  101.2 156.8 %all-gather.3.cloned.1.call-done = bf16[4096,512]{1,0:T(8,128)(2,1)} async-done(((bf16[256,512]{1,0:T(8,128)(2,1)}), bf16[4096,512]{1,0:T(8,128)(2,1)}) %all-gather.3.cloned.1.call-update) | async-done | bytes 4194320 | tf_op jit(solution)/shard_map/all_gather | solution.py:39
  258.0 0.0 all-to-all-done
  258.0 6.8 %convolution_multiply_fusion = f32[512,512]{1,0:T(8,128)} fusion(bf16[4096,512]{1,0:T(8,128)(2,1)} %all-gather.3.cloned.1.call-done, bf16[4096,512]{1,0:T(8,128)(2,1)} %bitcast.2), kind=kOutput, calls=%fused_computation.1 | convolution fusion | flops 2147745792 | bytes 9437184 | tf_op jit(solution)/shard_map/dot_general | solution.py:40
  (7 shorter events, 0.1 us)
Async XLA Ops:
  6.5 83.1 %all-gather.5.cloned.1.call-start = ((), (), s32[]{:S(2)}) async-start(), calls=%async_computation.2 | async-start | bytes 4456448 | tf_op jit(solution)/shard_map/all_gather | solution.py:37
  8.3 8.6 %collective-permute-start = (bf16[240,512]{1,0:T(8,128)(2,1)S(1)}, bf16[240,512]{1,0:T(8,128)(2,1)S(1)}, u32[]{:S(2)}, u32[]{:S(2)}) collective-permute-start(bf16[240,512]{1,0:T(8,128)(2,1)S(1)} %slice.9), channel_id=1, source_target_pairs={{0,16},{16,32},{32,48},{48,64},{64,80},{80,96},{96,112},{112,128},... | collective-permute-start | bytes 737288 | tf_op jit(solution)/shard_map/ppermute | solution.py:10
  18.1 239.9 %all-gather.3.cloned.1.call-start = ((), (), s32[]{:S(2)}) async-start(), calls=%async_computation.1 | async-start | bytes 4456448 | tf_op jit(solution)/shard_map/all_gather | solution.py:39
  94.3 163.7 %all-to-all-start = ((bf16[256,16,512]{2,0,1:T(8,128)(2,1)}), bf16[256,16,512]{2,0,1:T(8,128)(2,1)}, u32[]{:S(2)}, u32[]{:S(2)}) async-start(bf16[256,16,512]{2,0,1:T(8,128)(2,1)} %bitcast.13), calls=%async_computation | async-start | bytes 8388608 | tf_op jit(solution)/shard_map/all_to_all | solution.py:38
Sparse Core Ops, SparseCore 0:
  18.2 71.4 all-gather.4
  91.5 166.4 all-gather.2
where the time goes:
time: 274 us; the launch traced here: 272 us
  waiting for transfers between devices  230 us (84%)
  between operations  14.1 us (5%)
  starting transfers between devices  11 us (4%)
  matrix products  7.89 us (3%)
  local copies, waits for them, and re-layouts  6.49 us (2%)
    all_gather x1, waiting for transfers between devices, on_device(): left_cols = lax.all_gather(white, 'epoch', axis=0, tiled=True)  157 us
    all_gather x1, waiting for transfers between devices, on_device(): widened = lax.all_gather(white, 'col', axis=1, tiled=True)  70.9 us
    all_to_all x1, starting transfers between devices, on_device(): lax.all_to_all(widened, 'epoch', split_axis=1, concat_axis=0, tiled=True)  6.91 us
    dot_general x1, matrix products, on_device(): lax.dot_general(left_cols, right_cols, contract, preferred_element_type=j...  6.79 us
  transfers between devices with their start and end apart: 4, of which 3 were waited for; matrix products, arithmetic and copies ran while one was open for 2% of the time, Pallas kernels for 0%

commit v1 on v0

v1 whole, which is shorter than its diff:
```python
import functools

import jax
import jax.numpy as jnp
from jax import lax
from jax.experimental import pallas as pl
from jax.experimental.pallas import tpu as pltpu
from jax.sharding import Mesh, PartitionSpec as P

NZ, NYL, NX, NYH, NC = 8, 2, 4, 2, 2
EPOCH = ("z", "yl")
COL = ("x", "yh", "c")
BF16, F32 = jnp.bfloat16, jnp.float32


def ring(n, step):
    return [(i, (i + step) % n) for i in range(n)]


def around(block, axis, n, step):
    return lax.ppermute(block, axis, ring(n, step))


def transposing_route():
    route = []
    for z_from in range(NZ):
        for x_from in range(NX):
            for yh_from in range(NYH):
                z = 2 * x_from + yh_from
                g = (z_from - z if z % 2 == 0 else z - z_from) % NZ
                x, yh = g // 2, g % 2
                route.append(((z_from * NX + x_from) * NYH + yh_from, (z * NX + x) * NYH + yh))
    return route


def filter_table(first, rows, halo, taps, boundary):
    width = rows + halo
    padded_taps = jnp.concatenate([taps[::-1], jnp.zeros((rows,), taps.dtype)], axis=0)
    values = jnp.tile(padded_taps, rows)[: rows * width].reshape(rows, width)
    later = jnp.arange(rows, dtype=jnp.int32)
    source = jnp.arange(width, dtype=jnp.int32)
    lag = later[:, None] + halo - source[None, :]
    arc_later = first + later >= boundary
    arc_source = first - halo + source >= boundary
    keep = (lag >= 0) & (lag <= halo) & (arc_later[:, None] == arc_source[None, :])
    return jnp.where(keep, values, jnp.zeros_like(values))


def gram_kernel(scale, index_ref, *refs):
    left = refs[0:8]
    right = refs[8:16]
    keep_ref, send_ref, left_all, right_all, sems = refs[16:]
    rows = right[0].shape[0] // 2
    copies = []
    for d in range(8):
        copies.append(pltpu.make_async_copy(left[d], left_all.at[:, pl.ds(d * rows, rows)], sems.at[d]))
    for q in range(2):
        for s in range(4):
            for h in range(2):
                n = (q * 4 + s) * 2 + h
                start = pl.multiple_of(index_ref[s * 2 + h] * rows, rows)
                target = right_all.at[index_ref[8 + q], pl.ds(start, rows), :]
                copies.append(pltpu.make_async_copy(right[q * 4 + s].at[pl.ds(h * rows, rows), :], target, sems.at[8 + n]))
    for copy in copies:
        copy.start()
    for copy in copies:
        copy.wait()
    send_ref[...] = (jnp.dot(left_all[...], right_all[1], preferred_element_type=F32) * scale).astype(BF16)
    keep_ref[...] = jnp.dot(left_all[...], right_all[0], preferred_element_type=F32) * scale


def gram(index, left, right, scale):
    cols, rows = left[0].shape
    return pl.pallas_call(
        functools.partial(gram_kernel, scale),
        out_shape=[jax.ShapeDtypeStruct((cols, cols), F32), jax.ShapeDtypeStruct((cols, cols), BF16)],
        in_specs=[pl.BlockSpec(memory_space=pltpu.SMEM)] + [pl.BlockSpec(memory_space=pl.ANY)] * 16,
        out_specs=[pl.BlockSpec(memory_space=pltpu.VMEM)] * 2,
        scratch_shapes=[
            pltpu.VMEM((cols, 8 * rows), BF16),
            pltpu.VMEM((2, 8 * rows, cols), BF16),
            pltpu.SemaphoreType.DMA((24,)),
        ],
        compiler_params=pltpu.CompilerParams(vmem_limit_bytes=32 * 1024 * 1024),
        name="gram",
    )(index, *left, *right)


def on_device(partials, gaps, arc_start, taps):
    rows = partials.shape[0]
    halo = taps.shape[0] - 1
    masked = partials * gaps[:, None].astype(BF16)
    epochs = range(NZ * NYL)
    earlier = lax.ppermute(masked[rows - halo :], EPOCH, [(e, e + 1) for e in epochs if e + 1 in epochs])
    z, yl = lax.axis_index("z"), lax.axis_index("yl")
    x, yh, core = lax.axis_index("x"), lax.axis_index("yh"), lax.axis_index("c")
    first = (z * NYL + yl) * rows
    table = filter_table(first, rows, halo, taps, arc_start[0])
    stacked = jnp.concatenate([earlier, masked], axis=0)
    white = jnp.dot(table, stacked, preferred_element_type=F32).astype(BF16)
    white_t = lax.dot_general(stacked, table, (((0,), (1,)), ((), ())), preferred_element_type=F32).astype(BF16)

    here = lax.ppermute(white, ("z", "x", "yh"), transposing_route())
    pair = jnp.concatenate([here, around(here, "yh", NYH, 1)], axis=0)
    x_up = around(pair, "x", NX, 1)
    x_down = around(pair, "x", NX, -1)
    x_far = jnp.concatenate([around(x_up[:rows], "x", NX, 1), around(x_down[rows:], "x", NX, -1)], axis=0)
    own = [pair, x_up, x_down, x_far]
    other = [around(piece, "c", NC, 1) for piece in own]

    left = [None] * NZ
    left[0] = up = down = white_t
    for step in range(1, 4):
        up = around(up, "z", NZ, 1)
        down = around(down, "z", NZ, -1)
        left[NZ - step], left[step] = up, down
    half = white_t.shape[0] // 2
    left[4] = jnp.concatenate([around(up[:half], "z", NZ, 1), around(down[half:], "z", NZ, -1)], axis=0)

    sign = jnp.where(z % 2 == 0, 1, -1)
    places = [
        (sign * (2 * ((x + dx) % NX) + (yh + dy) % NYH)) % NZ
        for dx in (0, -1, 1, 2)
        for dy in (0, 1)
    ]
    swapped = jnp.where(core == yl, 0, 1)
    index = jnp.stack(places + [swapped, 1 - swapped]).astype(jnp.int32)
    scale = (rows * NZ * NYL) ** (-0.5)
    keep, send = gram(index, left, own + other, scale)
    return keep + around(send, "yl", NYL, 1).astype(F32)


def solution(mesh):
    fine = Mesh(mesh.devices.reshape(NZ, NYL, NX, NYH, NC), EPOCH + COL)
    in_specs = (P(EPOCH, COL), P(EPOCH), P(), P())
    return jax.shard_map(on_device, mesh=fine, in_specs=in_specs, out_specs=P(COL, EPOCH), check_vma=False)
```

time: 274 us -> 120 us (0.44)
  the two profiles are of different devices: /device:TPU:1 before, /device:TPU:96 now
where the time goes in v1:
time: 120 us
  waiting for transfers between devices  56.6 us (47%)
  starting transfers between devices  47.4 us (40%)
  local copies, waits for them, and re-layouts  5.37 us (4%)
  Pallas kernels  4.92 us (4%)
  other arithmetic  3.86 us (3%)
    ppermute x18, starting transfers between devices, around(): return lax.ppermute(block, axis, ring(n, step))  41.3 us
    ppermute x18, waiting for transfers between devices, around(): return lax.ppermute(block, axis, ring(n, step))  41 us
    ppermute x1, waiting for transfers between devices, on_device(): here = lax.ppermute(white, ('z', 'x', 'yh'), transposing_route())  11.2 us
    pallas_call x1, Pallas kernels, gram(): pl.pallas_call(functools.partial(gram_kernel, scale), out_shape=[jax.Shap...  4.92 us
    ppermute x1, waiting for transfers between devices, on_device(): lax.ppermute(masked[rows - halo:], EPOCH, [(e, e + 1) for e in epochs if...  4.39 us
    unnamed x24, local copies, waits for them, and re-layouts  4.12 us
    ppermute x1, starting transfers between devices, on_device(): lax.ppermute(masked[rows - halo:], EPOCH, [(e, e + 1) for e in epochs if...  3.48 us
    ppermute x1, starting transfers between devices, on_device(): here = lax.ppermute(white, ('z', 'x', 'yh'), transposing_route())  2.57 us
  transfers between devices with their start and end apart: 20, of which 10 were waited for; matrix products, arithmetic and copies ran while one was open for 2% of the time, Pallas kernels for 0%

profile of v1, /device:TPU:96, one launch (start us, length us, event | category | flops | bytes accessed | tf_op | source)
XLA Modules:
  0.0 119.9 jit_solution(7828017991286316971)
XLA Ops:
  0.0 0.7 convert_element_type.13
  0.7 1.0 broadcast_multiply_fusion
  1.8 3.5 %collective-permute-start = (bf16[240,512]{1,0:T(8,128)(2,1)S(1)}, bf16[240,512]{1,0:T(8,128)(2,1)S(1)}, u32[]{:S(2)}, u32[]{:S(2)}) collective-permute-start(bf16[240,512]{1,0:T(8,128)(2,1)S(1)} %slice.24), channel_id=1, source_target_pairs={{0,16},{16,32},{32,48},{48,64},{64,80},{80,96},{96,112},{112,128},... | collective-permute-start | bytes 737288 | tf_op jit(solution)/shard_map/ppermute | solution.py:94
  7.9 4.4 %collective-permute-done = bf16[240,512]{1,0:T(8,128)(2,1)S(1)} collective-permute-done((bf16[240,512]{1,0:T(8,128)(2,1)S(1)}, bf16[240,512]{1,0:T(8,128)(2,1)S(1)}, u32[]{:S(2)}, u32[]{:S(2)}) %collective-permute-start) | collective-permute-done | bytes 245792 | tf_op jit(solution)/shard_map/ppermute | solution.py:94
  12.6 2.6 %collective-permute-start.9 = (bf16[256,512]{1,0:T(8,128)(2,1)S(1)}, bf16[256,512]{1,0:T(8,128)(2,1)S(1)}, u32[]{:S(2)}, u32[]{:S(2)}) collective-permute-start(bf16[256,512]{1,0:T(8,128)(2,1)S(1)} %convolution_convert_fusion), channel_id=1, source_target_pairs={{0,0},{2,34},{4,76},{6,102},{8,136},{10,170},{12,196},{14,238},{32... | collective-permute-start | bytes 786440 | tf_op jit(solution)/shard_map/ppermute | solution.py:103
  15.2 11.2 %collective-permute-done.9 = bf16[256,512]{1,0:T(8,128)(2,1)S(1)} collective-permute-done((bf16[256,512]{1,0:T(8,128)(2,1)S(1)}, bf16[256,512]{1,0:T(8,128)(2,1)S(1)}, u32[]{:S(2)}, u32[]{:S(2)}) %collective-permute-start.9) | collective-permute-done | bytes 262176 | tf_op jit(solution)/shard_map/ppermute | solution.py:103
  26.4 14.6 %collective-permute-start.10 = (bf16[256,512]{1,0:T(8,128)(2,1)S(1)}, bf16[256,512]{1,0:T(8,128)(2,1)S(1)}, u32[]{:S(2)}, u32[]{:S(2)}) collective-permute-start(bf16[256,512]{1,0:T(8,128)(2,1)S(1)} %collective-permute-done.9), channel_id=1, source_target_pairs={{0,2},{2,0},{1,3},{3,1},{4,6},{6,4},{5,7},{7,5},{8,10},{10,8},{9,1... | collective-permute-start | bytes 786440 | tf_op jit(solution)/shard_map/ppermute | solution.py:21
  41.0 4.3 %collective-permute-done.10 = bf16[256,512]{1,0:T(8,128)(2,1)S(1)} collective-permute-done((bf16[256,512]{1,0:T(8,128)(2,1)S(1)}, bf16[256,512]{1,0:T(8,128)(2,1)S(1)}, u32[]{:S(2)}, u32[]{:S(2)}) %collective-permute-start.10) | collective-permute-done | bytes 262176 | tf_op jit(solution)/shard_map/ppermute | solution.py:21
  45.4 9.7 %collective-permute-start.12 = (bf16[512,512]{1,0:T(8,128)(2,1)S(1)}, bf16[512,512]{1,0:T(8,128)(2,1)S(1)}, u32[]{:S(2)}, u32[]{:S(2)}) collective-permute-start(bf16[512,512]{1,0:T(8,128)(2,1)S(1)} %constant_dynamic-update-slice_fusion.refs_8_), channel_id=1, source_target_pairs={{0,12},{4,0},{8,4},{12,8},{1,13},{5,1},{9,5},{13,9},{2,14},{6,2},{... | collective-permute-start | bytes 1572872 | tf_op jit(solution)/shard_map/ppermute | solution.py:21
  55.6 5.6 %collective-permute-start.4 = (bf16[512,256]{1,0:T(8,128)(2,1)S(1)}, bf16[512,256]{1,0:T(8,128)(2,1)S(1)}, u32[]{:S(2)}, u32[]{:S(2)}) collective-permute-start(bf16[512,256]{1,0:T(8,128)(2,1)S(1)} %convolution_convert_fusion.1.refs_0_), channel_id=1, source_target_pairs={{0,32},{32,64},{64,96},{96,128},{128,160},{160,192},{192,224},{224... | collective-permute-start | bytes 786440 | tf_op jit(solution)/shard_map/ppermute | solution.py:21
  61.2 4.9 %collective-permute-done.4.refs_7_ = bf16[512,256]{1,0:T(8,128)(2,1)S(1)} collective-permute-done((bf16[512,256]{1,0:T(8,128)(2,1)S(1)}, bf16[512,256]{1,0:T(8,128)(2,1)S(1)}, u32[]{:S(2)}, u32[]{:S(2)}) %collective-permute-start.4) | collective-permute-done | bytes 262176 | tf_op jit(solution)/shard_map/ppermute | solution.py:21
  66.1 3.7 %collective-permute-start.5 = (bf16[512,256]{1,0:T(8,128)(2,1)S(1)}, bf16[512,256]{1,0:T(8,128)(2,1)S(1)}, u32[]{:S(2)}, u32[]{:S(2)}) collective-permute-start(bf16[512,256]{1,0:T(8,128)(2,1)S(1)} %collective-permute-done.4.refs_7_), channel_id=1, source_target_pairs={{0,32},{32,64},{64,96},{96,128},{128,160},{160,192},{192,224},{224... | collective-permute-start | bytes 786440 | tf_op jit(solution)/shard_map/ppermute | solution.py:21
  70.5 3.3 %collective-permute-start.14 = (bf16[256,512]{1,0:T(8,128)(2,1)S(1)}, bf16[256,512]{1,0:T(8,128)(2,1)S(1)}, u32[]{:S(2)}, u32[]{:S(2)}) collective-permute-start(bf16[256,512]{1,0:T(8,128)(2,1)S(1)} %slice.29), channel_id=1, source_target_pairs={{0,12},{4,0},{8,4},{12,8},{1,13},{5,1},{9,5},{13,9},{2,14},{6,2},{... | collective-permute-start | bytes 786440 | tf_op jit(solution)/shard_map/ppermute | solution.py:21
  73.8 3.6 %collective-permute-start.6 = (bf16[512,256]{1,0:T(8,128)(2,1)S(1)}, bf16[512,256]{1,0:T(8,128)(2,1)S(1)}, u32[]{:S(2)}, u32[]{:S(2)}) collective-permute-start(bf16[512,256]{1,0:T(8,128)(2,1)S(1)} %collective-permute-done.5.refs_6_), channel_id=1, source_target_pairs={{0,32},{32,64},{64,96},{96,128},{128,160},{160,192},{192,224},{224... | collective-permute-start | bytes 786440 | tf_op jit(solution)/shard_map/ppermute | solution.py:21
  78.7 2.6 %collective-permute-done.6.refs_5_ = bf16[512,256]{1,0:T(8,128)(2,1)S(1)} collective-permute-done((bf16[512,256]{1,0:T(8,128)(2,1)S(1)}, bf16[512,256]{1,0:T(8,128)(2,1)S(1)}, u32[]{:S(2)}, u32[]{:S(2)}) %collective-permute-start.6) | collective-permute-done | bytes 262176 | tf_op jit(solution)/shard_map/ppermute | solution.py:21
  81.3 6.0 %collective-permute-done.3.refs_3_ = bf16[512,256]{1,0:T(8,128)(2,1)S(1)} collective-permute-done((bf16[512,256]{1,0:T(8,128)(2,1)S(1)}, bf16[512,256]{1,0:T(8,128)(2,1)S(1)}, u32[]{:S(2)}, u32[]{:S(2)}) %collective-permute-start.3) | collective-permute-done | bytes 262176 | tf_op jit(solution)/shard_map/ppermute | solution.py:21
  87.4 5.0 %collective-permute-done.7 = bf16[256,256]{1,0:T(8,128)(2,1)S(1)} collective-permute-done((bf16[256,256]{1,0:T(8,128)(2,1)S(1)}, bf16[256,256]{1,0:T(8,128)(2,1)S(1)}, u32[]{:S(2)}, u32[]{:S(2)}) %collective-permute-start.7) | collective-permute-done | bytes 131104 | tf_op jit(solution)/shard_map/ppermute | solution.py:21
  93.2 6.2 %collective-permute-done.8 = bf16[256,256]{1,0:T(8,128)(2,1)} collective-permute-done((bf16[256,256]{1,0:T(8,128)(2,1)S(1)}, bf16[256,256]{1,0:T(8,128)(2,1)}, u32[]{:S(2)}, u32[]{:S(2)}) %collective-permute-start.8) | collective-permute-done | bytes 131104 | tf_op jit(solution)/shard_map/ppermute | solution.py:21
  99.4 1.0 pad_maximum_fusion.3.refs_4_
  100.4 0.9 copy-done.5
  101.4 0.9 copy-done.7
  102.3 4.9 %gram.1 = (f32[512,512]{1,0:T(8,128)S(1)}, bf16[512,512]{1,0:T(8,128)(2,1)S(1)}) custom-call(s32[10]{0:T(128)S(1)} %stack.43.index_ref, bf16[512,256]{1,0:T(8,128)(2,1)S(1)} %convolution_convert_fusion.1.refs_0_, bf16[512,256]{1,0:T(8,128)(2,1)S(1)} %copy-done.3, bf16[512,256]{1,0:T(8,128)(2,1)S(1)} %copy-done.7, ...), custom_call_target="tpu_custom_call" | custom-call | tf_op jit(solution)/shard_map/gram/pallas_call | solution.py:74
  107.3 11.4 %collective-permute-done.19 = bf16[512,512]{1,0:T(8,128)(2,1)S(1)} collective-permute-done((bf16[512,512]{1,0:T(8,128)(2,1)S(1)}, bf16[512,512]{1,0:T(8,128)(2,1)S(1)}, u32[]{:S(2)}, u32[]{:S(2)}) %collective-permute-start.19) | collective-permute-done | bytes 524320 | tf_op jit(solution)/shard_map/ppermute | solution.py:21
  118.8 1.1 convert_add_fusion
  (63 shorter events, 5.8 us)
Async XLA Ops:
  1.8 10.5 %collective-permute-start = (bf16[240,512]{1,0:T(8,128)(2,1)S(1)}, bf16[240,512]{1,0:T(8,128)(2,1)S(1)}, u32[]{:S(2)}, u32[]{:S(2)}) collective-permute-start(bf16[240,512]{1,0:T(8,128)(2,1)S(1)} %slice.24), channel_id=1, source_target_pairs={{0,16},{16,32},{32,48},{48,64},{64,80},{80,96},{96,112},{112,128},... | collective-permute-start | bytes 737288 | tf_op jit(solution)/shard_map/ppermute | solution.py:94
  12.6 13.7 %collective-permute-start.9 = (bf16[256,512]{1,0:T(8,128)(2,1)S(1)}, bf16[256,512]{1,0:T(8,128)(2,1)S(1)}, u32[]{:S(2)}, u32[]{:S(2)}) collective-permute-start(bf16[256,512]{1,0:T(8,128)(2,1)S(1)} %convolution_convert_fusion), channel_id=1, source_target_pairs={{0,0},{2,34},{4,76},{6,102},{8,136},{10,170},{12,196},{14,238},{32... | collective-permute-start | bytes 786440 | tf_op jit(solution)/shard_map/ppermute | solution.py:103
  26.4 18.9 %collective-permute-start.10 = (bf16[256,512]{1,0:T(8,128)(2,1)S(1)}, bf16[256,512]{1,0:T(8,128)(2,1)S(1)}, u32[]{:S(2)}, u32[]{:S(2)}) collective-permute-start(bf16[256,512]{1,0:T(8,128)(2,1)S(1)} %collective-permute-done.9), channel_id=1, source_target_pairs={{0,2},{2,0},{1,3},{3,1},{4,6},{6,4},{5,7},{7,5},{8,10},{10,8},{9,1... | collective-permute-start | bytes 786440 | tf_op jit(solution)/shard_map/ppermute | solution.py:21
  45.3 24.4 %collective-permute-start.11 = (bf16[512,512]{1,0:T(8,128)(2,1)S(1)}, bf16[512,512]{1,0:T(8,128)(2,1)S(1)}, u32[]{:S(2)}, u32[]{:S(2)}) collective-permute-start(bf16[512,512]{1,0:T(8,128)(2,1)S(1)} %constant_dynamic-update-slice_fusion.refs_8_), channel_id=1, source_target_pairs={{0,4},{4,8},{8,12},{12,0},{1,5},{5,9},{9,13},{13,1},{2,6},{6,10},{... | collective-permute-start | bytes 1572872 | tf_op jit(solution)/shard_map/ppermute | solution.py:21
  45.4 25.0 %collective-permute-start.12 = (bf16[512,512]{1,0:T(8,128)(2,1)S(1)}, bf16[512,512]{1,0:T(8,128)(2,1)S(1)}, u32[]{:S(2)}, u32[]{:S(2)}) collective-permute-start(bf16[512,512]{1,0:T(8,128)(2,1)S(1)} %constant_dynamic-update-slice_fusion.refs_8_), channel_id=1, source_target_pairs={{0,12},{4,0},{8,4},{12,8},{1,13},{5,1},{9,5},{13,9},{2,14},{6,2},{... | collective-permute-start | bytes 1572872 | tf_op jit(solution)/shard_map/ppermute | solution.py:21
  55.6 10.5 %collective-permute-start.4 = (bf16[512,256]{1,0:T(8,128)(2,1)S(1)}, bf16[512,256]{1,0:T(8,128)(2,1)S(1)}, u32[]{:S(2)}, u32[]{:S(2)}) collective-permute-start(bf16[512,256]{1,0:T(8,128)(2,1)S(1)} %convolution_convert_fusion.1.refs_0_), channel_id=1, source_target_pairs={{0,32},{32,64},{64,96},{96,128},{128,160},{160,192},{192,224},{224... | collective-permute-start | bytes 786440 | tf_op jit(solution)/shard_map/ppermute | solution.py:21
  61.2 8.6 %collective-permute-start.1 = (bf16[512,256]{1,0:T(8,128)(2,1)S(1)}, bf16[512,256]{1,0:T(8,128)(2,1)S(1)}, u32[]{:S(2)}, u32[]{:S(2)}) collective-permute-start(bf16[512,256]{1,0:T(8,128)(2,1)S(1)} %convolution_convert_fusion.1.refs_0_), channel_id=1, source_target_pairs={{0,224},{32,0},{64,32},{96,64},{128,96},{160,128},{192,160},{224,1... | collective-permute-start | bytes 786440 | tf_op jit(solution)/shard_map/ppermute | solution.py:21
  66.1 3.7 %copy-start = (bf16[512,256]{1,0:T(8,128)(2,1)}, bf16[512,256]{1,0:T(8,128)(2,1)S(1)}, u32[]{:S(2)}) copy-start(bf16[512,256]{1,0:T(8,128)(2,1)S(1)} %collective-permute-done.4.refs_7_) | copy-start | bytes 786436
  66.1 7.7 %collective-permute-start.5 = (bf16[512,256]{1,0:T(8,128)(2,1)S(1)}, bf16[512,256]{1,0:T(8,128)(2,1)S(1)}, u32[]{:S(2)}, u32[]{:S(2)}) collective-permute-start(bf16[512,256]{1,0:T(8,128)(2,1)S(1)} %collective-permute-done.4.refs_7_), channel_id=1, source_target_pairs={{0,32},{32,64},{64,96},{96,128},{128,160},{160,192},{192,224},{224... | collective-permute-start | bytes 786440 | tf_op jit(solution)/shard_map/ppermute | solution.py:21
  69.8 7.6 %collective-permute-start.2 = (bf16[512,256]{1,0:T(8,128)(2,1)S(1)}, bf16[512,256]{1,0:T(8,128)(2,1)S(1)}, u32[]{:S(2)}, u32[]{:S(2)}) collective-permute-start(bf16[512,256]{1,0:T(8,128)(2,1)S(1)} %collective-permute-done.1.refs_1_), channel_id=1, source_target_pairs={{0,224},{32,0},{64,32},{96,64},{128,96},{160,128},{192,160},{224,1... | collective-permute-start | bytes 786440 | tf_op jit(solution)/shard_map/ppermute | solution.py:21
  70.5 7.6 %collective-permute-start.13 = (bf16[256,512]{1,0:T(8,128)(2,1)S(1)}, bf16[256,512]{1,0:T(8,128)(2,1)S(1)}, u32[]{:S(2)}, u32[]{:S(2)}) collective-permute-start(bf16[256,512]{1,0:T(8,128)(2,1)S(1)} %slice.28), channel_id=1, source_target_pairs={{0,4},{4,8},{8,12},{12,0},{1,5},{5,9},{9,13},{13,1},{2,6},{6,10},{... | collective-permute-start | bytes 786440 | tf_op jit(solution)/shard_map/ppermute | solution.py:21
  70.5 7.6 %collective-permute-start.14 = (bf16[256,512]{1,0:T(8,128)(2,1)S(1)}, bf16[256,512]{1,0:T(8,128)(2,1)S(1)}, u32[]{:S(2)}, u32[]{:S(2)}) collective-permute-start(bf16[256,512]{1,0:T(8,128)(2,1)S(1)} %slice.29), channel_id=1, source_target_pairs={{0,12},{4,0},{8,4},{12,8},{1,13},{5,1},{9,5},{13,9},{2,14},{6,2},{... | collective-permute-start | bytes 786440 | tf_op jit(solution)/shard_map/ppermute | solution.py:21
  73.8 4.3 %copy-start.4 = (bf16[512,256]{1,0:T(8,128)(2,1)}, bf16[512,256]{1,0:T(8,128)(2,1)S(1)}, u32[]{:S(2)}) copy-start(bf16[512,256]{1,0:T(8,128)(2,1)S(1)} %collective-permute-done.5.refs_6_) | copy-start | bytes 786436
  73.8 7.5 %collective-permute-start.6 = (bf16[512,256]{1,0:T(8,128)(2,1)S(1)}, bf16[512,256]{1,0:T(8,128)(2,1)S(1)}, u32[]{:S(2)}, u32[]{:S(2)}) collective-permute-start(bf16[512,256]{1,0:T(8,128)(2,1)S(1)} %collective-permute-done.5.refs_6_), channel_id=1, source_target_pairs={{0,32},{32,64},{64,96},{96,128},{128,160},{160,192},{192,224},{224... | collective-permute-start | bytes 786440 | tf_op jit(solution)/shard_map/ppermute | solution.py:21
  77.4 22.9 %collective-permute-start.15 = (bf16[512,512]{1,0:T(8,128)(2,1)S(1)}, bf16[512,512]{1,0:T(8,128)(2,1)S(1)}, u32[]{:S(2)}, u32[]{:S(2)}) collective-permute-start(bf16[512,512]{1,0:T(8,128)(2,1)S(1)} %constant_dynamic-update-slice_fusion.refs_8_), channel_id=1, source_target_pairs={{0,1},{1,0},{2,3},{3,2},{4,5},{5,4},{6,7},{7,6},{8,9},{9,8},{10,11... | collective-permute-start | bytes 1572872 | tf_op jit(solution)/shard_map/ppermute | solution.py:21
  77.4 9.9 %collective-permute-start.3 = (bf16[512,256]{1,0:T(8,128)(2,1)S(1)}, bf16[512,256]{1,0:T(8,128)(2,1)S(1)}, u32[]{:S(2)}, u32[]{:S(2)}) collective-permute-start(bf16[512,256]{1,0:T(8,128)(2,1)S(1)} %collective-permute-done.2.refs_2_), channel_id=1, source_target_pairs={{0,224},{32,0},{64,32},{96,64},{128,96},{160,128},{192,160},{224,1... | collective-permute-start | bytes 786440 | tf_op jit(solution)/shard_map/ppermute | solution.py:21
  78.1 22.3 %collective-permute-start.17 = (bf16[512,512]{1,0:T(8,128)(2,1)S(1)}, bf16[512,512]{1,0:T(8,128)(2,1)}, u32[]{:S(2)}, u32[]{:S(2)}) collective-permute-start(bf16[512,512]{1,0:T(8,128)(2,1)S(1)} %collective-permute-done.12.refs_10_), channel_id=1, source_target_pairs={{0,1},{1,0},{2,3},{3,2},{4,5},{5,4},{6,7},{7,6},{8,9},{9,8},{10,11... | collective-permute-start | bytes 1572872 | tf_op jit(solution)/shard_map/ppermute | solution.py:21
  78.1 22.2 %collective-permute-start.16 = (bf16[512,512]{1,0:T(8,128)(2,1)S(1)}, bf16[512,512]{1,0:T(8,128)(2,1)}, u32[]{:S(2)}, u32[]{:S(2)}) collective-permute-start(bf16[512,512]{1,0:T(8,128)(2,1)S(1)} %collective-permute-done.11.refs_9_), channel_id=1, source_target_pairs={{0,1},{1,0},{2,3},{3,2},{4,5},{5,4},{6,7},{7,6},{8,9},{9,8},{10,11... | collective-permute-start | bytes 1572872 | tf_op jit(solution)/shard_map/ppermute | solution.py:21
  81.3 19.1 %collective-permute-start.18 = (bf16[512,512]{1,0:T(8,128)(2,1)S(1)}, bf16[512,512]{1,0:T(8,128)(2,1)}, u32[]{:S(2)}, u32[]{:S(2)}) collective-permute-start(bf16[512,512]{1,0:T(8,128)(2,1)S(1)} %constant_dynamic-update-slice_fusion.2.refs_11_), channel_id=1, source_target_pairs={{0,1},{1,0},{2,3},{3,2},{4,5},{5,4},{6,7},{7,6},{8,9},{9,8},{10,11... | collective-permute-start | bytes 1572872 | tf_op jit(solution)/shard_map/ppermute | solution.py:21
  87.4 5.1 %collective-permute-start.7 = (bf16[256,256]{1,0:T(8,128)(2,1)S(1)}, bf16[256,256]{1,0:T(8,128)(2,1)S(1)}, u32[]{:S(2)}, u32[]{:S(2)}) collective-permute-start(bf16[256,256]{1,0:T(8,128)(2,1)S(1)} %slice.26), channel_id=1, source_target_pairs={{0,32},{32,64},{64,96},{96,128},{128,160},{160,192},{192,224},{224... | collective-permute-start | bytes 393224 | tf_op jit(solution)/shard_map/ppermute | solution.py:21
  93.1 6.3 %collective-permute-start.8 = (bf16[256,256]{1,0:T(8,128)(2,1)S(1)}, bf16[256,256]{1,0:T(8,128)(2,1)}, u32[]{:S(2)}, u32[]{:S(2)}) collective-permute-start(bf16[256,256]{1,0:T(8,128)(2,1)S(1)} %slice.27), channel_id=1, source_target_pairs={{0,224},{32,0},{64,32},{96,64},{128,96},{160,128},{192,160},{224,1... | collective-permute-start | bytes 393224 | tf_op jit(solution)/shard_map/ppermute | solution.py:21
  93.2 7.2 %copy-start.1 = (bf16[512,256]{1,0:T(8,128)(2,1)S(1)}, bf16[512,256]{1,0:T(8,128)(2,1)}, u32[]{:S(2)}) copy-start(bf16[512,256]{1,0:T(8,128)(2,1)} %copy-done) | copy-start | bytes 786436
  93.2 7.2 %copy-start.3 = (bf16[512,256]{1,0:T(8,128)(2,1)S(1)}, bf16[512,256]{1,0:T(8,128)(2,1)}, u32[]{:S(2)}) copy-start(bf16[512,256]{1,0:T(8,128)(2,1)} %copy-done.2) | copy-start | bytes 786436
  107.2 11.5 %collective-permute-start.19 = (bf16[512,512]{1,0:T(8,128)(2,1)S(1)}, bf16[512,512]{1,0:T(8,128)(2,1)S(1)}, u32[]{:S(2)}, u32[]{:S(2)}) collective-permute-start(bf16[512,512]{1,0:T(8,128)(2,1)S(1)} %get-tuple-element.8), channel_id=1, source_target_pairs={{0,16},{16,0},{1,17},{17,1},{2,18},{18,2},{3,19},{19,3},{4,20},{20... | collective-permute-start | bytes 1572872 | tf_op jit(solution)/shard_map/ppermute | solution.py:21
  (6 other events, 4.6 us)

commit v2 on v0

v2 whole, which is shorter than its diff:
```python
import functools

import jax
import jax.numpy as jnp
from jax import lax
from jax.experimental import pallas as pl
from jax.experimental.pallas import tpu as pltpu
from jax.sharding import Mesh, PartitionSpec as P

NZ, NYL, NX, NYH, NC = 8, 2, 4, 2, 2
EPOCH = ("z", "yl")
COL = ("x", "yh", "c")
NE = NZ * NYL
BF16, F32 = jnp.bfloat16, jnp.float32
DX = (0, -1, 1, 2)
LEFT_Z = (0, -1, 1, -2, 2, -3, 3)


def around(block, axis, n, step):
    return lax.ppermute(block, axis, [(i, (i + step) % n) for i in range(n)])


def line_of(z_from, z, half):
    return (z_from + z + half * (NZ // 2)) % NZ


def in_plane(block, half):
    axes = ("z", "yl", "x", "yh", "c")
    sizes = (NZ, NYL, NX, NYH, NC)

    def flat(place):
        index = 0
        for size, at in zip(sizes, place):
            index = index * size + at
        return index

    route = []
    for z in range(NZ):
        for yl in range(NYL):
            for x in range(NX):
                for yh in range(NYH):
                    for c in range(NC):
                        line = line_of(z, NYH * x + yh, half)
                        route.append((flat((z, yl, x, yh, c)), flat((z, c, line // NYH, line % NYH, yl))))
    return lax.ppermute(block, axes, route)


def along_z(block, half):
    route = []
    for z_from in range(NZ):
        for z in range(NZ):
            line = line_of(z_from, z, half)
            route.append(((z_from * NX + line // NYH) * NYH + line % NYH, (z * NX + line // NYH) * NYH + line % NYH))
    return lax.ppermute(block, ("z", "x", "yh"), route)


def filter_tables(rows, taps, boundary):
    width = 2 * rows
    padded_taps = jnp.concatenate([jnp.zeros((rows + 1 - taps.shape[0],), taps.dtype), taps[::-1], jnp.zeros((rows,), taps.dtype)])
    values = jnp.tile(padded_taps, rows)[: rows * width].reshape(rows, width)
    later = jnp.arange(rows, dtype=jnp.int32)[:, None]
    source = jnp.arange(width, dtype=jnp.int32)[None, :]
    lag = later + rows - source
    base = jnp.where((lag >= 0) & (lag <= rows), values, jnp.zeros_like(values))
    tables = [base]
    for block in (boundary // rows, boundary // rows + 1):
        split = (block * rows + later >= boundary) & ((block - 1) * rows + source < boundary)
        tables.append(jnp.where(split, jnp.zeros_like(base), base))
    return jnp.stack(tables)


def prepare_kernel(partials_ref, gaps_ref, first_ref, second_ref, turned_ref):
    rows, cols = partials_ref.shape
    kept = jnp.broadcast_to(gaps_ref[...].astype(F32), (128, rows))
    kept_t = kept.T.astype(BF16)
    for i in range(cols // 128):
        part = partials_ref[:, i * 128 : (i + 1) * 128] * kept_t
        turned_ref[i * 128 : (i + 1) * 128, :] = part.T
        half = (first_ref, second_ref)[i // (cols // 256)]
        at = i % (cols // 256) * 128
        half[:, at : at + 128] = part


def prepare(partials, gaps):
    rows, cols = partials.shape
    return pl.pallas_call(
        prepare_kernel,
        out_shape=[jax.ShapeDtypeStruct((rows, cols // 2), BF16)] * 2 + [jax.ShapeDtypeStruct((cols, rows), BF16)],
        name="prepare",
    )(partials, gaps[None, :])


def gram_kernel(scale, meta_ref, tables_ref, tables_t_ref, *refs):
    left_near, left_far, right = refs[0:7], refs[7:9], refs[9:17]
    out_ref, raw_left, raw_right, white_left, white_right = refs[17:]
    rows = raw_left.shape[2]
    cols = raw_left.shape[1]
    z, yl, x, yh, core, cut = [meta_ref[i] for i in range(6)]
    raw_left[0] = jnp.zeros(raw_left.shape[1:], BF16)
    for h in range(2):
        raw_right[h, 0] = jnp.zeros(raw_right.shape[2:], BF16)
    for dz, piece in zip(LEFT_Z, left_near):
        for b in range(2):
            raw_left[2 * ((z + dz) & 7) + (yl ^ b) + 1] = piece[b * cols : (b + 1) * cols]
    for b in range(2):
        raw_left[2 * ((z + 4) & 7) + (yl ^ b) + 1] = left_far[b][...]
    for q in range(2):
        for s in range(4):
            for b in range(4):
                line = NYH * ((x + DX[s]) & 3) + (yh ^ (b // 2))
                e = 2 * ((line - z + (b % 2) * (NZ // 2)) & 7) + (core ^ q)
                raw_right[b % 2, e + 1] = right[q * 4 + s][b * rows : (b + 1) * rows]

    @pl.loop(0, NE)
    def _(e):
        which = jnp.where(e == cut, 1, jnp.where(e == cut + 1, 2, 0))
        table_t = tables_t_ref[which]
        table = tables_ref[which]
        at = pl.multiple_of(e * rows, rows)
        left = jnp.dot(raw_left[e], table_t[:rows], preferred_element_type=F32)
        left += jnp.dot(raw_left[e + 1], table_t[rows:], preferred_element_type=F32)
        white_left[:, pl.ds(at, rows)] = left.astype(BF16)
        for h in range(2):
            right_h = jnp.dot(table[:, :rows], raw_right[h, e], preferred_element_type=F32)
            right_h += jnp.dot(table[:, rows:], raw_right[h, e + 1], preferred_element_type=F32)
            white_right[pl.ds(at, rows), pl.ds(h * rows, rows)] = right_h.astype(BF16)

    out_ref[...] = jnp.dot(white_left[...], white_right[...], preferred_element_type=F32) * scale


def gram(meta, tables, tables_t, left_near, left_far, right, rows, cols, scale):
    vmem = pl.BlockSpec(memory_space=pltpu.VMEM)
    return pl.pallas_call(
        functools.partial(gram_kernel, scale),
        out_shape=jax.ShapeDtypeStruct((cols, cols), F32),
        in_specs=[pl.BlockSpec(memory_space=pltpu.SMEM)] + [vmem] * 19,
        out_specs=vmem,
        scratch_shapes=[
            pltpu.VMEM((NE + 1, cols, rows), BF16),
            pltpu.VMEM((2, NE + 1, rows, rows), BF16),
            pltpu.VMEM((cols, NE * rows), BF16),
            pltpu.VMEM((NE * rows, cols), BF16),
        ],
        compiler_params=pltpu.CompilerParams(vmem_limit_bytes=24 * 1024 * 1024),
        name="gram",
    )(meta, tables, tables_t, *left_near, *left_far, *right)


def on_device(partials, gaps, arc_start, taps):
    rows, cols = partials.shape
    z, yl = lax.axis_index("z"), lax.axis_index("yl")
    x, yh, core = lax.axis_index("x"), lax.axis_index("yh"), lax.axis_index("c")
    first, second, masked_t = prepare(partials, gaps)

    both = jnp.concatenate([masked_t, around(masked_t, "yl", NYL, 1)], axis=0)
    left_near = [both]
    up = down = both
    for step in range(1, 4):
        up = around(up, "z", NZ, 1)
        down = around(down, "z", NZ, -1)
        left_near += [up, down]
    left_far = [around(up[:cols], "z", NZ, 1), around(down[cols:], "z", NZ, -1)]

    halves = [along_z(in_plane(piece, h), h) for h, piece in enumerate((first, second))]
    here = jnp.concatenate(halves, axis=0)
    pair = jnp.concatenate([here, around(here, "yh", NYH, 1)], axis=0)
    x_up = around(pair, "x", NX, 1)
    x_down = around(pair, "x", NX, -1)
    x_far = jnp.concatenate([around(x_up[: 2 * rows], "x", NX, 1), around(x_down[2 * rows :], "x", NX, -1)], axis=0)
    own = [pair, x_up, x_down, x_far]
    other = [around(piece, "c", NC, 1) for piece in own]

    boundary = arc_start[0]
    tables = filter_tables(rows, taps, boundary)
    tables_t = tables.transpose(0, 2, 1)

    meta = jnp.stack([z, yl, x, yh, core, boundary // rows]).astype(jnp.int32)
    scale = (rows * NE) ** (-0.5)
    return gram(meta, tables, tables_t, left_near, left_far, own + other, rows, cols, scale)


def solution(mesh):
    fine = Mesh(mesh.devices.reshape(NZ, NYL, NX, NYH, NC), EPOCH + COL)
    in_specs = (P(EPOCH, COL), P(EPOCH), P(), P())
    return jax.shard_map(on_device, mesh=fine, in_specs=in_specs, out_specs=P(COL, EPOCH), check_vma=False)
```

time: 274 us -> 109 us (0.40)
  waiting for transfers between devices: 230 us -> 32.2 us
  starting transfers between devices: 11 us -> 40.6 us
  Pallas kernels: 0 us -> 14.8 us
  between operations: 14.1 us -> 0.91 us
  local copies, waits for them, and re-layouts: 6.49 us -> 16.1 us
  matrix products: 7.89 us -> 0 us
    all_gather x2 -> x0, waiting for transfers between devices: 228 us -> none  [the longest x1 157 us: on_device(): left_cols = lax.all_gather(white, 'epoch', axis=0, tiled=True)]
    ppermute x1 -> x22, starting transfers between devices: 4.04 us -> 40.6 us  [the longest x18 24.7 us: around(): return lax.ppermute(block, axis, [(i, (i + step) % n) for i in range(n)])]
    ppermute x1 -> x22, waiting for transfers between devices: 2 us -> 32.2 us  [the longest x18 25.3 us: around(): return lax.ppermute(block, axis, [(i, (i + step) % n) for i in range(n)])]
    pallas_call x0 -> x2, Pallas kernels: none -> 14.8 us  [the longest x1 13 us: gram(): pl.pallas_call(functools.partial(gram_kernel, scale), out_shape=jax.Shape...]
    unnamed x2 -> x32, local copies, waits for them, and re-layouts: 0.82 us -> 8.94 us
    dot_general x2 -> x0, matrix products: 7.89 us -> none  [the longest x1 6.79 us: on_device(): lax.dot_general(left_cols, right_cols, contract, preferred_element_type=j...]
    all_to_all x1 -> x0, starting transfers between devices: 6.91 us -> none  [on_device(): lax.all_to_all(widened, 'epoch', split_axis=1, concat_axis=0, tiled=True)]
    all_to_all x1 -> x0, local copies, waits for them, and re-layouts: 4.6 us -> none  [on_device(): lax.all_to_all(widened, 'epoch', split_axis=1, concat_axis=0, tiled=True)]
  transfers between devices with their start and end apart: 4 -> 22, of which waited for: 3 -> 7; matrix products, arithmetic and copies ran while one was open for 2% -> 13% of each run, Pallas kernels for 0% -> 0%
where the time goes in v2:
time: 109 us; the launch traced here: 108 us
  starting transfers between devices  40.6 us (37%)
  waiting for transfers between devices  32.2 us (30%)
  local copies, waits for them, and re-layouts  16.1 us (15%)
  Pallas kernels  14.8 us (14%)
  other arithmetic  3.86 us (4%)
    ppermute x18, waiting for transfers between devices, around(): return lax.ppermute(block, axis, [(i, (i + step) % n) for i in range(n)])  25.3 us
    ppermute x18, starting transfers between devices, around(): return lax.ppermute(block, axis, [(i, (i + step) % n) for i in range(n)])  24.7 us
    pallas_call x1, Pallas kernels, gram(): pl.pallas_call(functools.partial(gram_kernel, scale), out_shape=jax.Shape...  13 us
    unnamed x32, local copies, waits for them, and re-layouts  8.94 us
    ppermute x2, starting transfers between devices, in_plane(): return lax.ppermute(block, axes, route)  8.01 us
    ppermute x2, starting transfers between devices, along_z(): return lax.ppermute(block, ('z', 'x', 'yh'), route)  7.8 us
    ppermute x2, waiting for transfers between devices, in_plane(): return lax.ppermute(block, axes, route)  3.87 us
    ppermute x2, waiting for transfers between devices, along_z(): return lax.ppermute(block, ('z', 'x', 'yh'), route)  3.01 us
  transfers between devices with their start and end apart: 22, of which 7 were waited for; matrix products, arithmetic and copies ran while one was open for 13% of the time, Pallas kernels for 0%

profile of v2, /device:TPU:1, one launch (start us, length us, event | category | flops | bytes accessed | tf_op | source)
XLA Modules:
  0.0 108.5 jit_solution(13197159975847257098)
XLA Ops:
  0.0 1.9 %prepare.1 = (bf16[256,256]{1,0:T(8,128)(2,1)}, bf16[256,256]{1,0:T(8,128)(2,1)}, bf16[512,256]{1,0:T(8,128)(2,1)}) custom-call(bf16[256,512]{1,0:T(8,128)(2,1)} %partials_ref.1, s32[1,256]{1,0:T(1,128)} %bitcast.17), custom_call_target="tpu_custom_call" | custom-call | tf_op jit(solution)/shard_map/prepare/pallas_call | solution.py:86
  1.9 2.1 %collective-permute-start = (bf16[512,256]{1,0:T(8,128)(2,1)}, bf16[512,256]{1,0:T(8,128)(2,1)S(1)}, u32[]{:S(2)}, u32[]{:S(2)}) collective-permute-start(bf16[512,256]{1,0:T(8,128)(2,1)} %get-tuple-element.8), channel_id=1, source_target_pairs={{0,16},{16,0},{1,17},{17,1},{2,18},{18,2},{3,19},{19,3},{4,20},{20... | collective-permute-start | bytes 786440 | tf_op jit(solution)/shard_map/ppermute | solution.py:20
  4.0 4.6 %collective-permute-start.9 = (bf16[256,256]{1,0:T(8,128)(2,1)}, bf16[256,256]{1,0:T(8,128)(2,1)S(1)}, u32[]{:S(2)}, u32[]{:S(2)}) collective-permute-start(bf16[256,256]{1,0:T(8,128)(2,1)} %get-tuple-element.9), channel_id=1, source_target_pairs={{0,0},{1,16},{2,2},{3,18},{4,4},{5,20},{6,6},{7,22},{8,8},{9,24},{... | collective-permute-start | bytes 393224 | tf_op jit(solution)/shard_map/ppermute | solution.py:45
  8.7 3.4 %collective-permute-start.11 = (bf16[256,256]{1,0:T(8,128)(2,1)}, bf16[256,256]{1,0:T(8,128)(2,1)S(1)}, u32[]{:S(2)}, u32[]{:S(2)}) collective-permute-start(bf16[256,256]{1,0:T(8,128)(2,1)} %get-tuple-element.10), channel_id=1, source_target_pairs={{0,8},{1,24},{2,10},{3,26},{4,12},{5,28},{6,14},{7,30},{8,0},{9,16... | collective-permute-start | bytes 393224 | tf_op jit(solution)/shard_map/ppermute | solution.py:45
  13.7 3.9 %collective-permute-done.11 = bf16[256,256]{1,0:T(8,128)(2,1)S(1)} collective-permute-done((bf16[256,256]{1,0:T(8,128)(2,1)}, bf16[256,256]{1,0:T(8,128)(2,1)S(1)}, u32[]{:S(2)}, u32[]{:S(2)}) %collective-permute-start.11) | collective-permute-done | bytes 131104 | tf_op jit(solution)/shard_map/ppermute | solution.py:45
  17.6 7.1 %collective-permute-start.12 = (bf16[256,256]{1,0:T(8,128)(2,1)S(1)}, bf16[256,256]{1,0:T(8,128)(2,1)S(1)}, u32[]{:S(2)}, u32[]{:S(2)}) collective-permute-start(bf16[256,256]{1,0:T(8,128)(2,1)S(1)} %collective-permute-done.11), channel_id=1, source_target_pairs={{8,8},{10,42},{12,76},{14,110},{0,128},{2,162},{4,196},{6,230},{42... | collective-permute-start | bytes 393224 | tf_op jit(solution)/shard_map/ppermute | solution.py:54
  24.8 5.6 %collective-permute-start.2 = (bf16[1024,256]{1,0:T(8,128)(2,1)S(1)}, bf16[1024,256]{1,0:T(8,128)(2,1)S(1)}, u32[]{:S(2)}, u32[]{:S(2)}) collective-permute-start(bf16[1024,256]{1,0:T(8,128)(2,1)S(1)} %constant_dynamic-update-slice_fusion.refs_0_), channel_id=1, source_target_pairs={{0,224},{32,0},{64,32},{96,64},{128,96},{160,128},{192,160},{224,1... | collective-permute-start | bytes 1572872 | tf_op jit(solution)/shard_map/ppermute | solution.py:20
  30.4 3.0 %collective-permute-done.12 = bf16[256,256]{1,0:T(8,128)(2,1)S(1)} collective-permute-done((bf16[256,256]{1,0:T(8,128)(2,1)S(1)}, bf16[256,256]{1,0:T(8,128)(2,1)S(1)}, u32[]{:S(2)}, u32[]{:S(2)}) %collective-permute-start.12) | collective-permute-done | bytes 131104 | tf_op jit(solution)/shard_map/ppermute | solution.py:54
  33.4 1.1 collective-permute-start.13
  34.5 8.2 %collective-permute-done.13 = bf16[512,256]{1,0:T(8,128)(2,1)S(1)} collective-permute-done((bf16[512,256]{1,0:T(8,128)(2,1)S(1)}, bf16[512,256]{1,0:T(8,128)(2,1)S(1)}, u32[]{:S(2)}, u32[]{:S(2)}) %collective-permute-start.13) | collective-permute-done | bytes 262176 | tf_op jit(solution)/shard_map/ppermute | solution.py:20
  43.0 5.4 %collective-permute-start.15 = (bf16[1024,256]{1,0:T(8,128)(2,1)S(1)}, bf16[1024,256]{1,0:T(8,128)(2,1)S(1)}, u32[]{:S(2)}, u32[]{:S(2)}) collective-permute-start(bf16[1024,256]{1,0:T(8,128)(2,1)S(1)} %constant_dynamic-update-slice_fusion.2.refs_9_), channel_id=1, source_target_pairs={{0,12},{4,0},{8,4},{12,8},{1,13},{5,1},{9,5},{13,9},{2,14},{6,2},{... | collective-permute-start | bytes 1572872 | tf_op jit(solution)/shard_map/ppermute | solution.py:20
  49.6 7.7 %collective-permute-done.14.refs_10_ = bf16[1024,256]{1,0:T(8,128)(2,1)S(1)} collective-permute-done((bf16[1024,256]{1,0:T(8,128)(2,1)S(1)}, bf16[1024,256]{1,0:T(8,128)(2,1)S(1)}, u32[]{:S(2)}, u32[]{:S(2)}) %collective-permute-start.14) | collective-permute-done | bytes 524320 | tf_op jit(solution)/shard_map/ppermute | solution.py:20
  59.5 3.3 %collective-permute-start.17 = (bf16[512,256]{1,0:T(8,128)(2,1)}, bf16[512,256]{1,0:T(8,128)(2,1)}, u32[]{:S(2)}, u32[]{:S(2)}) collective-permute-start(bf16[512,256]{1,0:T(8,128)(2,1)} %slice.24), channel_id=1, source_target_pairs={{0,12},{4,0},{8,4},{12,8},{1,13},{5,1},{9,5},{13,9},{2,14},{6,2},{... | collective-permute-start | bytes 786440 | tf_op jit(solution)/shard_map/ppermute | solution.py:20
  62.8 3.3 %collective-permute-start.18 = (bf16[1024,256]{1,0:T(8,128)(2,1)S(1)}, bf16[1024,256]{1,0:T(8,128)(2,1)}, u32[]{:S(2)}, u32[]{:S(2)}) collective-permute-start(bf16[1024,256]{1,0:T(8,128)(2,1)S(1)} %constant_dynamic-update-slice_fusion.2.refs_9_), channel_id=1, source_target_pairs={{0,1},{1,0},{2,3},{3,2},{4,5},{5,4},{6,7},{7,6},{8,9},{9,8},{10,11... | collective-permute-start | bytes 1572872 | tf_op jit(solution)/shard_map/ppermute | solution.py:20
  67.1 1.2 %collective-permute-start.20 = (bf16[1024,256]{1,0:T(8,128)(2,1)S(1)}, bf16[1024,256]{1,0:T(8,128)(2,1)}, u32[]{:S(2)}, u32[]{:S(2)}) collective-permute-start(bf16[1024,256]{1,0:T(8,128)(2,1)S(1)} %collective-permute-done.15.refs_11_), channel_id=1, source_target_pairs={{0,1},{1,0},{2,3},{3,2},{4,5},{5,4},{6,7},{7,6},{8,9},{9,8},{10,11... | collective-permute-start | bytes 1572872 | tf_op jit(solution)/shard_map/ppermute | solution.py:20
  68.3 1.7 %constant_dynamic-update-slice_fusion.6 = bf16[1024,256]{1,0:T(8,128)(2,1)} fusion(bf16[512,256]{1,0:T(8,128)(2,1)} %collective-permute-done.16), kind=kLoop, calls=%fused_computation.15 | loop fusion | bytes 524288
  70.2 1.7 %constant_dynamic-update-slice_fusion.5.refs_12_ = bf16[1024,256]{1,0:T(8,128)(2,1)} fusion(bf16[1024,256]{1,0:T(8,128)(2,1)} %constant_dynamic-update-slice_fusion.6, bf16[512,256]{1,0:T(8,128)(2,1)} %collective-permute-done.17), kind=kLoop, calls=%fused_computation.14 | loop fusion | bytes 524288 | tf_op jit(solution)/shard_map/concatenate | solution.py:169
  74.3 6.8 %collective-permute-done.5.refs_5_ = bf16[1024,256]{1,0:T(8,128)(2,1)S(1)} collective-permute-done((bf16[1024,256]{1,0:T(8,128)(2,1)}, bf16[1024,256]{1,0:T(8,128)(2,1)S(1)}, u32[]{:S(2)}, u32[]{:S(2)}) %collective-permute-start.5) | collective-permute-done | bytes 524320 | tf_op jit(solution)/shard_map/ppermute | solution.py:20
  81.8 1.4 %collective-permute-start.7 = (bf16[512,256]{1,0:T(8,128)(2,1)}, bf16[512,256]{1,0:T(8,128)(2,1)}, u32[]{:S(2)}, u32[]{:S(2)}) collective-permute-start(bf16[512,256]{1,0:T(8,128)(2,1)} %slice.21), channel_id=1, source_target_pairs={{0,32},{32,64},{64,96},{96,128},{128,160},{160,192},{192,224},{224... | collective-permute-start | bytes 786440 | tf_op jit(solution)/shard_map/ppermute | solution.py:20
  84.2 2.0 %fusion.4 = (bf16[3,512,256]{2,1,0:T(8,128)(2,1)S(1)}, bf16[3,256,512]{1,2,0:T(8,128)(2,1)}) fusion(bf16[1,256,512]{1,2,0:T(8,128)(2,1)} %and_select_fusion, bf16[1,256,512]{1,2,0:T(8,128)(2,1)S(1)} %copy-done.11, bf16[1,256,512]{1,2,0:T(8,128)(2,1)} %copy-done.10), kind=kLoop, calls=%fused_computation.22 | loop fusion | flops 786432 | bytes 2359296 | tf_op jit(solution)/shard_map/transpose | solution.py:175
  86.2 1.4 %copy.7.tables_ref = bf16[3,256,512]{2,1,0:T(8,128)(2,1)S(1)} copy(bf16[3,256,512]{1,2,0:T(8,128)(2,1)} %get-tuple-element.14) | data formatting | bytes 1572864 | tf_op jit(solution)/shard_map/stack | solution.py:69
  88.3 2.0 %collective-permute-done.7.refs_7_ = bf16[512,256]{1,0:T(8,128)(2,1)} collective-permute-done((bf16[512,256]{1,0:T(8,128)(2,1)}, bf16[512,256]{1,0:T(8,128)(2,1)}, u32[]{:S(2)}, u32[]{:S(2)}) %collective-permute-start.7) | collective-permute-done | bytes 262176 | tf_op jit(solution)/shard_map/ppermute | solution.py:20
  90.3 1.0 copy-done.1
  95.5 13.0 %gram.1 = f32[512,512]{1,0:T(8,128)} custom-call(s32[6]{0:T(128)S(1)} %stack.33.meta_ref, bf16[3,256,512]{2,1,0:T(8,128)(2,1)S(1)} %copy.7.tables_ref, bf16[3,512,256]{2,1,0:T(8,128)(2,1)S(1)} %get-tuple-element.13.tables_t_ref, bf16[1024,256]{1,0:T(8,128)(2,1)S(1)} %copy-done.3, bf16[1024,256]{1,0:T(8,128)(2,1)S(1)} %copy-done.9, ...), custom_call_target="tpu_custom_call" | custom-call | tf_op jit(solution)/shard_map/gram/pallas_call | solution.py:133
  (78 shorter events, 14.8 us)
Async XLA Ops:
  1.9 22.8 %collective-permute-start = (bf16[512,256]{1,0:T(8,128)(2,1)}, bf16[512,256]{1,0:T(8,128)(2,1)S(1)}, u32[]{:S(2)}, u32[]{:S(2)}) collective-permute-start(bf16[512,256]{1,0:T(8,128)(2,1)} %get-tuple-element.8), channel_id=1, source_target_pairs={{0,16},{16,0},{1,17},{17,1},{2,18},{18,2},{3,19},{19,3},{4,20},{20... | collective-permute-start | bytes 786440 | tf_op jit(solution)/shard_map/ppermute | solution.py:20
  4.0 9.0 %collective-permute-start.9 = (bf16[256,256]{1,0:T(8,128)(2,1)}, bf16[256,256]{1,0:T(8,128)(2,1)S(1)}, u32[]{:S(2)}, u32[]{:S(2)}) collective-permute-start(bf16[256,256]{1,0:T(8,128)(2,1)} %get-tuple-element.9), channel_id=1, source_target_pairs={{0,0},{1,16},{2,2},{3,18},{4,4},{5,20},{6,6},{7,22},{8,8},{9,24},{... | collective-permute-start | bytes 393224 | tf_op jit(solution)/shard_map/ppermute | solution.py:45
  8.7 8.9 %collective-permute-start.11 = (bf16[256,256]{1,0:T(8,128)(2,1)}, bf16[256,256]{1,0:T(8,128)(2,1)S(1)}, u32[]{:S(2)}, u32[]{:S(2)}) collective-permute-start(bf16[256,256]{1,0:T(8,128)(2,1)} %get-tuple-element.10), channel_id=1, source_target_pairs={{0,8},{1,24},{2,10},{3,26},{4,12},{5,28},{6,14},{7,30},{8,0},{9,16... | collective-permute-start | bytes 393224 | tf_op jit(solution)/shard_map/ppermute | solution.py:45
  13.0 17.4 %collective-permute-start.10 = (bf16[256,256]{1,0:T(8,128)(2,1)S(1)}, bf16[256,256]{1,0:T(8,128)(2,1)S(1)}, u32[]{:S(2)}, u32[]{:S(2)}) collective-permute-start(bf16[256,256]{1,0:T(8,128)(2,1)S(1)} %collective-permute-done.9), channel_id=1, source_target_pairs={{0,0},{2,34},{4,68},{6,102},{8,136},{10,170},{12,204},{14,238},{34... | collective-permute-start | bytes 393224 | tf_op jit(solution)/shard_map/ppermute | solution.py:54
  17.6 15.8 %collective-permute-start.12 = (bf16[256,256]{1,0:T(8,128)(2,1)S(1)}, bf16[256,256]{1,0:T(8,128)(2,1)S(1)}, u32[]{:S(2)}, u32[]{:S(2)}) collective-permute-start(bf16[256,256]{1,0:T(8,128)(2,1)S(1)} %collective-permute-done.11), channel_id=1, source_target_pairs={{8,8},{10,42},{12,76},{14,110},{0,128},{2,162},{4,196},{6,230},{42... | collective-permute-start | bytes 393224 | tf_op jit(solution)/shard_map/ppermute | solution.py:54
  24.8 18.2 %collective-permute-start.2 = (bf16[1024,256]{1,0:T(8,128)(2,1)S(1)}, bf16[1024,256]{1,0:T(8,128)(2,1)S(1)}, u32[]{:S(2)}, u32[]{:S(2)}) collective-permute-start(bf16[1024,256]{1,0:T(8,128)(2,1)S(1)} %constant_dynamic-update-slice_fusion.refs_0_), channel_id=1, source_target_pairs={{0,224},{32,0},{64,32},{96,64},{128,96},{160,128},{192,160},{224,1... | collective-permute-start | bytes 1572872 | tf_op jit(solution)/shard_map/ppermute | solution.py:20
  33.4 9.4 %collective-permute-start.13 = (bf16[512,256]{1,0:T(8,128)(2,1)S(1)}, bf16[512,256]{1,0:T(8,128)(2,1)S(1)}, u32[]{:S(2)}, u32[]{:S(2)}) collective-permute-start(bf16[512,256]{1,0:T(8,128)(2,1)S(1)} %pad_maximum_fusion.1), channel_id=1, source_target_pairs={{0,2},{2,0},{1,3},{3,1},{4,6},{6,4},{5,7},{7,5},{8,10},{10,8},{9,1... | collective-permute-start | bytes 786440 | tf_op jit(solution)/shard_map/ppermute | solution.py:20
  34.5 13.9 %collective-permute-start.1 = (bf16[1024,256]{1,0:T(8,128)(2,1)S(1)}, bf16[1024,256]{1,0:T(8,128)(2,1)S(1)}, u32[]{:S(2)}, u32[]{:S(2)}) collective-permute-start(bf16[1024,256]{1,0:T(8,128)(2,1)S(1)} %constant_dynamic-update-slice_fusion.refs_0_), channel_id=1, source_target_pairs={{0,32},{32,64},{64,96},{96,128},{128,160},{160,192},{192,224},{224... | collective-permute-start | bytes 1572872 | tf_op jit(solution)/shard_map/ppermute | solution.py:20
  42.8 20.0 %copy-start.4 = (bf16[1024,256]{1,0:T(8,128)(2,1)}, bf16[1024,256]{1,0:T(8,128)(2,1)S(1)}, u32[]{:S(2)}) copy-start(bf16[1024,256]{1,0:T(8,128)(2,1)S(1)} %constant_dynamic-update-slice_fusion.2.refs_9_) | copy-start | bytes 1572868
  42.8 14.5 %collective-permute-start.14 = (bf16[1024,256]{1,0:T(8,128)(2,1)S(1)}, bf16[1024,256]{1,0:T(8,128)(2,1)S(1)}, u32[]{:S(2)}, u32[]{:S(2)}) collective-permute-start(bf16[1024,256]{1,0:T(8,128)(2,1)S(1)} %constant_dynamic-update-slice_fusion.2.refs_9_), channel_id=1, source_target_pairs={{0,4},{4,8},{8,12},{12,0},{1,5},{5,9},{9,13},{13,1},{2,6},{6,10},{... | collective-permute-start | bytes 1572872 | tf_op jit(solution)/shard_map/ppermute | solution.py:20
  42.9 16.6 %copy-start.6 = (bf16[1024,256]{1,0:T(8,128)(2,1)}, bf16[1024,256]{1,0:T(8,128)(2,1)S(1)}, u32[]{:S(2)}) copy-start(bf16[1024,256]{1,0:T(8,128)(2,1)S(1)} %collective-permute-done.2.refs_2_) | copy-start | bytes 1572868
  42.9 15.1 %collective-permute-start.4 = (bf16[1024,256]{1,0:T(8,128)(2,1)S(1)}, bf16[1024,256]{1,0:T(8,128)(2,1)}, u32[]{:S(2)}, u32[]{:S(2)}) collective-permute-start(bf16[1024,256]{1,0:T(8,128)(2,1)S(1)} %collective-permute-done.2.refs_2_), channel_id=1, source_target_pairs={{0,224},{32,0},{64,32},{96,64},{128,96},{160,128},{192,160},{224,1... | collective-permute-start | bytes 1572872 | tf_op jit(solution)/shard_map/ppermute | solution.py:20
  43.0 15.7 %collective-permute-start.15 = (bf16[1024,256]{1,0:T(8,128)(2,1)S(1)}, bf16[1024,256]{1,0:T(8,128)(2,1)S(1)}, u32[]{:S(2)}, u32[]{:S(2)}) collective-permute-start(bf16[1024,256]{1,0:T(8,128)(2,1)S(1)} %constant_dynamic-update-slice_fusion.2.refs_9_), channel_id=1, source_target_pairs={{0,12},{4,0},{8,4},{12,8},{1,13},{5,1},{9,5},{13,9},{2,14},{6,2},{... | collective-permute-start | bytes 1572872 | tf_op jit(solution)/shard_map/ppermute | solution.py:20
  48.4 17.7 %collective-permute-start.3 = (bf16[1024,256]{1,0:T(8,128)(2,1)S(1)}, bf16[1024,256]{1,0:T(8,128)(2,1)}, u32[]{:S(2)}, u32[]{:S(2)}) collective-permute-start(bf16[1024,256]{1,0:T(8,128)(2,1)S(1)} %collective-permute-done.1.refs_1_), channel_id=1, source_target_pairs={{0,32},{32,64},{64,96},{96,128},{128,160},{160,192},{192,224},{224... | collective-permute-start | bytes 1572872 | tf_op jit(solution)/shard_map/ppermute | solution.py:20
  58.0 9.1 %collective-permute-start.16 = (bf16[512,256]{1,0:T(8,128)(2,1)}, bf16[512,256]{1,0:T(8,128)(2,1)}, u32[]{:S(2)}, u32[]{:S(2)}) collective-permute-start(bf16[512,256]{1,0:T(8,128)(2,1)} %slice.23), channel_id=1, source_target_pairs={{0,4},{4,8},{8,12},{12,0},{1,5},{5,9},{9,13},{13,1},{2,6},{6,10},{... | collective-permute-start | bytes 786440 | tf_op jit(solution)/shard_map/ppermute | solution.py:20
  58.1 13.8 %collective-permute-start.6 = (bf16[1024,256]{1,0:T(8,128)(2,1)}, bf16[1024,256]{1,0:T(8,128)(2,1)S(1)}, u32[]{:S(2)}, u32[]{:S(2)}) collective-permute-start(bf16[1024,256]{1,0:T(8,128)(2,1)} %collective-permute-done.4.refs_4_), channel_id=1, source_target_pairs={{0,224},{32,0},{64,32},{96,64},{128,96},{160,128},{192,160},{224,1... | collective-permute-start | bytes 1572872 | tf_op jit(solution)/shard_map/ppermute | solution.py:20
  59.5 10.5 %collective-permute-start.17 = (bf16[512,256]{1,0:T(8,128)(2,1)}, bf16[512,256]{1,0:T(8,128)(2,1)}, u32[]{:S(2)}, u32[]{:S(2)}) collective-permute-start(bf16[512,256]{1,0:T(8,128)(2,1)} %slice.24), channel_id=1, source_target_pairs={{0,12},{4,0},{8,4},{12,8},{1,13},{5,1},{9,5},{13,9},{2,14},{6,2},{... | collective-permute-start | bytes 786440 | tf_op jit(solution)/shard_map/ppermute | solution.py:20
  62.8 19.1 %collective-permute-start.18 = (bf16[1024,256]{1,0:T(8,128)(2,1)S(1)}, bf16[1024,256]{1,0:T(8,128)(2,1)}, u32[]{:S(2)}, u32[]{:S(2)}) collective-permute-start(bf16[1024,256]{1,0:T(8,128)(2,1)S(1)} %constant_dynamic-update-slice_fusion.2.refs_9_), channel_id=1, source_target_pairs={{0,1},{1,0},{2,3},{3,2},{4,5},{5,4},{6,7},{7,6},{8,9},{9,8},{10,11... | collective-permute-start | bytes 1572872 | tf_op jit(solution)/shard_map/ppermute | solution.py:20
  66.1 14.9 %collective-permute-start.5 = (bf16[1024,256]{1,0:T(8,128)(2,1)}, bf16[1024,256]{1,0:T(8,128)(2,1)S(1)}, u32[]{:S(2)}, u32[]{:S(2)}) collective-permute-start(bf16[1024,256]{1,0:T(8,128)(2,1)} %collective-permute-done.3.refs_3_), channel_id=1, source_target_pairs={{0,32},{32,64},{64,96},{96,128},{128,160},{160,192},{192,224},{224... | collective-permute-start | bytes 1572872 | tf_op jit(solution)/shard_map/ppermute | solution.py:20
  67.1 20.6 %collective-permute-start.20 = (bf16[1024,256]{1,0:T(8,128)(2,1)S(1)}, bf16[1024,256]{1,0:T(8,128)(2,1)}, u32[]{:S(2)}, u32[]{:S(2)}) collective-permute-start(bf16[1024,256]{1,0:T(8,128)(2,1)S(1)} %collective-permute-done.15.refs_11_), channel_id=1, source_target_pairs={{0,1},{1,0},{2,3},{3,2},{4,5},{5,4},{6,7},{7,6},{8,9},{9,8},{10,11... | collective-permute-start | bytes 1572872 | tf_op jit(solution)/shard_map/ppermute | solution.py:20
  70.0 17.7 %collective-permute-start.19 = (bf16[1024,256]{1,0:T(8,128)(2,1)S(1)}, bf16[1024,256]{1,0:T(8,128)(2,1)}, u32[]{:S(2)}, u32[]{:S(2)}) collective-permute-start(bf16[1024,256]{1,0:T(8,128)(2,1)S(1)} %collective-permute-done.14.refs_10_), channel_id=1, source_target_pairs={{0,1},{1,0},{2,3},{3,2},{4,5},{5,4},{6,7},{7,6},{8,9},{9,8},{10,11... | collective-permute-start | bytes 1572872 | tf_op jit(solution)/shard_map/ppermute | solution.py:20
  71.9 15.8 %collective-permute-start.21 = (bf16[1024,256]{1,0:T(8,128)(2,1)}, bf16[1024,256]{1,0:T(8,128)(2,1)}, u32[]{:S(2)}, u32[]{:S(2)}) collective-permute-start(bf16[1024,256]{1,0:T(8,128)(2,1)} %constant_dynamic-update-slice_fusion.5.refs_12_), channel_id=1, source_target_pairs={{0,1},{1,0},{2,3},{3,2},{4,5},{5,4},{6,7},{7,6},{8,9},{9,8},{10,11... | collective-permute-start | bytes 1572872 | tf_op jit(solution)/shard_map/ppermute | solution.py:20
  81.0 7.3 %collective-permute-start.8 = (bf16[512,256]{1,0:T(8,128)(2,1)}, bf16[512,256]{1,0:T(8,128)(2,1)S(1)}, u32[]{:S(2)}, u32[]{:S(2)}) collective-permute-start(bf16[512,256]{1,0:T(8,128)(2,1)} %slice.22), channel_id=1, source_target_pairs={{0,224},{32,0},{64,32},{96,64},{128,96},{160,128},{192,160},{224,1... | collective-permute-start | bytes 786440 | tf_op jit(solution)/shard_map/ppermute | solution.py:20
  81.8 8.5 %collective-permute-start.7 = (bf16[512,256]{1,0:T(8,128)(2,1)}, bf16[512,256]{1,0:T(8,128)(2,1)}, u32[]{:S(2)}, u32[]{:S(2)}) collective-permute-start(bf16[512,256]{1,0:T(8,128)(2,1)} %slice.21), channel_id=1, source_target_pairs={{0,32},{32,64},{64,96},{96,128},{128,160},{160,192},{192,224},{224... | collective-permute-start | bytes 786440 | tf_op jit(solution)/shard_map/ppermute | solution.py:20
  (11 other events, 36.9 us)

commit v3 on v2

v3 whole, which is shorter than its diff:
```python
import functools

import jax
import jax.numpy as jnp
from jax import lax
from jax.experimental import pallas as pl
from jax.experimental.pallas import tpu as pltpu
from jax.sharding import Mesh, PartitionSpec as P

NZ, NYL, NX, NYH, NC = 8, 2, 4, 2, 2
EPOCH = ("z", "yl")
COL = ("x", "yh", "c")
NE = NZ * NYL
BF16, F32 = jnp.bfloat16, jnp.float32
DX = (0, -1, 1, 2)
LEFT_Z = (0, -1, 1, -2, 2, -3, 3)


def around(block, axis, n, step):
    return lax.ppermute(block, axis, [(i, (i + step) % n) for i in range(n)])


def line_of(z_from, z, half):
    return (z_from + z + half * (NZ // 2)) % NZ


def in_plane(block, half):
    axes = ("z", "yl", "x", "yh", "c")
    sizes = (NZ, NYL, NX, NYH, NC)

    def flat(place):
        index = 0
        for size, at in zip(sizes, place):
            index = index * size + at
        return index

    route = []
    for z in range(NZ):
        for yl in range(NYL):
            for x in range(NX):
                for yh in range(NYH):
                    for c in range(NC):
                        line = line_of(z, NYH * x + yh, half)
                        route.append((flat((z, yl, x, yh, c)), flat((z, c, line // NYH, line % NYH, yl))))
    return lax.ppermute(block, axes, route)


def along_z(block, half):
    route = []
    for z_from in range(NZ):
        for z in range(NZ):
            line = line_of(z_from, z, half)
            route.append(((z_from * NX + line // NYH) * NYH + line % NYH, (z * NX + line // NYH) * NYH + line % NYH))
    return lax.ppermute(block, ("z", "x", "yh"), route)


def tables_kernel(meta_ref, taps_ref, tables_ref, turned_ref):
    rows, width = tables_ref.shape[1:]
    lags = lax.broadcasted_iota(jnp.int32, (rows, width), 0)
    places = lax.broadcasted_iota(jnp.int32, (rows, width), 1)
    flip = (lags + places == rows).astype(BF16)
    flipped = jnp.dot(jnp.broadcast_to(taps_ref[...], (8, rows)), flip, preferred_element_type=F32)
    base = pltpu.roll(jnp.broadcast_to(flipped[:1], (rows, width)), 0, 1, stride=1, stride_axis=0)
    boundary = meta_ref[5]
    cut = meta_ref[6]
    for i in range(3):
        table = base
        if i:
            first = (cut + i - 1) * rows
            split = (first + lags >= boundary) & (first - rows + places < boundary)
            table = jnp.where(split, 0.0, base)
        tables_ref[i] = table.astype(BF16)
        turned_ref[i] = table.T.astype(BF16)


def make_tables(meta, taps, rows):
    vmem = pl.BlockSpec(memory_space=pltpu.VMEM)
    padded = jnp.pad(taps, (0, rows - taps.shape[0]))[None, :]
    return pl.pallas_call(
        tables_kernel,
        out_shape=[jax.ShapeDtypeStruct((3, rows, 2 * rows), BF16), jax.ShapeDtypeStruct((3, 2 * rows, rows), BF16)],
        in_specs=[pl.BlockSpec(memory_space=pltpu.SMEM), vmem],
        out_specs=[vmem, vmem],
        compiler_params=pltpu.CompilerParams(vmem_limit_bytes=8 * 1024 * 1024),
        name="tables",
    )(meta, padded)


def prepare_kernel(partials_ref, gaps_ref, first_ref, second_ref, turned_ref):
    rows, cols = partials_ref.shape
    kept = jnp.broadcast_to(gaps_ref[...].astype(F32), (128, rows))
    kept_t = kept.T.astype(BF16)
    for i in range(cols // 128):
        part = partials_ref[:, i * 128 : (i + 1) * 128] * kept_t
        turned_ref[i * 128 : (i + 1) * 128, :] = part.T
        half = (first_ref, second_ref)[i // (cols // 256)]
        at = i % (cols // 256) * 128
        half[:, at : at + 128] = part


def prepare(partials, gaps):
    rows, cols = partials.shape
    return pl.pallas_call(
        prepare_kernel,
        out_shape=[jax.ShapeDtypeStruct((rows, cols // 2), BF16)] * 2 + [jax.ShapeDtypeStruct((cols, rows), BF16)],
        compiler_params=pltpu.CompilerParams(vmem_limit_bytes=4 * 1024 * 1024),
        name="prepare",
    )(partials, gaps[None, :])


def table_of(e, meta_ref):
    cut = meta_ref[6]
    return jnp.where(e == cut, 1, jnp.where(e == cut + 1, 2, 0))


def left_kernel(meta_ref, tables_ref, *refs):
    near, far, crossed = refs[0:7], refs[7:9], refs[9:14]
    out_ref, raw = refs[14:]
    cols, rows = raw.shape[1:]
    half = cols // 2
    z, yl = meta_ref[0], meta_ref[1]
    raw[0] = jnp.zeros(raw.shape[1:], BF16)
    for i, dz in enumerate(LEFT_Z):
        at = 2 * ((z + dz) & 7) + 1
        raw[at + yl] = near[i][:cols]
        raw[at + 1 - yl, half:] = near[i][cols:]
        if dz == 0:
            raw[at + 1 - yl, :half] = crossed[0][:half]
        else:
            raw[at + 1 - yl, :half] = crossed[(i + 1) // 2][(i - 1) % 2 * half : ((i - 1) % 2 + 1) * half]
    at = 2 * ((z + 4) & 7) + 1
    split = far[0].shape[0]
    raw[at + yl, :split] = far[0][...]
    raw[at + yl, split:] = far[1][: cols - split]
    raw[at + 1 - yl, half:] = far[1][cols - split :]
    raw[at + 1 - yl, :half] = crossed[4][...]

    @pl.loop(0, NE)
    def _(e):
        table = tables_ref[table_of(e, meta_ref)]
        white = jnp.dot(raw[e], table[:rows], preferred_element_type=F32)
        white += jnp.dot(raw[e + 1], table[rows:], preferred_element_type=F32)
        out_ref[:, pl.ds(pl.multiple_of(e * rows, rows), rows)] = white.astype(BF16)


def right_kernel(meta_ref, tables_ref, *refs):
    pieces = refs[0:8]
    out_ref, raw = refs[8:]
    rows, half = raw.shape[2:]
    z, x, yh, core = [meta_ref[i] for i in (0, 2, 3, 4)]
    for h in range(2):
        raw[h, 0] = jnp.zeros(raw.shape[2:], BF16)
    for q in range(2):
        for s in range(4):
            for b in range(4):
                line = NYH * ((x + DX[s]) & 3) + (yh ^ (b // 2))
                e = 2 * ((line - z + (b % 2) * (NZ // 2)) & 7) + (core ^ q)
                raw[b % 2, e + 1] = pieces[q * 4 + s][b * rows : (b + 1) * rows]

    @pl.loop(0, NE)
    def _(e):
        table = tables_ref[table_of(e, meta_ref)]
        for h in range(2):
            white = jnp.dot(table[:, :rows], raw[h, e], preferred_element_type=F32)
            white += jnp.dot(table[:, rows:], raw[h, e + 1], preferred_element_type=F32)
            out_ref[pl.ds(pl.multiple_of(e * rows, rows), rows), h * half : (h + 1) * half] = white.astype(BF16)


def product_kernel(scale, left_ref, right_ref, out_ref):
    out_ref[...] = jnp.dot(left_ref[...], right_ref[...], preferred_element_type=F32) * scale


def whitened(kernel, name, meta, tables, pieces, shape, raw_shape):
    vmem = pl.BlockSpec(memory_space=pltpu.VMEM)
    return pl.pallas_call(
        kernel,
        out_shape=jax.ShapeDtypeStruct(shape, BF16),
        in_specs=[pl.BlockSpec(memory_space=pltpu.SMEM)] + [vmem] * (1 + len(pieces)),
        out_specs=vmem,
        scratch_shapes=[pltpu.VMEM(raw_shape, BF16)],
        compiler_params=pltpu.CompilerParams(vmem_limit_bytes=16 * 1024 * 1024),
        name=name,
    )(meta, tables, *pieces)


def product(left, right, scale):
    vmem = pl.BlockSpec(memory_space=pltpu.VMEM)
    return pl.pallas_call(
        functools.partial(product_kernel, scale),
        out_shape=jax.ShapeDtypeStruct((left.shape[0], right.shape[1]), F32),
        in_specs=[vmem, vmem],
        out_specs=vmem,
        compiler_params=pltpu.CompilerParams(vmem_limit_bytes=16 * 1024 * 1024),
        name="product",
    )(left, right)


def on_device(partials, gaps, arc_start, taps):
    rows, cols = partials.shape
    half = cols // 2
    places = [lax.axis_index(axis) for axis in EPOCH + COL]
    meta = jnp.stack(places + [arc_start[0], arc_start[0] // rows]).astype(jnp.int32)
    first, second, masked_t = prepare(partials, gaps)

    neighbour = around(masked_t, "yl", NYL, 1)
    up = down = jnp.concatenate([masked_t, neighbour[half:]], axis=0)
    near, crossed = [up], [neighbour]
    for step in range(1, 4):
        if step == 3:
            up, down, crossed[1] = lax.optimization_barrier((up, down, crossed[1]))
        up = around(up, "z", NZ, 1)
        down = around(down, "z", NZ, -1)
        near += [up, down]
        crossed.append(around(jnp.concatenate([up[:half], down[:half]], axis=0), "yl", NYL, 1))
    up, down, crossed[2] = lax.optimization_barrier((up, down, crossed[2]))
    split = (cols + half) // 2
    ends = lax.optimization_barrier((up[:split], down[split:]))
    far = lax.optimization_barrier([around(ends[0], "z", NZ, 1), around(ends[1], "z", NZ, -1)])
    crossed.append(around(far[0][:half], "yl", NYL, 1))

    tables, tables_t = make_tables(meta, taps, rows)
    halves = [along_z(in_plane(piece, h), h) for h, piece in enumerate((first, second))]
    halves, tables, tables_t = lax.optimization_barrier((halves, tables, tables_t))
    here = jnp.concatenate(halves, axis=0)
    pair = jnp.concatenate([here, around(here, "yh", NYH, 1)], axis=0)
    own = [pair] + [around(pair, "x", NX, step) for step in (1, -1, 2)]
    other = [around(piece, "c", NC, 1) for piece in own]

    left = whitened(left_kernel, "left", meta, tables_t, near + far + crossed, (cols, NE * rows), (NE + 1, cols, rows))
    right = whitened(right_kernel, "right", meta, tables, own + other, (NE * rows, cols), (2, NE + 1, rows, half))
    return product(left, right, (rows * NE) ** (-0.5))


def solution(mesh):
    fine = Mesh(mesh.devices.reshape(NZ, NYL, NX, NYH, NC), EPOCH + COL)
    in_specs = (P(EPOCH, COL), P(EPOCH), P(), P())
    return jax.shard_map(on_device, mesh=fine, in_specs=in_specs, out_specs=P(COL, EPOCH), check_vma=False)
```

time: 109 us -> 114 us (1.046)
  starting transfers between devices: 40.6 us -> 58.3 us
  local copies, waits for them, and re-layouts: 16.1 us -> 2.53 us
  other arithmetic: 3.86 us -> 0.1 us
  waiting for transfers between devices: 32.2 us -> 35.4 us
  Pallas kernels: 14.8 us -> 16 us
    ppermute x18 -> x21, starting transfers between devices: 24.7 us -> 43.6 us  [around(): return lax.ppermute(block, axis, [(i, (i + step) % n) for i in range(n)])]
    unnamed x32 -> x6, local copies, waits for them, and re-layouts: 8.94 us -> 1.65 us
    ppermute x2, waiting for transfers between devices: 3.87 us -> 0.01 us  [in_plane(): return lax.ppermute(block, axes, route)]
    ppermute x18 -> x21, waiting for transfers between devices: 25.3 us -> 29 us  [around(): return lax.ppermute(block, axis, [(i, (i + step) % n) for i in range(n)])]
    ppermute x2, waiting for transfers between devices: 3.01 us -> 6.43 us  [along_z(): return lax.ppermute(block, ('z', 'x', 'yh'), route)]
    slice x5 -> x10, local copies, waits for them, and re-layouts: 3.01 us -> 0.11 us  [the longest x3 0.03 us: on_device(): up[:half]]
    pallas_call x1 -> x4, Pallas kernels: 13 us -> 15.7 us  [the longest x2 11.4 us: whitened(): pl.pallas_call(kernel, out_shape=jax.ShapeDtypeStruct(shape, BF16), in_sp...]
    ppermute x2, starting transfers between devices: 7.8 us -> 5.38 us  [along_z(): return lax.ppermute(block, ('z', 'x', 'yh'), route)]
  transfers between devices with their start and end apart: 22 -> 25, of which waited for: 7 -> 8; matrix products, arithmetic and copies ran while one was open for 13% -> 1% of each run, Pallas kernels for 0% -> 6%
where the time goes in v3:
time: 114 us; the launch traced here: 113 us
  starting transfers between devices  58.3 us (51%)
  waiting for transfers between devices  35.4 us (31%)
  Pallas kernels  16 us (14%)
  local copies, waits for them, and re-layouts  2.53 us (2%)
    ppermute x21, starting transfers between devices, around(): return lax.ppermute(block, axis, [(i, (i + step) % n) for i in range(n)])  43.6 us
    ppermute x21, waiting for transfers between devices, around(): return lax.ppermute(block, axis, [(i, (i + step) % n) for i in range(n)])  29 us
    pallas_call x2, Pallas kernels, whitened(): pl.pallas_call(kernel, out_shape=jax.ShapeDtypeStruct(shape, BF16), in_sp...  11.4 us
    ppermute x2, starting transfers between devices, in_plane(): return lax.ppermute(block, axes, route)  9.29 us
    ppermute x2, waiting for transfers between devices, along_z(): return lax.ppermute(block, ('z', 'x', 'yh'), route)  6.43 us
    ppermute x2, starting transfers between devices, along_z(): return lax.ppermute(block, ('z', 'x', 'yh'), route)  5.38 us
    pallas_call x1, Pallas kernels, product(): pl.pallas_call(functools.partial(product_kernel, scale), out_shape=jax.Sh...  3.3 us
  transfers between devices with their start and end apart: 25, of which 8 were waited for; matrix products, arithmetic and copies ran while one was open for 1% of the time, Pallas kernels for 6%

profile of v3, /device:TPU:1, one launch (start us, length us, event | category | flops | bytes accessed | tf_op | source)
XLA Modules:
  0.0 113.3 jit_solution(16774438307557772104)
XLA Ops:
  1.9 2.2 %collective-permute-start.4 = (bf16[512,256]{1,0:T(8,128)(2,1)S(1)}, bf16[512,256]{1,0:T(8,128)(2,1)S(1)}, u32[]{:S(2)}, u32[]{:S(2)}) collective-permute-start(bf16[512,256]{1,0:T(8,128)(2,1)S(1)} %get-tuple-element.29), channel_id=1, source_target_pairs={{0,16},{16,0},{1,17},{17,1},{2,18},{18,2},{3,19},{19,3},{4,20},{20... | collective-permute-start | bytes 786440 | tf_op jit(solution)/shard_map/ppermute | solution.py:20
  4.1 4.8 %collective-permute-done.4.refs_9_ = bf16[512,256]{1,0:T(8,128)(2,1)S(1)} collective-permute-done((bf16[512,256]{1,0:T(8,128)(2,1)S(1)}, bf16[512,256]{1,0:T(8,128)(2,1)S(1)}, u32[]{:S(2)}, u32[]{:S(2)}) %collective-permute-start.4) | collective-permute-done | bytes 262176 | tf_op jit(solution)/shard_map/ppermute | solution.py:20
  8.9 6.7 %collective-permute-start.6 = (bf16[768,256]{1,0:T(8,128)(2,1)S(1)}, bf16[768,256]{1,0:T(8,128)(2,1)S(1)}, u32[]{:S(2)}, u32[]{:S(2)}) collective-permute-start(bf16[768,256]{1,0:T(8,128)(2,1)S(1)} %pad_maximum_fusion.refs_0_), channel_id=1, source_target_pairs={{0,224},{32,0},{64,32},{96,64},{128,96},{160,128},{192,160},{224,1... | collective-permute-start | bytes 1179656 | tf_op jit(solution)/shard_map/ppermute | solution.py:20
  15.7 4.9 %collective-permute-start = (bf16[256,256]{1,0:T(8,128)(2,1)S(1)}, bf16[256,256]{1,0:T(8,128)(2,1)S(1)}, u32[]{:S(2)}, u32[]{:S(2)}) collective-permute-start(bf16[256,256]{1,0:T(8,128)(2,1)S(1)} %get-tuple-element.24), channel_id=1, source_target_pairs={{0,0},{1,16},{2,2},{3,18},{4,4},{5,20},{6,6},{7,22},{8,8},{9,24},{... | collective-permute-start | bytes 393224 | tf_op jit(solution)/shard_map/ppermute | solution.py:45
  20.6 4.4 %collective-permute-start.2 = (bf16[256,256]{1,0:T(8,128)(2,1)S(1)}, bf16[256,256]{1,0:T(8,128)(2,1)S(1)}, u32[]{:S(2)}, u32[]{:S(2)}) collective-permute-start(bf16[256,256]{1,0:T(8,128)(2,1)S(1)} %get-tuple-element.25), channel_id=1, source_target_pairs={{0,8},{1,24},{2,10},{3,26},{4,12},{5,28},{6,14},{7,30},{8,0},{9,16... | collective-permute-start | bytes 393224 | tf_op jit(solution)/shard_map/ppermute | solution.py:45
  25.0 4.2 %collective-permute-start.8 = (bf16[768,256]{1,0:T(8,128)(2,1)S(1)}, bf16[768,256]{1,0:T(8,128)(2,1)S(1)}, u32[]{:S(2)}, u32[]{:S(2)}) collective-permute-start(bf16[768,256]{1,0:T(8,128)(2,1)S(1)} %collective-permute-done.6.refs_2_), channel_id=1, source_target_pairs={{0,224},{32,0},{64,32},{96,64},{128,96},{160,128},{192,160},{224,1... | collective-permute-start | bytes 1179656 | tf_op jit(solution)/shard_map/ppermute | solution.py:20
  29.9 4.7 %collective-permute-start.3 = (bf16[256,256]{1,0:T(8,128)(2,1)S(1)}, bf16[256,256]{1,0:T(8,128)(2,1)S(1)}, u32[]{:S(2)}, u32[]{:S(2)}) collective-permute-start(bf16[256,256]{1,0:T(8,128)(2,1)S(1)} %collective-permute-done.2), channel_id=1, source_target_pairs={{8,8},{10,42},{12,76},{14,110},{0,128},{2,162},{4,196},{6,230},{42... | collective-permute-start | bytes 393224 | tf_op jit(solution)/shard_map/ppermute | solution.py:54
  37.1 6.4 %collective-permute-done.3 = bf16[256,256]{1,0:T(8,128)(2,1)S(1)} collective-permute-done((bf16[256,256]{1,0:T(8,128)(2,1)S(1)}, bf16[256,256]{1,0:T(8,128)(2,1)S(1)}, u32[]{:S(2)}, u32[]{:S(2)}) %collective-permute-start.3) | collective-permute-done | bytes 131104 | tf_op jit(solution)/shard_map/ppermute | solution.py:54
  45.5 8.1 %collective-permute-done.9.refs_10_ = bf16[512,256]{1,0:T(8,128)(2,1)S(1)} collective-permute-done((bf16[512,256]{1,0:T(8,128)(2,1)S(1)}, bf16[512,256]{1,0:T(8,128)(2,1)S(1)}, u32[]{:S(2)}, u32[]{:S(2)}) %collective-permute-start.9) | collective-permute-done | bytes 262176 | tf_op jit(solution)/shard_map/ppermute | solution.py:20
  53.6 6.0 %collective-permute-start.10 = (bf16[768,256]{1,0:T(8,128)(2,1)S(1)}, bf16[768,256]{1,0:T(8,128)(2,1)S(1)}, u32[]{:S(2)}, u32[]{:S(2)}) collective-permute-start(bf16[768,256]{1,0:T(8,128)(2,1)S(1)} %collective-permute-done.7.refs_3_), channel_id=1, source_target_pairs={{0,32},{32,64},{64,96},{96,128},{128,160},{160,192},{192,224},{224... | collective-permute-start | bytes 1179656 | tf_op jit(solution)/shard_map/ppermute | solution.py:20
  59.8 2.1 %collective-permute-start.19 = (bf16[1024,256]{1,0:T(8,128)(2,1)S(1)}, bf16[1024,256]{1,0:T(8,128)(2,1)S(1)}, u32[]{:S(2)}, u32[]{:S(2)}) collective-permute-start(bf16[1024,256]{1,0:T(8,128)(2,1)S(1)} %constant_dynamic-update-slice_fusion.refs_0_), channel_id=1, source_target_pairs={{0,12},{4,0},{8,4},{12,8},{1,13},{5,1},{9,5},{13,9},{2,14},{6,2},{... | collective-permute-start | bytes 1572872 | tf_op jit(solution)/shard_map/ppermute | solution.py:20
  61.9 2.5 %collective-permute-done.10.refs_5_ = bf16[768,256]{1,0:T(8,128)(2,1)S(1)} collective-permute-done((bf16[768,256]{1,0:T(8,128)(2,1)S(1)}, bf16[768,256]{1,0:T(8,128)(2,1)S(1)}, u32[]{:S(2)}, u32[]{:S(2)}) %collective-permute-start.10) | collective-permute-done | bytes 393248 | tf_op jit(solution)/shard_map/ppermute | solution.py:20
  64.4 2.2 %collective-permute-done.11.refs_6_ = bf16[768,256]{1,0:T(8,128)(2,1)S(1)} collective-permute-done((bf16[768,256]{1,0:T(8,128)(2,1)S(1)}, bf16[768,256]{1,0:T(8,128)(2,1)S(1)}, u32[]{:S(2)}, u32[]{:S(2)}) %collective-permute-start.11) | collective-permute-done | bytes 393248 | tf_op jit(solution)/shard_map/ppermute | solution.py:20
  66.7 7.5 %collective-permute-start.21 = (bf16[1024,256]{1,0:T(8,128)(2,1)S(1)}, bf16[1024,256]{1,0:T(8,128)(2,1)S(1)}, u32[]{:S(2)}, u32[]{:S(2)}) collective-permute-start(bf16[1024,256]{1,0:T(8,128)(2,1)S(1)} %constant_dynamic-update-slice_fusion.refs_0_), channel_id=1, source_target_pairs={{0,1},{1,0},{2,3},{3,2},{4,5},{5,4},{6,7},{7,6},{8,9},{9,8},{10,11... | collective-permute-start | bytes 1572872 | tf_op jit(solution)/shard_map/ppermute | solution.py:20
  74.2 6.6 %collective-permute-start.24 = (bf16[1024,256]{1,0:T(8,128)(2,1)S(1)}, bf16[1024,256]{1,0:T(8,128)(2,1)S(1)}, u32[]{:S(2)}, u32[]{:S(2)}) collective-permute-start(bf16[1024,256]{1,0:T(8,128)(2,1)S(1)} %collective-permute-done.20.refs_3_), channel_id=1, source_target_pairs={{0,1},{1,0},{2,3},{3,2},{4,5},{5,4},{6,7},{7,6},{8,9},{9,8},{10,11... | collective-permute-start | bytes 1572872 | tf_op jit(solution)/shard_map/ppermute | solution.py:20
  80.8 2.8 %collective-permute-done.19.refs_2_ = bf16[1024,256]{1,0:T(8,128)(2,1)S(1)} collective-permute-done((bf16[1024,256]{1,0:T(8,128)(2,1)S(1)}, bf16[1024,256]{1,0:T(8,128)(2,1)S(1)}, u32[]{:S(2)}, u32[]{:S(2)}) %collective-permute-start.19) | collective-permute-done | bytes 524320 | tf_op jit(solution)/shard_map/ppermute | solution.py:20
  83.6 2.2 %collective-permute-start.23 = (bf16[1024,256]{1,0:T(8,128)(2,1)S(1)}, bf16[1024,256]{1,0:T(8,128)(2,1)S(1)}, u32[]{:S(2)}, u32[]{:S(2)}) collective-permute-start(bf16[1024,256]{1,0:T(8,128)(2,1)S(1)} %collective-permute-done.19.refs_2_), channel_id=1, source_target_pairs={{0,1},{1,0},{2,3},{3,2},{4,5},{5,4},{6,7},{7,6},{8,9},{9,8},{10,11... | collective-permute-start | bytes 1572872 | tf_op jit(solution)/shard_map/ppermute | solution.py:20
  85.8 1.1 collective-permute-start.22
  87.7 5.7 %collective-permute-done.14.refs_8_ = bf16[384,256]{1,0:T(8,128)(2,1)S(1)} collective-permute-done((bf16[384,256]{1,0:T(8,128)(2,1)S(1)}, bf16[384,256]{1,0:T(8,128)(2,1)S(1)}, u32[]{:S(2)}, u32[]{:S(2)}) %collective-permute-start.14) | collective-permute-done | bytes 196640 | tf_op jit(solution)/shard_map/ppermute | solution.py:20
  93.4 2.2 %collective-permute-start.15 = (bf16[512,256]{1,0:T(8,128)(2,1)S(1)}, bf16[512,256]{1,0:T(8,128)(2,1)S(1)}, u32[]{:S(2)}, u32[]{:S(2)}) collective-permute-start(bf16[512,256]{1,0:T(8,128)(2,1)S(1)} %pad_maximum_fusion.3), channel_id=1, source_target_pairs={{0,16},{16,0},{1,17},{17,1},{2,18},{18,2},{3,19},{19,3},{4,20},{20... | collective-permute-start | bytes 786440 | tf_op jit(solution)/shard_map/ppermute | solution.py:20
  95.7 5.7 %right.1.right_ref = bf16[4096,512]{1,0:T(8,128)(2,1)S(1)} custom-call(s32[7]{0:T(128)S(1)} %stack.27.meta_ref, bf16[3,256,512]{2,1,0:T(8,128)(2,1)S(1)} %get-tuple-element.40.tables_ref, bf16[1024,256]{1,0:T(8,128)(2,1)S(1)} %constant_dynamic-update-slice_fusion.refs_0_, bf16[1024,256]{1,0:T(8,128)(2,1)S(1)} %collective-permute-done.18.refs_1_, ...), custom_call_target="tpu_custom_call" | custom-call | tf_op jit(solution)/shard_map/right/pallas_call | solution.py:175
  101.5 2.8 %collective-permute-done.16.refs_13_ = bf16[256,256]{1,0:T(8,128)(2,1)S(1)} collective-permute-done((bf16[256,256]{1,0:T(8,128)(2,1)S(1)}, bf16[256,256]{1,0:T(8,128)(2,1)S(1)}, u32[]{:S(2)}, u32[]{:S(2)}) %collective-permute-start.16) | collective-permute-done | bytes 131104 | tf_op jit(solution)/shard_map/ppermute | solution.py:20
  104.3 5.7 %left.1.left_ref = bf16[512,4096]{1,0:T(8,128)(2,1)S(1)} custom-call(s32[7]{0:T(128)S(1)} %stack.27.meta_ref, bf16[3,512,256]{2,1,0:T(8,128)(2,1)S(1)} %get-tuple-element.28.tables_ref, bf16[768,256]{1,0:T(8,128)(2,1)S(1)} %pad_maximum_fusion.refs_0_, bf16[768,256]{1,0:T(8,128)(2,1)S(1)} %collective-permute-done.5.refs_1_, ...), custom_call_target="tpu_custom_call" | custom-call | tf_op jit(solution)/shard_map/left/pallas_call | solution.py:175
  110.0 3.3 %product.1 = f32[512,512]{1,0:T(8,128)} custom-call(bf16[512,4096]{1,0:T(8,128)(2,1)S(1)} %left.1.left_ref, bf16[4096,512]{1,0:T(8,128)(2,1)S(1)} %right.1.right_ref), custom_call_target="tpu_custom_call" | custom-call | tf_op jit(solution)/shard_map/product/pallas_call | solution.py:188
  (56 shorter events, 7.4 us)
Async XLA Ops:
  1.9 7.0 %collective-permute-start.4 = (bf16[512,256]{1,0:T(8,128)(2,1)S(1)}, bf16[512,256]{1,0:T(8,128)(2,1)S(1)}, u32[]{:S(2)}, u32[]{:S(2)}) collective-permute-start(bf16[512,256]{1,0:T(8,128)(2,1)S(1)} %get-tuple-element.29), channel_id=1, source_target_pairs={{0,16},{16,0},{1,17},{17,1},{2,18},{18,2},{3,19},{19,3},{4,20},{20... | collective-permute-start | bytes 786440 | tf_op jit(solution)/shard_map/ppermute | solution.py:20
  8.9 16.1 %collective-permute-start.6 = (bf16[768,256]{1,0:T(8,128)(2,1)S(1)}, bf16[768,256]{1,0:T(8,128)(2,1)S(1)}, u32[]{:S(2)}, u32[]{:S(2)}) collective-permute-start(bf16[768,256]{1,0:T(8,128)(2,1)S(1)} %pad_maximum_fusion.refs_0_), channel_id=1, source_target_pairs={{0,224},{32,0},{64,32},{96,64},{128,96},{160,128},{192,160},{224,1... | collective-permute-start | bytes 1179656 | tf_op jit(solution)/shard_map/ppermute | solution.py:20
  15.7 13.5 %collective-permute-start.5 = (bf16[768,256]{1,0:T(8,128)(2,1)S(1)}, bf16[768,256]{1,0:T(8,128)(2,1)S(1)}, u32[]{:S(2)}, u32[]{:S(2)}) collective-permute-start(bf16[768,256]{1,0:T(8,128)(2,1)S(1)} %pad_maximum_fusion.refs_0_), channel_id=1, source_target_pairs={{0,32},{32,64},{64,96},{96,128},{128,160},{160,192},{192,224},{224... | collective-permute-start | bytes 1179656 | tf_op jit(solution)/shard_map/ppermute | solution.py:20
  15.7 13.5 %collective-permute-start = (bf16[256,256]{1,0:T(8,128)(2,1)S(1)}, bf16[256,256]{1,0:T(8,128)(2,1)S(1)}, u32[]{:S(2)}, u32[]{:S(2)}) collective-permute-start(bf16[256,256]{1,0:T(8,128)(2,1)S(1)} %get-tuple-element.24), channel_id=1, source_target_pairs={{0,0},{1,16},{2,2},{3,18},{4,4},{5,20},{6,6},{7,22},{8,8},{9,24},{... | collective-permute-start | bytes 393224 | tf_op jit(solution)/shard_map/ppermute | solution.py:45
  20.6 9.3 %collective-permute-start.2 = (bf16[256,256]{1,0:T(8,128)(2,1)S(1)}, bf16[256,256]{1,0:T(8,128)(2,1)S(1)}, u32[]{:S(2)}, u32[]{:S(2)}) collective-permute-start(bf16[256,256]{1,0:T(8,128)(2,1)S(1)} %get-tuple-element.25), channel_id=1, source_target_pairs={{0,8},{1,24},{2,10},{3,26},{4,12},{5,28},{6,14},{7,30},{8,0},{9,16... | collective-permute-start | bytes 393224 | tf_op jit(solution)/shard_map/ppermute | solution.py:45
  25.0 19.5 %collective-permute-start.8 = (bf16[768,256]{1,0:T(8,128)(2,1)S(1)}, bf16[768,256]{1,0:T(8,128)(2,1)S(1)}, u32[]{:S(2)}, u32[]{:S(2)}) collective-permute-start(bf16[768,256]{1,0:T(8,128)(2,1)S(1)} %collective-permute-done.6.refs_2_), channel_id=1, source_target_pairs={{0,224},{32,0},{64,32},{96,64},{128,96},{160,128},{192,160},{224,1... | collective-permute-start | bytes 1179656 | tf_op jit(solution)/shard_map/ppermute | solution.py:20
  29.2 15.3 %collective-permute-start.7 = (bf16[768,256]{1,0:T(8,128)(2,1)S(1)}, bf16[768,256]{1,0:T(8,128)(2,1)S(1)}, u32[]{:S(2)}, u32[]{:S(2)}) collective-permute-start(bf16[768,256]{1,0:T(8,128)(2,1)S(1)} %collective-permute-done.5.refs_1_), channel_id=1, source_target_pairs={{0,32},{32,64},{64,96},{96,128},{128,160},{160,192},{192,224},{224... | collective-permute-start | bytes 1179656 | tf_op jit(solution)/shard_map/ppermute | solution.py:20
  29.2 7.9 %collective-permute-start.1 = (bf16[256,256]{1,0:T(8,128)(2,1)S(1)}, bf16[256,256]{1,0:T(8,128)(2,1)S(1)}, u32[]{:S(2)}, u32[]{:S(2)}) collective-permute-start(bf16[256,256]{1,0:T(8,128)(2,1)S(1)} %collective-permute-done), channel_id=1, source_target_pairs={{0,0},{2,34},{4,68},{6,102},{8,136},{10,170},{12,204},{14,238},{34... | collective-permute-start | bytes 393224 | tf_op jit(solution)/shard_map/ppermute | solution.py:54
  29.9 13.6 %collective-permute-start.3 = (bf16[256,256]{1,0:T(8,128)(2,1)S(1)}, bf16[256,256]{1,0:T(8,128)(2,1)S(1)}, u32[]{:S(2)}, u32[]{:S(2)}) collective-permute-start(bf16[256,256]{1,0:T(8,128)(2,1)S(1)} %collective-permute-done.2), channel_id=1, source_target_pairs={{8,8},{10,42},{12,76},{14,110},{0,128},{2,162},{4,196},{6,230},{42... | collective-permute-start | bytes 393224 | tf_op jit(solution)/shard_map/ppermute | solution.py:54
  43.5 16.1 %collective-permute-start.17 = (bf16[512,256]{1,0:T(8,128)(2,1)S(1)}, bf16[512,256]{1,0:T(8,128)(2,1)S(1)}, u32[]{:S(2)}, u32[]{:S(2)}) collective-permute-start(bf16[512,256]{1,0:T(8,128)(2,1)S(1)} %pad_maximum_fusion.4), channel_id=1, source_target_pairs={{0,2},{2,0},{1,3},{3,1},{4,6},{6,4},{5,7},{7,5},{8,10},{10,8},{9,1... | collective-permute-start | bytes 786440 | tf_op jit(solution)/shard_map/ppermute | solution.py:20
  43.7 9.9 %collective-permute-start.9 = (bf16[512,256]{1,0:T(8,128)(2,1)S(1)}, bf16[512,256]{1,0:T(8,128)(2,1)S(1)}, u32[]{:S(2)}, u32[]{:S(2)}) collective-permute-start(bf16[512,256]{1,0:T(8,128)(2,1)S(1)} %pad_maximum_fusion.1), channel_id=1, source_target_pairs={{0,16},{16,0},{1,17},{17,1},{2,18},{18,2},{3,19},{19,3},{4,20},{20... | collective-permute-start | bytes 786440 | tf_op jit(solution)/shard_map/ppermute | solution.py:20
  44.6 17.3 %collective-permute-start.12 = (bf16[512,256]{1,0:T(8,128)(2,1)S(1)}, bf16[512,256]{1,0:T(8,128)(2,1)S(1)}, u32[]{:S(2)}, u32[]{:S(2)}) collective-permute-start(bf16[512,256]{1,0:T(8,128)(2,1)S(1)} %pad_maximum_fusion.2), channel_id=1, source_target_pairs={{0,16},{16,0},{1,17},{17,1},{2,18},{18,2},{3,19},{19,3},{4,20},{20... | collective-permute-start | bytes 786440 | tf_op jit(solution)/shard_map/ppermute | solution.py:20
  53.6 10.8 %collective-permute-start.10 = (bf16[768,256]{1,0:T(8,128)(2,1)S(1)}, bf16[768,256]{1,0:T(8,128)(2,1)S(1)}, u32[]{:S(2)}, u32[]{:S(2)}) collective-permute-start(bf16[768,256]{1,0:T(8,128)(2,1)S(1)} %collective-permute-done.7.refs_3_), channel_id=1, source_target_pairs={{0,32},{32,64},{64,96},{96,128},{128,160},{160,192},{192,224},{224... | collective-permute-start | bytes 1179656 | tf_op jit(solution)/shard_map/ppermute | solution.py:20
  59.6 6.9 %collective-permute-start.11 = (bf16[768,256]{1,0:T(8,128)(2,1)S(1)}, bf16[768,256]{1,0:T(8,128)(2,1)S(1)}, u32[]{:S(2)}, u32[]{:S(2)}) collective-permute-start(bf16[768,256]{1,0:T(8,128)(2,1)S(1)} %collective-permute-done.8.refs_4_), channel_id=1, source_target_pairs={{0,224},{32,0},{64,32},{96,64},{128,96},{160,128},{192,160},{224,1... | collective-permute-start | bytes 1179656 | tf_op jit(solution)/shard_map/ppermute | solution.py:20
  59.7 14.5 %collective-permute-start.20 = (bf16[1024,256]{1,0:T(8,128)(2,1)S(1)}, bf16[1024,256]{1,0:T(8,128)(2,1)S(1)}, u32[]{:S(2)}, u32[]{:S(2)}) collective-permute-start(bf16[1024,256]{1,0:T(8,128)(2,1)S(1)} %constant_dynamic-update-slice_fusion.refs_0_), channel_id=1, source_target_pairs={{0,8},{4,12},{8,0},{12,4},{1,9},{5,13},{9,1},{13,5},{2,10},{6,14},... | collective-permute-start | bytes 1572872 | tf_op jit(solution)/shard_map/ppermute | solution.py:20
  59.8 23.8 %collective-permute-start.19 = (bf16[1024,256]{1,0:T(8,128)(2,1)S(1)}, bf16[1024,256]{1,0:T(8,128)(2,1)S(1)}, u32[]{:S(2)}, u32[]{:S(2)}) collective-permute-start(bf16[1024,256]{1,0:T(8,128)(2,1)S(1)} %constant_dynamic-update-slice_fusion.refs_0_), channel_id=1, source_target_pairs={{0,12},{4,0},{8,4},{12,8},{1,13},{5,1},{9,5},{13,9},{2,14},{6,2},{... | collective-permute-start | bytes 1572872 | tf_op jit(solution)/shard_map/ppermute | solution.py:20
  61.9 23.9 %collective-permute-start.18 = (bf16[1024,256]{1,0:T(8,128)(2,1)S(1)}, bf16[1024,256]{1,0:T(8,128)(2,1)S(1)}, u32[]{:S(2)}, u32[]{:S(2)}) collective-permute-start(bf16[1024,256]{1,0:T(8,128)(2,1)S(1)} %constant_dynamic-update-slice_fusion.refs_0_), channel_id=1, source_target_pairs={{0,4},{4,8},{8,12},{12,0},{1,5},{5,9},{9,13},{13,1},{2,6},{6,10},{... | collective-permute-start | bytes 1572872 | tf_op jit(solution)/shard_map/ppermute | solution.py:20
  66.6 20.2 %collective-permute-start.13 = (bf16[384,256]{1,0:T(8,128)(2,1)S(1)}, bf16[384,256]{1,0:T(8,128)(2,1)S(1)}, u32[]{:S(2)}, u32[]{:S(2)}) collective-permute-start(bf16[384,256]{1,0:T(8,128)(2,1)S(1)} %slice.35), channel_id=1, source_target_pairs={{0,32},{32,64},{64,96},{96,128},{128,160},{160,192},{192,224},{224... | collective-permute-start | bytes 589832 | tf_op jit(solution)/shard_map/ppermute | solution.py:20
  66.7 28.9 %collective-permute-start.21 = (bf16[1024,256]{1,0:T(8,128)(2,1)S(1)}, bf16[1024,256]{1,0:T(8,128)(2,1)S(1)}, u32[]{:S(2)}, u32[]{:S(2)}) collective-permute-start(bf16[1024,256]{1,0:T(8,128)(2,1)S(1)} %constant_dynamic-update-slice_fusion.refs_0_), channel_id=1, source_target_pairs={{0,1},{1,0},{2,3},{3,2},{4,5},{5,4},{6,7},{7,6},{8,9},{9,8},{10,11... | collective-permute-start | bytes 1572872 | tf_op jit(solution)/shard_map/ppermute | solution.py:20
  74.2 21.5 %collective-permute-start.24 = (bf16[1024,256]{1,0:T(8,128)(2,1)S(1)}, bf16[1024,256]{1,0:T(8,128)(2,1)S(1)}, u32[]{:S(2)}, u32[]{:S(2)}) collective-permute-start(bf16[1024,256]{1,0:T(8,128)(2,1)S(1)} %collective-permute-done.20.refs_3_), channel_id=1, source_target_pairs={{0,1},{1,0},{2,3},{3,2},{4,5},{5,4},{6,7},{7,6},{8,9},{9,8},{10,11... | collective-permute-start | bytes 1572872 | tf_op jit(solution)/shard_map/ppermute | solution.py:20
  83.6 12.1 %collective-permute-start.23 = (bf16[1024,256]{1,0:T(8,128)(2,1)S(1)}, bf16[1024,256]{1,0:T(8,128)(2,1)S(1)}, u32[]{:S(2)}, u32[]{:S(2)}) collective-permute-start(bf16[1024,256]{1,0:T(8,128)(2,1)S(1)} %collective-permute-done.19.refs_2_), channel_id=1, source_target_pairs={{0,1},{1,0},{2,3},{3,2},{4,5},{5,4},{6,7},{7,6},{8,9},{9,8},{10,11... | collective-permute-start | bytes 1572872 | tf_op jit(solution)/shard_map/ppermute | solution.py:20
  85.8 10.0 %collective-permute-start.22 = (bf16[1024,256]{1,0:T(8,128)(2,1)S(1)}, bf16[1024,256]{1,0:T(8,128)(2,1)S(1)}, u32[]{:S(2)}, u32[]{:S(2)}) collective-permute-start(bf16[1024,256]{1,0:T(8,128)(2,1)S(1)} %collective-permute-done.18.refs_1_), channel_id=1, source_target_pairs={{0,1},{1,0},{2,3},{3,2},{4,5},{5,4},{6,7},{7,6},{8,9},{9,8},{10,11... | collective-permute-start | bytes 1572872 | tf_op jit(solution)/shard_map/ppermute | solution.py:20
  93.4 8.1 %collective-permute-start.15 = (bf16[512,256]{1,0:T(8,128)(2,1)S(1)}, bf16[512,256]{1,0:T(8,128)(2,1)S(1)}, u32[]{:S(2)}, u32[]{:S(2)}) collective-permute-start(bf16[512,256]{1,0:T(8,128)(2,1)S(1)} %pad_maximum_fusion.3), channel_id=1, source_target_pairs={{0,16},{16,0},{1,17},{17,1},{2,18},{18,2},{3,19},{19,3},{4,20},{20... | collective-permute-start | bytes 786440 | tf_op jit(solution)/shard_map/ppermute | solution.py:20
  95.6 8.7 %collective-permute-start.16 = (bf16[256,256]{1,0:T(8,128)(2,1)S(1)}, bf16[256,256]{1,0:T(8,128)(2,1)S(1)}, u32[]{:S(2)}, u32[]{:S(2)}) collective-permute-start(bf16[256,256]{1,0:T(8,128)(2,1)S(1)} %slice.39), channel_id=1, source_target_pairs={{0,16},{16,0},{1,17},{17,1},{2,18},{18,2},{3,19},{19,3},{4,20},{20... | collective-permute-start | bytes 393224 | tf_op jit(solution)/shard_map/ppermute | solution.py:20
  (3 other events, 8.2 us)

commit v4 on v3

v4 whole, which is shorter than its diff:
```python
import functools

import jax
import jax.numpy as jnp
from jax import lax
from jax.experimental import pallas as pl
from jax.experimental.pallas import tpu as pltpu
from jax.sharding import Mesh, PartitionSpec as P

NZ, NYL, NX, NYH, NC = 8, 2, 4, 2, 2
EPOCH = ("z", "yl")
COL = ("x", "yh", "c")
NE = NZ * NYL
BF16, F32 = jnp.bfloat16, jnp.float32
DX = (0, -1, 1, 2)


def around(block, axis, n, step):
    return lax.ppermute(block, axis, [(i, (i + step) % n) for i in range(n)])


def line_of(z_from, z, half):
    return (z_from + z + half * (NZ // 2)) % NZ


def in_plane(block, half):
    axes = ("z", "yl", "x", "yh", "c")
    sizes = (NZ, NYL, NX, NYH, NC)

    def flat(place):
        index = 0
        for size, at in zip(sizes, place):
            index = index * size + at
        return index

    route = []
    for z in range(NZ):
        for yl in range(NYL):
            for x in range(NX):
                for yh in range(NYH):
                    for c in range(NC):
                        line = line_of(z, NYH * x + yh, half)
                        route.append((flat((z, yl, x, yh, c)), flat((z, c, line // NYH, line % NYH, yl))))
    return lax.ppermute(block, axes, route)


def along_z(block, half):
    route = []
    for z_from in range(NZ):
        for z in range(NZ):
            line = line_of(z_from, z, half)
            route.append(((z_from * NX + line // NYH) * NYH + line % NYH, (z * NX + line // NYH) * NYH + line % NYH))
    return lax.ppermute(block, ("z", "x", "yh"), route)


def tables_kernel(meta_ref, taps_ref, tables_ref, turned_ref):
    rows, width = tables_ref.shape[1:]
    lags = lax.broadcasted_iota(jnp.int32, (rows, width), 0)
    places = lax.broadcasted_iota(jnp.int32, (rows, width), 1)
    flip = (lags + places == rows).astype(BF16)
    flipped = jnp.dot(jnp.broadcast_to(taps_ref[...], (8, rows)), flip, preferred_element_type=F32)
    base = pltpu.roll(jnp.broadcast_to(flipped[:1], (rows, width)), 0, 1, stride=1, stride_axis=0)
    boundary = meta_ref[5]
    cut = meta_ref[6]
    for i in range(4):
        table = base
        if i == 3:
            table = jnp.where(places < rows, 0.0, base)
        elif i:
            first = (cut + i - 1) * rows
            split = (first + lags >= boundary) & (first - rows + places < boundary)
            table = jnp.where(split, 0.0, base)
        tables_ref[i] = table.astype(BF16)
        turned_ref[i] = table.T.astype(BF16)


def make_tables(meta, taps, rows):
    vmem = pl.BlockSpec(memory_space=pltpu.VMEM)
    padded = jnp.pad(taps, (0, rows - taps.shape[0]))[None, :]
    return pl.pallas_call(
        tables_kernel,
        out_shape=[jax.ShapeDtypeStruct((4, rows, 2 * rows), BF16), jax.ShapeDtypeStruct((4, 2 * rows, rows), BF16)],
        in_specs=[pl.BlockSpec(memory_space=pltpu.SMEM), vmem],
        out_specs=[vmem, vmem],
        compiler_params=pltpu.CompilerParams(vmem_limit_bytes=8 * 1024 * 1024),
        name="tables",
    )(meta, padded)


def prepare_kernel(partials_ref, gaps_ref, first_ref, second_ref, turned_ref):
    rows, cols = partials_ref.shape
    kept = jnp.broadcast_to(gaps_ref[...].astype(F32), (128, rows))
    kept_t = kept.T.astype(BF16)
    for i in range(cols // 128):
        part = partials_ref[:, i * 128 : (i + 1) * 128] * kept_t
        turned_ref[i * 128 : (i + 1) * 128, :] = part.T
        half = (first_ref, second_ref)[i // (cols // 256)]
        at = i % (cols // 256) * 128
        half[:, at : at + 128] = part


def prepare(partials, gaps):
    rows, cols = partials.shape
    return pl.pallas_call(
        prepare_kernel,
        out_shape=[jax.ShapeDtypeStruct((rows, cols // 2), BF16)] * 2 + [jax.ShapeDtypeStruct((cols, rows), BF16)],
        compiler_params=pltpu.CompilerParams(vmem_limit_bytes=4 * 1024 * 1024),
        name="prepare",
    )(partials, gaps[None, :])


def table_of(e, meta_ref):
    cut = meta_ref[6]
    return jnp.where(e == 0, 3, jnp.where(e == cut, 1, jnp.where(e == cut + 1, 2, 0)))


def filter_left(raw, table, i, rows):
    white = jnp.dot(raw[i - 1], table[:rows], preferred_element_type=F32)
    white += jnp.dot(raw[i], table[rows:], preferred_element_type=F32)
    return white.astype(BF16)


def left_kernel(meta_ref, tables_ref, own, other, up_1, down_1, up_2, down_2, out_ref, raw):
    cols, rows = raw.shape[1:]
    z, yl = meta_ref[0], meta_ref[1]
    raw[4 + yl] = own[...]
    raw[5 - yl] = other[...]
    for dz, piece in ((-2, up_2), (-1, up_1), (1, down_1), (2, down_2)):
        raw[4 + 2 * dz + yl] = piece[:cols]
        raw[5 + 2 * dz - yl] = piece[cols:]
    for i in range(NE):
        e = (2 * z + i - 4) & (NE - 1)
        to = pl.ds(pl.multiple_of(e * rows, rows), rows)
        if 1 <= i < 10:
            out_ref[:, to] = filter_left(raw, tables_ref[table_of(e, meta_ref)], i, rows)
        else:
            out_ref[:, to] = jnp.zeros((cols, rows), BF16)


def right_kernel(meta_ref, tables_ref, *refs):
    pieces = refs[0:12]
    out_ref, raw = refs[12:]
    rows, half = raw.shape[2:]
    z, x, yh, core = [meta_ref[i] for i in (0, 2, 3, 4)]
    for h in range(2):
        raw[h, 0] = jnp.zeros(raw.shape[2:], BF16)

    def place(piece, b, h, dx, dy, q):
        line = NYH * ((x + dx) & 3) + (yh ^ dy)
        e = 2 * ((line - z + h * (NZ // 2)) & 7) + (core ^ q)
        raw[h, e + 1] = piece[b * rows : (b + 1) * rows]

    for q in range(2):
        for dy in range(2):
            for b in range(4):
                place(pieces[6 * q + dy], b, 0, DX[b], dy, q)
        for i in range(4):
            for dy in range(2):
                place(pieces[6 * q + 2 + i], dy, 1, DX[i], dy, q)

    @pl.loop(0, NE)
    def _(e):
        table = tables_ref[table_of(e, meta_ref)]
        for h in range(2):
            white = jnp.dot(table[:, :rows], raw[h, e], preferred_element_type=F32)
            white += jnp.dot(table[:, rows:], raw[h, e + 1], preferred_element_type=F32)
            out_ref[pl.ds(pl.multiple_of(e * rows, rows), rows), h * half : (h + 1) * half] = white.astype(BF16)


def product_kernel(scale, meta_ref, tables_ref, left_in, right_ref, up_2, down_2, up_3, down_3, far_own, far_other, out_ref, left_ref, raw):
    cols, rows = raw.shape[1:]
    z, yl = meta_ref[0], meta_ref[1]
    raw[0] = down_2[pl.ds(pl.multiple_of((1 ^ yl) * cols, cols), cols)]
    raw[7] = up_2[pl.ds(pl.multiple_of(yl * cols, cols), cols)]
    for at, piece in ((1, down_3), (5, up_3)):
        raw[at + yl] = piece[:cols]
        raw[at + 1 - yl] = piece[cols:]
    raw[3 + yl] = far_own[...]
    raw[4 - yl] = far_other[...]
    for i in range(1, 8):
        e = (2 * z + i + 5) & (NE - 1)
        to = pl.ds(pl.multiple_of(e * rows, rows), rows)
        left_ref[:, to] = filter_left(raw, tables_ref[table_of(e, meta_ref)], i, rows)
    out_ref[...] = jnp.dot(left_ref[...], right_ref[...], preferred_element_type=F32) * scale


def whitened(kernel, name, meta, tables, pieces, shape, raw_shape):
    vmem = pl.BlockSpec(memory_space=pltpu.VMEM)
    return pl.pallas_call(
        kernel,
        out_shape=jax.ShapeDtypeStruct(shape, BF16),
        in_specs=[pl.BlockSpec(memory_space=pltpu.SMEM)] + [vmem] * (1 + len(pieces)),
        out_specs=vmem,
        scratch_shapes=[pltpu.VMEM(raw_shape, BF16)],
        compiler_params=pltpu.CompilerParams(vmem_limit_bytes=16 * 1024 * 1024),
        name=name,
    )(meta, tables, *pieces)


def product(meta, tables, left, right, pieces, rows, scale):
    vmem = pl.BlockSpec(memory_space=pltpu.VMEM)
    cols = right.shape[1]
    return pl.pallas_call(
        functools.partial(product_kernel, scale),
        out_shape=[jax.ShapeDtypeStruct((cols, cols), F32), jax.ShapeDtypeStruct(left.shape, BF16)],
        in_specs=[pl.BlockSpec(memory_space=pltpu.SMEM)] + [vmem] * (3 + len(pieces)),
        out_specs=[vmem, vmem],
        scratch_shapes=[pltpu.VMEM((8, cols, rows), BF16)],
        input_output_aliases={2: 1},
        compiler_params=pltpu.CompilerParams(vmem_limit_bytes=16 * 1024 * 1024),
        name="product",
    )(meta, tables, left, right, *pieces)[0]


def on_device(partials, gaps, arc_start, taps):
    rows, cols = partials.shape
    half = cols // 2
    places = [lax.axis_index(axis) for axis in EPOCH + COL]
    meta = jnp.stack(places + [arc_start[0], arc_start[0] // rows]).astype(jnp.int32)
    a, b, own = prepare(partials, gaps)

    def up(block):
        return around(block, "z", NZ, 1)

    def down(block):
        return around(block, "z", NZ, -1)

    def along_x(block):
        return [around(block, "x", NX, step) for step in (1, -1, 2)]

    def swapped(block):
        return around(block, "c", NC, 1)

    def across(block):
        return around(block, "yh", NYH, 1)

    sync = lax.optimization_barrier
    other, up_own, down_own, a, b = sync((around(own, "yl", NYL, 1), up(own), down(own), in_plane(a, 0), in_plane(b, 1)))
    up_other, down_other, a, b, tables = sync((up(other), down(other), along_z(a, 0), along_z(b, 1), make_tables(meta, taps, rows)))
    up_1 = jnp.concatenate([up_own, up_other], axis=0)
    down_1 = jnp.concatenate([down_own, down_other], axis=0)
    up_2, down_2, a_x, b_y = sync((up(up_1), down(down_1), along_x(a), across(b)))
    a_pack = jnp.concatenate([a] + a_x, axis=0)
    b_pack = jnp.concatenate([b, b_y], axis=0)
    left = whitened(left_kernel, "left", meta, tables[1], [own, other, up_1, down_1, up_2, down_2], (cols, NE * rows), (10, cols, rows))
    up_3, down_3, a_far, b_x, left = sync((up(up_2), down(down_2), across(a_pack), along_x(b_pack), left))
    far_own, far_other = up(up_3[:cols]), down(down_3[cols:])
    mine = [a_pack, a_far, b_pack] + b_x
    theirs = [swapped(piece) for piece in mine]
    right = whitened(right_kernel, "right", meta, tables[0], mine + theirs, (NE * rows, cols), (2, NE + 1, rows, half))
    pieces = [up_2, down_2, up_3, down_3, far_own, far_other]
    return product(meta, tables[1], left, right, pieces, rows, (rows * NE) ** (-0.5))


def solution(mesh):
    fine = Mesh(mesh.devices.reshape(NZ, NYL, NX, NYH, NC), EPOCH + COL)
    in_specs = (P(EPOCH, COL), P(EPOCH), P(), P())
    return jax.shard_map(on_device, mesh=fine, in_specs=in_specs, out_specs=P(COL, EPOCH), check_vma=False)
```

time: 114 us -> 100 us (0.88)
  starting transfers between devices: 58.3 us -> 45 us
  waiting for transfers between devices: 35.4 us -> 36.7 us
  Pallas kernels: 16 us -> 14.8 us
    ppermute x21 -> x25, starting transfers between devices: 43.6 us -> 33.5 us  [around(): return lax.ppermute(block, axis, [(i, (i + step) % n) for i in range(n)])]
    ppermute x21 -> x25, waiting for transfers between devices: 29 us -> 21.9 us  [around(): return lax.ppermute(block, axis, [(i, (i + step) % n) for i in range(n)])]
    ppermute x2, waiting for transfers between devices: 6.43 us -> 10.9 us  [along_z(): return lax.ppermute(block, ('z', 'x', 'yh'), route)]
    ppermute x2, waiting for transfers between devices: 0.01 us -> 3.86 us  [in_plane(): return lax.ppermute(block, axes, route)]
    pallas_call x2, Pallas kernels: 11.4 us -> 8.22 us  [whitened(): pl.pallas_call(kernel, out_shape=jax.ShapeDtypeStruct(shape, BF16), in_sp...]
    pallas_call x2, Pallas kernels: 4.35 us -> 6.3 us  [the longest x1 5.21 us: product(): pl.pallas_call(functools.partial(product_kernel, scale), out_shape=[jax.S...]
    ppermute x2, starting transfers between devices: 5.38 us -> 3.5 us  [along_z(): return lax.ppermute(block, ('z', 'x', 'yh'), route)]
    ppermute x2, starting transfers between devices: 9.29 us -> 8.01 us  [in_plane(): return lax.ppermute(block, axes, route)]
  transfers between devices with their start and end apart: 25 -> 29, of which waited for: 8 -> 12; matrix products, arithmetic and copies ran while one was open for 1% -> 1% of each run, Pallas kernels for 6% -> 9%
where the time goes in v4:
time: 100 us; the launch traced here: 99.9 us
  starting transfers between devices  45 us (45%)
  waiting for transfers between devices  36.7 us (37%)
  Pallas kernels  14.8 us (15%)
  local copies, waits for them, and re-layouts  2.55 us (3%)
    ppermute x25, starting transfers between devices, around(): return lax.ppermute(block, axis, [(i, (i + step) % n) for i in range(n)])  33.5 us
    ppermute x25, waiting for transfers between devices, around(): return lax.ppermute(block, axis, [(i, (i + step) % n) for i in range(n)])  21.9 us
    ppermute x2, waiting for transfers between devices, along_z(): return lax.ppermute(block, ('z', 'x', 'yh'), route)  10.9 us
    pallas_call x2, Pallas kernels, whitened(): pl.pallas_call(kernel, out_shape=jax.ShapeDtypeStruct(shape, BF16), in_sp...  8.22 us
    ppermute x2, starting transfers between devices, in_plane(): return lax.ppermute(block, axes, route)  8.01 us
    pallas_call x1, Pallas kernels, product(): pl.pallas_call(functools.partial(product_kernel, scale), out_shape=[jax.S...  5.21 us
    ppermute x2, waiting for transfers between devices, in_plane(): return lax.ppermute(block, axes, route)  3.86 us
    ppermute x2, starting transfers between devices, along_z(): return lax.ppermute(block, ('z', 'x', 'yh'), route)  3.5 us
  transfers between devices with their start and end apart: 29, of which 12 were waited for; matrix products, arithmetic and copies ran while one was open for 1% of the time, Pallas kernels for 9%

profile of v4, /device:TPU:1, one launch (start us, length us, event | category | flops | bytes accessed | tf_op | source)
XLA Modules:
  0.0 99.9 jit_solution(9614745738218660031)
XLA Ops:
  0.0 0.9 copy-done
  1.9 6.5 %collective-permute-start.2 = (bf16[512,256]{1,0:T(8,128)(2,1)S(1)}, bf16[512,256]{1,0:T(8,128)(2,1)S(1)}, u32[]{:S(2)}, u32[]{:S(2)}) collective-permute-start(bf16[512,256]{1,0:T(8,128)(2,1)S(1)} %get-tuple-element.35.own), channel_id=1, source_target_pairs={{0,224},{32,0},{64,32},{96,64},{128,96},{160,128},{192,160},{224,1... | collective-permute-start | bytes 786440 | tf_op jit(solution)/shard_map/ppermute | solution.py:19
  8.4 1.3 %collective-permute-start = (bf16[512,256]{1,0:T(8,128)(2,1)S(1)}, bf16[512,256]{1,0:T(8,128)(2,1)S(1)}, u32[]{:S(2)}, u32[]{:S(2)}) collective-permute-start(bf16[512,256]{1,0:T(8,128)(2,1)S(1)} %get-tuple-element.35.own), channel_id=1, source_target_pairs={{0,16},{16,0},{1,17},{17,1},{2,18},{18,2},{3,19},{19,3},{4,20},{20... | collective-permute-start | bytes 786440 | tf_op jit(solution)/shard_map/ppermute | solution.py:19
  9.7 3.2 %collective-permute-start.3 = (bf16[256,256]{1,0:T(8,128)(2,1)S(1)}, bf16[256,256]{1,0:T(8,128)(2,1)S(1)}, u32[]{:S(2)}, u32[]{:S(2)}) collective-permute-start(bf16[256,256]{1,0:T(8,128)(2,1)S(1)} %get-tuple-element.36), channel_id=1, source_target_pairs={{0,0},{1,16},{2,2},{3,18},{4,4},{5,20},{6,6},{7,22},{8,8},{9,24},{... | collective-permute-start | bytes 393224 | tf_op jit(solution)/shard_map/ppermute | solution.py:44
  12.8 4.8 %collective-permute-start.4 = (bf16[256,256]{1,0:T(8,128)(2,1)S(1)}, bf16[256,256]{1,0:T(8,128)(2,1)S(1)}, u32[]{:S(2)}, u32[]{:S(2)}) collective-permute-start(bf16[256,256]{1,0:T(8,128)(2,1)S(1)} %get-tuple-element.37), channel_id=1, source_target_pairs={{0,8},{1,24},{2,10},{3,26},{4,12},{5,28},{6,14},{7,30},{8,0},{9,16... | collective-permute-start | bytes 393224 | tf_op jit(solution)/shard_map/ppermute | solution.py:44
  17.9 3.6 %collective-permute-done.4 = bf16[256,256]{1,0:T(8,128)(2,1)S(1)} collective-permute-done((bf16[256,256]{1,0:T(8,128)(2,1)S(1)}, bf16[256,256]{1,0:T(8,128)(2,1)S(1)}, u32[]{:S(2)}, u32[]{:S(2)}) %collective-permute-start.4) | collective-permute-done | bytes 131104 | tf_op jit(solution)/shard_map/ppermute | solution.py:44
  21.5 8.5 %collective-permute-start.6 = (bf16[512,256]{1,0:T(8,128)(2,1)S(1)}, bf16[512,256]{1,0:T(8,128)(2,1)S(1)}, u32[]{:S(2)}, u32[]{:S(2)}) collective-permute-start(bf16[512,256]{1,0:T(8,128)(2,1)S(1)} %collective-permute-done.other), channel_id=1, source_target_pairs={{0,224},{32,0},{64,32},{96,64},{128,96},{160,128},{192,160},{224,1... | collective-permute-start | bytes 786440 | tf_op jit(solution)/shard_map/ppermute | solution.py:19
  31.4 1.1 %tables.1 = (bf16[4,256,512]{2,1,0:T(8,128)(2,1)S(1)}, bf16[4,512,256]{2,1,0:T(8,128)(2,1)S(1)}) custom-call(s32[7]{0:T(128)S(1)} %stack.27.meta_ref, bf16[1,256]{1,0:T(2,128)(2,1)S(1)} %broadcast_in_dim.7.taps_ref), custom_call_target="tpu_custom_call" | custom-call | tf_op jit(solution)/shard_map/tables/pallas_call | solution.py:80
  33.2 2.8 %collective-permute-start.8 = (bf16[256,256]{1,0:T(8,128)(2,1)S(1)}, bf16[256,256]{1,0:T(8,128)(2,1)S(1)}, u32[]{:S(2)}, u32[]{:S(2)}) collective-permute-start(bf16[256,256]{1,0:T(8,128)(2,1)S(1)} %collective-permute-done.4), channel_id=1, source_target_pairs={{8,8},{10,42},{12,76},{14,110},{0,128},{2,162},{4,196},{6,230},{42... | collective-permute-start | bytes 393224 | tf_op jit(solution)/shard_map/ppermute | solution.py:53
  36.1 10.9 %collective-permute-done.8 = bf16[256,256]{1,0:T(8,128)(2,1)S(1)} collective-permute-done((bf16[256,256]{1,0:T(8,128)(2,1)S(1)}, bf16[256,256]{1,0:T(8,128)(2,1)S(1)}, u32[]{:S(2)}, u32[]{:S(2)}) %collective-permute-start.8) | collective-permute-done | bytes 131104 | tf_op jit(solution)/shard_map/ppermute | solution.py:53
  47.0 3.0 %collective-permute-start.10 = (bf16[1024,256]{1,0:T(8,128)(2,1)S(1)}, bf16[1024,256]{1,0:T(8,128)(2,1)S(1)}, u32[]{:S(2)}, u32[]{:S(2)}) collective-permute-start(bf16[1024,256]{1,0:T(8,128)(2,1)S(1)} %constant_dynamic-update-slice_fusion.2.down_1), channel_id=1, source_target_pairs={{0,224},{32,0},{64,32},{96,64},{128,96},{160,128},{192,160},{224,1... | collective-permute-start | bytes 1572872 | tf_op jit(solution)/shard_map/ppermute | solution.py:19
  50.4 5.1 %collective-permute-done.14 = bf16[256,256]{1,0:T(8,128)(2,1)S(1)} collective-permute-done((bf16[256,256]{1,0:T(8,128)(2,1)S(1)}, bf16[256,256]{1,0:T(8,128)(2,1)S(1)}, u32[]{:S(2)}, u32[]{:S(2)}) %collective-permute-start.14) | collective-permute-done | bytes 131104 | tf_op jit(solution)/shard_map/ppermute | solution.py:19
  55.7 5.2 %collective-permute-done.11 = bf16[256,256]{1,0:T(8,128)(2,1)S(1)} collective-permute-done((bf16[256,256]{1,0:T(8,128)(2,1)S(1)}, bf16[256,256]{1,0:T(8,128)(2,1)S(1)}, u32[]{:S(2)}, u32[]{:S(2)}) %collective-permute-start.11) | collective-permute-done | bytes 131104 | tf_op jit(solution)/shard_map/ppermute | solution.py:19
  60.9 2.7 %collective-permute-done.9.up_2 = bf16[1024,256]{1,0:T(8,128)(2,1)S(1)} collective-permute-done((bf16[1024,256]{1,0:T(8,128)(2,1)S(1)}, bf16[1024,256]{1,0:T(8,128)(2,1)S(1)}, u32[]{:S(2)}, u32[]{:S(2)}) %collective-permute-start.9) | collective-permute-done | bytes 524320 | tf_op jit(solution)/shard_map/ppermute | solution.py:19
  64.0 2.7 %collective-permute-start.16 = (bf16[1024,256]{1,0:T(8,128)(2,1)S(1)}, bf16[1024,256]{1,0:T(8,128)(2,1)S(1)}, u32[]{:S(2)}, u32[]{:S(2)}) collective-permute-start(bf16[1024,256]{1,0:T(8,128)(2,1)S(1)} %collective-permute-done.10.down_2), channel_id=1, source_target_pairs={{0,224},{32,0},{64,32},{96,64},{128,96},{160,128},{192,160},{224,1... | collective-permute-start | bytes 1572872 | tf_op jit(solution)/shard_map/ppermute | solution.py:19
  66.6 4.3 %collective-permute-done.20.refs_5_ = bf16[512,256]{1,0:T(8,128)(2,1)S(1)} collective-permute-done((bf16[512,256]{1,0:T(8,128)(2,1)S(1)}, bf16[512,256]{1,0:T(8,128)(2,1)S(1)}, u32[]{:S(2)}, u32[]{:S(2)}) %collective-permute-start.20) | collective-permute-done | bytes 262176 | tf_op jit(solution)/shard_map/ppermute | solution.py:19
  70.9 1.2 %collective-permute-done.19.refs_4_ = bf16[512,256]{1,0:T(8,128)(2,1)S(1)} collective-permute-done((bf16[512,256]{1,0:T(8,128)(2,1)S(1)}, bf16[512,256]{1,0:T(8,128)(2,1)S(1)}, u32[]{:S(2)}, u32[]{:S(2)}) %collective-permute-start.19) | collective-permute-done | bytes 262176 | tf_op jit(solution)/shard_map/ppermute | solution.py:19
  72.1 3.5 %collective-permute-start.21 = (bf16[1024,256]{1,0:T(8,128)(2,1)S(1)}, bf16[1024,256]{1,0:T(8,128)(2,1)S(1)}, u32[]{:S(2)}, u32[]{:S(2)}) collective-permute-start(bf16[1024,256]{1,0:T(8,128)(2,1)S(1)} %constant_dynamic-update-slice_fusion.4.refs_0_), channel_id=1, source_target_pairs={{0,1},{1,0},{2,3},{3,2},{4,5},{5,4},{6,7},{7,6},{8,9},{9,8},{10,11... | collective-permute-start | bytes 1572872 | tf_op jit(solution)/shard_map/ppermute | solution.py:19
  75.6 2.5 %left.1.left_in = bf16[512,4096]{1,0:T(8,128)(2,1)S(1)} custom-call(s32[7]{0:T(128)S(1)} %stack.27.meta_ref, bf16[4,512,256]{2,1,0:T(8,128)(2,1)S(1)} %get-tuple-element.43.tables_ref, bf16[512,256]{1,0:T(8,128)(2,1)S(1)} %get-tuple-element.35.own, bf16[512,256]{1,0:T(8,128)(2,1)S(1)} %collective-permute-done.other, ...), custom_call_target="tpu_custom_call" | custom-call | tf_op jit(solution)/shard_map/left/pallas_call | solution.py:189
  78.2 4.3 %collective-permute-start.23 = (bf16[512,256]{1,0:T(8,128)(2,1)S(1)}, bf16[512,256]{1,0:T(8,128)(2,1)S(1)}, u32[]{:S(2)}, u32[]{:S(2)}) collective-permute-start(bf16[512,256]{1,0:T(8,128)(2,1)S(1)} %constant_dynamic-update-slice_fusion.8.refs_2_), channel_id=1, source_target_pairs={{0,1},{1,0},{2,3},{3,2},{4,5},{5,4},{6,7},{7,6},{8,9},{9,8},{10,11... | collective-permute-start | bytes 786440 | tf_op jit(solution)/shard_map/ppermute | solution.py:19
  84.1 1.9 %collective-permute-start.28 = (bf16[512,256]{1,0:T(8,128)(2,1)S(1)}, bf16[512,256]{1,0:T(8,128)(2,1)S(1)}, u32[]{:S(2)}, u32[]{:S(2)}) collective-permute-start(bf16[512,256]{1,0:T(8,128)(2,1)S(1)} %slice.7), channel_id=1, source_target_pairs={{0,224},{32,0},{64,32},{96,64},{128,96},{160,128},{192,160},{224,1... | collective-permute-start | bytes 786440 | tf_op jit(solution)/shard_map/ppermute | solution.py:19
  86.1 5.7 %right.1.right_ref = bf16[4096,512]{1,0:T(8,128)(2,1)S(1)} custom-call(s32[7]{0:T(128)S(1)} %stack.27.meta_ref, bf16[4,256,512]{2,1,0:T(8,128)(2,1)S(1)} %get-tuple-element.57.tables_ref, bf16[1024,256]{1,0:T(8,128)(2,1)S(1)} %constant_dynamic-update-slice_fusion.4.refs_0_, bf16[1024,256]{1,0:T(8,128)(2,1)S(1)} %collective-permute-done.17.refs_1_, ...), custom_call_target="tpu_custom_call" | custom-call | tf_op jit(solution)/shard_map/right/pallas_call | solution.py:189
  91.9 2.8 %collective-permute-done.27.far_own = bf16[512,256]{1,0:T(8,128)(2,1)S(1)} collective-permute-done((bf16[512,256]{1,0:T(8,128)(2,1)S(1)}, bf16[512,256]{1,0:T(8,128)(2,1)S(1)}, u32[]{:S(2)}, u32[]{:S(2)}) %collective-permute-start.27) | collective-permute-done | bytes 262176 | tf_op jit(solution)/shard_map/ppermute | solution.py:19
  94.7 5.2 %product.1 = (f32[512,512]{1,0:T(8,128)}, bf16[512,4096]{1,0:T(8,128)(2,1)S(1)}) custom-call(s32[7]{0:T(128)S(1)} %stack.27.meta_ref, bf16[4,512,256]{2,1,0:T(8,128)(2,1)S(1)} %get-tuple-element.43.tables_ref, bf16[512,4096]{1,0:T(8,128)(2,1)S(1)} %left.1.left_in, bf16[4096,512]{1,0:T(8,128)(2,1)S(1)} %right.1.right_ref, ...), custom_call_target="tpu_custom_call", output_to_operand_aliasing={{1}: (2, {})} | custom-call | tf_op jit(solution)/shard_map/product/pallas_call | solution.py:203
  (58 shorter events, 5.1 us)
Async XLA Ops:
  1.9 19.7 %collective-permute-start.2 = (bf16[512,256]{1,0:T(8,128)(2,1)S(1)}, bf16[512,256]{1,0:T(8,128)(2,1)S(1)}, u32[]{:S(2)}, u32[]{:S(2)}) collective-permute-start(bf16[512,256]{1,0:T(8,128)(2,1)S(1)} %get-tuple-element.35.own), channel_id=1, source_target_pairs={{0,224},{32,0},{64,32},{96,64},{128,96},{160,128},{192,160},{224,1... | collective-permute-start | bytes 786440 | tf_op jit(solution)/shard_map/ppermute | solution.py:19
  8.4 13.2 %collective-permute-start.1 = (bf16[512,256]{1,0:T(8,128)(2,1)S(1)}, bf16[512,256]{1,0:T(8,128)(2,1)S(1)}, u32[]{:S(2)}, u32[]{:S(2)}) collective-permute-start(bf16[512,256]{1,0:T(8,128)(2,1)S(1)} %get-tuple-element.35.own), channel_id=1, source_target_pairs={{0,32},{32,64},{64,96},{96,128},{128,160},{160,192},{192,224},{224... | collective-permute-start | bytes 786440 | tf_op jit(solution)/shard_map/ppermute | solution.py:19
  8.4 13.2 %collective-permute-start = (bf16[512,256]{1,0:T(8,128)(2,1)S(1)}, bf16[512,256]{1,0:T(8,128)(2,1)S(1)}, u32[]{:S(2)}, u32[]{:S(2)}) collective-permute-start(bf16[512,256]{1,0:T(8,128)(2,1)S(1)} %get-tuple-element.35.own), channel_id=1, source_target_pairs={{0,16},{16,0},{1,17},{17,1},{2,18},{18,2},{3,19},{19,3},{4,20},{20... | collective-permute-start | bytes 786440 | tf_op jit(solution)/shard_map/ppermute | solution.py:19
  9.7 8.2 %collective-permute-start.3 = (bf16[256,256]{1,0:T(8,128)(2,1)S(1)}, bf16[256,256]{1,0:T(8,128)(2,1)S(1)}, u32[]{:S(2)}, u32[]{:S(2)}) collective-permute-start(bf16[256,256]{1,0:T(8,128)(2,1)S(1)} %get-tuple-element.36), channel_id=1, source_target_pairs={{0,0},{1,16},{2,2},{3,18},{4,4},{5,20},{6,6},{7,22},{8,8},{9,24},{... | collective-permute-start | bytes 393224 | tf_op jit(solution)/shard_map/ppermute | solution.py:44
  12.8 8.7 %collective-permute-start.4 = (bf16[256,256]{1,0:T(8,128)(2,1)S(1)}, bf16[256,256]{1,0:T(8,128)(2,1)S(1)}, u32[]{:S(2)}, u32[]{:S(2)}) collective-permute-start(bf16[256,256]{1,0:T(8,128)(2,1)S(1)} %get-tuple-element.37), channel_id=1, source_target_pairs={{0,8},{1,24},{2,10},{3,26},{4,12},{5,28},{6,14},{7,30},{8,0},{9,16... | collective-permute-start | bytes 393224 | tf_op jit(solution)/shard_map/ppermute | solution.py:44
  21.5 25.4 %collective-permute-start.6 = (bf16[512,256]{1,0:T(8,128)(2,1)S(1)}, bf16[512,256]{1,0:T(8,128)(2,1)S(1)}, u32[]{:S(2)}, u32[]{:S(2)}) collective-permute-start(bf16[512,256]{1,0:T(8,128)(2,1)S(1)} %collective-permute-done.other), channel_id=1, source_target_pairs={{0,224},{32,0},{64,32},{96,64},{128,96},{160,128},{192,160},{224,1... | collective-permute-start | bytes 786440 | tf_op jit(solution)/shard_map/ppermute | solution.py:19
  30.0 17.0 %collective-permute-start.5 = (bf16[512,256]{1,0:T(8,128)(2,1)S(1)}, bf16[512,256]{1,0:T(8,128)(2,1)S(1)}, u32[]{:S(2)}, u32[]{:S(2)}) collective-permute-start(bf16[512,256]{1,0:T(8,128)(2,1)S(1)} %collective-permute-done.other), channel_id=1, source_target_pairs={{0,32},{32,64},{64,96},{96,128},{128,160},{160,192},{192,224},{224... | collective-permute-start | bytes 786440 | tf_op jit(solution)/shard_map/ppermute | solution.py:19
  33.2 13.8 %collective-permute-start.8 = (bf16[256,256]{1,0:T(8,128)(2,1)S(1)}, bf16[256,256]{1,0:T(8,128)(2,1)S(1)}, u32[]{:S(2)}, u32[]{:S(2)}) collective-permute-start(bf16[256,256]{1,0:T(8,128)(2,1)S(1)} %collective-permute-done.4), channel_id=1, source_target_pairs={{8,8},{10,42},{12,76},{14,110},{0,128},{2,162},{4,196},{6,230},{42... | collective-permute-start | bytes 393224 | tf_op jit(solution)/shard_map/ppermute | solution.py:53
  47.0 13.9 %collective-permute-start.10 = (bf16[1024,256]{1,0:T(8,128)(2,1)S(1)}, bf16[1024,256]{1,0:T(8,128)(2,1)S(1)}, u32[]{:S(2)}, u32[]{:S(2)}) collective-permute-start(bf16[1024,256]{1,0:T(8,128)(2,1)S(1)} %constant_dynamic-update-slice_fusion.2.down_1), channel_id=1, source_target_pairs={{0,224},{32,0},{64,32},{96,64},{128,96},{160,128},{192,160},{224,1... | collective-permute-start | bytes 1572872 | tf_op jit(solution)/shard_map/ppermute | solution.py:19
  50.1 13.5 %collective-permute-start.9 = (bf16[1024,256]{1,0:T(8,128)(2,1)S(1)}, bf16[1024,256]{1,0:T(8,128)(2,1)S(1)}, u32[]{:S(2)}, u32[]{:S(2)}) collective-permute-start(bf16[1024,256]{1,0:T(8,128)(2,1)S(1)} %constant_dynamic-update-slice_fusion.up_1), channel_id=1, source_target_pairs={{0,32},{32,64},{64,96},{96,128},{128,160},{160,192},{192,224},{224... | collective-permute-start | bytes 1572872 | tf_op jit(solution)/shard_map/ppermute | solution.py:19
  50.2 5.4 %collective-permute-start.14 = (bf16[256,256]{1,0:T(8,128)(2,1)S(1)}, bf16[256,256]{1,0:T(8,128)(2,1)S(1)}, u32[]{:S(2)}, u32[]{:S(2)}) collective-permute-start(bf16[256,256]{1,0:T(8,128)(2,1)S(1)} %collective-permute-done.8), channel_id=1, source_target_pairs={{0,2},{2,0},{1,3},{3,1},{4,6},{6,4},{5,7},{7,5},{8,10},{10,8},{9,1... | collective-permute-start | bytes 393224 | tf_op jit(solution)/shard_map/ppermute | solution.py:19
  50.3 5.4 %collective-permute-start.13 = (bf16[256,256]{1,0:T(8,128)(2,1)S(1)}, bf16[256,256]{1,0:T(8,128)(2,1)S(1)}, u32[]{:S(2)}, u32[]{:S(2)}) collective-permute-start(bf16[256,256]{1,0:T(8,128)(2,1)S(1)} %collective-permute-done.7), channel_id=1, source_target_pairs={{0,8},{4,12},{8,0},{12,4},{1,9},{5,13},{9,1},{13,5},{2,10},{6,14},... | collective-permute-start | bytes 393224 | tf_op jit(solution)/shard_map/ppermute | solution.py:19
  50.4 5.3 %collective-permute-start.12 = (bf16[256,256]{1,0:T(8,128)(2,1)S(1)}, bf16[256,256]{1,0:T(8,128)(2,1)S(1)}, u32[]{:S(2)}, u32[]{:S(2)}) collective-permute-start(bf16[256,256]{1,0:T(8,128)(2,1)S(1)} %collective-permute-done.7), channel_id=1, source_target_pairs={{0,12},{4,0},{8,4},{12,8},{1,13},{5,1},{9,5},{13,9},{2,14},{6,2},{... | collective-permute-start | bytes 393224 | tf_op jit(solution)/shard_map/ppermute | solution.py:19
  55.6 5.3 %collective-permute-start.11 = (bf16[256,256]{1,0:T(8,128)(2,1)S(1)}, bf16[256,256]{1,0:T(8,128)(2,1)S(1)}, u32[]{:S(2)}, u32[]{:S(2)}) collective-permute-start(bf16[256,256]{1,0:T(8,128)(2,1)S(1)} %collective-permute-done.7), channel_id=1, source_target_pairs={{0,4},{4,8},{8,12},{12,0},{1,5},{5,9},{9,13},{13,1},{2,6},{6,10},{... | collective-permute-start | bytes 393224 | tf_op jit(solution)/shard_map/ppermute | solution.py:19
  63.6 7.3 %collective-permute-start.20 = (bf16[512,256]{1,0:T(8,128)(2,1)S(1)}, bf16[512,256]{1,0:T(8,128)(2,1)S(1)}, u32[]{:S(2)}, u32[]{:S(2)}) collective-permute-start(bf16[512,256]{1,0:T(8,128)(2,1)S(1)} %constant_dynamic-update-slice_fusion.8.refs_2_), channel_id=1, source_target_pairs={{0,8},{4,12},{8,0},{12,4},{1,9},{5,13},{9,1},{13,5},{2,10},{6,14},... | collective-permute-start | bytes 786440 | tf_op jit(solution)/shard_map/ppermute | solution.py:19
  63.8 18.8 %collective-permute-start.17 = (bf16[1024,256]{1,0:T(8,128)(2,1)S(1)}, bf16[1024,256]{1,0:T(8,128)(2,1)S(1)}, u32[]{:S(2)}, u32[]{:S(2)}) collective-permute-start(bf16[1024,256]{1,0:T(8,128)(2,1)S(1)} %constant_dynamic-update-slice_fusion.4.refs_0_), channel_id=1, source_target_pairs={{0,2},{2,0},{1,3},{3,1},{4,6},{6,4},{5,7},{7,5},{8,10},{10,8},{9,1... | collective-permute-start | bytes 1572872 | tf_op jit(solution)/shard_map/ppermute | solution.py:19
  63.9 18.7 %collective-permute-start.15 = (bf16[1024,256]{1,0:T(8,128)(2,1)S(1)}, bf16[1024,256]{1,0:T(8,128)(2,1)S(1)}, u32[]{:S(2)}, u32[]{:S(2)}) collective-permute-start(bf16[1024,256]{1,0:T(8,128)(2,1)S(1)} %collective-permute-done.9.up_2), channel_id=1, source_target_pairs={{0,32},{32,64},{64,96},{96,128},{128,160},{160,192},{192,224},{224... | collective-permute-start | bytes 1572872 | tf_op jit(solution)/shard_map/ppermute | solution.py:19
  64.0 18.6 %collective-permute-start.16 = (bf16[1024,256]{1,0:T(8,128)(2,1)S(1)}, bf16[1024,256]{1,0:T(8,128)(2,1)S(1)}, u32[]{:S(2)}, u32[]{:S(2)}) collective-permute-start(bf16[1024,256]{1,0:T(8,128)(2,1)S(1)} %collective-permute-done.10.down_2), channel_id=1, source_target_pairs={{0,224},{32,0},{64,32},{96,64},{128,96},{160,128},{192,160},{224,1... | collective-permute-start | bytes 1572872 | tf_op jit(solution)/shard_map/ppermute | solution.py:19
  66.6 5.5 %collective-permute-start.19 = (bf16[512,256]{1,0:T(8,128)(2,1)S(1)}, bf16[512,256]{1,0:T(8,128)(2,1)S(1)}, u32[]{:S(2)}, u32[]{:S(2)}) collective-permute-start(bf16[512,256]{1,0:T(8,128)(2,1)S(1)} %constant_dynamic-update-slice_fusion.8.refs_2_), channel_id=1, source_target_pairs={{0,12},{4,0},{8,4},{12,8},{1,13},{5,1},{9,5},{13,9},{2,14},{6,2},{... | collective-permute-start | bytes 786440 | tf_op jit(solution)/shard_map/ppermute | solution.py:19
  70.9 7.3 %collective-permute-start.18 = (bf16[512,256]{1,0:T(8,128)(2,1)S(1)}, bf16[512,256]{1,0:T(8,128)(2,1)S(1)}, u32[]{:S(2)}, u32[]{:S(2)}) collective-permute-start(bf16[512,256]{1,0:T(8,128)(2,1)S(1)} %constant_dynamic-update-slice_fusion.8.refs_2_), channel_id=1, source_target_pairs={{0,4},{4,8},{8,12},{12,0},{1,5},{5,9},{9,13},{13,1},{2,6},{6,10},{... | collective-permute-start | bytes 786440 | tf_op jit(solution)/shard_map/ppermute | solution.py:19
  72.1 11.9 %collective-permute-start.21 = (bf16[1024,256]{1,0:T(8,128)(2,1)S(1)}, bf16[1024,256]{1,0:T(8,128)(2,1)S(1)}, u32[]{:S(2)}, u32[]{:S(2)}) collective-permute-start(bf16[1024,256]{1,0:T(8,128)(2,1)S(1)} %constant_dynamic-update-slice_fusion.4.refs_0_), channel_id=1, source_target_pairs={{0,1},{1,0},{2,3},{3,2},{4,5},{5,4},{6,7},{7,6},{8,9},{9,8},{10,11... | collective-permute-start | bytes 1572872 | tf_op jit(solution)/shard_map/ppermute | solution.py:19
  78.2 5.5 %collective-permute-start.23 = (bf16[512,256]{1,0:T(8,128)(2,1)S(1)}, bf16[512,256]{1,0:T(8,128)(2,1)S(1)}, u32[]{:S(2)}, u32[]{:S(2)}) collective-permute-start(bf16[512,256]{1,0:T(8,128)(2,1)S(1)} %constant_dynamic-update-slice_fusion.8.refs_2_), channel_id=1, source_target_pairs={{0,1},{1,0},{2,3},{3,2},{4,5},{5,4},{6,7},{7,6},{8,9},{9,8},{10,11... | collective-permute-start | bytes 786440 | tf_op jit(solution)/shard_map/ppermute | solution.py:19
  84.1 7.8 %collective-permute-start.28 = (bf16[512,256]{1,0:T(8,128)(2,1)S(1)}, bf16[512,256]{1,0:T(8,128)(2,1)S(1)}, u32[]{:S(2)}, u32[]{:S(2)}) collective-permute-start(bf16[512,256]{1,0:T(8,128)(2,1)S(1)} %slice.7), channel_id=1, source_target_pairs={{0,224},{32,0},{64,32},{96,64},{128,96},{160,128},{192,160},{224,1... | collective-permute-start | bytes 786440 | tf_op jit(solution)/shard_map/ppermute | solution.py:19
  86.0 8.7 %collective-permute-start.27 = (bf16[512,256]{1,0:T(8,128)(2,1)S(1)}, bf16[512,256]{1,0:T(8,128)(2,1)S(1)}, u32[]{:S(2)}, u32[]{:S(2)}) collective-permute-start(bf16[512,256]{1,0:T(8,128)(2,1)S(1)} %slice.6), channel_id=1, source_target_pairs={{0,32},{32,64},{64,96},{96,128},{128,160},{160,192},{192,224},{224... | collective-permute-start | bytes 786440 | tf_op jit(solution)/shard_map/ppermute | solution.py:19
  (7 other events, 17.4 us)

commit v5 on v4

--- a/solution.py
+++ b/solution.py
@@ -87,12 +87,17 @@
     )(meta, padded)
 
 
-def prepare_kernel(partials_ref, gaps_ref, first_ref, second_ref, turned_ref):
-    rows, cols = partials_ref.shape
-    kept = jnp.broadcast_to(gaps_ref[...].astype(F32), (128, rows))
+def prepare_kernel(partials_ref, gaps_ref, first_ref, second_ref, turned_ref, held, held_gaps, sems):
+    rows, cols = held.shape
+    copies = [pltpu.make_async_copy(gaps_ref, held_gaps, sems.at[0]), pltpu.make_async_copy(partials_ref, held, sems.at[1])]
+    for copy in copies:
+        copy.start()
+    for copy in copies:
+        copy.wait()
+    kept = jnp.broadcast_to(held_gaps[...][None, :].astype(F32), (128, rows))
     kept_t = kept.T.astype(BF16)
     for i in range(cols // 128):
-        part = partials_ref[:, i * 128 : (i + 1) * 128] * kept_t
+        part = held[:, i * 128 : (i + 1) * 128] * kept_t
         turned_ref[i * 128 : (i + 1) * 128, :] = part.T
         half = (first_ref, second_ref)[i // (cols // 256)]
         at = i % (cols // 256) * 128
@@ -104,9 +109,12 @@
     return pl.pallas_call(
         prepare_kernel,
         out_shape=[jax.ShapeDtypeStruct((rows, cols // 2), BF16)] * 2 + [jax.ShapeDtypeStruct((cols, rows), BF16)],
+        in_specs=[pl.BlockSpec(memory_space=pltpu.HBM)] * 2,
+        out_specs=[pl.BlockSpec(memory_space=pltpu.VMEM)] * 3,
+        scratch_shapes=[pltpu.VMEM((rows, cols), BF16), pltpu.VMEM((rows,), jnp.int32), pltpu.SemaphoreType.DMA((2,))],
         compiler_params=pltpu.CompilerParams(vmem_limit_bytes=4 * 1024 * 1024),
         name="prepare",
-    )(partials, gaps[None, :])
+    )(partials, gaps)
 
 
 def table_of(e, meta_ref):
@@ -114,41 +122,45 @@
     return jnp.where(e == 0, 3, jnp.where(e == cut, 1, jnp.where(e == cut + 1, 2, 0)))
 
 
-def filter_left(raw, table, i, rows):
-    white = jnp.dot(raw[i - 1], table[:rows], preferred_element_type=F32)
-    white += jnp.dot(raw[i], table[rows:], preferred_element_type=F32)
-    return white.astype(BF16)
+def at_block(i, rows):
+    return pl.ds(pl.multiple_of(i * rows, rows), rows)
+
+
+def filter_left(raw, i, e, meta_ref, tables_ref):
+    rows = tables_ref.shape[2]
+    table = tables_ref[table_of(e, meta_ref)]
+    window = raw[:, (i - 1) * rows : (i + 1) * rows]
+    return jnp.dot(window, table, preferred_element_type=F32).astype(BF16)
 
 
 def left_kernel(meta_ref, tables_ref, own, other, up_1, down_1, up_2, down_2, out_ref, raw):
-    cols, rows = raw.shape[1:]
+    cols, rows = own.shape
     z, yl = meta_ref[0], meta_ref[1]
-    raw[4 + yl] = own[...]
-    raw[5 - yl] = other[...]
+    raw[:, at_block(4 + yl, rows)] = own[...]
+    raw[:, at_block(5 - yl, rows)] = other[...]
     for dz, piece in ((-2, up_2), (-1, up_1), (1, down_1), (2, down_2)):
-        raw[4 + 2 * dz + yl] = piece[:cols]
-        raw[5 + 2 * dz - yl] = piece[cols:]
+        raw[:, at_block(4 + 2 * dz + yl, rows)] = piece[:cols]
+        raw[:, at_block(5 + 2 * dz - yl, rows)] = piece[cols:]
     for i in range(NE):
         e = (2 * z + i - 4) & (NE - 1)
-        to = pl.ds(pl.multiple_of(e * rows, rows), rows)
         if 1 <= i < 10:
-            out_ref[:, to] = filter_left(raw, tables_ref[table_of(e, meta_ref)], i, rows)
+            out_ref[:, at_block(e, rows)] = filter_left(raw, i, e, meta_ref, tables_ref)
         else:
-            out_ref[:, to] = jnp.zeros((cols, rows), BF16)
+            out_ref[:, at_block(e, rows)] = jnp.zeros((cols, rows), BF16)
 
 
 def right_kernel(meta_ref, tables_ref, *refs):
     pieces = refs[0:12]
     out_ref, raw = refs[12:]
-    rows, half = raw.shape[2:]
+    half = pieces[0].shape[1]
+    rows = tables_ref.shape[1]
     z, x, yh, core = [meta_ref[i] for i in (0, 2, 3, 4)]
-    for h in range(2):
-        raw[h, 0] = jnp.zeros(raw.shape[2:], BF16)
+    raw[:rows] = jnp.zeros((rows, raw.shape[1]), BF16)
 
     def place(piece, b, h, dx, dy, q):
         line = NYH * ((x + dx) & 3) + (yh ^ dy)
         e = 2 * ((line - z + h * (NZ // 2)) & 7) + (core ^ q)
-        raw[h, e + 1] = piece[b * rows : (b + 1) * rows]
+        raw[at_block(e + 1, rows), h * half : (h + 1) * half] = piece[b * rows : (b + 1) * rows]
 
     for q in range(2):
         for dy in range(2):
@@ -157,30 +169,25 @@
         for i in range(4):
             for dy in range(2):
                 place(pieces[6 * q + 2 + i], dy, 1, DX[i], dy, q)
-
-    @pl.loop(0, NE)
-    def _(e):
+    for e in range(NE):
         table = tables_ref[table_of(e, meta_ref)]
-        for h in range(2):
-            white = jnp.dot(table[:, :rows], raw[h, e], preferred_element_type=F32)
-            white += jnp.dot(table[:, rows:], raw[h, e + 1], preferred_element_type=F32)
-            out_ref[pl.ds(pl.multiple_of(e * rows, rows), rows), h * half : (h + 1) * half] = white.astype(BF16)
+        white = jnp.dot(table, raw[e * rows : (e + 2) * rows], preferred_element_type=F32)
+        out_ref[e * rows : (e + 1) * rows] = white.astype(BF16)
 
 
 def product_kernel(scale, meta_ref, tables_ref, left_in, right_ref, up_2, down_2, up_3, down_3, far_own, far_other, out_ref, left_ref, raw):
-    cols, rows = raw.shape[1:]
+    cols, rows = far_own.shape
     z, yl = meta_ref[0], meta_ref[1]
-    raw[0] = down_2[pl.ds(pl.multiple_of((1 ^ yl) * cols, cols), cols)]
-    raw[7] = up_2[pl.ds(pl.multiple_of(yl * cols, cols), cols)]
+    raw[:, :rows] = down_2[at_block(1 ^ yl, cols)]
+    raw[:, 7 * rows :] = up_2[at_block(yl, cols)]
     for at, piece in ((1, down_3), (5, up_3)):
-        raw[at + yl] = piece[:cols]
-        raw[at + 1 - yl] = piece[cols:]
-    raw[3 + yl] = far_own[...]
-    raw[4 - yl] = far_other[...]
+        raw[:, at_block(at + yl, rows)] = piece[:cols]
+        raw[:, at_block(at + 1 - yl, rows)] = piece[cols:]
+    raw[:, at_block(3 + yl, rows)] = far_own[...]
+    raw[:, at_block(4 - yl, rows)] = far_other[...]
     for i in range(1, 8):
         e = (2 * z + i + 5) & (NE - 1)
-        to = pl.ds(pl.multiple_of(e * rows, rows), rows)
-        left_ref[:, to] = filter_left(raw, tables_ref[table_of(e, meta_ref)], i, rows)
+        left_ref[:, at_block(e, rows)] = filter_left(raw, i, e, meta_ref, tables_ref)
     out_ref[...] = jnp.dot(left_ref[...], right_ref[...], preferred_element_type=F32) * scale
 
 
@@ -205,7 +212,7 @@
         out_shape=[jax.ShapeDtypeStruct((cols, cols), F32), jax.ShapeDtypeStruct(left.shape, BF16)],
         in_specs=[pl.BlockSpec(memory_space=pltpu.SMEM)] + [vmem] * (3 + len(pieces)),
         out_specs=[vmem, vmem],
-        scratch_shapes=[pltpu.VMEM((8, cols, rows), BF16)],
+        scratch_shapes=[pltpu.VMEM((cols, 8 * rows), BF16)],
         input_output_aliases={2: 1},
         compiler_params=pltpu.CompilerParams(vmem_limit_bytes=16 * 1024 * 1024),
         name="product",
@@ -235,19 +242,22 @@
         return around(block, "yh", NYH, 1)
 
     sync = lax.optimization_barrier
-    other, up_own, down_own, a, b = sync((around(own, "yl", NYL, 1), up(own), down(own), in_plane(a, 0), in_plane(b, 1)))
-    up_other, down_other, a, b, tables = sync((up(other), down(other), along_z(a, 0), along_z(b, 1), make_tables(meta, taps, rows)))
+    a, b = in_plane(a, 0), in_plane(b, 1)
+    other = around(own, "yl", NYL, 1)
+    up_own, down_own = up(own), down(own)
+    up_own, down_own, up_other, down_other, a, b = sync((up_own, down_own, up(other), down(other), along_z(a, 0), along_z(b, 1)))
     up_1 = jnp.concatenate([up_own, up_other], axis=0)
     down_1 = jnp.concatenate([down_own, down_other], axis=0)
-    up_2, down_2, a_x, b_y = sync((up(up_1), down(down_1), along_x(a), across(b)))
+    tables = make_tables(meta, taps, rows)
+    up_2, down_2, a_x, b_y, tables = sync((up(up_1), down(down_1), along_x(a), across(b), tables))
     a_pack = jnp.concatenate([a] + a_x, axis=0)
     b_pack = jnp.concatenate([b, b_y], axis=0)
-    left = whitened(left_kernel, "left", meta, tables[1], [own, other, up_1, down_1, up_2, down_2], (cols, NE * rows), (10, cols, rows))
+    left = whitened(left_kernel, "left", meta, tables[1], [own, other, up_1, down_1, up_2, down_2], (cols, NE * rows), (cols, 10 * rows))
     up_3, down_3, a_far, b_x, left = sync((up(up_2), down(down_2), across(a_pack), along_x(b_pack), left))
     far_own, far_other = up(up_3[:cols]), down(down_3[cols:])
     mine = [a_pack, a_far, b_pack] + b_x
     theirs = [swapped(piece) for piece in mine]
-    right = whitened(right_kernel, "right", meta, tables[0], mine + theirs, (NE * rows, cols), (2, NE + 1, rows, half))
+    right = whitened(right_kernel, "right", meta, tables[0], mine + theirs, (NE * rows, cols), ((NE + 1) * rows, cols))
     pieces = [up_2, down_2, up_3, down_3, far_own, far_other]
     return product(meta, tables[1], left, right, pieces, rows, (rows * NE) ** (-0.5))
 

time: 100 us -> 95.5 us (0.955)
  waiting for transfers between devices: 36.7 us -> 33.5 us
  Pallas kernels: 14.8 us -> 12.5 us
    ppermute x2, starting transfers between devices: 3.5 us -> 7.76 us  [along_z(): return lax.ppermute(block, ('z', 'x', 'yh'), route)]
    ppermute x2, waiting for transfers between devices: 10.9 us -> 14.6 us  [along_z(): return lax.ppermute(block, ('z', 'x', 'yh'), route)]
    ppermute x25, waiting for transfers between devices: 21.9 us -> 18.4 us  [around(): return lax.ppermute(block, axis, [(i, (i + step) % n) for i in range(n)])]
    ppermute x2, waiting for transfers between devices: 3.86 us -> 0.47 us  [in_plane(): return lax.ppermute(block, axes, route)]
    ppermute x25, starting transfers between devices: 33.5 us -> 30.1 us  [around(): return lax.ppermute(block, axis, [(i, (i + step) % n) for i in range(n)])]
    pallas_call x2, Pallas kernels: 8.22 us -> 5.76 us  [whitened(): pl.pallas_call(kernel, out_shape=jax.ShapeDtypeStruct(shape, BF16), in_sp...]
  transfers between devices with their start and end apart: 29 -> 29, of which waited for: 12 -> 12; matrix products, arithmetic and copies ran while one was open for 1% -> 1% of each run, Pallas kernels for 9% -> 7%
where the time goes in v5:
time: 95.5 us; the launch traced here: 95.3 us
  starting transfers between devices  45.9 us (48%)
  waiting for transfers between devices  33.5 us (35%)
  Pallas kernels  12.5 us (13%)
  local copies, waits for them, and re-layouts  2.55 us (3%)
    ppermute x25, starting transfers between devices, around(): return lax.ppermute(block, axis, [(i, (i + step) % n) for i in range(n)])  30.1 us
    ppermute x25, waiting for transfers between devices, around(): return lax.ppermute(block, axis, [(i, (i + step) % n) for i in range(n)])  18.4 us
    ppermute x2, waiting for transfers between devices, along_z(): return lax.ppermute(block, ('z', 'x', 'yh'), route)  14.6 us
    ppermute x2, starting transfers between devices, in_plane(): return lax.ppermute(block, axes, route)  8.01 us
    ppermute x2, starting transfers between devices, along_z(): return lax.ppermute(block, ('z', 'x', 'yh'), route)  7.76 us
    pallas_call x2, Pallas kernels, whitened(): pl.pallas_call(kernel, out_shape=jax.ShapeDtypeStruct(shape, BF16), in_sp...  5.76 us
    pallas_call x1, Pallas kernels, product(): pl.pallas_call(functools.partial(product_kernel, scale), out_shape=[jax.S...  5.33 us
  transfers between devices with their start and end apart: 29, of which 12 were waited for; matrix products, arithmetic and copies ran while one was open for 1% of the time, Pallas kernels for 7%

profile of v5, /device:TPU:1, one launch (start us, length us, event | category | flops | bytes accessed | tf_op | source)
XLA Modules:
  0.0 95.3 jit_solution(14129738393674632125)
XLA Ops:
  1.9 2.2 %collective-permute-start.2 = (bf16[512,256]{1,0:T(8,128)(2,1)S(1)}, bf16[512,256]{1,0:T(8,128)(2,1)S(1)}, u32[]{:S(2)}, u32[]{:S(2)}) collective-permute-start(bf16[512,256]{1,0:T(8,128)(2,1)S(1)} %get-tuple-element.32.own), channel_id=1, source_target_pairs={{0,16},{16,0},{1,17},{17,1},{2,18},{18,2},{3,19},{19,3},{4,20},{20... | collective-permute-start | bytes 786440 | tf_op jit(solution)/shard_map/ppermute | solution.py:19
  4.1 4.6 %collective-permute-start.5 = (bf16[256,256]{1,0:T(8,128)(2,1)S(1)}, bf16[256,256]{1,0:T(8,128)(2,1)S(1)}, u32[]{:S(2)}, u32[]{:S(2)}) collective-permute-start(bf16[256,256]{1,0:T(8,128)(2,1)S(1)} %get-tuple-element.33), channel_id=1, source_target_pairs={{0,0},{1,16},{2,2},{3,18},{4,4},{5,20},{6,6},{7,22},{8,8},{9,24},{... | collective-permute-start | bytes 393224 | tf_op jit(solution)/shard_map/ppermute | solution.py:44
  8.8 3.4 %collective-permute-start.7 = (bf16[256,256]{1,0:T(8,128)(2,1)S(1)}, bf16[256,256]{1,0:T(8,128)(2,1)S(1)}, u32[]{:S(2)}, u32[]{:S(2)}) collective-permute-start(bf16[256,256]{1,0:T(8,128)(2,1)S(1)} %get-tuple-element.34), channel_id=1, source_target_pairs={{0,8},{1,24},{2,10},{3,26},{4,12},{5,28},{6,14},{7,30},{8,0},{9,16... | collective-permute-start | bytes 393224 | tf_op jit(solution)/shard_map/ppermute | solution.py:44
  13.3 8.0 %collective-permute-start.1 = (bf16[512,256]{1,0:T(8,128)(2,1)S(1)}, bf16[512,256]{1,0:T(8,128)(2,1)S(1)}, u32[]{:S(2)}, u32[]{:S(2)}) collective-permute-start(bf16[512,256]{1,0:T(8,128)(2,1)S(1)} %get-tuple-element.32.own), channel_id=1, source_target_pairs={{0,224},{32,0},{64,32},{96,64},{128,96},{160,128},{192,160},{224,1... | collective-permute-start | bytes 786440 | tf_op jit(solution)/shard_map/ppermute | solution.py:19
  21.8 2.2 %collective-permute-start.4 = (bf16[512,256]{1,0:T(8,128)(2,1)S(1)}, bf16[512,256]{1,0:T(8,128)(2,1)S(1)}, u32[]{:S(2)}, u32[]{:S(2)}) collective-permute-start(bf16[512,256]{1,0:T(8,128)(2,1)S(1)} %collective-permute-done.2.other), channel_id=1, source_target_pairs={{0,224},{32,0},{64,32},{96,64},{128,96},{160,128},{192,160},{224,1... | collective-permute-start | bytes 786440 | tf_op jit(solution)/shard_map/ppermute | solution.py:19
  24.0 7.1 %collective-permute-start.8 = (bf16[256,256]{1,0:T(8,128)(2,1)S(1)}, bf16[256,256]{1,0:T(8,128)(2,1)S(1)}, u32[]{:S(2)}, u32[]{:S(2)}) collective-permute-start(bf16[256,256]{1,0:T(8,128)(2,1)S(1)} %collective-permute-done.7), channel_id=1, source_target_pairs={{8,8},{10,42},{12,76},{14,110},{0,128},{2,162},{4,196},{6,230},{42... | collective-permute-start | bytes 393224 | tf_op jit(solution)/shard_map/ppermute | solution.py:53
  31.1 14.6 %collective-permute-done.8 = bf16[256,256]{1,0:T(8,128)(2,1)S(1)} collective-permute-done((bf16[256,256]{1,0:T(8,128)(2,1)S(1)}, bf16[256,256]{1,0:T(8,128)(2,1)S(1)}, u32[]{:S(2)}, u32[]{:S(2)}) %collective-permute-start.8) | collective-permute-done | bytes 131104 | tf_op jit(solution)/shard_map/ppermute | solution.py:53
  45.9 1.5 %collective-permute-start.9 = (bf16[1024,256]{1,0:T(8,128)(2,1)S(1)}, bf16[1024,256]{1,0:T(8,128)(2,1)S(1)}, u32[]{:S(2)}, u32[]{:S(2)}) collective-permute-start(bf16[1024,256]{1,0:T(8,128)(2,1)S(1)} %constant_dynamic-update-slice_fusion.up_1), channel_id=1, source_target_pairs={{0,32},{32,64},{64,96},{96,128},{128,160},{160,192},{192,224},{224... | collective-permute-start | bytes 1572872 | tf_op jit(solution)/shard_map/ppermute | solution.py:19
  50.1 1.6 %collective-permute-start.12 = (bf16[256,256]{1,0:T(8,128)(2,1)S(1)}, bf16[256,256]{1,0:T(8,128)(2,1)S(1)}, u32[]{:S(2)}, u32[]{:S(2)}) collective-permute-start(bf16[256,256]{1,0:T(8,128)(2,1)S(1)} %collective-permute-done.6), channel_id=1, source_target_pairs={{0,12},{4,0},{8,4},{12,8},{1,13},{5,1},{9,5},{13,9},{2,14},{6,2},{... | collective-permute-start | bytes 393224 | tf_op jit(solution)/shard_map/ppermute | solution.py:19
  51.6 1.1 %collective-permute-done.14 = bf16[256,256]{1,0:T(8,128)(2,1)S(1)} collective-permute-done((bf16[256,256]{1,0:T(8,128)(2,1)S(1)}, bf16[256,256]{1,0:T(8,128)(2,1)S(1)}, u32[]{:S(2)}, u32[]{:S(2)}) %collective-permute-start.14) | collective-permute-done | bytes 131104 | tf_op jit(solution)/shard_map/ppermute | solution.py:19
  52.8 2.6 %collective-permute-done.13 = bf16[256,256]{1,0:T(8,128)(2,1)S(1)} collective-permute-done((bf16[256,256]{1,0:T(8,128)(2,1)S(1)}, bf16[256,256]{1,0:T(8,128)(2,1)S(1)}, u32[]{:S(2)}, u32[]{:S(2)}) %collective-permute-start.13) | collective-permute-done | bytes 131104 | tf_op jit(solution)/shard_map/ppermute | solution.py:19
  55.4 1.2 %collective-permute-done.12 = bf16[256,256]{1,0:T(8,128)(2,1)S(1)} collective-permute-done((bf16[256,256]{1,0:T(8,128)(2,1)S(1)}, bf16[256,256]{1,0:T(8,128)(2,1)S(1)}, u32[]{:S(2)}, u32[]{:S(2)}) %collective-permute-start.12) | collective-permute-done | bytes 131104 | tf_op jit(solution)/shard_map/ppermute | solution.py:19
  56.6 2.7 %collective-permute-done.11 = bf16[256,256]{1,0:T(8,128)(2,1)S(1)} collective-permute-done((bf16[256,256]{1,0:T(8,128)(2,1)S(1)}, bf16[256,256]{1,0:T(8,128)(2,1)S(1)}, u32[]{:S(2)}, u32[]{:S(2)}) %collective-permute-start.11) | collective-permute-done | bytes 131104 | tf_op jit(solution)/shard_map/ppermute | solution.py:19
  60.2 1.8 %collective-permute-start.20 = (bf16[512,256]{1,0:T(8,128)(2,1)S(1)}, bf16[512,256]{1,0:T(8,128)(2,1)S(1)}, u32[]{:S(2)}, u32[]{:S(2)}) collective-permute-start(bf16[512,256]{1,0:T(8,128)(2,1)S(1)} %constant_dynamic-update-slice_fusion.8.refs_2_), channel_id=1, source_target_pairs={{0,8},{4,12},{8,0},{12,4},{1,9},{5,13},{9,1},{13,5},{2,10},{6,14},... | collective-permute-start | bytes 786440 | tf_op jit(solution)/shard_map/ppermute | solution.py:19
  62.5 2.7 %collective-permute-start.16 = (bf16[1024,256]{1,0:T(8,128)(2,1)S(1)}, bf16[1024,256]{1,0:T(8,128)(2,1)S(1)}, u32[]{:S(2)}, u32[]{:S(2)}) collective-permute-start(bf16[1024,256]{1,0:T(8,128)(2,1)S(1)} %collective-permute-done.10.down_2), channel_id=1, source_target_pairs={{0,224},{32,0},{64,32},{96,64},{128,96},{160,128},{192,160},{224,1... | collective-permute-start | bytes 1572872 | tf_op jit(solution)/shard_map/ppermute | solution.py:19
  65.8 2.3 %collective-permute-done.20.refs_5_ = bf16[512,256]{1,0:T(8,128)(2,1)S(1)} collective-permute-done((bf16[512,256]{1,0:T(8,128)(2,1)S(1)}, bf16[512,256]{1,0:T(8,128)(2,1)S(1)}, u32[]{:S(2)}, u32[]{:S(2)}) %collective-permute-start.20) | collective-permute-done | bytes 262176 | tf_op jit(solution)/shard_map/ppermute | solution.py:19
  68.1 2.9 %collective-permute-done.19.refs_4_ = bf16[512,256]{1,0:T(8,128)(2,1)S(1)} collective-permute-done((bf16[512,256]{1,0:T(8,128)(2,1)S(1)}, bf16[512,256]{1,0:T(8,128)(2,1)S(1)}, u32[]{:S(2)}, u32[]{:S(2)}) %collective-permute-start.19) | collective-permute-done | bytes 262176 | tf_op jit(solution)/shard_map/ppermute | solution.py:19
  71.0 4.0 %collective-permute-start.21 = (bf16[1024,256]{1,0:T(8,128)(2,1)S(1)}, bf16[1024,256]{1,0:T(8,128)(2,1)S(1)}, u32[]{:S(2)}, u32[]{:S(2)}) collective-permute-start(bf16[1024,256]{1,0:T(8,128)(2,1)S(1)} %constant_dynamic-update-slice_fusion.4.refs_0_), channel_id=1, source_target_pairs={{0,1},{1,0},{2,3},{3,2},{4,5},{5,4},{6,7},{7,6},{8,9},{9,8},{10,11... | collective-permute-start | bytes 1572872 | tf_op jit(solution)/shard_map/ppermute | solution.py:19
  75.1 2.5 %left.1.left_in = bf16[512,4096]{1,0:T(8,128)(2,1)S(1)} custom-call(s32[7]{0:T(128)S(1)} %stack.27.meta_ref, bf16[4,512,256]{2,1,0:T(8,128)(2,1)S(1)} %get-tuple-element.43.tables_ref, bf16[512,256]{1,0:T(8,128)(2,1)S(1)} %get-tuple-element.32.own, bf16[512,256]{1,0:T(8,128)(2,1)S(1)} %collective-permute-done.2.other, ...), custom_call_target="tpu_custom_call" | custom-call | tf_op jit(solution)/shard_map/left/pallas_call | solution.py:196
  79.6 1.9 %collective-permute-start.28 = (bf16[512,256]{1,0:T(8,128)(2,1)S(1)}, bf16[512,256]{1,0:T(8,128)(2,1)S(1)}, u32[]{:S(2)}, u32[]{:S(2)}) collective-permute-start(bf16[512,256]{1,0:T(8,128)(2,1)S(1)} %slice.7), channel_id=1, source_target_pairs={{0,224},{32,0},{64,32},{96,64},{128,96},{160,128},{192,160},{224,1... | collective-permute-start | bytes 786440 | tf_op jit(solution)/shard_map/ppermute | solution.py:19
  82.3 3.2 %right.1.right_ref = bf16[4096,512]{1,0:T(8,128)(2,1)S(1)} custom-call(s32[7]{0:T(128)S(1)} %stack.27.meta_ref, bf16[4,256,512]{2,1,0:T(8,128)(2,1)S(1)} %get-tuple-element.51.tables_ref, bf16[1024,256]{1,0:T(8,128)(2,1)S(1)} %constant_dynamic-update-slice_fusion.4.refs_0_, bf16[1024,256]{1,0:T(8,128)(2,1)S(1)} %collective-permute-done.17.refs_1_, ...), custom_call_target="tpu_custom_call" | custom-call | tf_op jit(solution)/shard_map/right/pallas_call | solution.py:196
  85.6 2.2 %collective-permute-done.28.far_other = bf16[512,256]{1,0:T(8,128)(2,1)S(1)} collective-permute-done((bf16[512,256]{1,0:T(8,128)(2,1)S(1)}, bf16[512,256]{1,0:T(8,128)(2,1)S(1)}, u32[]{:S(2)}, u32[]{:S(2)}) %collective-permute-start.28) | collective-permute-done | bytes 262176 | tf_op jit(solution)/shard_map/ppermute | solution.py:19
  87.8 2.1 %collective-permute-done.27.far_own = bf16[512,256]{1,0:T(8,128)(2,1)S(1)} collective-permute-done((bf16[512,256]{1,0:T(8,128)(2,1)S(1)}, bf16[512,256]{1,0:T(8,128)(2,1)S(1)}, u32[]{:S(2)}, u32[]{:S(2)}) %collective-permute-start.27) | collective-permute-done | bytes 262176 | tf_op jit(solution)/shard_map/ppermute | solution.py:19
  90.0 5.3 %product.1 = (f32[512,512]{1,0:T(8,128)}, bf16[512,4096]{1,0:T(8,128)(2,1)S(1)}) custom-call(s32[7]{0:T(128)S(1)} %stack.27.meta_ref, bf16[4,512,256]{2,1,0:T(8,128)(2,1)S(1)} %get-tuple-element.43.tables_ref, bf16[512,4096]{1,0:T(8,128)(2,1)S(1)} %left.1.left_in, bf16[4096,512]{1,0:T(8,128)(2,1)S(1)} %right.1.right_ref, ...), custom_call_target="tpu_custom_call", output_to_operand_aliasing={{1}: (2, {})} | custom-call | tf_op jit(solution)/shard_map/product/pallas_call | solution.py:210
  (58 shorter events, 10.5 us)
Async XLA Ops:
  1.9 19.8 %collective-permute-start.2 = (bf16[512,256]{1,0:T(8,128)(2,1)S(1)}, bf16[512,256]{1,0:T(8,128)(2,1)S(1)}, u32[]{:S(2)}, u32[]{:S(2)}) collective-permute-start(bf16[512,256]{1,0:T(8,128)(2,1)S(1)} %get-tuple-element.32.own), channel_id=1, source_target_pairs={{0,16},{16,0},{1,17},{17,1},{2,18},{18,2},{3,19},{19,3},{4,20},{20... | collective-permute-start | bytes 786440 | tf_op jit(solution)/shard_map/ppermute | solution.py:19
  4.1 8.5 %collective-permute-start.5 = (bf16[256,256]{1,0:T(8,128)(2,1)S(1)}, bf16[256,256]{1,0:T(8,128)(2,1)S(1)}, u32[]{:S(2)}, u32[]{:S(2)}) collective-permute-start(bf16[256,256]{1,0:T(8,128)(2,1)S(1)} %get-tuple-element.33), channel_id=1, source_target_pairs={{0,0},{1,16},{2,2},{3,18},{4,4},{5,20},{6,6},{7,22},{8,8},{9,24},{... | collective-permute-start | bytes 393224 | tf_op jit(solution)/shard_map/ppermute | solution.py:44
  8.8 15.2 %collective-permute-start.7 = (bf16[256,256]{1,0:T(8,128)(2,1)S(1)}, bf16[256,256]{1,0:T(8,128)(2,1)S(1)}, u32[]{:S(2)}, u32[]{:S(2)}) collective-permute-start(bf16[256,256]{1,0:T(8,128)(2,1)S(1)} %get-tuple-element.34), channel_id=1, source_target_pairs={{0,8},{1,24},{2,10},{3,26},{4,12},{5,28},{6,14},{7,30},{8,0},{9,16... | collective-permute-start | bytes 393224 | tf_op jit(solution)/shard_map/ppermute | solution.py:44
  12.6 11.3 %collective-permute-start.6 = (bf16[256,256]{1,0:T(8,128)(2,1)S(1)}, bf16[256,256]{1,0:T(8,128)(2,1)S(1)}, u32[]{:S(2)}, u32[]{:S(2)}) collective-permute-start(bf16[256,256]{1,0:T(8,128)(2,1)S(1)} %collective-permute-done.5), channel_id=1, source_target_pairs={{0,0},{2,34},{4,68},{6,102},{8,136},{10,170},{12,204},{14,238},{34... | collective-permute-start | bytes 393224 | tf_op jit(solution)/shard_map/ppermute | solution.py:53
  13.3 32.4 %collective-permute-start.1 = (bf16[512,256]{1,0:T(8,128)(2,1)S(1)}, bf16[512,256]{1,0:T(8,128)(2,1)S(1)}, u32[]{:S(2)}, u32[]{:S(2)}) collective-permute-start(bf16[512,256]{1,0:T(8,128)(2,1)S(1)} %get-tuple-element.32.own), channel_id=1, source_target_pairs={{0,224},{32,0},{64,32},{96,64},{128,96},{160,128},{192,160},{224,1... | collective-permute-start | bytes 786440 | tf_op jit(solution)/shard_map/ppermute | solution.py:19
  21.3 24.4 %collective-permute-start = (bf16[512,256]{1,0:T(8,128)(2,1)S(1)}, bf16[512,256]{1,0:T(8,128)(2,1)S(1)}, u32[]{:S(2)}, u32[]{:S(2)}) collective-permute-start(bf16[512,256]{1,0:T(8,128)(2,1)S(1)} %get-tuple-element.32.own), channel_id=1, source_target_pairs={{0,32},{32,64},{64,96},{96,128},{128,160},{160,192},{192,224},{224... | collective-permute-start | bytes 786440 | tf_op jit(solution)/shard_map/ppermute | solution.py:19
  21.8 23.9 %collective-permute-start.4 = (bf16[512,256]{1,0:T(8,128)(2,1)S(1)}, bf16[512,256]{1,0:T(8,128)(2,1)S(1)}, u32[]{:S(2)}, u32[]{:S(2)}) collective-permute-start(bf16[512,256]{1,0:T(8,128)(2,1)S(1)} %collective-permute-done.2.other), channel_id=1, source_target_pairs={{0,224},{32,0},{64,32},{96,64},{128,96},{160,128},{192,160},{224,1... | collective-permute-start | bytes 786440 | tf_op jit(solution)/shard_map/ppermute | solution.py:19
  23.9 21.8 %collective-permute-start.3 = (bf16[512,256]{1,0:T(8,128)(2,1)S(1)}, bf16[512,256]{1,0:T(8,128)(2,1)S(1)}, u32[]{:S(2)}, u32[]{:S(2)}) collective-permute-start(bf16[512,256]{1,0:T(8,128)(2,1)S(1)} %collective-permute-done.2.other), channel_id=1, source_target_pairs={{0,32},{32,64},{64,96},{96,128},{128,160},{160,192},{192,224},{224... | collective-permute-start | bytes 786440 | tf_op jit(solution)/shard_map/ppermute | solution.py:19
  24.0 21.7 %collective-permute-start.8 = (bf16[256,256]{1,0:T(8,128)(2,1)S(1)}, bf16[256,256]{1,0:T(8,128)(2,1)S(1)}, u32[]{:S(2)}, u32[]{:S(2)}) collective-permute-start(bf16[256,256]{1,0:T(8,128)(2,1)S(1)} %collective-permute-done.7), channel_id=1, source_target_pairs={{8,8},{10,42},{12,76},{14,110},{0,128},{2,162},{4,196},{6,230},{42... | collective-permute-start | bytes 393224 | tf_op jit(solution)/shard_map/ppermute | solution.py:53
  45.8 13.4 %collective-permute-start.10 = (bf16[1024,256]{1,0:T(8,128)(2,1)S(1)}, bf16[1024,256]{1,0:T(8,128)(2,1)S(1)}, u32[]{:S(2)}, u32[]{:S(2)}) collective-permute-start(bf16[1024,256]{1,0:T(8,128)(2,1)S(1)} %constant_dynamic-update-slice_fusion.2.down_1), channel_id=1, source_target_pairs={{0,224},{32,0},{64,32},{96,64},{128,96},{160,128},{192,160},{224,1... | collective-permute-start | bytes 1572872 | tf_op jit(solution)/shard_map/ppermute | solution.py:19
  45.9 14.2 %collective-permute-start.9 = (bf16[1024,256]{1,0:T(8,128)(2,1)S(1)}, bf16[1024,256]{1,0:T(8,128)(2,1)S(1)}, u32[]{:S(2)}, u32[]{:S(2)}) collective-permute-start(bf16[1024,256]{1,0:T(8,128)(2,1)S(1)} %constant_dynamic-update-slice_fusion.up_1), channel_id=1, source_target_pairs={{0,32},{32,64},{64,96},{96,128},{128,160},{160,192},{192,224},{224... | collective-permute-start | bytes 1572872 | tf_op jit(solution)/shard_map/ppermute | solution.py:19
  47.4 5.3 %collective-permute-start.14 = (bf16[256,256]{1,0:T(8,128)(2,1)S(1)}, bf16[256,256]{1,0:T(8,128)(2,1)S(1)}, u32[]{:S(2)}, u32[]{:S(2)}) collective-permute-start(bf16[256,256]{1,0:T(8,128)(2,1)S(1)} %collective-permute-done.8), channel_id=1, source_target_pairs={{0,2},{2,0},{1,3},{3,1},{4,6},{6,4},{5,7},{7,5},{8,10},{10,8},{9,1... | collective-permute-start | bytes 393224 | tf_op jit(solution)/shard_map/ppermute | solution.py:19
  50.0 5.4 %collective-permute-start.13 = (bf16[256,256]{1,0:T(8,128)(2,1)S(1)}, bf16[256,256]{1,0:T(8,128)(2,1)S(1)}, u32[]{:S(2)}, u32[]{:S(2)}) collective-permute-start(bf16[256,256]{1,0:T(8,128)(2,1)S(1)} %collective-permute-done.6), channel_id=1, source_target_pairs={{0,8},{4,12},{8,0},{12,4},{1,9},{5,13},{9,1},{13,5},{2,10},{6,14},... | collective-permute-start | bytes 393224 | tf_op jit(solution)/shard_map/ppermute | solution.py:19
  50.1 6.5 %collective-permute-start.12 = (bf16[256,256]{1,0:T(8,128)(2,1)S(1)}, bf16[256,256]{1,0:T(8,128)(2,1)S(1)}, u32[]{:S(2)}, u32[]{:S(2)}) collective-permute-start(bf16[256,256]{1,0:T(8,128)(2,1)S(1)} %collective-permute-done.6), channel_id=1, source_target_pairs={{0,12},{4,0},{8,4},{12,8},{1,13},{5,1},{9,5},{13,9},{2,14},{6,2},{... | collective-permute-start | bytes 393224 | tf_op jit(solution)/shard_map/ppermute | solution.py:19
  52.8 6.5 %collective-permute-start.11 = (bf16[256,256]{1,0:T(8,128)(2,1)S(1)}, bf16[256,256]{1,0:T(8,128)(2,1)S(1)}, u32[]{:S(2)}, u32[]{:S(2)}) collective-permute-start(bf16[256,256]{1,0:T(8,128)(2,1)S(1)} %collective-permute-done.6), channel_id=1, source_target_pairs={{0,4},{4,8},{8,12},{12,0},{1,5},{5,9},{9,13},{13,1},{2,6},{6,10},{... | collective-permute-start | bytes 393224 | tf_op jit(solution)/shard_map/ppermute | solution.py:19
  60.2 8.0 %collective-permute-start.20 = (bf16[512,256]{1,0:T(8,128)(2,1)S(1)}, bf16[512,256]{1,0:T(8,128)(2,1)S(1)}, u32[]{:S(2)}, u32[]{:S(2)}) collective-permute-start(bf16[512,256]{1,0:T(8,128)(2,1)S(1)} %constant_dynamic-update-slice_fusion.8.refs_2_), channel_id=1, source_target_pairs={{0,8},{4,12},{8,0},{12,4},{1,9},{5,13},{9,1},{13,5},{2,10},{6,14},... | collective-permute-start | bytes 786440 | tf_op jit(solution)/shard_map/ppermute | solution.py:19
  62.0 16.1 %collective-permute-start.17 = (bf16[1024,256]{1,0:T(8,128)(2,1)S(1)}, bf16[1024,256]{1,0:T(8,128)(2,1)S(1)}, u32[]{:S(2)}, u32[]{:S(2)}) collective-permute-start(bf16[1024,256]{1,0:T(8,128)(2,1)S(1)} %constant_dynamic-update-slice_fusion.4.refs_0_), channel_id=1, source_target_pairs={{0,2},{2,0},{1,3},{3,1},{4,6},{6,4},{5,7},{7,5},{8,10},{10,8},{9,1... | collective-permute-start | bytes 1572872 | tf_op jit(solution)/shard_map/ppermute | solution.py:19
  62.5 15.6 %collective-permute-start.15 = (bf16[1024,256]{1,0:T(8,128)(2,1)S(1)}, bf16[1024,256]{1,0:T(8,128)(2,1)S(1)}, u32[]{:S(2)}, u32[]{:S(2)}) collective-permute-start(bf16[1024,256]{1,0:T(8,128)(2,1)S(1)} %collective-permute-done.9.up_2), channel_id=1, source_target_pairs={{0,32},{32,64},{64,96},{96,128},{128,160},{160,192},{192,224},{224... | collective-permute-start | bytes 1572872 | tf_op jit(solution)/shard_map/ppermute | solution.py:19
  62.5 15.6 %collective-permute-start.16 = (bf16[1024,256]{1,0:T(8,128)(2,1)S(1)}, bf16[1024,256]{1,0:T(8,128)(2,1)S(1)}, u32[]{:S(2)}, u32[]{:S(2)}) collective-permute-start(bf16[1024,256]{1,0:T(8,128)(2,1)S(1)} %collective-permute-done.10.down_2), channel_id=1, source_target_pairs={{0,224},{32,0},{64,32},{96,64},{128,96},{160,128},{192,160},{224,1... | collective-permute-start | bytes 1572872 | tf_op jit(solution)/shard_map/ppermute | solution.py:19
  65.2 5.8 %collective-permute-start.19 = (bf16[512,256]{1,0:T(8,128)(2,1)S(1)}, bf16[512,256]{1,0:T(8,128)(2,1)S(1)}, u32[]{:S(2)}, u32[]{:S(2)}) collective-permute-start(bf16[512,256]{1,0:T(8,128)(2,1)S(1)} %constant_dynamic-update-slice_fusion.8.refs_2_), channel_id=1, source_target_pairs={{0,12},{4,0},{8,4},{12,8},{1,13},{5,1},{9,5},{13,9},{2,14},{6,2},{... | collective-permute-start | bytes 786440 | tf_op jit(solution)/shard_map/ppermute | solution.py:19
  68.1 9.4 %collective-permute-start.18 = (bf16[512,256]{1,0:T(8,128)(2,1)S(1)}, bf16[512,256]{1,0:T(8,128)(2,1)S(1)}, u32[]{:S(2)}, u32[]{:S(2)}) collective-permute-start(bf16[512,256]{1,0:T(8,128)(2,1)S(1)} %constant_dynamic-update-slice_fusion.8.refs_2_), channel_id=1, source_target_pairs={{0,4},{4,8},{8,12},{12,0},{1,5},{5,9},{9,13},{13,1},{2,6},{6,10},{... | collective-permute-start | bytes 786440 | tf_op jit(solution)/shard_map/ppermute | solution.py:19
  71.0 8.6 %collective-permute-start.21 = (bf16[1024,256]{1,0:T(8,128)(2,1)S(1)}, bf16[1024,256]{1,0:T(8,128)(2,1)S(1)}, u32[]{:S(2)}, u32[]{:S(2)}) collective-permute-start(bf16[1024,256]{1,0:T(8,128)(2,1)S(1)} %constant_dynamic-update-slice_fusion.4.refs_0_), channel_id=1, source_target_pairs={{0,1},{1,0},{2,3},{3,2},{4,5},{5,4},{6,7},{7,6},{8,9},{9,8},{10,11... | collective-permute-start | bytes 1572872 | tf_op jit(solution)/shard_map/ppermute | solution.py:19
  79.6 8.2 %collective-permute-start.28 = (bf16[512,256]{1,0:T(8,128)(2,1)S(1)}, bf16[512,256]{1,0:T(8,128)(2,1)S(1)}, u32[]{:S(2)}, u32[]{:S(2)}) collective-permute-start(bf16[512,256]{1,0:T(8,128)(2,1)S(1)} %slice.7), channel_id=1, source_target_pairs={{0,224},{32,0},{64,32},{96,64},{128,96},{160,128},{192,160},{224,1... | collective-permute-start | bytes 786440 | tf_op jit(solution)/shard_map/ppermute | solution.py:19
  81.6 8.4 %collective-permute-start.27 = (bf16[512,256]{1,0:T(8,128)(2,1)S(1)}, bf16[512,256]{1,0:T(8,128)(2,1)S(1)}, u32[]{:S(2)}, u32[]{:S(2)}) collective-permute-start(bf16[512,256]{1,0:T(8,128)(2,1)S(1)} %slice.6), channel_id=1, source_target_pairs={{0,32},{32,64},{64,96},{96,128},{128,160},{160,192},{192,224},{224... | collective-permute-start | bytes 786440 | tf_op jit(solution)/shard_map/ppermute | solution.py:19
  (7 other events, 17.6 us)

commit v6 on v5

--- a/solution.py
+++ b/solution.py
@@ -2,6 +2,7 @@
 
 import jax
 import jax.numpy as jnp
+import numpy as np
 from jax import lax
 from jax.experimental import pallas as pl
 from jax.experimental.pallas import tpu as pltpu
@@ -13,17 +14,23 @@
 NE = NZ * NYL
 BF16, F32 = jnp.bfloat16, jnp.float32
 DX = (0, -1, 1, 2)
+LINE = (
+    (5, 4, 7, 6, 1, 0, 2, 3),
+    (0, 1, 3, 2, 4, 5, 7, 6),
+    (2, 6, 5, 0, 3, 7, 1, 4),
+    (3, 7, 4, 1, 2, 6, 0, 5),
+    (1, 0, 6, 7, 5, 4, 3, 2),
+    (4, 5, 2, 3, 0, 1, 6, 7),
+    (6, 3, 1, 4, 7, 2, 5, 0),
+    (7, 2, 0, 5, 6, 3, 4, 1),
+)
 
 
 def around(block, axis, n, step):
     return lax.ppermute(block, axis, [(i, (i + step) % n) for i in range(n)])
 
 
-def line_of(z_from, z, half):
-    return (z_from + z + half * (NZ // 2)) % NZ
-
-
-def in_plane(block, half):
+def in_plane(block):
     axes = ("z", "yl", "x", "yh", "c")
     sizes = (NZ, NYL, NX, NYH, NC)
 
@@ -39,16 +46,16 @@
             for x in range(NX):
                 for yh in range(NYH):
                     for c in range(NC):
-                        line = line_of(z, NYH * x + yh, half)
+                        line = LINE[z][NYH * x + yh]
                         route.append((flat((z, yl, x, yh, c)), flat((z, c, line // NYH, line % NYH, yl))))
     return lax.ppermute(block, axes, route)
 
 
-def along_z(block, half):
+def along_z(block):
     route = []
     for z_from in range(NZ):
         for z in range(NZ):
-            line = line_of(z_from, z, half)
+            line = LINE[z_from][z]
             route.append(((z_from * NX + line // NYH) * NYH + line % NYH, (z * NX + line // NYH) * NYH + line % NYH))
     return lax.ppermute(block, ("z", "x", "yh"), route)
 
@@ -87,7 +94,7 @@
     )(meta, padded)
 
 
-def prepare_kernel(partials_ref, gaps_ref, first_ref, second_ref, turned_ref, held, held_gaps, sems):
+def prepare_kernel(partials_ref, gaps_ref, halves_ref, turned_ref, held, held_gaps, sems):
     rows, cols = held.shape
     copies = [pltpu.make_async_copy(gaps_ref, held_gaps, sems.at[0]), pltpu.make_async_copy(partials_ref, held, sems.at[1])]
     for copy in copies:
@@ -99,18 +106,17 @@
     for i in range(cols // 128):
         part = held[:, i * 128 : (i + 1) * 128] * kept_t
         turned_ref[i * 128 : (i + 1) * 128, :] = part.T
-        half = (first_ref, second_ref)[i // (cols // 256)]
-        at = i % (cols // 256) * 128
-        half[:, at : at + 128] = part
+        half, at = i // (cols // 256), i % (cols // 256) * 128
+        halves_ref[half * rows : (half + 1) * rows, at : at + 128] = part
 
 
 def prepare(partials, gaps):
     rows, cols = partials.shape
     return pl.pallas_call(
         prepare_kernel,
-        out_shape=[jax.ShapeDtypeStruct((rows, cols // 2), BF16)] * 2 + [jax.ShapeDtypeStruct((cols, rows), BF16)],
+        out_shape=[jax.ShapeDtypeStruct((2 * rows, cols // 2), BF16), jax.ShapeDtypeStruct((cols, rows), BF16)],
         in_specs=[pl.BlockSpec(memory_space=pltpu.HBM)] * 2,
-        out_specs=[pl.BlockSpec(memory_space=pltpu.VMEM)] * 3,
+        out_specs=[pl.BlockSpec(memory_space=pltpu.VMEM)] * 2,
         scratch_shapes=[pltpu.VMEM((rows, cols), BF16), pltpu.VMEM((rows,), jnp.int32), pltpu.SemaphoreType.DMA((2,))],
         compiler_params=pltpu.CompilerParams(vmem_limit_bytes=4 * 1024 * 1024),
         name="prepare",
@@ -154,12 +160,12 @@
     out_ref, raw = refs[12:]
     half = pieces[0].shape[1]
     rows = tables_ref.shape[1]
-    z, x, yh, core = [meta_ref[i] for i in (0, 2, 3, 4)]
+    x, yh, core = [meta_ref[i] for i in (2, 3, 4)]
     raw[:rows] = jnp.zeros((rows, raw.shape[1]), BF16)
 
     def place(piece, b, h, dx, dy, q):
         line = NYH * ((x + dx) & 3) + (yh ^ dy)
-        e = 2 * ((line - z + h * (NZ // 2)) & 7) + (core ^ q)
+        e = 2 * meta_ref[7 + line] + (core ^ q)
         raw[at_block(e + 1, rows), h * half : (h + 1) * half] = piece[b * rows : (b + 1) * rows]
 
     for q in range(2):
@@ -223,8 +229,10 @@
     rows, cols = partials.shape
     half = cols // 2
     places = [lax.axis_index(axis) for axis in EPOCH + COL]
+    origin = np.argsort(np.array(LINE, np.int32), axis=0).T.astype(np.int32)
     meta = jnp.stack(places + [arc_start[0], arc_start[0] // rows]).astype(jnp.int32)
-    a, b, own = prepare(partials, gaps)
+    meta = jnp.concatenate([meta, jnp.asarray(origin)[places[0]]])
+    halves, own = prepare(partials, gaps)
 
     def up(block):
         return around(block, "z", NZ, 1)
@@ -242,16 +250,18 @@
         return around(block, "yh", NYH, 1)
 
     sync = lax.optimization_barrier
-    a, b = in_plane(a, 0), in_plane(b, 1)
+    halves = in_plane(halves)
     other = around(own, "yl", NYL, 1)
     up_own, down_own = up(own), down(own)
-    up_own, down_own, up_other, down_other, a, b = sync((up_own, down_own, up(other), down(other), along_z(a, 0), along_z(b, 1)))
+    up_own, down_own, up_other, down_other, halves = sync((up_own, down_own, up(other), down(other), along_z(halves)))
+    a, b = halves[:rows], halves[rows:]
     up_1 = jnp.concatenate([up_own, up_other], axis=0)
     down_1 = jnp.concatenate([down_own, down_other], axis=0)
     tables = make_tables(meta, taps, rows)
-    up_2, down_2, a_x, b_y, tables = sync((up(up_1), down(down_1), along_x(a), across(b), tables))
+    a_x, b_y, tables = sync((along_x(a), across(b), tables))
     a_pack = jnp.concatenate([a] + a_x, axis=0)
     b_pack = jnp.concatenate([b, b_y], axis=0)
+    up_2, down_2, a_pack, b_pack = sync((up(up_1), down(down_1), a_pack, b_pack))
     left = whitened(left_kernel, "left", meta, tables[1], [own, other, up_1, down_1, up_2, down_2], (cols, NE * rows), (cols, 10 * rows))
     up_3, down_3, a_far, b_x, left = sync((up(up_2), down(down_2), across(a_pack), along_x(b_pack), left))
     far_own, far_other = up(up_3[:cols]), down(down_3[cols:])

time: 95.5 us -> 93.9 us (0.983)
  waiting for transfers between devices: 33.5 us -> 24.7 us
  starting transfers between devices: 45.9 us -> 52.4 us
    ppermute x2 -> x1, waiting for transfers between devices: 14.6 us -> 3.8 us  [along_z(): return lax.ppermute(block, ('z', 'x', 'yh'), route)]
    ppermute x25, starting transfers between devices: 30.1 us -> 38.4 us  [around(): return lax.ppermute(block, axis, [(i, (i + step) % n) for i in range(n)])]
    ppermute x2 -> x1, starting transfers between devices: 7.76 us -> 5.52 us  [along_z(): return lax.ppermute(block, ('z', 'x', 'yh'), route)]
    ppermute x2 -> x1, waiting for transfers between devices: 0.47 us -> 2.23 us  [in_plane(): return lax.ppermute(block, axes, route)]
    ppermute x2 -> x1, starting transfers between devices: 8.01 us -> 8.49 us  [in_plane(): return lax.ppermute(block, axes, route)]
  transfers between devices with their start and end apart: 29 -> 27, of which waited for: 12 -> 11; matrix products, arithmetic and copies ran while one was open for 1% -> 2% of each run, Pallas kernels for 7% -> 7%
where the time goes in v6:
time: 93.9 us; the launch traced here: 93.7 us
  starting transfers between devices  52.4 us (56%)
  waiting for transfers between devices  24.7 us (26%)
  Pallas kernels  12.4 us (13%)
  local copies, waits for them, and re-layouts  3.2 us (3%)
    ppermute x25, starting transfers between devices, around(): return lax.ppermute(block, axis, [(i, (i + step) % n) for i in range(n)])  38.4 us
    ppermute x25, waiting for transfers between devices, around(): return lax.ppermute(block, axis, [(i, (i + step) % n) for i in range(n)])  18.7 us
    ppermute x1, starting transfers between devices, in_plane(): return lax.ppermute(block, axes, route)  8.49 us
    pallas_call x2, Pallas kernels, whitened(): pl.pallas_call(kernel, out_shape=jax.ShapeDtypeStruct(shape, BF16), in_sp...  5.75 us
    ppermute x1, starting transfers between devices, along_z(): return lax.ppermute(block, ('z', 'x', 'yh'), route)  5.52 us
    pallas_call x1, Pallas kernels, product(): pl.pallas_call(functools.partial(product_kernel, scale), out_shape=[jax.S...  5.33 us
    ppermute x1, waiting for transfers between devices, along_z(): return lax.ppermute(block, ('z', 'x', 'yh'), route)  3.8 us
    ppermute x1, waiting for transfers between devices, in_plane(): return lax.ppermute(block, axes, route)  2.23 us
  transfers between devices with their start and end apart: 27, of which 11 were waited for; matrix products, arithmetic and copies ran while one was open for 2% of the time, Pallas kernels for 7%

profile of v6, /device:TPU:1, one launch (start us, length us, event | category | flops | bytes accessed | tf_op | source)
XLA Modules:
  0.0 93.7 jit_solution(6274528432491535808)
XLA Ops:
  1.9 8.5 %collective-permute-start.5 = (bf16[512,256]{1,0:T(8,128)(2,1)S(1)}, bf16[512,256]{1,0:T(8,128)(2,1)S(1)}, u32[]{:S(2)}, u32[]{:S(2)}) collective-permute-start(bf16[512,256]{1,0:T(8,128)(2,1)S(1)} %get-tuple-element.33), channel_id=1, source_target_pairs={{0,10},{1,26},{2,8},{3,24},{4,14},{5,30},{6,12},{7,28},{8,2},{9,18... | collective-permute-start | bytes 786440 | tf_op jit(solution)/shard_map/ppermute | solution.py:51
  10.5 5.4 %collective-permute-start.1 = (bf16[512,256]{1,0:T(8,128)(2,1)S(1)}, bf16[512,256]{1,0:T(8,128)(2,1)S(1)}, u32[]{:S(2)}, u32[]{:S(2)}) collective-permute-start(bf16[512,256]{1,0:T(8,128)(2,1)S(1)} %get-tuple-element.32.own), channel_id=1, source_target_pairs={{0,224},{32,0},{64,32},{96,64},{128,96},{160,128},{192,160},{224,1... | collective-permute-start | bytes 786440 | tf_op jit(solution)/shard_map/ppermute | solution.py:30
  15.9 2.2 %collective-permute-done.5 = bf16[512,256]{1,0:T(8,128)(2,1)S(1)} collective-permute-done((bf16[512,256]{1,0:T(8,128)(2,1)S(1)}, bf16[512,256]{1,0:T(8,128)(2,1)S(1)}, u32[]{:S(2)}, u32[]{:S(2)}) %collective-permute-start.5) | collective-permute-done | bytes 262176 | tf_op jit(solution)/shard_map/ppermute | solution.py:51
  18.1 5.5 %collective-permute-start.6 = (bf16[512,256]{1,0:T(8,128)(2,1)S(1)}, bf16[512,256]{1,0:T(8,128)(2,1)S(1)}, u32[]{:S(2)}, u32[]{:S(2)}) collective-permute-start(bf16[512,256]{1,0:T(8,128)(2,1)S(1)} %collective-permute-done.5), channel_id=1, source_target_pairs={{10,10},{8,40},{14,78},{12,108},{2,130},{0,160},{4,196},{6,230},{3... | collective-permute-start | bytes 786440 | tf_op jit(solution)/shard_map/ppermute | solution.py:60
  25.2 3.8 %collective-permute-done.6 = bf16[512,256]{1,0:T(8,128)(2,1)S(1)} collective-permute-done((bf16[512,256]{1,0:T(8,128)(2,1)S(1)}, bf16[512,256]{1,0:T(8,128)(2,1)S(1)}, u32[]{:S(2)}, u32[]{:S(2)}) %collective-permute-start.6) | collective-permute-done | bytes 262176 | tf_op jit(solution)/shard_map/ppermute | solution.py:60
  29.0 5.6 %collective-permute-done.4 = bf16[512,256]{1,0:T(8,128)(2,1)S(1)} collective-permute-done((bf16[512,256]{1,0:T(8,128)(2,1)S(1)}, bf16[512,256]{1,0:T(8,128)(2,1)S(1)}, u32[]{:S(2)}, u32[]{:S(2)}) %collective-permute-start.4) | collective-permute-done | bytes 262176 | tf_op jit(solution)/shard_map/ppermute | solution.py:30
  34.6 1.2 %collective-permute-done.3 = bf16[512,256]{1,0:T(8,128)(2,1)S(1)} collective-permute-done((bf16[512,256]{1,0:T(8,128)(2,1)S(1)}, bf16[512,256]{1,0:T(8,128)(2,1)S(1)}, u32[]{:S(2)}, u32[]{:S(2)}) %collective-permute-start.3) | collective-permute-done | bytes 262176 | tf_op jit(solution)/shard_map/ppermute | solution.py:30
  35.9 2.3 %collective-permute-start.12 = (bf16[1024,256]{1,0:T(8,128)(2,1)S(1)}, bf16[1024,256]{1,0:T(8,128)(2,1)S(1)}, u32[]{:S(2)}, u32[]{:S(2)}) collective-permute-start(bf16[1024,256]{1,0:T(8,128)(2,1)S(1)} %constant_dynamic-update-slice_fusion.2.down_1), channel_id=1, source_target_pairs={{0,224},{32,0},{64,32},{96,64},{128,96},{160,128},{192,160},{224,1... | collective-permute-start | bytes 1572872 | tf_op jit(solution)/shard_map/ppermute | solution.py:30
  38.4 7.4 %collective-permute-start.10 = (bf16[256,256]{1,0:T(8,128)(2,1)S(1)}, bf16[256,256]{1,0:T(8,128)(2,1)S(1)}, u32[]{:S(2)}, u32[]{:S(2)}) collective-permute-start(bf16[256,256]{1,0:T(8,128)(2,1)S(1)} %get-tuple-element.59), channel_id=1, source_target_pairs={{0,2},{2,0},{1,3},{3,1},{4,6},{6,4},{5,7},{7,5},{8,10},{10,8},{9,1... | collective-permute-start | bytes 393224 | tf_op jit(solution)/shard_map/ppermute | solution.py:30
  45.8 3.2 %collective-permute-start.9 = (bf16[256,256]{1,0:T(8,128)(2,1)S(1)}, bf16[256,256]{1,0:T(8,128)(2,1)S(1)}, u32[]{:S(2)}, u32[]{:S(2)}) collective-permute-start(bf16[256,256]{1,0:T(8,128)(2,1)S(1)} %get-tuple-element.60), channel_id=1, source_target_pairs={{0,8},{4,12},{8,0},{12,4},{1,9},{5,13},{9,1},{13,5},{2,10},{6,14},... | collective-permute-start | bytes 393224 | tf_op jit(solution)/shard_map/ppermute | solution.py:30
  49.0 1.5 %collective-permute-start.7 = (bf16[256,256]{1,0:T(8,128)(2,1)S(1)}, bf16[256,256]{1,0:T(8,128)(2,1)S(1)}, u32[]{:S(2)}, u32[]{:S(2)}) collective-permute-start(bf16[256,256]{1,0:T(8,128)(2,1)S(1)} %get-tuple-element.60), channel_id=1, source_target_pairs={{0,4},{4,8},{8,12},{12,0},{1,5},{5,9},{9,13},{13,1},{2,6},{6,10},{... | collective-permute-start | bytes 393224 | tf_op jit(solution)/shard_map/ppermute | solution.py:30
  52.6 1.1 %tables.1 = (bf16[4,256,512]{2,1,0:T(8,128)(2,1)S(1)}, bf16[4,512,256]{2,1,0:T(8,128)(2,1)S(1)}) custom-call(s32[15]{0:T(128)S(1)} %concatenate.15.meta_ref, bf16[1,256]{1,0:T(2,128)(2,1)S(1)} %broadcast_in_dim.3.taps_ref), custom_call_target="tpu_custom_call" | custom-call | tf_op jit(solution)/shard_map/tables/pallas_call | solution.py:87
  53.7 1.6 %collective-permute-done.7 = bf16[256,256]{1,0:T(8,128)(2,1)S(1)} collective-permute-done((bf16[256,256]{1,0:T(8,128)(2,1)S(1)}, bf16[256,256]{1,0:T(8,128)(2,1)S(1)}, u32[]{:S(2)}, u32[]{:S(2)}) %collective-permute-start.7) | collective-permute-done | bytes 131104 | tf_op jit(solution)/shard_map/ppermute | solution.py:30
  55.4 1.1 %collective-permute-start.18 = (bf16[512,256]{1,0:T(8,128)(2,1)S(1)}, bf16[512,256]{1,0:T(8,128)(2,1)S(1)}, u32[]{:S(2)}, u32[]{:S(2)}) collective-permute-start(bf16[512,256]{1,0:T(8,128)(2,1)S(1)} %pad_maximum_fusion.1.refs_2_), channel_id=1, source_target_pairs={{0,8},{4,12},{8,0},{12,4},{1,9},{5,13},{9,1},{13,5},{2,10},{6,14},... | collective-permute-start | bytes 786440 | tf_op jit(solution)/shard_map/ppermute | solution.py:30
  56.4 2.2 %collective-permute-start.13 = (bf16[1024,256]{1,0:T(8,128)(2,1)S(1)}, bf16[1024,256]{1,0:T(8,128)(2,1)S(1)}, u32[]{:S(2)}, u32[]{:S(2)}) collective-permute-start(bf16[1024,256]{1,0:T(8,128)(2,1)S(1)} %collective-permute-done.11.up_2), channel_id=1, source_target_pairs={{0,32},{32,64},{64,96},{96,128},{128,160},{160,192},{192,224},{224... | collective-permute-start | bytes 1572872 | tf_op jit(solution)/shard_map/ppermute | solution.py:30
  59.1 5.0 %collective-permute-start.15 = (bf16[1024,256]{1,0:T(8,128)(2,1)S(1)}, bf16[1024,256]{1,0:T(8,128)(2,1)S(1)}, u32[]{:S(2)}, u32[]{:S(2)}) collective-permute-start(bf16[1024,256]{1,0:T(8,128)(2,1)S(1)} %pad_maximum_fusion.refs_0_), channel_id=1, source_target_pairs={{0,2},{2,0},{1,3},{3,1},{4,6},{6,4},{5,7},{7,5},{8,10},{10,8},{9,1... | collective-permute-start | bytes 1572872 | tf_op jit(solution)/shard_map/ppermute | solution.py:30
  64.1 1.5 %collective-permute-start.16 = (bf16[512,256]{1,0:T(8,128)(2,1)S(1)}, bf16[512,256]{1,0:T(8,128)(2,1)S(1)}, u32[]{:S(2)}, u32[]{:S(2)}) collective-permute-start(bf16[512,256]{1,0:T(8,128)(2,1)S(1)} %pad_maximum_fusion.1.refs_2_), channel_id=1, source_target_pairs={{0,4},{4,8},{8,12},{12,0},{1,5},{5,9},{9,13},{13,1},{2,6},{6,10},{... | collective-permute-start | bytes 786440 | tf_op jit(solution)/shard_map/ppermute | solution.py:30
  65.6 4.0 %collective-permute-done.17.refs_4_ = bf16[512,256]{1,0:T(8,128)(2,1)S(1)} collective-permute-done((bf16[512,256]{1,0:T(8,128)(2,1)S(1)}, bf16[512,256]{1,0:T(8,128)(2,1)S(1)}, u32[]{:S(2)}, u32[]{:S(2)}) %collective-permute-start.17) | collective-permute-done | bytes 262176 | tf_op jit(solution)/shard_map/ppermute | solution.py:30
  69.7 4.6 %collective-permute-start.19 = (bf16[1024,256]{1,0:T(8,128)(2,1)S(1)}, bf16[1024,256]{1,0:T(8,128)(2,1)S(1)}, u32[]{:S(2)}, u32[]{:S(2)}) collective-permute-start(bf16[1024,256]{1,0:T(8,128)(2,1)S(1)} %pad_maximum_fusion.refs_0_), channel_id=1, source_target_pairs={{0,1},{1,0},{2,3},{3,2},{4,5},{5,4},{6,7},{7,6},{8,9},{9,8},{10,11... | collective-permute-start | bytes 1572872 | tf_op jit(solution)/shard_map/ppermute | solution.py:30
  74.2 2.5 %left.1.left_in = bf16[512,4096]{1,0:T(8,128)(2,1)S(1)} custom-call(s32[15]{0:T(128)S(1)} %concatenate.15.meta_ref, bf16[4,512,256]{2,1,0:T(8,128)(2,1)S(1)} %get-tuple-element.37.tables_ref, bf16[512,256]{1,0:T(8,128)(2,1)S(1)} %get-tuple-element.32.own, bf16[512,256]{1,0:T(8,128)(2,1)S(1)} %collective-permute-done.2.other, ...), custom_call_target="tpu_custom_call" | custom-call | tf_op jit(solution)/shard_map/left/pallas_call | solution.py:202
  80.3 3.2 %right.1.right_ref = bf16[4096,512]{1,0:T(8,128)(2,1)S(1)} custom-call(s32[15]{0:T(128)S(1)} %concatenate.15.meta_ref, bf16[4,256,512]{2,1,0:T(8,128)(2,1)S(1)} %get-tuple-element.51.tables_ref, bf16[1024,256]{1,0:T(8,128)(2,1)S(1)} %pad_maximum_fusion.refs_0_, bf16[1024,256]{1,0:T(8,128)(2,1)S(1)} %collective-permute-done.15.refs_1_, ...), custom_call_target="tpu_custom_call" | custom-call | tf_op jit(solution)/shard_map/right/pallas_call | solution.py:202
  83.5 2.6 %collective-permute-done.26.far_other = bf16[512,256]{1,0:T(8,128)(2,1)S(1)} collective-permute-done((bf16[512,256]{1,0:T(8,128)(2,1)S(1)}, bf16[512,256]{1,0:T(8,128)(2,1)S(1)}, u32[]{:S(2)}, u32[]{:S(2)}) %collective-permute-start.26) | collective-permute-done | bytes 262176 | tf_op jit(solution)/shard_map/ppermute | solution.py:30
  86.1 2.2 %collective-permute-done.25.far_own = bf16[512,256]{1,0:T(8,128)(2,1)S(1)} collective-permute-done((bf16[512,256]{1,0:T(8,128)(2,1)S(1)}, bf16[512,256]{1,0:T(8,128)(2,1)S(1)}, u32[]{:S(2)}, u32[]{:S(2)}) %collective-permute-start.25) | collective-permute-done | bytes 262176 | tf_op jit(solution)/shard_map/ppermute | solution.py:30
  88.4 5.3 %product.1 = (f32[512,512]{1,0:T(8,128)}, bf16[512,4096]{1,0:T(8,128)(2,1)S(1)}) custom-call(s32[15]{0:T(128)S(1)} %concatenate.15.meta_ref, bf16[4,512,256]{2,1,0:T(8,128)(2,1)S(1)} %get-tuple-element.37.tables_ref, bf16[512,4096]{1,0:T(8,128)(2,1)S(1)} %left.1.left_in, bf16[4096,512]{1,0:T(8,128)(2,1)S(1)} %right.1.right_ref, ...), custom_call_target="tpu_custom_call", output_to_operand_aliasing={{1}: (2, {})} | custom-call | tf_op jit(solution)/shard_map/product/pallas_call | solution.py:216
  (52 shorter events, 9.2 us)
Async XLA Ops:
  1.9 16.2 %collective-permute-start.5 = (bf16[512,256]{1,0:T(8,128)(2,1)S(1)}, bf16[512,256]{1,0:T(8,128)(2,1)S(1)}, u32[]{:S(2)}, u32[]{:S(2)}) collective-permute-start(bf16[512,256]{1,0:T(8,128)(2,1)S(1)} %get-tuple-element.33), channel_id=1, source_target_pairs={{0,10},{1,26},{2,8},{3,24},{4,14},{5,30},{6,12},{7,28},{8,2},{9,18... | collective-permute-start | bytes 786440 | tf_op jit(solution)/shard_map/ppermute | solution.py:51
  10.4 13.2 %collective-permute-start.2 = (bf16[512,256]{1,0:T(8,128)(2,1)S(1)}, bf16[512,256]{1,0:T(8,128)(2,1)S(1)}, u32[]{:S(2)}, u32[]{:S(2)}) collective-permute-start(bf16[512,256]{1,0:T(8,128)(2,1)S(1)} %get-tuple-element.32.own), channel_id=1, source_target_pairs={{0,16},{16,0},{1,17},{17,1},{2,18},{18,2},{3,19},{19,3},{4,20},{20... | collective-permute-start | bytes 786440 | tf_op jit(solution)/shard_map/ppermute | solution.py:30
  10.5 14.7 %collective-permute-start.1 = (bf16[512,256]{1,0:T(8,128)(2,1)S(1)}, bf16[512,256]{1,0:T(8,128)(2,1)S(1)}, u32[]{:S(2)}, u32[]{:S(2)}) collective-permute-start(bf16[512,256]{1,0:T(8,128)(2,1)S(1)} %get-tuple-element.32.own), channel_id=1, source_target_pairs={{0,224},{32,0},{64,32},{96,64},{128,96},{160,128},{192,160},{224,1... | collective-permute-start | bytes 786440 | tf_op jit(solution)/shard_map/ppermute | solution.py:30
  15.9 9.3 %collective-permute-start = (bf16[512,256]{1,0:T(8,128)(2,1)S(1)}, bf16[512,256]{1,0:T(8,128)(2,1)S(1)}, u32[]{:S(2)}, u32[]{:S(2)}) collective-permute-start(bf16[512,256]{1,0:T(8,128)(2,1)S(1)} %get-tuple-element.32.own), channel_id=1, source_target_pairs={{0,32},{32,64},{64,96},{96,128},{128,160},{160,192},{192,224},{224... | collective-permute-start | bytes 786440 | tf_op jit(solution)/shard_map/ppermute | solution.py:30
  18.1 10.9 %collective-permute-start.6 = (bf16[512,256]{1,0:T(8,128)(2,1)S(1)}, bf16[512,256]{1,0:T(8,128)(2,1)S(1)}, u32[]{:S(2)}, u32[]{:S(2)}) collective-permute-start(bf16[512,256]{1,0:T(8,128)(2,1)S(1)} %collective-permute-done.5), channel_id=1, source_target_pairs={{10,10},{8,40},{14,78},{12,108},{2,130},{0,160},{4,196},{6,230},{3... | collective-permute-start | bytes 786440 | tf_op jit(solution)/shard_map/ppermute | solution.py:60
  23.7 11.0 %collective-permute-start.4 = (bf16[512,256]{1,0:T(8,128)(2,1)S(1)}, bf16[512,256]{1,0:T(8,128)(2,1)S(1)}, u32[]{:S(2)}, u32[]{:S(2)}) collective-permute-start(bf16[512,256]{1,0:T(8,128)(2,1)S(1)} %collective-permute-done.2.other), channel_id=1, source_target_pairs={{0,224},{32,0},{64,32},{96,64},{128,96},{160,128},{192,160},{224,1... | collective-permute-start | bytes 786440 | tf_op jit(solution)/shard_map/ppermute | solution.py:30
  24.6 11.2 %collective-permute-start.3 = (bf16[512,256]{1,0:T(8,128)(2,1)S(1)}, bf16[512,256]{1,0:T(8,128)(2,1)S(1)}, u32[]{:S(2)}, u32[]{:S(2)}) collective-permute-start(bf16[512,256]{1,0:T(8,128)(2,1)S(1)} %collective-permute-done.2.other), channel_id=1, source_target_pairs={{0,32},{32,64},{64,96},{96,128},{128,160},{160,192},{192,224},{224... | collective-permute-start | bytes 786440 | tf_op jit(solution)/shard_map/ppermute | solution.py:30
  35.9 19.5 %collective-permute-start.12 = (bf16[1024,256]{1,0:T(8,128)(2,1)S(1)}, bf16[1024,256]{1,0:T(8,128)(2,1)S(1)}, u32[]{:S(2)}, u32[]{:S(2)}) collective-permute-start(bf16[1024,256]{1,0:T(8,128)(2,1)S(1)} %constant_dynamic-update-slice_fusion.2.down_1), channel_id=1, source_target_pairs={{0,224},{32,0},{64,32},{96,64},{128,96},{160,128},{192,160},{224,1... | collective-permute-start | bytes 1572872 | tf_op jit(solution)/shard_map/ppermute | solution.py:30
  38.2 17.1 %collective-permute-start.11 = (bf16[1024,256]{1,0:T(8,128)(2,1)S(1)}, bf16[1024,256]{1,0:T(8,128)(2,1)S(1)}, u32[]{:S(2)}, u32[]{:S(2)}) collective-permute-start(bf16[1024,256]{1,0:T(8,128)(2,1)S(1)} %constant_dynamic-update-slice_fusion.up_1), channel_id=1, source_target_pairs={{0,32},{32,64},{64,96},{96,128},{128,160},{160,192},{192,224},{224... | collective-permute-start | bytes 1572872 | tf_op jit(solution)/shard_map/ppermute | solution.py:30
  38.4 10.7 %collective-permute-start.10 = (bf16[256,256]{1,0:T(8,128)(2,1)S(1)}, bf16[256,256]{1,0:T(8,128)(2,1)S(1)}, u32[]{:S(2)}, u32[]{:S(2)}) collective-permute-start(bf16[256,256]{1,0:T(8,128)(2,1)S(1)} %get-tuple-element.59), channel_id=1, source_target_pairs={{0,2},{2,0},{1,3},{3,1},{4,6},{6,4},{5,7},{7,5},{8,10},{10,8},{9,1... | collective-permute-start | bytes 393224 | tf_op jit(solution)/shard_map/ppermute | solution.py:30
  45.8 7.9 %collective-permute-start.9 = (bf16[256,256]{1,0:T(8,128)(2,1)S(1)}, bf16[256,256]{1,0:T(8,128)(2,1)S(1)}, u32[]{:S(2)}, u32[]{:S(2)}) collective-permute-start(bf16[256,256]{1,0:T(8,128)(2,1)S(1)} %get-tuple-element.60), channel_id=1, source_target_pairs={{0,8},{4,12},{8,0},{12,4},{1,9},{5,13},{9,1},{13,5},{2,10},{6,14},... | collective-permute-start | bytes 393224 | tf_op jit(solution)/shard_map/ppermute | solution.py:30
  49.0 4.7 %collective-permute-start.8 = (bf16[256,256]{1,0:T(8,128)(2,1)S(1)}, bf16[256,256]{1,0:T(8,128)(2,1)S(1)}, u32[]{:S(2)}, u32[]{:S(2)}) collective-permute-start(bf16[256,256]{1,0:T(8,128)(2,1)S(1)} %get-tuple-element.60), channel_id=1, source_target_pairs={{0,12},{4,0},{8,4},{12,8},{1,13},{5,1},{9,5},{13,9},{2,14},{6,2},{... | collective-permute-start | bytes 393224 | tf_op jit(solution)/shard_map/ppermute | solution.py:30
  49.0 6.3 %collective-permute-start.7 = (bf16[256,256]{1,0:T(8,128)(2,1)S(1)}, bf16[256,256]{1,0:T(8,128)(2,1)S(1)}, u32[]{:S(2)}, u32[]{:S(2)}) collective-permute-start(bf16[256,256]{1,0:T(8,128)(2,1)S(1)} %get-tuple-element.60), channel_id=1, source_target_pairs={{0,4},{4,8},{8,12},{12,0},{1,5},{5,9},{9,13},{13,1},{2,6},{6,10},{... | collective-permute-start | bytes 393224 | tf_op jit(solution)/shard_map/ppermute | solution.py:30
  55.4 8.8 %collective-permute-start.18 = (bf16[512,256]{1,0:T(8,128)(2,1)S(1)}, bf16[512,256]{1,0:T(8,128)(2,1)S(1)}, u32[]{:S(2)}, u32[]{:S(2)}) collective-permute-start(bf16[512,256]{1,0:T(8,128)(2,1)S(1)} %pad_maximum_fusion.1.refs_2_), channel_id=1, source_target_pairs={{0,8},{4,12},{8,0},{12,4},{1,9},{5,13},{9,1},{13,5},{2,10},{6,14},... | collective-permute-start | bytes 786440 | tf_op jit(solution)/shard_map/ppermute | solution.py:30
  56.4 20.4 %collective-permute-start.13 = (bf16[1024,256]{1,0:T(8,128)(2,1)S(1)}, bf16[1024,256]{1,0:T(8,128)(2,1)S(1)}, u32[]{:S(2)}, u32[]{:S(2)}) collective-permute-start(bf16[1024,256]{1,0:T(8,128)(2,1)S(1)} %collective-permute-done.11.up_2), channel_id=1, source_target_pairs={{0,32},{32,64},{64,96},{96,128},{128,160},{160,192},{192,224},{224... | collective-permute-start | bytes 1572872 | tf_op jit(solution)/shard_map/ppermute | solution.py:30
  58.6 18.2 %collective-permute-start.14 = (bf16[1024,256]{1,0:T(8,128)(2,1)S(1)}, bf16[1024,256]{1,0:T(8,128)(2,1)S(1)}, u32[]{:S(2)}, u32[]{:S(2)}) collective-permute-start(bf16[1024,256]{1,0:T(8,128)(2,1)S(1)} %collective-permute-done.12.down_2), channel_id=1, source_target_pairs={{0,224},{32,0},{64,32},{96,64},{128,96},{160,128},{192,160},{224,1... | collective-permute-start | bytes 1572872 | tf_op jit(solution)/shard_map/ppermute | solution.py:30
  59.1 17.8 %collective-permute-start.15 = (bf16[1024,256]{1,0:T(8,128)(2,1)S(1)}, bf16[1024,256]{1,0:T(8,128)(2,1)S(1)}, u32[]{:S(2)}, u32[]{:S(2)}) collective-permute-start(bf16[1024,256]{1,0:T(8,128)(2,1)S(1)} %pad_maximum_fusion.refs_0_), channel_id=1, source_target_pairs={{0,2},{2,0},{1,3},{3,1},{4,6},{6,4},{5,7},{7,5},{8,10},{10,8},{9,1... | collective-permute-start | bytes 1572872 | tf_op jit(solution)/shard_map/ppermute | solution.py:30
  64.1 5.5 %collective-permute-start.17 = (bf16[512,256]{1,0:T(8,128)(2,1)S(1)}, bf16[512,256]{1,0:T(8,128)(2,1)S(1)}, u32[]{:S(2)}, u32[]{:S(2)}) collective-permute-start(bf16[512,256]{1,0:T(8,128)(2,1)S(1)} %pad_maximum_fusion.1.refs_2_), channel_id=1, source_target_pairs={{0,12},{4,0},{8,4},{12,8},{1,13},{5,1},{9,5},{13,9},{2,14},{6,2},{... | collective-permute-start | bytes 786440 | tf_op jit(solution)/shard_map/ppermute | solution.py:30
  64.1 12.6 %collective-permute-start.16 = (bf16[512,256]{1,0:T(8,128)(2,1)S(1)}, bf16[512,256]{1,0:T(8,128)(2,1)S(1)}, u32[]{:S(2)}, u32[]{:S(2)}) collective-permute-start(bf16[512,256]{1,0:T(8,128)(2,1)S(1)} %pad_maximum_fusion.1.refs_2_), channel_id=1, source_target_pairs={{0,4},{4,8},{8,12},{12,0},{1,5},{5,9},{9,13},{13,1},{2,6},{6,10},{... | collective-permute-start | bytes 786440 | tf_op jit(solution)/shard_map/ppermute | solution.py:30
  69.7 8.9 %collective-permute-start.19 = (bf16[1024,256]{1,0:T(8,128)(2,1)S(1)}, bf16[1024,256]{1,0:T(8,128)(2,1)S(1)}, u32[]{:S(2)}, u32[]{:S(2)}) collective-permute-start(bf16[1024,256]{1,0:T(8,128)(2,1)S(1)} %pad_maximum_fusion.refs_0_), channel_id=1, source_target_pairs={{0,1},{1,0},{2,3},{3,2},{4,5},{5,4},{6,7},{7,6},{8,9},{9,8},{10,11... | collective-permute-start | bytes 1572872 | tf_op jit(solution)/shard_map/ppermute | solution.py:30
  76.9 3.4 %collective-permute-start.20 = (bf16[1024,256]{1,0:T(8,128)(2,1)S(1)}, bf16[1024,256]{1,0:T(8,128)(2,1)S(1)}, u32[]{:S(2)}, u32[]{:S(2)}) collective-permute-start(bf16[1024,256]{1,0:T(8,128)(2,1)S(1)} %collective-permute-done.15.refs_1_), channel_id=1, source_target_pairs={{0,1},{1,0},{2,3},{3,2},{4,5},{5,4},{6,7},{7,6},{8,9},{9,8},{10,11... | collective-permute-start | bytes 1572872 | tf_op jit(solution)/shard_map/ppermute | solution.py:30
  77.6 2.5 %collective-permute-start.23 = (bf16[512,256]{1,0:T(8,128)(2,1)S(1)}, bf16[512,256]{1,0:T(8,128)(2,1)S(1)}, u32[]{:S(2)}, u32[]{:S(2)}) collective-permute-start(bf16[512,256]{1,0:T(8,128)(2,1)S(1)} %collective-permute-done.17.refs_4_), channel_id=1, source_target_pairs={{0,1},{1,0},{2,3},{3,2},{4,5},{5,4},{6,7},{7,6},{8,9},{9,8},{10,11... | collective-permute-start | bytes 786440 | tf_op jit(solution)/shard_map/ppermute | solution.py:30
  78.6 7.6 %collective-permute-start.26 = (bf16[512,256]{1,0:T(8,128)(2,1)S(1)}, bf16[512,256]{1,0:T(8,128)(2,1)S(1)}, u32[]{:S(2)}, u32[]{:S(2)}) collective-permute-start(bf16[512,256]{1,0:T(8,128)(2,1)S(1)} %slice.15), channel_id=1, source_target_pairs={{0,224},{32,0},{64,32},{96,64},{128,96},{160,128},{192,160},{224,1... | collective-permute-start | bytes 786440 | tf_op jit(solution)/shard_map/ppermute | solution.py:30
  79.5 8.9 %collective-permute-start.25 = (bf16[512,256]{1,0:T(8,128)(2,1)S(1)}, bf16[512,256]{1,0:T(8,128)(2,1)S(1)}, u32[]{:S(2)}, u32[]{:S(2)}) collective-permute-start(bf16[512,256]{1,0:T(8,128)(2,1)S(1)} %slice.14), channel_id=1, source_target_pairs={{0,32},{32,64},{64,96},{96,128},{128,160},{160,192},{192,224},{224... | collective-permute-start | bytes 786440 | tf_op jit(solution)/shard_map/ppermute | solution.py:30
  (5 other events, 7.2 us)

commit v7 on v6

--- a/solution.py
+++ b/solution.py
@@ -118,7 +118,7 @@
         in_specs=[pl.BlockSpec(memory_space=pltpu.HBM)] * 2,
         out_specs=[pl.BlockSpec(memory_space=pltpu.VMEM)] * 2,
         scratch_shapes=[pltpu.VMEM((rows, cols), BF16), pltpu.VMEM((rows,), jnp.int32), pltpu.SemaphoreType.DMA((2,))],
-        compiler_params=pltpu.CompilerParams(vmem_limit_bytes=4 * 1024 * 1024),
+        compiler_params=pltpu.CompilerParams(vmem_limit_bytes=60 * 1024 * 1024),
         name="prepare",
     )(partials, gaps)
 
@@ -160,12 +160,12 @@
     out_ref, raw = refs[12:]
     half = pieces[0].shape[1]
     rows = tables_ref.shape[1]
-    x, yh, core = [meta_ref[i] for i in (2, 3, 4)]
+    z, x, yh, core = [meta_ref[i] for i in (0, 2, 3, 4)]
     raw[:rows] = jnp.zeros((rows, raw.shape[1]), BF16)
 
     def place(piece, b, h, dx, dy, q):
         line = NYH * ((x + dx) & 3) + (yh ^ dy)
-        e = 2 * meta_ref[7 + line] + (core ^ q)
+        e = 2 * meta_ref[7 + NZ * z + line] + (core ^ q)
         raw[at_block(e + 1, rows), h * half : (h + 1) * half] = piece[b * rows : (b + 1) * rows]
 
     for q in range(2):
@@ -181,20 +181,33 @@
         out_ref[e * rows : (e + 1) * rows] = white.astype(BF16)
 
 
-def product_kernel(scale, meta_ref, tables_ref, left_in, right_ref, up_2, down_2, up_3, down_3, far_own, far_other, out_ref, left_ref, raw):
+def most_kernel(meta_ref, tables_ref, left_in, right_ref, up_2, down_2, up_3, down_3, out_ref, left_ref, raw):
+    rows = tables_ref.shape[2]
+    cols = out_ref.shape[0]
+    z, yl = meta_ref[0], meta_ref[1]
+    raw[:, :rows] = down_2[at_block(1 ^ yl, cols)]
+    raw[:, 5 * rows :] = up_2[at_block(yl, cols)]
+    for at, piece in ((1, down_3), (3, up_3)):
+        raw[:, at_block(at + yl, rows)] = piece[:cols]
+        raw[:, at_block(at + 1 - yl, rows)] = piece[cols:]
+    for i, shift in ((1, 5), (2, 5), (4, -9), (5, -9)):
+        e = (2 * z + i + shift) & (NE - 1)
+        left_ref[:, at_block(e, rows)] = filter_left(raw, i, e, meta_ref, tables_ref)
+    out_ref[...] = jnp.dot(left_ref[...], right_ref[...], preferred_element_type=F32)
+
+
+def last_kernel(scale, meta_ref, tables_ref, most_ref, right_ref, up_3, down_3, far_own, far_other, out_ref, raw, left, right):
     cols, rows = far_own.shape
     z, yl = meta_ref[0], meta_ref[1]
-    raw[:, :rows] = down_2[at_block(1 ^ yl, cols)]
-    raw[:, 7 * rows :] = up_2[at_block(yl, cols)]
-    for at, piece in ((1, down_3), (5, up_3)):
-        raw[:, at_block(at + yl, rows)] = piece[:cols]
-        raw[:, at_block(at + 1 - yl, rows)] = piece[cols:]
-    raw[:, at_block(3 + yl, rows)] = far_own[...]
-    raw[:, at_block(4 - yl, rows)] = far_other[...]
-    for i in range(1, 8):
-        e = (2 * z + i + 5) & (NE - 1)
-        left_ref[:, at_block(e, rows)] = filter_left(raw, i, e, meta_ref, tables_ref)
-    out_ref[...] = jnp.dot(left_ref[...], right_ref[...], preferred_element_type=F32) * scale
+    raw[:, :rows] = down_3[at_block(1 ^ yl, cols)]
+    raw[:, 3 * rows :] = up_3[at_block(yl, cols)]
+    raw[:, at_block(1 + yl, rows)] = far_own[...]
+    raw[:, at_block(2 - yl, rows)] = far_other[...]
+    for i in range(1, 4):
+        e = (2 * z + i + 7) & (NE - 1)
+        left[:, (i - 1) * rows : i * rows] = filter_left(raw, i, e, meta_ref, tables_ref)
+        right[(i - 1) * rows : i * rows] = right_ref[at_block(e, rows)]
+    out_ref[...] = (most_ref[...] + jnp.dot(left[...], right[...], preferred_element_type=F32)) * scale
 
 
 def whitened(kernel, name, meta, tables, pieces, shape, raw_shape):
@@ -210,19 +223,33 @@
     )(meta, tables, *pieces)
 
 
-def product(meta, tables, left, right, pieces, rows, scale):
+def most_of_product(meta, tables, left, right, pieces, rows):
     vmem = pl.BlockSpec(memory_space=pltpu.VMEM)
     cols = right.shape[1]
     return pl.pallas_call(
-        functools.partial(product_kernel, scale),
+        most_kernel,
         out_shape=[jax.ShapeDtypeStruct((cols, cols), F32), jax.ShapeDtypeStruct(left.shape, BF16)],
         in_specs=[pl.BlockSpec(memory_space=pltpu.SMEM)] + [vmem] * (3 + len(pieces)),
         out_specs=[vmem, vmem],
-        scratch_shapes=[pltpu.VMEM((cols, 8 * rows), BF16)],
+        scratch_shapes=[pltpu.VMEM((cols, 6 * rows), BF16)],
         input_output_aliases={2: 1},
         compiler_params=pltpu.CompilerParams(vmem_limit_bytes=16 * 1024 * 1024),
+        name="most",
+    )(meta, tables, left, right, *pieces)[0]
+
+
+def product(meta, tables, most, right, pieces, rows, scale):
+    vmem = pl.BlockSpec(memory_space=pltpu.VMEM)
+    cols = right.shape[1]
+    return pl.pallas_call(
+        functools.partial(last_kernel, scale),
+        out_shape=jax.ShapeDtypeStruct((cols, cols), F32),
+        in_specs=[pl.BlockSpec(memory_space=pltpu.SMEM)] + [vmem] * (3 + len(pieces)),
+        out_specs=vmem,
+        scratch_shapes=[pltpu.VMEM((cols, 4 * rows), BF16), pltpu.VMEM((cols, 3 * rows), BF16), pltpu.VMEM((3 * rows, cols), BF16)],
+        compiler_params=pltpu.CompilerParams(vmem_limit_bytes=16 * 1024 * 1024),
         name="product",
-    )(meta, tables, left, right, *pieces)[0]
+    )(meta, tables, most, right, *pieces)
 
 
 def on_device(partials, gaps, arc_start, taps):
@@ -231,7 +258,7 @@
     places = [lax.axis_index(axis) for axis in EPOCH + COL]
     origin = np.argsort(np.array(LINE, np.int32), axis=0).T.astype(np.int32)
     meta = jnp.stack(places + [arc_start[0], arc_start[0] // rows]).astype(jnp.int32)
-    meta = jnp.concatenate([meta, jnp.asarray(origin)[places[0]]])
+    meta = jnp.concatenate([meta, jnp.asarray(origin.reshape(-1))])
     halves, own = prepare(partials, gaps)
 
     def up(block):
@@ -253,23 +280,25 @@
     halves = in_plane(halves)
     other = around(own, "yl", NYL, 1)
     up_own, down_own = up(own), down(own)
+    halves, tables = sync((halves, make_tables(meta, taps, rows)))
     up_own, down_own, up_other, down_other, halves = sync((up_own, down_own, up(other), down(other), along_z(halves)))
     a, b = halves[:rows], halves[rows:]
     up_1 = jnp.concatenate([up_own, up_other], axis=0)
     down_1 = jnp.concatenate([down_own, down_other], axis=0)
-    tables = make_tables(meta, taps, rows)
-    a_x, b_y, tables = sync((along_x(a), across(b), tables))
+    a_x, b_y = sync((along_x(a), across(b)))
     a_pack = jnp.concatenate([a] + a_x, axis=0)
     b_pack = jnp.concatenate([b, b_y], axis=0)
     up_2, down_2, a_pack, b_pack = sync((up(up_1), down(down_1), a_pack, b_pack))
     left = whitened(left_kernel, "left", meta, tables[1], [own, other, up_1, down_1, up_2, down_2], (cols, NE * rows), (cols, 10 * rows))
-    up_3, down_3, a_far, b_x, left = sync((up(up_2), down(down_2), across(a_pack), along_x(b_pack), left))
+    b_x = along_x(b_pack)
+    early = []
+    up_3, down_3, a_far, b_x, left, early = sync((up(up_2), down(down_2), across(a_pack), b_x, left, early))
     far_own, far_other = up(up_3[:cols]), down(down_3[cols:])
     mine = [a_pack, a_far, b_pack] + b_x
     theirs = [swapped(piece) for piece in mine]
     right = whitened(right_kernel, "right", meta, tables[0], mine + theirs, (NE * rows, cols), ((NE + 1) * rows, cols))
-    pieces = [up_2, down_2, up_3, down_3, far_own, far_other]
-    return product(meta, tables[1], left, right, pieces, rows, (rows * NE) ** (-0.5))
+    most = most_of_product(meta, tables[1], left, right, [up_2, down_2, up_3, down_3], rows)
+    return product(meta, tables[1], most, right, [up_3, down_3, far_own, far_other], rows, (rows * NE) ** (-0.5))
 
 
 def solution(mesh):

time: 93.9 us -> 96.7 us (1.030)
  the two profiles are of different devices: /device:TPU:1 before, /device:TPU:2 now
where the time goes in v7:
time: 96.7 us; the launch traced here: 96.5 us
  starting transfers between devices  54.9 us (57%)
  waiting for transfers between devices  24 us (25%)
  Pallas kernels  15.1 us (16%)
  local copies, waits for them, and re-layouts  1.54 us (2%)
    ppermute x25, starting transfers between devices, around(): return lax.ppermute(block, axis, [(i, (i + step) % n) for i in range(n)])  39.6 us
    ppermute x25, waiting for transfers between devices, around(): return lax.ppermute(block, axis, [(i, (i + step) % n) for i in range(n)])  20.6 us
    ppermute x1, starting transfers between devices, along_z(): return lax.ppermute(block, ('z', 'x', 'yh'), route)  8.45 us
    ppermute x1, starting transfers between devices, in_plane(): return lax.ppermute(block, axes, route)  6.79 us
    pallas_call x2, Pallas kernels, whitened(): pl.pallas_call(kernel, out_shape=jax.ShapeDtypeStruct(shape, BF16), in_sp...  5.76 us
    pallas_call x1, Pallas kernels, most_of_product(): pl.pallas_call(most_kernel, out_shape=[jax.ShapeDtypeStruct((cols, cols),...  3.74 us
    ppermute x1, waiting for transfers between devices, along_z(): return lax.ppermute(block, ('z', 'x', 'yh'), route)  3.41 us
    pallas_call x1, Pallas kernels, product(): pl.pallas_call(functools.partial(last_kernel, scale), out_shape=jax.Shape...  2.63 us
  transfers between devices with their start and end apart: 27, of which 8 were waited for; matrix products, arithmetic and copies ran while one was open for 2% of the time, Pallas kernels for 11%

profile of v7, /device:TPU:2, one launch (start us, length us, event | category | flops | bytes accessed | tf_op | source)
XLA Modules:
  0.0 96.5 jit_solution(7784253471786328279)
XLA Ops:
  0.0 1.9 %prepare.1 = (bf16[512,256]{1,0:T(8,128)(2,1)}, bf16[512,256]{1,0:T(8,128)(2,1)}) custom-call(bf16[256,512]{1,0:T(8,128)(2,1)} %partials_ref.1, s32[256]{0:T(256)} %gaps_ref.1), custom_call_target="tpu_custom_call" | custom-call | tf_op jit(solution)/shard_map/prepare/pallas_call | solution.py:115
  1.9 6.8 %collective-permute-start = (bf16[512,256]{1,0:T(8,128)(2,1)}, bf16[512,256]{1,0:T(8,128)(2,1)S(1)}, u32[]{:S(2)}, u32[]{:S(2)}) collective-permute-start(bf16[512,256]{1,0:T(8,128)(2,1)} %get-tuple-element.33), channel_id=1, source_target_pairs={{0,10},{1,26},{2,8},{3,24},{4,14},{5,30},{6,12},{7,28},{8,2},{9,18... | collective-permute-start | bytes 786440 | tf_op jit(solution)/shard_map/ppermute | solution.py:51
  9.3 2.9 %collective-permute-start.2 = (bf16[512,256]{1,0:T(8,128)(2,1)}, bf16[512,256]{1,0:T(8,128)(2,1)S(1)}, u32[]{:S(2)}, u32[]{:S(2)}) collective-permute-start(bf16[512,256]{1,0:T(8,128)(2,1)} %get-tuple-element.37.own), channel_id=1, source_target_pairs={{0,224},{32,0},{64,32},{96,64},{128,96},{160,128},{192,160},{224,1... | collective-permute-start | bytes 786440 | tf_op jit(solution)/shard_map/ppermute | solution.py:30
  13.5 0.7 concatenate.15.meta_ref
  14.2 1.1 %tables.1 = (bf16[4,256,512]{2,1,0:T(8,128)(2,1)S(1)}, bf16[4,512,256]{2,1,0:T(8,128)(2,1)S(1)}) custom-call(s32[71]{0:T(128)S(1)} %concatenate.15.meta_ref, bf16[1,256]{1,0:T(2,128)(2,1)S(1)} %broadcast_in_dim.3.taps_ref), custom_call_target="tpu_custom_call" | custom-call | tf_op jit(solution)/shard_map/tables/pallas_call | solution.py:87
  15.3 8.5 %collective-permute-start.6 = (bf16[512,256]{1,0:T(8,128)(2,1)S(1)}, bf16[512,256]{1,0:T(8,128)(2,1)S(1)}, u32[]{:S(2)}, u32[]{:S(2)}) collective-permute-start(bf16[512,256]{1,0:T(8,128)(2,1)S(1)} %collective-permute-done), channel_id=1, source_target_pairs={{10,10},{8,40},{14,78},{12,108},{2,130},{0,160},{4,196},{6,230},{3... | collective-permute-start | bytes 786440 | tf_op jit(solution)/shard_map/ppermute | solution.py:60
  23.9 3.2 %collective-permute-start.5 = (bf16[512,256]{1,0:T(8,128)(2,1)S(1)}, bf16[512,256]{1,0:T(8,128)(2,1)S(1)}, u32[]{:S(2)}, u32[]{:S(2)}) collective-permute-start(bf16[512,256]{1,0:T(8,128)(2,1)S(1)} %collective-permute-done.3.other), channel_id=1, source_target_pairs={{0,224},{32,0},{64,32},{96,64},{128,96},{160,128},{192,160},{224,1... | collective-permute-start | bytes 786440 | tf_op jit(solution)/shard_map/ppermute | solution.py:30
  27.1 3.4 %collective-permute-done.6 = bf16[512,256]{1,0:T(8,128)(2,1)S(1)} collective-permute-done((bf16[512,256]{1,0:T(8,128)(2,1)S(1)}, bf16[512,256]{1,0:T(8,128)(2,1)S(1)}, u32[]{:S(2)}, u32[]{:S(2)}) %collective-permute-start.6) | collective-permute-done | bytes 262176 | tf_op jit(solution)/shard_map/ppermute | solution.py:60
  30.5 4.0 %collective-permute-done.4 = bf16[512,256]{1,0:T(8,128)(2,1)S(1)} collective-permute-done((bf16[512,256]{1,0:T(8,128)(2,1)S(1)}, bf16[512,256]{1,0:T(8,128)(2,1)S(1)}, u32[]{:S(2)}, u32[]{:S(2)}) %collective-permute-start.4) | collective-permute-done | bytes 262176 | tf_op jit(solution)/shard_map/ppermute | solution.py:30
  35.0 3.8 %collective-permute-start.8 = (bf16[1024,256]{1,0:T(8,128)(2,1)S(1)}, bf16[1024,256]{1,0:T(8,128)(2,1)S(1)}, u32[]{:S(2)}, u32[]{:S(2)}) collective-permute-start(bf16[1024,256]{1,0:T(8,128)(2,1)S(1)} %constant_dynamic-update-slice_fusion.2.down_1), channel_id=1, source_target_pairs={{0,224},{32,0},{64,32},{96,64},{128,96},{160,128},{192,160},{224,1... | collective-permute-start | bytes 1572872 | tf_op jit(solution)/shard_map/ppermute | solution.py:30
  39.3 2.0 %collective-permute-start.11 = (bf16[256,256]{1,0:T(8,128)(2,1)S(1)}, bf16[256,256]{1,0:T(8,128)(2,1)S(1)}, u32[]{:S(2)}, u32[]{:S(2)}) collective-permute-start(bf16[256,256]{1,0:T(8,128)(2,1)S(1)} %get-tuple-element.62), channel_id=1, source_target_pairs={{0,8},{4,12},{8,0},{12,4},{1,9},{5,13},{9,1},{13,5},{2,10},{6,14},... | collective-permute-start | bytes 393224 | tf_op jit(solution)/shard_map/ppermute | solution.py:30
  41.3 9.6 %collective-permute-start.12 = (bf16[256,256]{1,0:T(8,128)(2,1)S(1)}, bf16[256,256]{1,0:T(8,128)(2,1)S(1)}, u32[]{:S(2)}, u32[]{:S(2)}) collective-permute-start(bf16[256,256]{1,0:T(8,128)(2,1)S(1)} %get-tuple-element.61), channel_id=1, source_target_pairs={{0,2},{2,0},{1,3},{3,1},{4,6},{6,4},{5,7},{7,5},{8,10},{10,8},{9,1... | collective-permute-start | bytes 393224 | tf_op jit(solution)/shard_map/ppermute | solution.py:30
  50.9 2.9 %collective-permute-done.12 = bf16[256,256]{1,0:T(8,128)(2,1)S(1)} collective-permute-done((bf16[256,256]{1,0:T(8,128)(2,1)S(1)}, bf16[256,256]{1,0:T(8,128)(2,1)S(1)}, u32[]{:S(2)}, u32[]{:S(2)}) %collective-permute-start.12) | collective-permute-done | bytes 131104 | tf_op jit(solution)/shard_map/ppermute | solution.py:30
  53.8 2.0 %collective-permute-done.9 = bf16[256,256]{1,0:T(8,128)(2,1)S(1)} collective-permute-done((bf16[256,256]{1,0:T(8,128)(2,1)S(1)}, bf16[256,256]{1,0:T(8,128)(2,1)S(1)}, u32[]{:S(2)}, u32[]{:S(2)}) %collective-permute-start.9) | collective-permute-done | bytes 131104 | tf_op jit(solution)/shard_map/ppermute | solution.py:30
  56.1 3.3 %collective-permute-start.14 = (bf16[1024,256]{1,0:T(8,128)(2,1)S(1)}, bf16[1024,256]{1,0:T(8,128)(2,1)S(1)}, u32[]{:S(2)}, u32[]{:S(2)}) collective-permute-start(bf16[1024,256]{1,0:T(8,128)(2,1)S(1)} %collective-permute-done.8.down_2), channel_id=1, source_target_pairs={{0,224},{32,0},{64,32},{96,64},{128,96},{160,128},{192,160},{224,1... | collective-permute-start | bytes 1572872 | tf_op jit(solution)/shard_map/ppermute | solution.py:30
  59.4 7.9 %collective-permute-start.15 = (bf16[1024,256]{1,0:T(8,128)(2,1)S(1)}, bf16[1024,256]{1,0:T(8,128)(2,1)S(1)}, u32[]{:S(2)}, u32[]{:S(2)}) collective-permute-start(bf16[1024,256]{1,0:T(8,128)(2,1)S(1)} %pad_maximum_fusion.refs_0_), channel_id=1, source_target_pairs={{0,2},{2,0},{1,3},{3,1},{4,6},{6,4},{5,7},{7,5},{8,10},{10,8},{9,1... | collective-permute-start | bytes 1572872 | tf_op jit(solution)/shard_map/ppermute | solution.py:30
  67.3 1.5 %collective-permute-start.18 = (bf16[512,256]{1,0:T(8,128)(2,1)S(1)}, bf16[512,256]{1,0:T(8,128)(2,1)S(1)}, u32[]{:S(2)}, u32[]{:S(2)}) collective-permute-start(bf16[512,256]{1,0:T(8,128)(2,1)S(1)} %pad_maximum_fusion.1.refs_2_), channel_id=1, source_target_pairs={{0,8},{4,12},{8,0},{12,4},{1,9},{5,13},{9,1},{13,5},{2,10},{6,14},... | collective-permute-start | bytes 786440 | tf_op jit(solution)/shard_map/ppermute | solution.py:30
  68.7 10.1 %collective-permute-done.17.refs_4_ = bf16[512,256]{1,0:T(8,128)(2,1)S(1)} collective-permute-done((bf16[512,256]{1,0:T(8,128)(2,1)S(1)}, bf16[512,256]{1,0:T(8,128)(2,1)S(1)}, u32[]{:S(2)}, u32[]{:S(2)}) %collective-permute-start.17) | collective-permute-done | bytes 262176 | tf_op jit(solution)/shard_map/ppermute | solution.py:30
  78.8 2.5 %left.1.left_in = bf16[512,4096]{1,0:T(8,128)(2,1)S(1)} custom-call(s32[71]{0:T(128)S(1)} %concatenate.15.meta_ref, bf16[4,512,256]{2,1,0:T(8,128)(2,1)S(1)} %get-tuple-element.36.tables_ref, bf16[512,256]{1,0:T(8,128)(2,1)S(1)} %copy-done, bf16[512,256]{1,0:T(8,128)(2,1)S(1)} %collective-permute-done.3.other, ...), custom_call_target="tpu_custom_call" | custom-call | tf_op jit(solution)/shard_map/left/pallas_call | solution.py:215
  83.6 0.7 collective-permute-done.22.refs_9_
  84.3 2.5 %collective-permute-start.26 = (bf16[512,256]{1,0:T(8,128)(2,1)S(1)}, bf16[512,256]{1,0:T(8,128)(2,1)S(1)}, u32[]{:S(2)}, u32[]{:S(2)}) collective-permute-start(bf16[512,256]{1,0:T(8,128)(2,1)S(1)} %slice.15), channel_id=1, source_target_pairs={{0,224},{32,0},{64,32},{96,64},{128,96},{160,128},{192,160},{224,1... | collective-permute-start | bytes 786440 | tf_op jit(solution)/shard_map/ppermute | solution.py:30
  86.9 3.3 %right.1.right_ref = bf16[4096,512]{1,0:T(8,128)(2,1)S(1)} custom-call(s32[71]{0:T(128)S(1)} %concatenate.15.meta_ref, bf16[4,256,512]{2,1,0:T(8,128)(2,1)S(1)} %get-tuple-element.53.tables_ref, bf16[1024,256]{1,0:T(8,128)(2,1)S(1)} %pad_maximum_fusion.refs_0_, bf16[1024,256]{1,0:T(8,128)(2,1)S(1)} %collective-permute-done.15.refs_1_, ...), custom_call_target="tpu_custom_call" | custom-call | tf_op jit(solution)/shard_map/right/pallas_call | solution.py:215
  90.1 3.7 %most.1 = (f32[512,512]{1,0:T(8,128)S(1)}, bf16[512,4096]{1,0:T(8,128)(2,1)S(1)}) custom-call(s32[71]{0:T(128)S(1)} %concatenate.15.meta_ref, bf16[4,512,256]{2,1,0:T(8,128)(2,1)S(1)} %get-tuple-element.36.tables_ref, bf16[512,4096]{1,0:T(8,128)(2,1)S(1)} %left.1.left_in, bf16[4096,512]{1,0:T(8,128)(2,1)S(1)} %right.1.right_ref, ...), custom_call_target="tpu_custom_call", output_to_operand_aliasing={{1}: (2, {})} | custom-call | tf_op jit(solution)/shard_map/most/pallas_call | solution.py:229
  93.9 2.6 %product.1 = f32[512,512]{1,0:T(8,128)} custom-call(s32[71]{0:T(128)S(1)} %concatenate.15.meta_ref, bf16[4,512,256]{2,1,0:T(8,128)(2,1)S(1)} %get-tuple-element.36.tables_ref, f32[512,512]{1,0:T(8,128)S(1)} %get-tuple-element.60.most_ref, bf16[4096,512]{1,0:T(8,128)(2,1)S(1)} %right.1.right_ref, bf16[1024,256]{1,0:T(8,128)(2,1)S(1)} %collective-permute-done.13.up_3, ...), custom_call_target="tpu_custom_call" | custom-call | tf_op jit(solution)/shard_map/product/pallas_call | solution.py:244
  (50 shorter events, 4.8 us)
Async XLA Ops:
  1.9 13.4 %collective-permute-start = (bf16[512,256]{1,0:T(8,128)(2,1)}, bf16[512,256]{1,0:T(8,128)(2,1)S(1)}, u32[]{:S(2)}, u32[]{:S(2)}) collective-permute-start(bf16[512,256]{1,0:T(8,128)(2,1)} %get-tuple-element.33), channel_id=1, source_target_pairs={{0,10},{1,26},{2,8},{3,24},{4,14},{5,30},{6,12},{7,28},{8,2},{9,18... | collective-permute-start | bytes 786440 | tf_op jit(solution)/shard_map/ppermute | solution.py:51
  8.7 15.1 %collective-permute-start.3 = (bf16[512,256]{1,0:T(8,128)(2,1)}, bf16[512,256]{1,0:T(8,128)(2,1)S(1)}, u32[]{:S(2)}, u32[]{:S(2)}) collective-permute-start(bf16[512,256]{1,0:T(8,128)(2,1)} %get-tuple-element.37.own), channel_id=1, source_target_pairs={{0,16},{16,0},{1,17},{17,1},{2,18},{18,2},{3,19},{19,3},{4,20},{20... | collective-permute-start | bytes 786440 | tf_op jit(solution)/shard_map/ppermute | solution.py:30
  8.8 18.3 %collective-permute-start.1 = (bf16[512,256]{1,0:T(8,128)(2,1)}, bf16[512,256]{1,0:T(8,128)(2,1)S(1)}, u32[]{:S(2)}, u32[]{:S(2)}) collective-permute-start(bf16[512,256]{1,0:T(8,128)(2,1)} %get-tuple-element.37.own), channel_id=1, source_target_pairs={{0,32},{32,64},{64,96},{96,128},{128,160},{160,192},{192,224},{224... | collective-permute-start | bytes 786440 | tf_op jit(solution)/shard_map/ppermute | solution.py:30
  9.3 17.9 %collective-permute-start.2 = (bf16[512,256]{1,0:T(8,128)(2,1)}, bf16[512,256]{1,0:T(8,128)(2,1)S(1)}, u32[]{:S(2)}, u32[]{:S(2)}) collective-permute-start(bf16[512,256]{1,0:T(8,128)(2,1)} %get-tuple-element.37.own), channel_id=1, source_target_pairs={{0,224},{32,0},{64,32},{96,64},{128,96},{160,128},{192,160},{224,1... | collective-permute-start | bytes 786440 | tf_op jit(solution)/shard_map/ppermute | solution.py:30
  15.3 15.2 %collective-permute-start.6 = (bf16[512,256]{1,0:T(8,128)(2,1)S(1)}, bf16[512,256]{1,0:T(8,128)(2,1)S(1)}, u32[]{:S(2)}, u32[]{:S(2)}) collective-permute-start(bf16[512,256]{1,0:T(8,128)(2,1)S(1)} %collective-permute-done), channel_id=1, source_target_pairs={{10,10},{8,40},{14,78},{12,108},{2,130},{0,160},{4,196},{6,230},{3... | collective-permute-start | bytes 786440 | tf_op jit(solution)/shard_map/ppermute | solution.py:60
  23.8 10.7 %collective-permute-start.4 = (bf16[512,256]{1,0:T(8,128)(2,1)S(1)}, bf16[512,256]{1,0:T(8,128)(2,1)S(1)}, u32[]{:S(2)}, u32[]{:S(2)}) collective-permute-start(bf16[512,256]{1,0:T(8,128)(2,1)S(1)} %collective-permute-done.3.other), channel_id=1, source_target_pairs={{0,32},{32,64},{64,96},{96,128},{128,160},{160,192},{192,224},{224... | collective-permute-start | bytes 786440 | tf_op jit(solution)/shard_map/ppermute | solution.py:30
  23.9 11.0 %collective-permute-start.5 = (bf16[512,256]{1,0:T(8,128)(2,1)S(1)}, bf16[512,256]{1,0:T(8,128)(2,1)S(1)}, u32[]{:S(2)}, u32[]{:S(2)}) collective-permute-start(bf16[512,256]{1,0:T(8,128)(2,1)S(1)} %collective-permute-done.3.other), channel_id=1, source_target_pairs={{0,224},{32,0},{64,32},{96,64},{128,96},{160,128},{192,160},{224,1... | collective-permute-start | bytes 786440 | tf_op jit(solution)/shard_map/ppermute | solution.py:30
  35.0 20.9 %collective-permute-start.8 = (bf16[1024,256]{1,0:T(8,128)(2,1)S(1)}, bf16[1024,256]{1,0:T(8,128)(2,1)S(1)}, u32[]{:S(2)}, u32[]{:S(2)}) collective-permute-start(bf16[1024,256]{1,0:T(8,128)(2,1)S(1)} %constant_dynamic-update-slice_fusion.2.down_1), channel_id=1, source_target_pairs={{0,224},{32,0},{64,32},{96,64},{128,96},{160,128},{192,160},{224,1... | collective-permute-start | bytes 1572872 | tf_op jit(solution)/shard_map/ppermute | solution.py:30
  38.8 17.1 %collective-permute-start.7 = (bf16[1024,256]{1,0:T(8,128)(2,1)S(1)}, bf16[1024,256]{1,0:T(8,128)(2,1)S(1)}, u32[]{:S(2)}, u32[]{:S(2)}) collective-permute-start(bf16[1024,256]{1,0:T(8,128)(2,1)S(1)} %constant_dynamic-update-slice_fusion.up_1), channel_id=1, source_target_pairs={{0,32},{32,64},{64,96},{96,128},{128,160},{160,192},{192,224},{224... | collective-permute-start | bytes 1572872 | tf_op jit(solution)/shard_map/ppermute | solution.py:30
  38.9 11.9 %collective-permute-start.10 = (bf16[256,256]{1,0:T(8,128)(2,1)S(1)}, bf16[256,256]{1,0:T(8,128)(2,1)S(1)}, u32[]{:S(2)}, u32[]{:S(2)}) collective-permute-start(bf16[256,256]{1,0:T(8,128)(2,1)S(1)} %get-tuple-element.62), channel_id=1, source_target_pairs={{0,12},{4,0},{8,4},{12,8},{1,13},{5,1},{9,5},{13,9},{2,14},{6,2},{... | collective-permute-start | bytes 393224 | tf_op jit(solution)/shard_map/ppermute | solution.py:30
  39.3 11.6 %collective-permute-start.11 = (bf16[256,256]{1,0:T(8,128)(2,1)S(1)}, bf16[256,256]{1,0:T(8,128)(2,1)S(1)}, u32[]{:S(2)}, u32[]{:S(2)}) collective-permute-start(bf16[256,256]{1,0:T(8,128)(2,1)S(1)} %get-tuple-element.62), channel_id=1, source_target_pairs={{0,8},{4,12},{8,0},{12,4},{1,9},{5,13},{9,1},{13,5},{2,10},{6,14},... | collective-permute-start | bytes 393224 | tf_op jit(solution)/shard_map/ppermute | solution.py:30
  41.3 12.5 %collective-permute-start.12 = (bf16[256,256]{1,0:T(8,128)(2,1)S(1)}, bf16[256,256]{1,0:T(8,128)(2,1)S(1)}, u32[]{:S(2)}, u32[]{:S(2)}) collective-permute-start(bf16[256,256]{1,0:T(8,128)(2,1)S(1)} %get-tuple-element.61), channel_id=1, source_target_pairs={{0,2},{2,0},{1,3},{3,1},{4,6},{6,4},{5,7},{7,5},{8,10},{10,8},{9,1... | collective-permute-start | bytes 393224 | tf_op jit(solution)/shard_map/ppermute | solution.py:30
  50.8 5.0 %collective-permute-start.9 = (bf16[256,256]{1,0:T(8,128)(2,1)S(1)}, bf16[256,256]{1,0:T(8,128)(2,1)S(1)}, u32[]{:S(2)}, u32[]{:S(2)}) collective-permute-start(bf16[256,256]{1,0:T(8,128)(2,1)S(1)} %get-tuple-element.62), channel_id=1, source_target_pairs={{0,4},{4,8},{8,12},{12,0},{1,5},{5,9},{9,13},{13,1},{2,6},{6,10},{... | collective-permute-start | bytes 393224 | tf_op jit(solution)/shard_map/ppermute | solution.py:30
  55.9 11.4 %collective-permute-start.16 = (bf16[512,256]{1,0:T(8,128)(2,1)S(1)}, bf16[512,256]{1,0:T(8,128)(2,1)S(1)}, u32[]{:S(2)}, u32[]{:S(2)}) collective-permute-start(bf16[512,256]{1,0:T(8,128)(2,1)S(1)} %pad_maximum_fusion.1.refs_2_), channel_id=1, source_target_pairs={{0,4},{4,8},{8,12},{12,0},{1,5},{5,9},{9,13},{13,1},{2,6},{6,10},{... | collective-permute-start | bytes 786440 | tf_op jit(solution)/shard_map/ppermute | solution.py:30
  56.0 26.0 %collective-permute-start.13 = (bf16[1024,256]{1,0:T(8,128)(2,1)S(1)}, bf16[1024,256]{1,0:T(8,128)(2,1)S(1)}, u32[]{:S(2)}, u32[]{:S(2)}) collective-permute-start(bf16[1024,256]{1,0:T(8,128)(2,1)S(1)} %collective-permute-done.7.up_2), channel_id=1, source_target_pairs={{0,32},{32,64},{64,96},{96,128},{128,160},{160,192},{192,224},{224... | collective-permute-start | bytes 1572872 | tf_op jit(solution)/shard_map/ppermute | solution.py:30
  56.1 25.9 %collective-permute-start.14 = (bf16[1024,256]{1,0:T(8,128)(2,1)S(1)}, bf16[1024,256]{1,0:T(8,128)(2,1)S(1)}, u32[]{:S(2)}, u32[]{:S(2)}) collective-permute-start(bf16[1024,256]{1,0:T(8,128)(2,1)S(1)} %collective-permute-done.8.down_2), channel_id=1, source_target_pairs={{0,224},{32,0},{64,32},{96,64},{128,96},{160,128},{192,160},{224,1... | collective-permute-start | bytes 1572872 | tf_op jit(solution)/shard_map/ppermute | solution.py:30
  59.4 22.6 %collective-permute-start.15 = (bf16[1024,256]{1,0:T(8,128)(2,1)S(1)}, bf16[1024,256]{1,0:T(8,128)(2,1)S(1)}, u32[]{:S(2)}, u32[]{:S(2)}) collective-permute-start(bf16[1024,256]{1,0:T(8,128)(2,1)S(1)} %pad_maximum_fusion.refs_0_), channel_id=1, source_target_pairs={{0,2},{2,0},{1,3},{3,1},{4,6},{6,4},{5,7},{7,5},{8,10},{10,8},{9,1... | collective-permute-start | bytes 1572872 | tf_op jit(solution)/shard_map/ppermute | solution.py:30
  67.3 11.6 %collective-permute-start.17 = (bf16[512,256]{1,0:T(8,128)(2,1)S(1)}, bf16[512,256]{1,0:T(8,128)(2,1)S(1)}, u32[]{:S(2)}, u32[]{:S(2)}) collective-permute-start(bf16[512,256]{1,0:T(8,128)(2,1)S(1)} %pad_maximum_fusion.1.refs_2_), channel_id=1, source_target_pairs={{0,12},{4,0},{8,4},{12,8},{1,13},{5,1},{9,5},{13,9},{2,14},{6,2},{... | collective-permute-start | bytes 786440 | tf_op jit(solution)/shard_map/ppermute | solution.py:30
  67.3 14.1 %collective-permute-start.18 = (bf16[512,256]{1,0:T(8,128)(2,1)S(1)}, bf16[512,256]{1,0:T(8,128)(2,1)S(1)}, u32[]{:S(2)}, u32[]{:S(2)}) collective-permute-start(bf16[512,256]{1,0:T(8,128)(2,1)S(1)} %pad_maximum_fusion.1.refs_2_), channel_id=1, source_target_pairs={{0,8},{4,12},{8,0},{12,4},{1,9},{5,13},{9,1},{13,5},{2,10},{6,14},... | collective-permute-start | bytes 786440 | tf_op jit(solution)/shard_map/ppermute | solution.py:30
  78.8 4.7 %collective-permute-start.19 = (bf16[1024,256]{1,0:T(8,128)(2,1)S(1)}, bf16[1024,256]{1,0:T(8,128)(2,1)S(1)}, u32[]{:S(2)}, u32[]{:S(2)}) collective-permute-start(bf16[1024,256]{1,0:T(8,128)(2,1)S(1)} %pad_maximum_fusion.refs_0_), channel_id=1, source_target_pairs={{0,1},{1,0},{2,3},{3,2},{4,5},{5,4},{6,7},{7,6},{8,9},{9,8},{10,11... | collective-permute-start | bytes 1572872 | tf_op jit(solution)/shard_map/ppermute | solution.py:30
  82.0 4.9 %collective-permute-start.20 = (bf16[1024,256]{1,0:T(8,128)(2,1)S(1)}, bf16[1024,256]{1,0:T(8,128)(2,1)S(1)}, u32[]{:S(2)}, u32[]{:S(2)}) collective-permute-start(bf16[1024,256]{1,0:T(8,128)(2,1)S(1)} %collective-permute-done.15.refs_1_), channel_id=1, source_target_pairs={{0,1},{1,0},{2,3},{3,2},{4,5},{5,4},{6,7},{7,6},{8,9},{9,8},{10,11... | collective-permute-start | bytes 1572872 | tf_op jit(solution)/shard_map/ppermute | solution.py:30
  82.6 4.3 %collective-permute-start.23 = (bf16[512,256]{1,0:T(8,128)(2,1)S(1)}, bf16[512,256]{1,0:T(8,128)(2,1)S(1)}, u32[]{:S(2)}, u32[]{:S(2)}) collective-permute-start(bf16[512,256]{1,0:T(8,128)(2,1)S(1)} %collective-permute-done.17.refs_4_), channel_id=1, source_target_pairs={{0,1},{1,0},{2,3},{3,2},{4,5},{5,4},{6,7},{7,6},{8,9},{9,8},{10,11... | collective-permute-start | bytes 786440 | tf_op jit(solution)/shard_map/ppermute | solution.py:30
  83.6 10.3 %collective-permute-start.25 = (bf16[512,256]{1,0:T(8,128)(2,1)S(1)}, bf16[512,256]{1,0:T(8,128)(2,1)S(1)}, u32[]{:S(2)}, u32[]{:S(2)}) collective-permute-start(bf16[512,256]{1,0:T(8,128)(2,1)S(1)} %slice.14), channel_id=1, source_target_pairs={{0,32},{32,64},{64,96},{96,128},{128,160},{160,192},{192,224},{224... | collective-permute-start | bytes 786440 | tf_op jit(solution)/shard_map/ppermute | solution.py:30
  84.3 9.6 %collective-permute-start.26 = (bf16[512,256]{1,0:T(8,128)(2,1)S(1)}, bf16[512,256]{1,0:T(8,128)(2,1)S(1)}, u32[]{:S(2)}, u32[]{:S(2)}) collective-permute-start(bf16[512,256]{1,0:T(8,128)(2,1)S(1)} %slice.15), channel_id=1, source_target_pairs={{0,224},{32,0},{64,32},{96,64},{128,96},{160,128},{192,160},{224,1... | collective-permute-start | bytes 786440 | tf_op jit(solution)/shard_map/ppermute | solution.py:30
  (4 other events, 84.7 us)

commit v8 on v7

--- a/solution.py
+++ b/solution.py
@@ -118,7 +118,7 @@
         in_specs=[pl.BlockSpec(memory_space=pltpu.HBM)] * 2,
         out_specs=[pl.BlockSpec(memory_space=pltpu.VMEM)] * 2,
         scratch_shapes=[pltpu.VMEM((rows, cols), BF16), pltpu.VMEM((rows,), jnp.int32), pltpu.SemaphoreType.DMA((2,))],
-        compiler_params=pltpu.CompilerParams(vmem_limit_bytes=60 * 1024 * 1024),
+        compiler_params=pltpu.CompilerParams(vmem_limit_bytes=4 * 1024 * 1024),
         name="prepare",
     )(partials, gaps)
 
@@ -280,22 +280,23 @@
     halves = in_plane(halves)
     other = around(own, "yl", NYL, 1)
     up_own, down_own = up(own), down(own)
-    halves, tables = sync((halves, make_tables(meta, taps, rows)))
-    up_own, down_own, up_other, down_other, halves = sync((up_own, down_own, up(other), down(other), along_z(halves)))
+    halves, tables, up_own, down_own = sync((halves, make_tables(meta, taps, rows), up_own, down_own))
+    halves = along_z(halves)
     a, b = halves[:rows], halves[rows:]
-    up_1 = jnp.concatenate([up_own, up_other], axis=0)
-    down_1 = jnp.concatenate([down_own, down_other], axis=0)
-    a_x, b_y = sync((along_x(a), across(b)))
+    a_x, b_y = along_x(a), across(b)
+    b_pack = jnp.concatenate([b, b_y], axis=0)
+    up_1 = jnp.concatenate([up_own, up(other)], axis=0)
+    down_1 = jnp.concatenate([down_own, down(other)], axis=0)
+    up_1, down_1, b_pack, a_x = sync((up_1, down_1, b_pack, a_x))
     a_pack = jnp.concatenate([a] + a_x, axis=0)
-    b_pack = jnp.concatenate([b, b_y], axis=0)
-    up_2, down_2, a_pack, b_pack = sync((up(up_1), down(down_1), a_pack, b_pack))
+    up_2, down_2 = up(up_1), down(down_1)
     left = whitened(left_kernel, "left", meta, tables[1], [own, other, up_1, down_1, up_2, down_2], (cols, NE * rows), (cols, 10 * rows))
-    b_x = along_x(b_pack)
-    early = []
-    up_3, down_3, a_far, b_x, left, early = sync((up(up_2), down(down_2), across(a_pack), b_x, left, early))
-    far_own, far_other = up(up_3[:cols]), down(down_3[cols:])
+    b_x, a_far = along_x(b_pack), across(a_pack)
+    up_2, down_2, b_x = sync((up_2, down_2, b_x))
     mine = [a_pack, a_far, b_pack] + b_x
     theirs = [swapped(piece) for piece in mine]
+    up_3, down_3, left, theirs = sync((up(up_2), down(down_2), left, theirs))
+    far_own, far_other = up(up_3[:cols]), down(down_3[cols:])
     right = whitened(right_kernel, "right", meta, tables[0], mine + theirs, (NE * rows, cols), ((NE + 1) * rows, cols))
     most = most_of_product(meta, tables[1], left, right, [up_2, down_2, up_3, down_3], rows)
     return product(meta, tables[1], most, right, [up_3, down_3, far_own, far_other], rows, (rows * NE) ** (-0.5))

time: 96.7 us -> 99.7 us (1.031)
  the two profiles are of different devices: /device:TPU:2 before, /device:TPU:1 now
where the time goes in v8:
time: 99.7 us; the launch traced here: 98.5 us
  starting transfers between devices  60.8 us (61%)
  waiting for transfers between devices  20.1 us (20%)
  Pallas kernels  13.5 us (14%)
  local copies, waits for them, and re-layouts  3.09 us (3%)
    ppermute x25, starting transfers between devices, around(): return lax.ppermute(block, axis, [(i, (i + step) % n) for i in range(n)])  51 us
    ppermute x25, waiting for transfers between devices, around(): return lax.ppermute(block, axis, [(i, (i + step) % n) for i in range(n)])  12 us
    ppermute x1, starting transfers between devices, in_plane(): return lax.ppermute(block, axes, route)  7.93 us
    pallas_call x2, Pallas kernels, whitened(): pl.pallas_call(kernel, out_shape=jax.ShapeDtypeStruct(shape, BF16), in_sp...  5.75 us
    ppermute x1, waiting for transfers between devices, along_z(): return lax.ppermute(block, ('z', 'x', 'yh'), route)  4.51 us
    pallas_call x1, Pallas kernels, most_of_product(): pl.pallas_call(most_kernel, out_shape=[jax.ShapeDtypeStruct((cols, cols),...  3.75 us
    ppermute x1, waiting for transfers between devices, in_plane(): return lax.ppermute(block, axes, route)  3.6 us
    pallas_call x1, Pallas kernels, product(): pl.pallas_call(functools.partial(last_kernel, scale), out_shape=jax.Shape...  2.63 us
  transfers between devices with their start and end apart: 27, of which 6 were waited for; matrix products, arithmetic and copies ran while one was open for 2% of the time, Pallas kernels for 11%

profile of v8, /device:TPU:1, one launch (start us, length us, event | category | flops | bytes accessed | tf_op | source)
XLA Modules:
  0.0 98.5 jit_solution(8324258746621383503)
XLA Ops:
  1.9 2.5 %collective-permute-start.1 = (bf16[512,256]{1,0:T(8,128)(2,1)S(1)}, bf16[512,256]{1,0:T(8,128)(2,1)S(1)}, u32[]{:S(2)}, u32[]{:S(2)}) collective-permute-start(bf16[512,256]{1,0:T(8,128)(2,1)S(1)} %get-tuple-element.38.own), channel_id=1, source_target_pairs={{0,32},{32,64},{64,96},{96,128},{128,160},{160,192},{192,224},{224... | collective-permute-start | bytes 786440 | tf_op jit(solution)/shard_map/ppermute | solution.py:30
  4.5 4.0 %collective-permute-start.2 = (bf16[512,256]{1,0:T(8,128)(2,1)S(1)}, bf16[512,256]{1,0:T(8,128)(2,1)S(1)}, u32[]{:S(2)}, u32[]{:S(2)}) collective-permute-start(bf16[512,256]{1,0:T(8,128)(2,1)S(1)} %get-tuple-element.38.own), channel_id=1, source_target_pairs={{0,224},{32,0},{64,32},{96,64},{128,96},{160,128},{192,160},{224,1... | collective-permute-start | bytes 786440 | tf_op jit(solution)/shard_map/ppermute | solution.py:30
  8.5 7.9 %collective-permute-start = (bf16[512,256]{1,0:T(8,128)(2,1)S(1)}, bf16[512,256]{1,0:T(8,128)(2,1)S(1)}, u32[]{:S(2)}, u32[]{:S(2)}) collective-permute-start(bf16[512,256]{1,0:T(8,128)(2,1)S(1)} %get-tuple-element.35), channel_id=1, source_target_pairs={{0,10},{1,26},{2,8},{3,24},{4,14},{5,30},{6,12},{7,28},{8,2},{9,18... | collective-permute-start | bytes 786440 | tf_op jit(solution)/shard_map/ppermute | solution.py:51
  19.7 3.6 %collective-permute-done = bf16[512,256]{1,0:T(8,128)(2,1)S(1)} collective-permute-done((bf16[512,256]{1,0:T(8,128)(2,1)S(1)}, bf16[512,256]{1,0:T(8,128)(2,1)S(1)}, u32[]{:S(2)}, u32[]{:S(2)}) %collective-permute-start) | collective-permute-done | bytes 262176 | tf_op jit(solution)/shard_map/ppermute | solution.py:51
  23.3 1.9 %collective-permute-start.6 = (bf16[512,256]{1,0:T(8,128)(2,1)S(1)}, bf16[512,256]{1,0:T(8,128)(2,1)S(1)}, u32[]{:S(2)}, u32[]{:S(2)}) collective-permute-start(bf16[512,256]{1,0:T(8,128)(2,1)S(1)} %collective-permute-done), channel_id=1, source_target_pairs={{10,10},{8,40},{14,78},{12,108},{2,130},{0,160},{4,196},{6,230},{3... | collective-permute-start | bytes 786440 | tf_op jit(solution)/shard_map/ppermute | solution.py:60
  26.2 1.5 %collective-permute-start.4 = (bf16[512,256]{1,0:T(8,128)(2,1)S(1)}, bf16[512,256]{1,0:T(8,128)(2,1)S(1)}, u32[]{:S(2)}, u32[]{:S(2)}) collective-permute-start(bf16[512,256]{1,0:T(8,128)(2,1)S(1)} %collective-permute-done.3.other), channel_id=1, source_target_pairs={{0,32},{32,64},{64,96},{96,128},{128,160},{160,192},{192,224},{224... | collective-permute-start | bytes 786440 | tf_op jit(solution)/shard_map/ppermute | solution.py:30
  27.6 4.5 %collective-permute-done.6 = bf16[512,256]{1,0:T(8,128)(2,1)S(1)} collective-permute-done((bf16[512,256]{1,0:T(8,128)(2,1)S(1)}, bf16[512,256]{1,0:T(8,128)(2,1)S(1)}, u32[]{:S(2)}, u32[]{:S(2)}) %collective-permute-start.6) | collective-permute-done | bytes 262176 | tf_op jit(solution)/shard_map/ppermute | solution.py:60
  32.2 4.5 %collective-permute-start.10 = (bf16[256,256]{1,0:T(8,128)(2,1)S(1)}, bf16[256,256]{1,0:T(8,128)(2,1)S(1)}, u32[]{:S(2)}, u32[]{:S(2)}) collective-permute-start(bf16[256,256]{1,0:T(8,128)(2,1)S(1)} %get-tuple-element.65), channel_id=1, source_target_pairs={{0,8},{4,12},{8,0},{12,4},{1,9},{5,13},{9,1},{13,5},{2,10},{6,14},... | collective-permute-start | bytes 393224 | tf_op jit(solution)/shard_map/ppermute | solution.py:30
  36.7 2.7 %collective-permute-start.9 = (bf16[256,256]{1,0:T(8,128)(2,1)S(1)}, bf16[256,256]{1,0:T(8,128)(2,1)S(1)}, u32[]{:S(2)}, u32[]{:S(2)}) collective-permute-start(bf16[256,256]{1,0:T(8,128)(2,1)S(1)} %get-tuple-element.65), channel_id=1, source_target_pairs={{0,12},{4,0},{8,4},{12,8},{1,13},{5,1},{9,5},{13,9},{2,14},{6,2},{... | collective-permute-start | bytes 393224 | tf_op jit(solution)/shard_map/ppermute | solution.py:30
  39.3 4.3 %collective-permute-start.7 = (bf16[256,256]{1,0:T(8,128)(2,1)S(1)}, bf16[256,256]{1,0:T(8,128)(2,1)S(1)}, u32[]{:S(2)}, u32[]{:S(2)}) collective-permute-start(bf16[256,256]{1,0:T(8,128)(2,1)S(1)} %get-tuple-element.66), channel_id=1, source_target_pairs={{0,2},{2,0},{1,3},{3,1},{4,6},{6,4},{5,7},{7,5},{8,10},{10,8},{9,1... | collective-permute-start | bytes 393224 | tf_op jit(solution)/shard_map/ppermute | solution.py:30
  43.7 2.3 %collective-permute-done.7 = bf16[256,256]{1,0:T(8,128)(2,1)S(1)} collective-permute-done((bf16[256,256]{1,0:T(8,128)(2,1)S(1)}, bf16[256,256]{1,0:T(8,128)(2,1)S(1)}, u32[]{:S(2)}, u32[]{:S(2)}) %collective-permute-start.7) | collective-permute-done | bytes 131104 | tf_op jit(solution)/shard_map/ppermute | solution.py:30
  46.1 2.7 %collective-permute-start.14 = (bf16[512,256]{1,0:T(8,128)(2,1)S(1)}, bf16[512,256]{1,0:T(8,128)(2,1)S(1)}, u32[]{:S(2)}, u32[]{:S(2)}) collective-permute-start(bf16[512,256]{1,0:T(8,128)(2,1)S(1)} %pad_maximum_fusion.3.refs_2_), channel_id=1, source_target_pairs={{0,12},{4,0},{8,4},{12,8},{1,13},{5,1},{9,5},{13,9},{2,14},{6,2},{... | collective-permute-start | bytes 786440 | tf_op jit(solution)/shard_map/ppermute | solution.py:30
  48.8 3.5 %collective-permute-start.12 = (bf16[1024,256]{1,0:T(8,128)(2,1)S(1)}, bf16[1024,256]{1,0:T(8,128)(2,1)S(1)}, u32[]{:S(2)}, u32[]{:S(2)}) collective-permute-start(bf16[1024,256]{1,0:T(8,128)(2,1)S(1)} %pad_maximum_fusion.1.down_1), channel_id=1, source_target_pairs={{0,224},{32,0},{64,32},{96,64},{128,96},{160,128},{192,160},{224,1... | collective-permute-start | bytes 1572872 | tf_op jit(solution)/shard_map/ppermute | solution.py:30
  52.3 3.1 %collective-permute-start.19 = (bf16[1024,256]{1,0:T(8,128)(2,1)S(1)}, bf16[1024,256]{1,0:T(8,128)(2,1)S(1)}, u32[]{:S(2)}, u32[]{:S(2)}) collective-permute-start(bf16[1024,256]{1,0:T(8,128)(2,1)S(1)} %pad_maximum_fusion.2.refs_0_), channel_id=1, source_target_pairs={{0,2},{2,0},{1,3},{3,1},{4,6},{6,4},{5,7},{7,5},{8,10},{10,8},{9,1... | collective-permute-start | bytes 1572872 | tf_op jit(solution)/shard_map/ppermute | solution.py:30
  55.3 3.6 %collective-permute-start.15 = (bf16[512,256]{1,0:T(8,128)(2,1)S(1)}, bf16[512,256]{1,0:T(8,128)(2,1)S(1)}, u32[]{:S(2)}, u32[]{:S(2)}) collective-permute-start(bf16[512,256]{1,0:T(8,128)(2,1)S(1)} %pad_maximum_fusion.3.refs_2_), channel_id=1, source_target_pairs={{0,8},{4,12},{8,0},{12,4},{1,9},{5,13},{9,1},{13,5},{2,10},{6,14},... | collective-permute-start | bytes 786440 | tf_op jit(solution)/shard_map/ppermute | solution.py:30
  58.9 5.3 %collective-permute-start.18 = (bf16[1024,256]{1,0:T(8,128)(2,1)S(1)}, bf16[1024,256]{1,0:T(8,128)(2,1)S(1)}, u32[]{:S(2)}, u32[]{:S(2)}) collective-permute-start(bf16[1024,256]{1,0:T(8,128)(2,1)S(1)} %pad_maximum_fusion.2.refs_0_), channel_id=1, source_target_pairs={{0,1},{1,0},{2,3},{3,2},{4,5},{5,4},{6,7},{7,6},{8,9},{9,8},{10,11... | collective-permute-start | bytes 1572872 | tf_op jit(solution)/shard_map/ppermute | solution.py:30
  64.2 6.9 %collective-permute-start.21 = (bf16[512,256]{1,0:T(8,128)(2,1)S(1)}, bf16[512,256]{1,0:T(8,128)(2,1)S(1)}, u32[]{:S(2)}, u32[]{:S(2)}) collective-permute-start(bf16[512,256]{1,0:T(8,128)(2,1)S(1)} %pad_maximum_fusion.3.refs_2_), channel_id=1, source_target_pairs={{0,1},{1,0},{2,3},{3,2},{4,5},{5,4},{6,7},{7,6},{8,9},{9,8},{10,11... | collective-permute-start | bytes 786440 | tf_op jit(solution)/shard_map/ppermute | solution.py:30
  72.2 2.1 %collective-permute-start.17 = (bf16[1024,256]{1,0:T(8,128)(2,1)S(1)}, bf16[1024,256]{1,0:T(8,128)(2,1)S(1)}, u32[]{:S(2)}, u32[]{:S(2)}) collective-permute-start(bf16[1024,256]{1,0:T(8,128)(2,1)S(1)} %collective-permute-done.12.down_2), channel_id=1, source_target_pairs={{0,224},{32,0},{64,32},{96,64},{128,96},{160,128},{192,160},{224,1... | collective-permute-start | bytes 1572872 | tf_op jit(solution)/shard_map/ppermute | solution.py:30
  75.0 2.5 %left.1.left_in = bf16[512,4096]{1,0:T(8,128)(2,1)S(1)} custom-call(s32[71]{0:T(128)S(1)} %concatenate.15.meta_ref, bf16[4,512,256]{2,1,0:T(8,128)(2,1)S(1)} %get-tuple-element.39.tables_ref, bf16[512,256]{1,0:T(8,128)(2,1)S(1)} %get-tuple-element.38.own, bf16[512,256]{1,0:T(8,128)(2,1)S(1)} %collective-permute-done.3.other, ...), custom_call_target="tpu_custom_call" | custom-call | tf_op jit(solution)/shard_map/left/pallas_call | solution.py:215
  77.6 8.2 %collective-permute-done.16.up_3 = bf16[1024,256]{1,0:T(8,128)(2,1)S(1)} collective-permute-done((bf16[1024,256]{1,0:T(8,128)(2,1)S(1)}, bf16[1024,256]{1,0:T(8,128)(2,1)S(1)}, u32[]{:S(2)}, u32[]{:S(2)}) %collective-permute-start.16) | collective-permute-done | bytes 524320 | tf_op jit(solution)/shard_map/ppermute | solution.py:30
  85.9 2.9 %collective-permute-start.26 = (bf16[512,256]{1,0:T(8,128)(2,1)S(1)}, bf16[512,256]{1,0:T(8,128)(2,1)S(1)}, u32[]{:S(2)}, u32[]{:S(2)}) collective-permute-start(bf16[512,256]{1,0:T(8,128)(2,1)S(1)} %slice.15), channel_id=1, source_target_pairs={{0,224},{32,0},{64,32},{96,64},{128,96},{160,128},{192,160},{224,1... | collective-permute-start | bytes 786440 | tf_op jit(solution)/shard_map/ppermute | solution.py:30
  88.9 3.2 %right.1.right_ref = bf16[4096,512]{1,0:T(8,128)(2,1)S(1)} custom-call(s32[71]{0:T(128)S(1)} %concatenate.15.meta_ref, bf16[4,256,512]{2,1,0:T(8,128)(2,1)S(1)} %get-tuple-element.55.tables_ref, bf16[1024,256]{1,0:T(8,128)(2,1)S(1)} %pad_maximum_fusion.2.refs_0_, bf16[1024,256]{1,0:T(8,128)(2,1)S(1)} %collective-permute-done.19.refs_1_, ...), custom_call_target="tpu_custom_call" | custom-call | tf_op jit(solution)/shard_map/right/pallas_call | solution.py:215
  92.1 3.7 %most.1 = (f32[512,512]{1,0:T(8,128)S(1)}, bf16[512,4096]{1,0:T(8,128)(2,1)S(1)}) custom-call(s32[71]{0:T(128)S(1)} %concatenate.15.meta_ref, bf16[4,512,256]{2,1,0:T(8,128)(2,1)S(1)} %get-tuple-element.39.tables_ref, bf16[512,4096]{1,0:T(8,128)(2,1)S(1)} %left.1.left_in, bf16[4096,512]{1,0:T(8,128)(2,1)S(1)} %right.1.right_ref, ...), custom_call_target="tpu_custom_call", output_to_operand_aliasing={{1}: (2, {})} | custom-call | tf_op jit(solution)/shard_map/most/pallas_call | solution.py:229
  95.9 2.6 %product.1 = f32[512,512]{1,0:T(8,128)} custom-call(s32[71]{0:T(128)S(1)} %concatenate.15.meta_ref, bf16[4,512,256]{2,1,0:T(8,128)(2,1)S(1)} %get-tuple-element.39.tables_ref, f32[512,512]{1,0:T(8,128)S(1)} %get-tuple-element.64.most_ref, bf16[4096,512]{1,0:T(8,128)(2,1)S(1)} %right.1.right_ref, bf16[1024,256]{1,0:T(8,128)(2,1)S(1)} %collective-permute-done.16.up_3, ...), custom_call_target="tpu_custom_call" | custom-call | tf_op jit(solution)/shard_map/product/pallas_call | solution.py:244
  (50 shorter events, 7.7 us)
Async XLA Ops:
  1.9 17.8 %collective-permute-start.1 = (bf16[512,256]{1,0:T(8,128)(2,1)S(1)}, bf16[512,256]{1,0:T(8,128)(2,1)S(1)}, u32[]{:S(2)}, u32[]{:S(2)}) collective-permute-start(bf16[512,256]{1,0:T(8,128)(2,1)S(1)} %get-tuple-element.38.own), channel_id=1, source_target_pairs={{0,32},{32,64},{64,96},{96,128},{128,160},{160,192},{192,224},{224... | collective-permute-start | bytes 786440 | tf_op jit(solution)/shard_map/ppermute | solution.py:30
  4.5 15.3 %collective-permute-start.2 = (bf16[512,256]{1,0:T(8,128)(2,1)S(1)}, bf16[512,256]{1,0:T(8,128)(2,1)S(1)}, u32[]{:S(2)}, u32[]{:S(2)}) collective-permute-start(bf16[512,256]{1,0:T(8,128)(2,1)S(1)} %get-tuple-element.38.own), channel_id=1, source_target_pairs={{0,224},{32,0},{64,32},{96,64},{128,96},{160,128},{192,160},{224,1... | collective-permute-start | bytes 786440 | tf_op jit(solution)/shard_map/ppermute | solution.py:30
  8.5 14.8 %collective-permute-start = (bf16[512,256]{1,0:T(8,128)(2,1)S(1)}, bf16[512,256]{1,0:T(8,128)(2,1)S(1)}, u32[]{:S(2)}, u32[]{:S(2)}) collective-permute-start(bf16[512,256]{1,0:T(8,128)(2,1)S(1)} %get-tuple-element.35), channel_id=1, source_target_pairs={{0,10},{1,26},{2,8},{3,24},{4,14},{5,30},{6,12},{7,28},{8,2},{9,18... | collective-permute-start | bytes 786440 | tf_op jit(solution)/shard_map/ppermute | solution.py:51
  16.4 9.8 %collective-permute-start.3 = (bf16[512,256]{1,0:T(8,128)(2,1)S(1)}, bf16[512,256]{1,0:T(8,128)(2,1)S(1)}, u32[]{:S(2)}, u32[]{:S(2)}) collective-permute-start(bf16[512,256]{1,0:T(8,128)(2,1)S(1)} %get-tuple-element.38.own), channel_id=1, source_target_pairs={{0,16},{16,0},{1,17},{17,1},{2,18},{18,2},{3,19},{19,3},{4,20},{20... | collective-permute-start | bytes 786440 | tf_op jit(solution)/shard_map/ppermute | solution.py:30
  23.3 8.8 %collective-permute-start.6 = (bf16[512,256]{1,0:T(8,128)(2,1)S(1)}, bf16[512,256]{1,0:T(8,128)(2,1)S(1)}, u32[]{:S(2)}, u32[]{:S(2)}) collective-permute-start(bf16[512,256]{1,0:T(8,128)(2,1)S(1)} %collective-permute-done), channel_id=1, source_target_pairs={{10,10},{8,40},{14,78},{12,108},{2,130},{0,160},{4,196},{6,230},{3... | collective-permute-start | bytes 786440 | tf_op jit(solution)/shard_map/ppermute | solution.py:60
  26.2 13.2 %collective-permute-start.5 = (bf16[512,256]{1,0:T(8,128)(2,1)S(1)}, bf16[512,256]{1,0:T(8,128)(2,1)S(1)}, u32[]{:S(2)}, u32[]{:S(2)}) collective-permute-start(bf16[512,256]{1,0:T(8,128)(2,1)S(1)} %collective-permute-done.3.other), channel_id=1, source_target_pairs={{0,224},{32,0},{64,32},{96,64},{128,96},{160,128},{192,160},{224,1... | collective-permute-start | bytes 786440 | tf_op jit(solution)/shard_map/ppermute | solution.py:30
  26.2 17.5 %collective-permute-start.4 = (bf16[512,256]{1,0:T(8,128)(2,1)S(1)}, bf16[512,256]{1,0:T(8,128)(2,1)S(1)}, u32[]{:S(2)}, u32[]{:S(2)}) collective-permute-start(bf16[512,256]{1,0:T(8,128)(2,1)S(1)} %collective-permute-done.3.other), channel_id=1, source_target_pairs={{0,32},{32,64},{64,96},{96,128},{128,160},{160,192},{192,224},{224... | collective-permute-start | bytes 786440 | tf_op jit(solution)/shard_map/ppermute | solution.py:30
  32.2 13.8 %collective-permute-start.10 = (bf16[256,256]{1,0:T(8,128)(2,1)S(1)}, bf16[256,256]{1,0:T(8,128)(2,1)S(1)}, u32[]{:S(2)}, u32[]{:S(2)}) collective-permute-start(bf16[256,256]{1,0:T(8,128)(2,1)S(1)} %get-tuple-element.65), channel_id=1, source_target_pairs={{0,8},{4,12},{8,0},{12,4},{1,9},{5,13},{9,1},{13,5},{2,10},{6,14},... | collective-permute-start | bytes 393224 | tf_op jit(solution)/shard_map/ppermute | solution.py:30
  36.7 9.4 %collective-permute-start.8 = (bf16[256,256]{1,0:T(8,128)(2,1)S(1)}, bf16[256,256]{1,0:T(8,128)(2,1)S(1)}, u32[]{:S(2)}, u32[]{:S(2)}) collective-permute-start(bf16[256,256]{1,0:T(8,128)(2,1)S(1)} %get-tuple-element.65), channel_id=1, source_target_pairs={{0,4},{4,8},{8,12},{12,0},{1,5},{5,9},{9,13},{13,1},{2,6},{6,10},{... | collective-permute-start | bytes 393224 | tf_op jit(solution)/shard_map/ppermute | solution.py:30
  36.7 9.4 %collective-permute-start.9 = (bf16[256,256]{1,0:T(8,128)(2,1)S(1)}, bf16[256,256]{1,0:T(8,128)(2,1)S(1)}, u32[]{:S(2)}, u32[]{:S(2)}) collective-permute-start(bf16[256,256]{1,0:T(8,128)(2,1)S(1)} %get-tuple-element.65), channel_id=1, source_target_pairs={{0,12},{4,0},{8,4},{12,8},{1,13},{5,1},{9,5},{13,9},{2,14},{6,2},{... | collective-permute-start | bytes 393224 | tf_op jit(solution)/shard_map/ppermute | solution.py:30
  39.3 6.6 %collective-permute-start.7 = (bf16[256,256]{1,0:T(8,128)(2,1)S(1)}, bf16[256,256]{1,0:T(8,128)(2,1)S(1)}, u32[]{:S(2)}, u32[]{:S(2)}) collective-permute-start(bf16[256,256]{1,0:T(8,128)(2,1)S(1)} %get-tuple-element.66), channel_id=1, source_target_pairs={{0,2},{2,0},{1,3},{3,1},{4,6},{6,4},{5,7},{7,5},{8,10},{10,8},{9,1... | collective-permute-start | bytes 393224 | tf_op jit(solution)/shard_map/ppermute | solution.py:30
  46.0 9.3 %collective-permute-start.13 = (bf16[512,256]{1,0:T(8,128)(2,1)S(1)}, bf16[512,256]{1,0:T(8,128)(2,1)S(1)}, u32[]{:S(2)}, u32[]{:S(2)}) collective-permute-start(bf16[512,256]{1,0:T(8,128)(2,1)S(1)} %pad_maximum_fusion.3.refs_2_), channel_id=1, source_target_pairs={{0,4},{4,8},{8,12},{12,0},{1,5},{5,9},{9,13},{13,1},{2,6},{6,10},{... | collective-permute-start | bytes 786440 | tf_op jit(solution)/shard_map/ppermute | solution.py:30
  46.1 12.8 %collective-permute-start.14 = (bf16[512,256]{1,0:T(8,128)(2,1)S(1)}, bf16[512,256]{1,0:T(8,128)(2,1)S(1)}, u32[]{:S(2)}, u32[]{:S(2)}) collective-permute-start(bf16[512,256]{1,0:T(8,128)(2,1)S(1)} %pad_maximum_fusion.3.refs_2_), channel_id=1, source_target_pairs={{0,12},{4,0},{8,4},{12,8},{1,13},{5,1},{9,5},{13,9},{2,14},{6,2},{... | collective-permute-start | bytes 786440 | tf_op jit(solution)/shard_map/ppermute | solution.py:30
  48.8 22.3 %collective-permute-start.11 = (bf16[1024,256]{1,0:T(8,128)(2,1)S(1)}, bf16[1024,256]{1,0:T(8,128)(2,1)S(1)}, u32[]{:S(2)}, u32[]{:S(2)}) collective-permute-start(bf16[1024,256]{1,0:T(8,128)(2,1)S(1)} %pad_maximum_fusion.up_1), channel_id=1, source_target_pairs={{0,32},{32,64},{64,96},{96,128},{128,160},{160,192},{192,224},{224... | collective-permute-start | bytes 1572872 | tf_op jit(solution)/shard_map/ppermute | solution.py:30
  48.8 22.3 %collective-permute-start.12 = (bf16[1024,256]{1,0:T(8,128)(2,1)S(1)}, bf16[1024,256]{1,0:T(8,128)(2,1)S(1)}, u32[]{:S(2)}, u32[]{:S(2)}) collective-permute-start(bf16[1024,256]{1,0:T(8,128)(2,1)S(1)} %pad_maximum_fusion.1.down_1), channel_id=1, source_target_pairs={{0,224},{32,0},{64,32},{96,64},{128,96},{160,128},{192,160},{224,1... | collective-permute-start | bytes 1572872 | tf_op jit(solution)/shard_map/ppermute | solution.py:30
  52.3 19.0 %collective-permute-start.19 = (bf16[1024,256]{1,0:T(8,128)(2,1)S(1)}, bf16[1024,256]{1,0:T(8,128)(2,1)S(1)}, u32[]{:S(2)}, u32[]{:S(2)}) collective-permute-start(bf16[1024,256]{1,0:T(8,128)(2,1)S(1)} %pad_maximum_fusion.2.refs_0_), channel_id=1, source_target_pairs={{0,2},{2,0},{1,3},{3,1},{4,6},{6,4},{5,7},{7,5},{8,10},{10,8},{9,1... | collective-permute-start | bytes 1572872 | tf_op jit(solution)/shard_map/ppermute | solution.py:30
  55.3 8.9 %collective-permute-start.15 = (bf16[512,256]{1,0:T(8,128)(2,1)S(1)}, bf16[512,256]{1,0:T(8,128)(2,1)S(1)}, u32[]{:S(2)}, u32[]{:S(2)}) collective-permute-start(bf16[512,256]{1,0:T(8,128)(2,1)S(1)} %pad_maximum_fusion.3.refs_2_), channel_id=1, source_target_pairs={{0,8},{4,12},{8,0},{12,4},{1,9},{5,13},{9,1},{13,5},{2,10},{6,14},... | collective-permute-start | bytes 786440 | tf_op jit(solution)/shard_map/ppermute | solution.py:30
  58.9 15.4 %collective-permute-start.18 = (bf16[1024,256]{1,0:T(8,128)(2,1)S(1)}, bf16[1024,256]{1,0:T(8,128)(2,1)S(1)}, u32[]{:S(2)}, u32[]{:S(2)}) collective-permute-start(bf16[1024,256]{1,0:T(8,128)(2,1)S(1)} %pad_maximum_fusion.2.refs_0_), channel_id=1, source_target_pairs={{0,1},{1,0},{2,3},{3,2},{4,5},{5,4},{6,7},{7,6},{8,9},{9,8},{10,11... | collective-permute-start | bytes 1572872 | tf_op jit(solution)/shard_map/ppermute | solution.py:30
  64.2 8.0 %collective-permute-start.21 = (bf16[512,256]{1,0:T(8,128)(2,1)S(1)}, bf16[512,256]{1,0:T(8,128)(2,1)S(1)}, u32[]{:S(2)}, u32[]{:S(2)}) collective-permute-start(bf16[512,256]{1,0:T(8,128)(2,1)S(1)} %pad_maximum_fusion.3.refs_2_), channel_id=1, source_target_pairs={{0,1},{1,0},{2,3},{3,2},{4,5},{5,4},{6,7},{7,6},{8,9},{9,8},{10,11... | collective-permute-start | bytes 786440 | tf_op jit(solution)/shard_map/ppermute | solution.py:30
  71.1 14.7 %collective-permute-start.16 = (bf16[1024,256]{1,0:T(8,128)(2,1)S(1)}, bf16[1024,256]{1,0:T(8,128)(2,1)S(1)}, u32[]{:S(2)}, u32[]{:S(2)}) collective-permute-start(bf16[1024,256]{1,0:T(8,128)(2,1)S(1)} %collective-permute-done.11.up_2), channel_id=1, source_target_pairs={{0,32},{32,64},{64,96},{96,128},{128,160},{160,192},{192,224},{224... | collective-permute-start | bytes 1572872 | tf_op jit(solution)/shard_map/ppermute | solution.py:30
  71.3 6.3 %collective-permute-start.20 = (bf16[1024,256]{1,0:T(8,128)(2,1)S(1)}, bf16[1024,256]{1,0:T(8,128)(2,1)S(1)}, u32[]{:S(2)}, u32[]{:S(2)}) collective-permute-start(bf16[1024,256]{1,0:T(8,128)(2,1)S(1)} %collective-permute-done.19.refs_1_), channel_id=1, source_target_pairs={{0,1},{1,0},{2,3},{3,2},{4,5},{5,4},{6,7},{7,6},{8,9},{9,8},{10,11... | collective-permute-start | bytes 1572872 | tf_op jit(solution)/shard_map/ppermute | solution.py:30
  72.2 13.6 %collective-permute-start.17 = (bf16[1024,256]{1,0:T(8,128)(2,1)S(1)}, bf16[1024,256]{1,0:T(8,128)(2,1)S(1)}, u32[]{:S(2)}, u32[]{:S(2)}) collective-permute-start(bf16[1024,256]{1,0:T(8,128)(2,1)S(1)} %collective-permute-done.12.down_2), channel_id=1, source_target_pairs={{0,224},{32,0},{64,32},{96,64},{128,96},{160,128},{192,160},{224,1... | collective-permute-start | bytes 1572872 | tf_op jit(solution)/shard_map/ppermute | solution.py:30
  85.8 10.1 %collective-permute-start.25 = (bf16[512,256]{1,0:T(8,128)(2,1)S(1)}, bf16[512,256]{1,0:T(8,128)(2,1)S(1)}, u32[]{:S(2)}, u32[]{:S(2)}) collective-permute-start(bf16[512,256]{1,0:T(8,128)(2,1)S(1)} %slice.14), channel_id=1, source_target_pairs={{0,32},{32,64},{64,96},{96,128},{128,160},{160,192},{192,224},{224... | collective-permute-start | bytes 786440 | tf_op jit(solution)/shard_map/ppermute | solution.py:30
  85.9 10.0 %collective-permute-start.26 = (bf16[512,256]{1,0:T(8,128)(2,1)S(1)}, bf16[512,256]{1,0:T(8,128)(2,1)S(1)}, u32[]{:S(2)}, u32[]{:S(2)}) collective-permute-start(bf16[512,256]{1,0:T(8,128)(2,1)S(1)} %slice.15), channel_id=1, source_target_pairs={{0,224},{32,0},{64,32},{96,64},{128,96},{160,128},{192,160},{224,1... | collective-permute-start | bytes 786440 | tf_op jit(solution)/shard_map/ppermute | solution.py:30
  (5 other events, 11.3 us)

commit v9 on v8

--- a/solution.py
+++ b/solution.py
@@ -94,7 +94,7 @@
     )(meta, padded)
 
 
-def prepare_kernel(partials_ref, gaps_ref, halves_ref, turned_ref, held, held_gaps, sems):
+def prepare_kernel(partials_ref, gaps_ref, masked_ref, turned_ref, held, held_gaps, sems):
     rows, cols = held.shape
     copies = [pltpu.make_async_copy(gaps_ref, held_gaps, sems.at[0]), pltpu.make_async_copy(partials_ref, held, sems.at[1])]
     for copy in copies:
@@ -106,15 +106,14 @@
     for i in range(cols // 128):
         part = held[:, i * 128 : (i + 1) * 128] * kept_t
         turned_ref[i * 128 : (i + 1) * 128, :] = part.T
-        half, at = i // (cols // 256), i % (cols // 256) * 128
-        halves_ref[half * rows : (half + 1) * rows, at : at + 128] = part
+        masked_ref[:, i * 128 : (i + 1) * 128] = part
 
 
 def prepare(partials, gaps):
     rows, cols = partials.shape
     return pl.pallas_call(
         prepare_kernel,
-        out_shape=[jax.ShapeDtypeStruct((2 * rows, cols // 2), BF16), jax.ShapeDtypeStruct((cols, rows), BF16)],
+        out_shape=[jax.ShapeDtypeStruct((rows, cols), BF16), jax.ShapeDtypeStruct((cols, rows), BF16)],
         in_specs=[pl.BlockSpec(memory_space=pltpu.HBM)] * 2,
         out_specs=[pl.BlockSpec(memory_space=pltpu.VMEM)] * 2,
         scratch_shapes=[pltpu.VMEM((rows, cols), BF16), pltpu.VMEM((rows,), jnp.int32), pltpu.SemaphoreType.DMA((2,))],
@@ -156,25 +155,17 @@
 
 
 def right_kernel(meta_ref, tables_ref, *refs):
-    pieces = refs[0:12]
-    out_ref, raw = refs[12:]
-    half = pieces[0].shape[1]
+    pieces = refs[0:8]
+    out_ref, raw = refs[8:]
     rows = tables_ref.shape[1]
     z, x, yh, core = [meta_ref[i] for i in (0, 2, 3, 4)]
     raw[:rows] = jnp.zeros((rows, raw.shape[1]), BF16)
-
-    def place(piece, b, h, dx, dy, q):
-        line = NYH * ((x + dx) & 3) + (yh ^ dy)
-        e = 2 * meta_ref[7 + NZ * z + line] + (core ^ q)
-        raw[at_block(e + 1, rows), h * half : (h + 1) * half] = piece[b * rows : (b + 1) * rows]
-
     for q in range(2):
-        for dy in range(2):
-            for b in range(4):
-                place(pieces[6 * q + dy], b, 0, DX[b], dy, q)
-        for i in range(4):
+        for s in range(4):
             for dy in range(2):
-                place(pieces[6 * q + 2 + i], dy, 1, DX[i], dy, q)
+                line = NYH * ((x + DX[s]) & 3) + (yh ^ dy)
+                e = 2 * meta_ref[7 + NZ * z + line] + (core ^ q)
+                raw[at_block(e + 1, rows)] = pieces[4 * q + s][dy * rows : (dy + 1) * rows]
     for e in range(NE):
         table = tables_ref[table_of(e, meta_ref)]
         white = jnp.dot(table, raw[e * rows : (e + 2) * rows], preferred_element_type=F32)
@@ -254,12 +245,11 @@
 
 def on_device(partials, gaps, arc_start, taps):
     rows, cols = partials.shape
-    half = cols // 2
     places = [lax.axis_index(axis) for axis in EPOCH + COL]
     origin = np.argsort(np.array(LINE, np.int32), axis=0).T.astype(np.int32)
     meta = jnp.stack(places + [arc_start[0], arc_start[0] // rows]).astype(jnp.int32)
     meta = jnp.concatenate([meta, jnp.asarray(origin.reshape(-1))])
-    halves, own = prepare(partials, gaps)
+    masked, own = prepare(partials, gaps)
 
     def up(block):
         return around(block, "z", NZ, 1)
@@ -277,25 +267,19 @@
         return around(block, "yh", NYH, 1)
 
     sync = lax.optimization_barrier
-    halves = in_plane(halves)
+    here = in_plane(masked)
     other = around(own, "yl", NYL, 1)
     up_own, down_own = up(own), down(own)
-    halves, tables, up_own, down_own = sync((halves, make_tables(meta, taps, rows), up_own, down_own))
-    halves = along_z(halves)
-    a, b = halves[:rows], halves[rows:]
-    a_x, b_y = along_x(a), across(b)
-    b_pack = jnp.concatenate([b, b_y], axis=0)
-    up_1 = jnp.concatenate([up_own, up(other)], axis=0)
-    down_1 = jnp.concatenate([down_own, down(other)], axis=0)
-    up_1, down_1, b_pack, a_x = sync((up_1, down_1, b_pack, a_x))
-    a_pack = jnp.concatenate([a] + a_x, axis=0)
+    here, tables = sync((here, make_tables(meta, taps, rows)))
+    up_own, down_own, up_other, down_other, here = sync((up_own, down_own, up(other), down(other), along_z(here)))
+    up_1 = jnp.concatenate([up_own, up_other], axis=0)
+    down_1 = jnp.concatenate([down_own, down_other], axis=0)
+    pair = jnp.concatenate([here, across(here)], axis=0)
     up_2, down_2 = up(up_1), down(down_1)
     left = whitened(left_kernel, "left", meta, tables[1], [own, other, up_1, down_1, up_2, down_2], (cols, NE * rows), (cols, 10 * rows))
-    b_x, a_far = along_x(b_pack), across(a_pack)
-    up_2, down_2, b_x = sync((up_2, down_2, b_x))
-    mine = [a_pack, a_far, b_pack] + b_x
+    mine = [pair] + along_x(pair)
     theirs = [swapped(piece) for piece in mine]
-    up_3, down_3, left, theirs = sync((up(up_2), down(down_2), left, theirs))
+    up_3, down_3, left = sync((up(up_2), down(down_2), left))
     far_own, far_other = up(up_3[:cols]), down(down_3[cols:])
     right = whitened(right_kernel, "right", meta, tables[0], mine + theirs, (NE * rows, cols), ((NE + 1) * rows, cols))
     most = most_of_product(meta, tables[1], left, right, [up_2, down_2, up_3, down_3], rows)

time: 99.7 us -> 92.4 us (0.927)
  starting transfers between devices: 60.8 us -> 47.6 us
  waiting for transfers between devices: 20.1 us -> 26.7 us
    ppermute x25 -> x19, starting transfers between devices: 51 us -> 34.5 us  [around(): return lax.ppermute(block, axis, [(i, (i + step) % n) for i in range(n)])]
    ppermute x25 -> x19, waiting for transfers between devices: 12 us -> 23.9 us  [around(): return lax.ppermute(block, axis, [(i, (i + step) % n) for i in range(n)])]
    ppermute x1, waiting for transfers between devices: 3.6 us -> 0.01 us  [in_plane(): return lax.ppermute(block, axes, route)]
    ppermute x1, starting transfers between devices: 1.91 us -> 4.61 us  [along_z(): return lax.ppermute(block, ('z', 'x', 'yh'), route)]
    ppermute x1, waiting for transfers between devices: 4.51 us -> 2.79 us  [along_z(): return lax.ppermute(block, ('z', 'x', 'yh'), route)]
  transfers between devices with their start and end apart: 27 -> 21, of which waited for: 6 -> 11; matrix products, arithmetic and copies ran while one was open for 2% -> 2% of each run, Pallas kernels for 11% -> 11%
where the time goes in v9:
time: 92.4 us; the launch traced here: 91.8 us
  starting transfers between devices  47.6 us (52%)
  waiting for transfers between devices  26.7 us (29%)
  Pallas kernels  13.4 us (15%)
  local copies, waits for them, and re-layouts  3.18 us (3%)
    ppermute x19, starting transfers between devices, around(): return lax.ppermute(block, axis, [(i, (i + step) % n) for i in range(n)])  34.5 us
    ppermute x19, waiting for transfers between devices, around(): return lax.ppermute(block, axis, [(i, (i + step) % n) for i in range(n)])  23.9 us
    ppermute x1, starting transfers between devices, in_plane(): return lax.ppermute(block, axes, route)  8.49 us
    pallas_call x2, Pallas kernels, whitened(): pl.pallas_call(kernel, out_shape=jax.ShapeDtypeStruct(shape, BF16), in_sp...  5.7 us
    ppermute x1, starting transfers between devices, along_z(): return lax.ppermute(block, ('z', 'x', 'yh'), route)  4.61 us
    pallas_call x1, Pallas kernels, most_of_product(): pl.pallas_call(most_kernel, out_shape=[jax.ShapeDtypeStruct((cols, cols),...  3.74 us
    ppermute x1, waiting for transfers between devices, along_z(): return lax.ppermute(block, ('z', 'x', 'yh'), route)  2.79 us
    pallas_call x1, Pallas kernels, product(): pl.pallas_call(functools.partial(last_kernel, scale), out_shape=jax.Shape...  2.63 us
  transfers between devices with their start and end apart: 21, of which 11 were waited for; matrix products, arithmetic and copies ran while one was open for 2% of the time, Pallas kernels for 11%

profile of v9, /device:TPU:1, one launch (start us, length us, event | category | flops | bytes accessed | tf_op | source)
XLA Modules:
  0.0 91.8 jit_solution(18059254125869887804)
XLA Ops:
  1.9 8.5 %collective-permute-start = (bf16[256,512]{1,0:T(8,128)(2,1)S(1)}, bf16[256,512]{1,0:T(8,128)(2,1)S(1)}, u32[]{:S(2)}, u32[]{:S(2)}) collective-permute-start(bf16[256,512]{1,0:T(8,128)(2,1)S(1)} %get-tuple-element.21), channel_id=1, source_target_pairs={{0,10},{1,26},{2,8},{3,24},{4,14},{5,30},{6,12},{7,28},{8,2},{9,18... | collective-permute-start | bytes 786440 | tf_op jit(solution)/shard_map/ppermute | solution.py:51
  10.5 5.4 %collective-permute-start.2 = (bf16[512,256]{1,0:T(8,128)(2,1)S(1)}, bf16[512,256]{1,0:T(8,128)(2,1)S(1)}, u32[]{:S(2)}, u32[]{:S(2)}) collective-permute-start(bf16[512,256]{1,0:T(8,128)(2,1)S(1)} %get-tuple-element.25.own), channel_id=1, source_target_pairs={{0,224},{32,0},{64,32},{96,64},{128,96},{160,128},{192,160},{224,1... | collective-permute-start | bytes 786440 | tf_op jit(solution)/shard_map/ppermute | solution.py:30
  19.1 1.2 %collective-permute-done.3.other = bf16[512,256]{1,0:T(8,128)(2,1)S(1)} collective-permute-done((bf16[512,256]{1,0:T(8,128)(2,1)S(1)}, bf16[512,256]{1,0:T(8,128)(2,1)S(1)}, u32[]{:S(2)}, u32[]{:S(2)}) %collective-permute-start.3) | collective-permute-done | bytes 262176 | tf_op jit(solution)/shard_map/ppermute | solution.py:30
  20.3 4.3 %collective-permute-start.5 = (bf16[512,256]{1,0:T(8,128)(2,1)S(1)}, bf16[512,256]{1,0:T(8,128)(2,1)S(1)}, u32[]{:S(2)}, u32[]{:S(2)}) collective-permute-start(bf16[512,256]{1,0:T(8,128)(2,1)S(1)} %collective-permute-done.3.other), channel_id=1, source_target_pairs={{0,224},{32,0},{64,32},{96,64},{128,96},{160,128},{192,160},{224,1... | collective-permute-start | bytes 786440 | tf_op jit(solution)/shard_map/ppermute | solution.py:30
  24.6 4.6 %collective-permute-start.6 = (bf16[256,512]{1,0:T(8,128)(2,1)S(1)}, bf16[256,512]{1,0:T(8,128)(2,1)S(1)}, u32[]{:S(2)}, u32[]{:S(2)}) collective-permute-start(bf16[256,512]{1,0:T(8,128)(2,1)S(1)} %collective-permute-done), channel_id=1, source_target_pairs={{10,10},{8,40},{14,78},{12,108},{2,130},{0,160},{4,196},{6,230},{3... | collective-permute-start | bytes 786440 | tf_op jit(solution)/shard_map/ppermute | solution.py:60
  29.5 3.1 %collective-permute-done.4 = bf16[512,256]{1,0:T(8,128)(2,1)S(1)} collective-permute-done((bf16[512,256]{1,0:T(8,128)(2,1)S(1)}, bf16[512,256]{1,0:T(8,128)(2,1)S(1)}, u32[]{:S(2)}, u32[]{:S(2)}) %collective-permute-start.4) | collective-permute-done | bytes 262176 | tf_op jit(solution)/shard_map/ppermute | solution.py:30
  32.6 2.8 %collective-permute-done.6 = bf16[256,512]{1,0:T(8,128)(2,1)S(1)} collective-permute-done((bf16[256,512]{1,0:T(8,128)(2,1)S(1)}, bf16[256,512]{1,0:T(8,128)(2,1)S(1)}, u32[]{:S(2)}, u32[]{:S(2)}) %collective-permute-start.6) | collective-permute-done | bytes 262176 | tf_op jit(solution)/shard_map/ppermute | solution.py:60
  35.4 9.0 %collective-permute-start.11 = (bf16[256,512]{1,0:T(8,128)(2,1)S(1)}, bf16[256,512]{1,0:T(8,128)(2,1)S(1)}, u32[]{:S(2)}, u32[]{:S(2)}) collective-permute-start(bf16[256,512]{1,0:T(8,128)(2,1)S(1)} %collective-permute-done.6), channel_id=1, source_target_pairs={{0,2},{2,0},{1,3},{3,1},{4,6},{6,4},{5,7},{7,5},{8,10},{10,8},{9,1... | collective-permute-start | bytes 786440 | tf_op jit(solution)/shard_map/ppermute | solution.py:30
  44.5 1.5 %collective-permute-start.7 = (bf16[1024,256]{1,0:T(8,128)(2,1)S(1)}, bf16[1024,256]{1,0:T(8,128)(2,1)S(1)}, u32[]{:S(2)}, u32[]{:S(2)}) collective-permute-start(bf16[1024,256]{1,0:T(8,128)(2,1)S(1)} %constant_dynamic-update-slice_fusion.up_1), channel_id=1, source_target_pairs={{0,32},{32,64},{64,96},{96,128},{128,160},{160,192},{192,224},{224... | collective-permute-start | bytes 1572872 | tf_op jit(solution)/shard_map/ppermute | solution.py:30
  46.1 3.4 %collective-permute-done.11 = bf16[256,512]{1,0:T(8,128)(2,1)S(1)} collective-permute-done((bf16[256,512]{1,0:T(8,128)(2,1)S(1)}, bf16[256,512]{1,0:T(8,128)(2,1)S(1)}, u32[]{:S(2)}, u32[]{:S(2)}) %collective-permute-start.11) | collective-permute-done | bytes 262176 | tf_op jit(solution)/shard_map/ppermute | solution.py:30
  50.3 1.2 %collective-permute-start.12 = (bf16[512,512]{1,0:T(8,128)(2,1)S(1)}, bf16[512,512]{1,0:T(8,128)(2,1)S(1)}, u32[]{:S(2)}, u32[]{:S(2)}) collective-permute-start(bf16[512,512]{1,0:T(8,128)(2,1)S(1)} %constant_dynamic-update-slice_fusion.4.refs_0_), channel_id=1, source_target_pairs={{0,4},{4,8},{8,12},{12,0},{1,5},{5,9},{9,13},{13,1},{2,6},{6,10},{... | collective-permute-start | bytes 1572872 | tf_op jit(solution)/shard_map/ppermute | solution.py:30
  51.5 4.6 %collective-permute-done.9.down_2 = bf16[1024,256]{1,0:T(8,128)(2,1)S(1)} collective-permute-done((bf16[1024,256]{1,0:T(8,128)(2,1)S(1)}, bf16[1024,256]{1,0:T(8,128)(2,1)S(1)}, u32[]{:S(2)}, u32[]{:S(2)}) %collective-permute-start.9) | collective-permute-done | bytes 524320 | tf_op jit(solution)/shard_map/ppermute | solution.py:30
  56.1 1.5 %collective-permute-start.10 = (bf16[1024,256]{1,0:T(8,128)(2,1)S(1)}, bf16[1024,256]{1,0:T(8,128)(2,1)S(1)}, u32[]{:S(2)}, u32[]{:S(2)}) collective-permute-start(bf16[1024,256]{1,0:T(8,128)(2,1)S(1)} %collective-permute-done.9.down_2), channel_id=1, source_target_pairs={{0,224},{32,0},{64,32},{96,64},{128,96},{160,128},{192,160},{224,1... | collective-permute-start | bytes 1572872 | tf_op jit(solution)/shard_map/ppermute | solution.py:30
  59.2 3.2 %collective-permute-done.14.refs_3_ = bf16[512,512]{1,0:T(8,128)(2,1)S(1)} collective-permute-done((bf16[512,512]{1,0:T(8,128)(2,1)S(1)}, bf16[512,512]{1,0:T(8,128)(2,1)S(1)}, u32[]{:S(2)}, u32[]{:S(2)}) %collective-permute-start.14) | collective-permute-done | bytes 524320 | tf_op jit(solution)/shard_map/ppermute | solution.py:30
  62.4 5.7 %collective-permute-start.15 = (bf16[512,512]{1,0:T(8,128)(2,1)S(1)}, bf16[512,512]{1,0:T(8,128)(2,1)S(1)}, u32[]{:S(2)}, u32[]{:S(2)}) collective-permute-start(bf16[512,512]{1,0:T(8,128)(2,1)S(1)} %constant_dynamic-update-slice_fusion.4.refs_0_), channel_id=1, source_target_pairs={{0,1},{1,0},{2,3},{3,2},{4,5},{5,4},{6,7},{7,6},{8,9},{9,8},{10,11... | collective-permute-start | bytes 1572872 | tf_op jit(solution)/shard_map/ppermute | solution.py:30
  68.1 4.9 %collective-permute-done.13.refs_2_ = bf16[512,512]{1,0:T(8,128)(2,1)S(1)} collective-permute-done((bf16[512,512]{1,0:T(8,128)(2,1)S(1)}, bf16[512,512]{1,0:T(8,128)(2,1)S(1)}, u32[]{:S(2)}, u32[]{:S(2)}) %collective-permute-start.13) | collective-permute-done | bytes 524320 | tf_op jit(solution)/shard_map/ppermute | solution.py:30
  73.0 2.0 %collective-permute-start.18 = (bf16[512,512]{1,0:T(8,128)(2,1)S(1)}, bf16[512,512]{1,0:T(8,128)(2,1)S(1)}, u32[]{:S(2)}, u32[]{:S(2)}) collective-permute-start(bf16[512,512]{1,0:T(8,128)(2,1)S(1)} %collective-permute-done.14.refs_3_), channel_id=1, source_target_pairs={{0,1},{1,0},{2,3},{3,2},{4,5},{5,4},{6,7},{7,6},{8,9},{9,8},{10,11... | collective-permute-start | bytes 1572872 | tf_op jit(solution)/shard_map/ppermute | solution.py:30
  74.9 1.2 %collective-permute-done.12.refs_1_ = bf16[512,512]{1,0:T(8,128)(2,1)S(1)} collective-permute-done((bf16[512,512]{1,0:T(8,128)(2,1)S(1)}, bf16[512,512]{1,0:T(8,128)(2,1)S(1)}, u32[]{:S(2)}, u32[]{:S(2)}) %collective-permute-start.12) | collective-permute-done | bytes 524320 | tf_op jit(solution)/shard_map/ppermute | solution.py:30
  76.7 2.5 %left.1.left_in = bf16[512,4096]{1,0:T(8,128)(2,1)S(1)} custom-call(s32[71]{0:T(128)S(1)} %concatenate.12.meta_ref, bf16[4,512,256]{2,1,0:T(8,128)(2,1)S(1)} %get-tuple-element.24.tables_ref, bf16[512,256]{1,0:T(8,128)(2,1)S(1)} %get-tuple-element.25.own, bf16[512,256]{1,0:T(8,128)(2,1)S(1)} %collective-permute-done.3.other, ...), custom_call_target="tpu_custom_call" | custom-call | tf_op jit(solution)/shard_map/left/pallas_call | solution.py:206
  79.2 1.6 %collective-permute-start.20 = (bf16[512,256]{1,0:T(8,128)(2,1)S(1)}, bf16[512,256]{1,0:T(8,128)(2,1)S(1)}, u32[]{:S(2)}, u32[]{:S(2)}) collective-permute-start(bf16[512,256]{1,0:T(8,128)(2,1)S(1)} %slice.7), channel_id=1, source_target_pairs={{0,224},{32,0},{64,32},{96,64},{128,96},{160,128},{192,160},{224,1... | collective-permute-start | bytes 786440 | tf_op jit(solution)/shard_map/ppermute | solution.py:30
  80.9 3.2 %right.1.right_ref = bf16[4096,512]{1,0:T(8,128)(2,1)S(1)} custom-call(s32[71]{0:T(128)S(1)} %concatenate.12.meta_ref, bf16[4,256,512]{2,1,0:T(8,128)(2,1)S(1)} %get-tuple-element.32.tables_ref, bf16[512,512]{1,0:T(8,128)(2,1)S(1)} %constant_dynamic-update-slice_fusion.4.refs_0_, bf16[512,512]{1,0:T(8,128)(2,1)S(1)} %collective-permute-done.12.refs_1_, ...), custom_call_target="tpu_custom_call" | custom-call | tf_op jit(solution)/shard_map/right/pallas_call | solution.py:206
  84.1 3.7 %most.1 = (f32[512,512]{1,0:T(8,128)S(1)}, bf16[512,4096]{1,0:T(8,128)(2,1)S(1)}) custom-call(s32[71]{0:T(128)S(1)} %concatenate.12.meta_ref, bf16[4,512,256]{2,1,0:T(8,128)(2,1)S(1)} %get-tuple-element.24.tables_ref, bf16[512,4096]{1,0:T(8,128)(2,1)S(1)} %left.1.left_in, bf16[4096,512]{1,0:T(8,128)(2,1)S(1)} %right.1.right_ref, ...), custom_call_target="tpu_custom_call", output_to_operand_aliasing={{1}: (2, {})} | custom-call | tf_op jit(solution)/shard_map/most/pallas_call | solution.py:220
  87.9 1.3 %collective-permute-done.19.far_own = bf16[512,256]{1,0:T(8,128)(2,1)S(1)} collective-permute-done((bf16[512,256]{1,0:T(8,128)(2,1)S(1)}, bf16[512,256]{1,0:T(8,128)(2,1)S(1)}, u32[]{:S(2)}, u32[]{:S(2)}) %collective-permute-start.19) | collective-permute-done | bytes 262176 | tf_op jit(solution)/shard_map/ppermute | solution.py:30
  89.2 2.6 %product.1 = f32[512,512]{1,0:T(8,128)} custom-call(s32[71]{0:T(128)S(1)} %concatenate.12.meta_ref, bf16[4,512,256]{2,1,0:T(8,128)(2,1)S(1)} %get-tuple-element.24.tables_ref, f32[512,512]{1,0:T(8,128)S(1)} %get-tuple-element.36.most_ref, bf16[4096,512]{1,0:T(8,128)(2,1)S(1)} %right.1.right_ref, bf16[1024,256]{1,0:T(8,128)(2,1)S(1)} %collective-permute-done.8.up_3, ...), custom_call_target="tpu_custom_call" | custom-call | tf_op jit(solution)/shard_map/product/pallas_call | solution.py:235
  (39 shorter events, 7.9 us)
Async XLA Ops:
  0.0 0.9 %copy-start = (bf16[256,512]{1,0:T(8,128)(2,1)S(1)}, bf16[256,512]{1,0:T(8,128)(2,1)}, u32[]{:S(2)}) copy-start(bf16[256,512]{1,0:T(8,128)(2,1)} %partials_ref.1) | copy-start | bytes 786436
  1.0 0.7 copy-start.1
  1.9 17.2 %collective-permute-start = (bf16[256,512]{1,0:T(8,128)(2,1)S(1)}, bf16[256,512]{1,0:T(8,128)(2,1)S(1)}, u32[]{:S(2)}, u32[]{:S(2)}) collective-permute-start(bf16[256,512]{1,0:T(8,128)(2,1)S(1)} %get-tuple-element.21), channel_id=1, source_target_pairs={{0,10},{1,26},{2,8},{3,24},{4,14},{5,30},{6,12},{7,28},{8,2},{9,18... | collective-permute-start | bytes 786440 | tf_op jit(solution)/shard_map/ppermute | solution.py:51
  10.4 9.9 %collective-permute-start.3 = (bf16[512,256]{1,0:T(8,128)(2,1)S(1)}, bf16[512,256]{1,0:T(8,128)(2,1)S(1)}, u32[]{:S(2)}, u32[]{:S(2)}) collective-permute-start(bf16[512,256]{1,0:T(8,128)(2,1)S(1)} %get-tuple-element.25.own), channel_id=1, source_target_pairs={{0,16},{16,0},{1,17},{17,1},{2,18},{18,2},{3,19},{19,3},{4,20},{20... | collective-permute-start | bytes 786440 | tf_op jit(solution)/shard_map/ppermute | solution.py:30
  10.5 18.7 %collective-permute-start.2 = (bf16[512,256]{1,0:T(8,128)(2,1)S(1)}, bf16[512,256]{1,0:T(8,128)(2,1)S(1)}, u32[]{:S(2)}, u32[]{:S(2)}) collective-permute-start(bf16[512,256]{1,0:T(8,128)(2,1)S(1)} %get-tuple-element.25.own), channel_id=1, source_target_pairs={{0,224},{32,0},{64,32},{96,64},{128,96},{160,128},{192,160},{224,1... | collective-permute-start | bytes 786440 | tf_op jit(solution)/shard_map/ppermute | solution.py:30
  15.9 13.3 %collective-permute-start.1 = (bf16[512,256]{1,0:T(8,128)(2,1)S(1)}, bf16[512,256]{1,0:T(8,128)(2,1)S(1)}, u32[]{:S(2)}, u32[]{:S(2)}) collective-permute-start(bf16[512,256]{1,0:T(8,128)(2,1)S(1)} %get-tuple-element.25.own), channel_id=1, source_target_pairs={{0,32},{32,64},{64,96},{96,128},{128,160},{160,192},{192,224},{224... | collective-permute-start | bytes 786440 | tf_op jit(solution)/shard_map/ppermute | solution.py:30
  20.3 9.2 %collective-permute-start.5 = (bf16[512,256]{1,0:T(8,128)(2,1)S(1)}, bf16[512,256]{1,0:T(8,128)(2,1)S(1)}, u32[]{:S(2)}, u32[]{:S(2)}) collective-permute-start(bf16[512,256]{1,0:T(8,128)(2,1)S(1)} %collective-permute-done.3.other), channel_id=1, source_target_pairs={{0,224},{32,0},{64,32},{96,64},{128,96},{160,128},{192,160},{224,1... | collective-permute-start | bytes 786440 | tf_op jit(solution)/shard_map/ppermute | solution.py:30
  24.6 8.0 %collective-permute-start.4 = (bf16[512,256]{1,0:T(8,128)(2,1)S(1)}, bf16[512,256]{1,0:T(8,128)(2,1)S(1)}, u32[]{:S(2)}, u32[]{:S(2)}) collective-permute-start(bf16[512,256]{1,0:T(8,128)(2,1)S(1)} %collective-permute-done.3.other), channel_id=1, source_target_pairs={{0,32},{32,64},{64,96},{96,128},{128,160},{160,192},{192,224},{224... | collective-permute-start | bytes 786440 | tf_op jit(solution)/shard_map/ppermute | solution.py:30
  24.6 10.8 %collective-permute-start.6 = (bf16[256,512]{1,0:T(8,128)(2,1)S(1)}, bf16[256,512]{1,0:T(8,128)(2,1)S(1)}, u32[]{:S(2)}, u32[]{:S(2)}) collective-permute-start(bf16[256,512]{1,0:T(8,128)(2,1)S(1)} %collective-permute-done), channel_id=1, source_target_pairs={{10,10},{8,40},{14,78},{12,108},{2,130},{0,160},{4,196},{6,230},{3... | collective-permute-start | bytes 786440 | tf_op jit(solution)/shard_map/ppermute | solution.py:60
  35.4 14.0 %collective-permute-start.11 = (bf16[256,512]{1,0:T(8,128)(2,1)S(1)}, bf16[256,512]{1,0:T(8,128)(2,1)S(1)}, u32[]{:S(2)}, u32[]{:S(2)}) collective-permute-start(bf16[256,512]{1,0:T(8,128)(2,1)S(1)} %collective-permute-done.6), channel_id=1, source_target_pairs={{0,2},{2,0},{1,3},{3,1},{4,6},{6,4},{5,7},{7,5},{8,10},{10,8},{9,1... | collective-permute-start | bytes 786440 | tf_op jit(solution)/shard_map/ppermute | solution.py:30
  44.4 11.7 %collective-permute-start.9 = (bf16[1024,256]{1,0:T(8,128)(2,1)S(1)}, bf16[1024,256]{1,0:T(8,128)(2,1)S(1)}, u32[]{:S(2)}, u32[]{:S(2)}) collective-permute-start(bf16[1024,256]{1,0:T(8,128)(2,1)S(1)} %constant_dynamic-update-slice_fusion.2.down_1), channel_id=1, source_target_pairs={{0,224},{32,0},{64,32},{96,64},{128,96},{160,128},{192,160},{224,1... | collective-permute-start | bytes 1572872 | tf_op jit(solution)/shard_map/ppermute | solution.py:30
  44.5 13.9 %collective-permute-start.7 = (bf16[1024,256]{1,0:T(8,128)(2,1)S(1)}, bf16[1024,256]{1,0:T(8,128)(2,1)S(1)}, u32[]{:S(2)}, u32[]{:S(2)}) collective-permute-start(bf16[1024,256]{1,0:T(8,128)(2,1)S(1)} %constant_dynamic-update-slice_fusion.up_1), channel_id=1, source_target_pairs={{0,32},{32,64},{64,96},{96,128},{128,160},{160,192},{192,224},{224... | collective-permute-start | bytes 1572872 | tf_op jit(solution)/shard_map/ppermute | solution.py:30
  49.5 12.9 %collective-permute-start.14 = (bf16[512,512]{1,0:T(8,128)(2,1)S(1)}, bf16[512,512]{1,0:T(8,128)(2,1)S(1)}, u32[]{:S(2)}, u32[]{:S(2)}) collective-permute-start(bf16[512,512]{1,0:T(8,128)(2,1)S(1)} %constant_dynamic-update-slice_fusion.4.refs_0_), channel_id=1, source_target_pairs={{0,8},{4,12},{8,0},{12,4},{1,9},{5,13},{9,1},{13,5},{2,10},{6,14},... | collective-permute-start | bytes 1572872 | tf_op jit(solution)/shard_map/ppermute | solution.py:30
  50.0 22.9 %collective-permute-start.13 = (bf16[512,512]{1,0:T(8,128)(2,1)S(1)}, bf16[512,512]{1,0:T(8,128)(2,1)S(1)}, u32[]{:S(2)}, u32[]{:S(2)}) collective-permute-start(bf16[512,512]{1,0:T(8,128)(2,1)S(1)} %constant_dynamic-update-slice_fusion.4.refs_0_), channel_id=1, source_target_pairs={{0,12},{4,0},{8,4},{12,8},{1,13},{5,1},{9,5},{13,9},{2,14},{6,2},{... | collective-permute-start | bytes 1572872 | tf_op jit(solution)/shard_map/ppermute | solution.py:30
  50.3 25.8 %collective-permute-start.12 = (bf16[512,512]{1,0:T(8,128)(2,1)S(1)}, bf16[512,512]{1,0:T(8,128)(2,1)S(1)}, u32[]{:S(2)}, u32[]{:S(2)}) collective-permute-start(bf16[512,512]{1,0:T(8,128)(2,1)S(1)} %constant_dynamic-update-slice_fusion.4.refs_0_), channel_id=1, source_target_pairs={{0,4},{4,8},{8,12},{12,0},{1,5},{5,9},{9,13},{13,1},{2,6},{6,10},{... | collective-permute-start | bytes 1572872 | tf_op jit(solution)/shard_map/ppermute | solution.py:30
  56.1 20.5 %collective-permute-start.10 = (bf16[1024,256]{1,0:T(8,128)(2,1)S(1)}, bf16[1024,256]{1,0:T(8,128)(2,1)S(1)}, u32[]{:S(2)}, u32[]{:S(2)}) collective-permute-start(bf16[1024,256]{1,0:T(8,128)(2,1)S(1)} %collective-permute-done.9.down_2), channel_id=1, source_target_pairs={{0,224},{32,0},{64,32},{96,64},{128,96},{160,128},{192,160},{224,1... | collective-permute-start | bytes 1572872 | tf_op jit(solution)/shard_map/ppermute | solution.py:30
  58.4 20.8 %collective-permute-start.8 = (bf16[1024,256]{1,0:T(8,128)(2,1)S(1)}, bf16[1024,256]{1,0:T(8,128)(2,1)S(1)}, u32[]{:S(2)}, u32[]{:S(2)}) collective-permute-start(bf16[1024,256]{1,0:T(8,128)(2,1)S(1)} %collective-permute-done.7.up_2), channel_id=1, source_target_pairs={{0,32},{32,64},{64,96},{96,128},{128,160},{160,192},{192,224},{224... | collective-permute-start | bytes 1572872 | tf_op jit(solution)/shard_map/ppermute | solution.py:30
  62.4 18.5 %collective-permute-start.15 = (bf16[512,512]{1,0:T(8,128)(2,1)S(1)}, bf16[512,512]{1,0:T(8,128)(2,1)S(1)}, u32[]{:S(2)}, u32[]{:S(2)}) collective-permute-start(bf16[512,512]{1,0:T(8,128)(2,1)S(1)} %constant_dynamic-update-slice_fusion.4.refs_0_), channel_id=1, source_target_pairs={{0,1},{1,0},{2,3},{3,2},{4,5},{5,4},{6,7},{7,6},{8,9},{9,8},{10,11... | collective-permute-start | bytes 1572872 | tf_op jit(solution)/shard_map/ppermute | solution.py:30
  73.0 7.9 %collective-permute-start.18 = (bf16[512,512]{1,0:T(8,128)(2,1)S(1)}, bf16[512,512]{1,0:T(8,128)(2,1)S(1)}, u32[]{:S(2)}, u32[]{:S(2)}) collective-permute-start(bf16[512,512]{1,0:T(8,128)(2,1)S(1)} %collective-permute-done.14.refs_3_), channel_id=1, source_target_pairs={{0,1},{1,0},{2,3},{3,2},{4,5},{5,4},{6,7},{7,6},{8,9},{9,8},{10,11... | collective-permute-start | bytes 1572872 | tf_op jit(solution)/shard_map/ppermute | solution.py:30
  76.1 4.8 %collective-permute-start.17 = (bf16[512,512]{1,0:T(8,128)(2,1)S(1)}, bf16[512,512]{1,0:T(8,128)(2,1)S(1)}, u32[]{:S(2)}, u32[]{:S(2)}) collective-permute-start(bf16[512,512]{1,0:T(8,128)(2,1)S(1)} %collective-permute-done.13.refs_2_), channel_id=1, source_target_pairs={{0,1},{1,0},{2,3},{3,2},{4,5},{5,4},{6,7},{7,6},{8,9},{9,8},{10,11... | collective-permute-start | bytes 1572872 | tf_op jit(solution)/shard_map/ppermute | solution.py:30
  76.6 4.3 %collective-permute-start.16 = (bf16[512,512]{1,0:T(8,128)(2,1)S(1)}, bf16[512,512]{1,0:T(8,128)(2,1)S(1)}, u32[]{:S(2)}, u32[]{:S(2)}) collective-permute-start(bf16[512,512]{1,0:T(8,128)(2,1)S(1)} %collective-permute-done.12.refs_1_), channel_id=1, source_target_pairs={{0,1},{1,0},{2,3},{3,2},{4,5},{5,4},{6,7},{7,6},{8,9},{9,8},{10,11... | collective-permute-start | bytes 1572872 | tf_op jit(solution)/shard_map/ppermute | solution.py:30
  79.2 8.6 %collective-permute-start.20 = (bf16[512,256]{1,0:T(8,128)(2,1)S(1)}, bf16[512,256]{1,0:T(8,128)(2,1)S(1)}, u32[]{:S(2)}, u32[]{:S(2)}) collective-permute-start(bf16[512,256]{1,0:T(8,128)(2,1)S(1)} %slice.7), channel_id=1, source_target_pairs={{0,224},{32,0},{64,32},{96,64},{128,96},{160,128},{192,160},{224,1... | collective-permute-start | bytes 786440 | tf_op jit(solution)/shard_map/ppermute | solution.py:30
  80.9 8.3 %collective-permute-start.19 = (bf16[512,256]{1,0:T(8,128)(2,1)S(1)}, bf16[512,256]{1,0:T(8,128)(2,1)S(1)}, u32[]{:S(2)}, u32[]{:S(2)}) collective-permute-start(bf16[512,256]{1,0:T(8,128)(2,1)S(1)} %slice.6), channel_id=1, source_target_pairs={{0,32},{32,64},{64,96},{96,128},{128,160},{160,192},{192,224},{224... | collective-permute-start | bytes 786440 | tf_op jit(solution)/shard_map/ppermute | solution.py:30

commit v10 on v9

--- a/solution.py
+++ b/solution.py
@@ -270,17 +270,21 @@
     here = in_plane(masked)
     other = around(own, "yl", NYL, 1)
     up_own, down_own = up(own), down(own)
-    here, tables = sync((here, make_tables(meta, taps, rows)))
-    up_own, down_own, up_other, down_other, here = sync((up_own, down_own, up(other), down(other), along_z(here)))
+    here, tables, up_own, down_own = sync((here, make_tables(meta, taps, rows), up_own, down_own))
+    here = along_z(here)
+    up_other, down_other = up(other), down(other)
     up_1 = jnp.concatenate([up_own, up_other], axis=0)
     down_1 = jnp.concatenate([down_own, down_other], axis=0)
     pair = jnp.concatenate([here, across(here)], axis=0)
+    up_1, down_1, pair = sync((up_1, down_1, pair))
     up_2, down_2 = up(up_1), down(down_1)
     left = whitened(left_kernel, "left", meta, tables[1], [own, other, up_1, down_1, up_2, down_2], (cols, NE * rows), (cols, 10 * rows))
     mine = [pair] + along_x(pair)
+    mine[3], left = sync((mine[3], left))
+    up_3, down_3 = up(up_2), down(down_2)
+    end_up, end_down = sync((up_3[:cols], down_3[cols:]))
     theirs = [swapped(piece) for piece in mine]
-    up_3, down_3, left = sync((up(up_2), down(down_2), left))
-    far_own, far_other = up(up_3[:cols]), down(down_3[cols:])
+    far_own, far_other = up(end_up), down(end_down)
     right = whitened(right_kernel, "right", meta, tables[0], mine + theirs, (NE * rows, cols), ((NE + 1) * rows, cols))
     most = most_of_product(meta, tables[1], left, right, [up_2, down_2, up_3, down_3], rows)
     return product(meta, tables[1], most, right, [up_3, down_3, far_own, far_other], rows, (rows * NE) ** (-0.5))

time: 92.4 us -> 90 us (0.974)
  the two profiles are of different devices: /device:TPU:1 before, /device:TPU:25 now
where the time goes in v10:
time: 90 us; the launch traced here: 89.8 us
  starting transfers between devices  36.6 us (41%)
  waiting for transfers between devices  35.8 us (40%)
  Pallas kernels  13.4 us (15%)
  local copies, waits for them, and re-layouts  3.07 us (3%)
    ppermute x19, starting transfers between devices, around(): return lax.ppermute(block, axis, [(i, (i + step) % n) for i in range(n)])  29.4 us
    ppermute x19, waiting for transfers between devices, around(): return lax.ppermute(block, axis, [(i, (i + step) % n) for i in range(n)])  15.5 us
    ppermute x1, waiting for transfers between devices, along_z(): return lax.ppermute(block, ('z', 'x', 'yh'), route)  15.3 us
    pallas_call x2, Pallas kernels, whitened(): pl.pallas_call(kernel, out_shape=jax.ShapeDtypeStruct(shape, BF16), in_sp...  5.7 us
    ppermute x1, starting transfers between devices, in_plane(): return lax.ppermute(block, axes, route)  5.31 us
    ppermute x1, waiting for transfers between devices, in_plane(): return lax.ppermute(block, axes, route)  4.97 us
    pallas_call x1, Pallas kernels, most_of_product(): pl.pallas_call(most_kernel, out_shape=[jax.ShapeDtypeStruct((cols, cols),...  3.74 us
    pallas_call x1, Pallas kernels, product(): pl.pallas_call(functools.partial(last_kernel, scale), out_shape=jax.Shape...  2.63 us
  transfers between devices with their start and end apart: 21, of which 6 were waited for; matrix products, arithmetic and copies ran while one was open for 2% of the time, Pallas kernels for 12%

profile of v10, /device:TPU:25, one launch (start us, length us, event | category | flops | bytes accessed | tf_op | source)
XLA Modules:
  0.0 89.8 jit_solution(5660014651190727410)
XLA Ops:
  0.0 0.9 %copy-done = bf16[256,512]{1,0:T(8,128)(2,1)S(1)} copy-done((bf16[256,512]{1,0:T(8,128)(2,1)S(1)}, bf16[256,512]{1,0:T(8,128)(2,1)}, u32[]{:S(2)}) %copy-start) | copy-done | bytes 262168
  1.9 1.7 %collective-permute-start.1 = (bf16[512,256]{1,0:T(8,128)(2,1)S(1)}, bf16[512,256]{1,0:T(8,128)(2,1)S(1)}, u32[]{:S(2)}, u32[]{:S(2)}) collective-permute-start(bf16[512,256]{1,0:T(8,128)(2,1)S(1)} %get-tuple-element.25.own), channel_id=1, source_target_pairs={{0,32},{32,64},{64,96},{96,128},{128,160},{160,192},{192,224},{224... | collective-permute-start | bytes 786440 | tf_op jit(solution)/shard_map/ppermute | solution.py:30
  3.6 4.0 %collective-permute-start.2 = (bf16[512,256]{1,0:T(8,128)(2,1)S(1)}, bf16[512,256]{1,0:T(8,128)(2,1)S(1)}, u32[]{:S(2)}, u32[]{:S(2)}) collective-permute-start(bf16[512,256]{1,0:T(8,128)(2,1)S(1)} %get-tuple-element.25.own), channel_id=1, source_target_pairs={{0,224},{32,0},{64,32},{96,64},{128,96},{160,128},{192,160},{224,1... | collective-permute-start | bytes 786440 | tf_op jit(solution)/shard_map/ppermute | solution.py:30
  7.7 5.3 %collective-permute-start = (bf16[256,512]{1,0:T(8,128)(2,1)S(1)}, bf16[256,512]{1,0:T(8,128)(2,1)S(1)}, u32[]{:S(2)}, u32[]{:S(2)}) collective-permute-start(bf16[256,512]{1,0:T(8,128)(2,1)S(1)} %get-tuple-element.22), channel_id=1, source_target_pairs={{0,10},{1,26},{2,8},{3,24},{4,14},{5,30},{6,12},{7,28},{8,2},{9,18... | collective-permute-start | bytes 786440 | tf_op jit(solution)/shard_map/ppermute | solution.py:51
  14.9 0.7 concatenate.12.meta_ref
  15.7 1.1 %tables.1 = (bf16[4,256,512]{2,1,0:T(8,128)(2,1)S(1)}, bf16[4,512,256]{2,1,0:T(8,128)(2,1)S(1)}) custom-call(s32[71]{0:T(128)S(1)} %concatenate.12.meta_ref, bf16[1,256]{1,0:T(2,128)(2,1)S(1)} %broadcast_in_dim.3.taps_ref), custom_call_target="tpu_custom_call" | custom-call | tf_op jit(solution)/shard_map/tables/pallas_call | solution.py:87
  16.8 5.0 %collective-permute-done = bf16[256,512]{1,0:T(8,128)(2,1)S(1)} collective-permute-done((bf16[256,512]{1,0:T(8,128)(2,1)S(1)}, bf16[256,512]{1,0:T(8,128)(2,1)S(1)}, u32[]{:S(2)}, u32[]{:S(2)}) %collective-permute-start) | collective-permute-done | bytes 262176 | tf_op jit(solution)/shard_map/ppermute | solution.py:51
  21.8 1.9 %collective-permute-start.6 = (bf16[256,512]{1,0:T(8,128)(2,1)S(1)}, bf16[256,512]{1,0:T(8,128)(2,1)S(1)}, u32[]{:S(2)}, u32[]{:S(2)}) collective-permute-start(bf16[256,512]{1,0:T(8,128)(2,1)S(1)} %collective-permute-done), channel_id=1, source_target_pairs={{10,10},{8,40},{14,78},{12,108},{2,130},{0,160},{4,196},{6,230},{3... | collective-permute-start | bytes 786440 | tf_op jit(solution)/shard_map/ppermute | solution.py:60
  23.8 1.5 %collective-permute-start.4 = (bf16[512,256]{1,0:T(8,128)(2,1)S(1)}, bf16[512,256]{1,0:T(8,128)(2,1)S(1)}, u32[]{:S(2)}, u32[]{:S(2)}) collective-permute-start(bf16[512,256]{1,0:T(8,128)(2,1)S(1)} %collective-permute-done.3.other), channel_id=1, source_target_pairs={{0,32},{32,64},{64,96},{96,128},{128,160},{160,192},{192,224},{224... | collective-permute-start | bytes 786440 | tf_op jit(solution)/shard_map/ppermute | solution.py:30
  25.2 15.3 %collective-permute-done.6 = bf16[256,512]{1,0:T(8,128)(2,1)S(1)} collective-permute-done((bf16[256,512]{1,0:T(8,128)(2,1)S(1)}, bf16[256,512]{1,0:T(8,128)(2,1)S(1)}, u32[]{:S(2)}, u32[]{:S(2)}) %collective-permute-start.6) | collective-permute-done | bytes 262176 | tf_op jit(solution)/shard_map/ppermute | solution.py:60
  40.6 3.0 %collective-permute-done.4 = bf16[512,256]{1,0:T(8,128)(2,1)S(1)} collective-permute-done((bf16[512,256]{1,0:T(8,128)(2,1)S(1)}, bf16[512,256]{1,0:T(8,128)(2,1)S(1)}, u32[]{:S(2)}, u32[]{:S(2)}) %collective-permute-start.4) | collective-permute-done | bytes 262176 | tf_op jit(solution)/shard_map/ppermute | solution.py:30
  43.7 3.6 %collective-permute-done.7 = bf16[256,512]{1,0:T(8,128)(2,1)S(1)} collective-permute-done((bf16[256,512]{1,0:T(8,128)(2,1)S(1)}, bf16[256,512]{1,0:T(8,128)(2,1)S(1)}, u32[]{:S(2)}, u32[]{:S(2)}) %collective-permute-start.7) | collective-permute-done | bytes 262176 | tf_op jit(solution)/shard_map/ppermute | solution.py:30
  47.4 2.7 %collective-permute-start.10 = (bf16[1024,256]{1,0:T(8,128)(2,1)S(1)}, bf16[1024,256]{1,0:T(8,128)(2,1)S(1)}, u32[]{:S(2)}, u32[]{:S(2)}) collective-permute-start(bf16[1024,256]{1,0:T(8,128)(2,1)S(1)} %pad_maximum_fusion.1.down_1), channel_id=1, source_target_pairs={{0,224},{32,0},{64,32},{96,64},{128,96},{160,128},{192,160},{224,1... | collective-permute-start | bytes 1572872 | tf_op jit(solution)/shard_map/ppermute | solution.py:30
  50.1 2.7 %collective-permute-start.12 = (bf16[512,512]{1,0:T(8,128)(2,1)S(1)}, bf16[512,512]{1,0:T(8,128)(2,1)S(1)}, u32[]{:S(2)}, u32[]{:S(2)}) collective-permute-start(bf16[512,512]{1,0:T(8,128)(2,1)S(1)} %pad_maximum_fusion.2.refs_0_), channel_id=1, source_target_pairs={{0,12},{4,0},{8,4},{12,8},{1,13},{5,1},{9,5},{13,9},{2,14},{6,2},{... | collective-permute-start | bytes 1572872 | tf_op jit(solution)/shard_map/ppermute | solution.py:30
  52.8 5.8 %collective-permute-done.9.up_2 = bf16[1024,256]{1,0:T(8,128)(2,1)S(1)} collective-permute-done((bf16[1024,256]{1,0:T(8,128)(2,1)S(1)}, bf16[1024,256]{1,0:T(8,128)(2,1)S(1)}, u32[]{:S(2)}, u32[]{:S(2)}) %collective-permute-start.9) | collective-permute-done | bytes 524320 | tf_op jit(solution)/shard_map/ppermute | solution.py:30
  58.5 2.7 %collective-permute-start.18 = (bf16[1024,256]{1,0:T(8,128)(2,1)S(1)}, bf16[1024,256]{1,0:T(8,128)(2,1)S(1)}, u32[]{:S(2)}, u32[]{:S(2)}) collective-permute-start(bf16[1024,256]{1,0:T(8,128)(2,1)S(1)} %collective-permute-done.10.down_2), channel_id=1, source_target_pairs={{0,224},{32,0},{64,32},{96,64},{128,96},{160,128},{192,160},{224,1... | collective-permute-start | bytes 1572872 | tf_op jit(solution)/shard_map/ppermute | solution.py:30
  61.2 9.3 %collective-permute-start.13 = (bf16[512,512]{1,0:T(8,128)(2,1)S(1)}, bf16[512,512]{1,0:T(8,128)(2,1)S(1)}, u32[]{:S(2)}, u32[]{:S(2)}) collective-permute-start(bf16[512,512]{1,0:T(8,128)(2,1)S(1)} %pad_maximum_fusion.2.refs_0_), channel_id=1, source_target_pairs={{0,1},{1,0},{2,3},{3,2},{4,5},{5,4},{6,7},{7,6},{8,9},{9,8},{10,11... | collective-permute-start | bytes 1572872 | tf_op jit(solution)/shard_map/ppermute | solution.py:30
  70.5 2.5 %left.1.left_in = bf16[512,4096]{1,0:T(8,128)(2,1)S(1)} custom-call(s32[71]{0:T(128)S(1)} %concatenate.12.meta_ref, bf16[4,512,256]{2,1,0:T(8,128)(2,1)S(1)} %get-tuple-element.26.tables_ref, bf16[512,256]{1,0:T(8,128)(2,1)S(1)} %get-tuple-element.25.own, bf16[512,256]{1,0:T(8,128)(2,1)S(1)} %collective-permute-done.3.other, ...), custom_call_target="tpu_custom_call" | custom-call | tf_op jit(solution)/shard_map/left/pallas_call | solution.py:206
  73.0 3.0 %collective-permute-done.11.refs_1_ = bf16[512,512]{1,0:T(8,128)(2,1)S(1)} collective-permute-done((bf16[512,512]{1,0:T(8,128)(2,1)S(1)}, bf16[512,512]{1,0:T(8,128)(2,1)S(1)}, u32[]{:S(2)}, u32[]{:S(2)}) %collective-permute-start.11) | collective-permute-done | bytes 524320 | tf_op jit(solution)/shard_map/ppermute | solution.py:30
  76.0 0.8 collective-permute-start.16
  77.5 2.7 %collective-permute-start.20 = (bf16[512,256]{1,0:T(8,128)(2,1)S(1)}, bf16[512,256]{1,0:T(8,128)(2,1)S(1)}, u32[]{:S(2)}, u32[]{:S(2)}) collective-permute-start(bf16[512,256]{1,0:T(8,128)(2,1)S(1)} %slice.9), channel_id=1, source_target_pairs={{0,224},{32,0},{64,32},{96,64},{128,96},{160,128},{192,160},{224,1... | collective-permute-start | bytes 786440 | tf_op jit(solution)/shard_map/ppermute | solution.py:30
  80.2 3.2 %right.1.right_ref = bf16[4096,512]{1,0:T(8,128)(2,1)S(1)} custom-call(s32[71]{0:T(128)S(1)} %concatenate.12.meta_ref, bf16[4,256,512]{2,1,0:T(8,128)(2,1)S(1)} %get-tuple-element.34.tables_ref, bf16[512,512]{1,0:T(8,128)(2,1)S(1)} %pad_maximum_fusion.2.refs_0_, bf16[512,512]{1,0:T(8,128)(2,1)S(1)} %collective-permute-done.11.refs_1_, ...), custom_call_target="tpu_custom_call" | custom-call | tf_op jit(solution)/shard_map/right/pallas_call | solution.py:206
  83.4 3.7 %most.1 = (f32[512,512]{1,0:T(8,128)S(1)}, bf16[512,4096]{1,0:T(8,128)(2,1)S(1)}) custom-call(s32[71]{0:T(128)S(1)} %concatenate.12.meta_ref, bf16[4,512,256]{2,1,0:T(8,128)(2,1)S(1)} %get-tuple-element.26.tables_ref, bf16[512,4096]{1,0:T(8,128)(2,1)S(1)} %left.1.left_in, bf16[4096,512]{1,0:T(8,128)(2,1)S(1)} %right.1.right_ref, ...), custom_call_target="tpu_custom_call", output_to_operand_aliasing={{1}: (2, {})} | custom-call | tf_op jit(solution)/shard_map/most/pallas_call | solution.py:220
  87.2 2.6 %product.1 = f32[512,512]{1,0:T(8,128)} custom-call(s32[71]{0:T(128)S(1)} %concatenate.12.meta_ref, bf16[4,512,256]{2,1,0:T(8,128)(2,1)S(1)} %get-tuple-element.26.tables_ref, f32[512,512]{1,0:T(8,128)S(1)} %get-tuple-element.36.most_ref, bf16[4096,512]{1,0:T(8,128)(2,1)S(1)} %right.1.right_ref, bf16[1024,256]{1,0:T(8,128)(2,1)S(1)} %collective-permute-done.17.up_3, ...), custom_call_target="tpu_custom_call" | custom-call | tf_op jit(solution)/shard_map/product/pallas_call | solution.py:235
  (36 shorter events, 3.2 us)
Async XLA Ops:
  0.0 0.9 %copy-start = (bf16[256,512]{1,0:T(8,128)(2,1)S(1)}, bf16[256,512]{1,0:T(8,128)(2,1)}, u32[]{:S(2)}) copy-start(bf16[256,512]{1,0:T(8,128)(2,1)} %partials_ref.1) | copy-start | bytes 786436
  1.0 0.7 copy-start.1
  1.9 14.8 %collective-permute-start.1 = (bf16[512,256]{1,0:T(8,128)(2,1)S(1)}, bf16[512,256]{1,0:T(8,128)(2,1)S(1)}, u32[]{:S(2)}, u32[]{:S(2)}) collective-permute-start(bf16[512,256]{1,0:T(8,128)(2,1)S(1)} %get-tuple-element.25.own), channel_id=1, source_target_pairs={{0,32},{32,64},{64,96},{96,128},{128,160},{160,192},{192,224},{224... | collective-permute-start | bytes 786440 | tf_op jit(solution)/shard_map/ppermute | solution.py:30
  3.6 13.1 %collective-permute-start.2 = (bf16[512,256]{1,0:T(8,128)(2,1)S(1)}, bf16[512,256]{1,0:T(8,128)(2,1)S(1)}, u32[]{:S(2)}, u32[]{:S(2)}) collective-permute-start(bf16[512,256]{1,0:T(8,128)(2,1)S(1)} %get-tuple-element.25.own), channel_id=1, source_target_pairs={{0,224},{32,0},{64,32},{96,64},{128,96},{160,128},{192,160},{224,1... | collective-permute-start | bytes 786440 | tf_op jit(solution)/shard_map/ppermute | solution.py:30
  7.7 14.1 %collective-permute-start = (bf16[256,512]{1,0:T(8,128)(2,1)S(1)}, bf16[256,512]{1,0:T(8,128)(2,1)S(1)}, u32[]{:S(2)}, u32[]{:S(2)}) collective-permute-start(bf16[256,512]{1,0:T(8,128)(2,1)S(1)} %get-tuple-element.22), channel_id=1, source_target_pairs={{0,10},{1,26},{2,8},{3,24},{4,14},{5,30},{6,12},{7,28},{8,2},{9,18... | collective-permute-start | bytes 786440 | tf_op jit(solution)/shard_map/ppermute | solution.py:51
  13.0 10.7 %collective-permute-start.3 = (bf16[512,256]{1,0:T(8,128)(2,1)S(1)}, bf16[512,256]{1,0:T(8,128)(2,1)S(1)}, u32[]{:S(2)}, u32[]{:S(2)}) collective-permute-start(bf16[512,256]{1,0:T(8,128)(2,1)S(1)} %get-tuple-element.25.own), channel_id=1, source_target_pairs={{0,16},{16,0},{1,17},{17,1},{2,18},{18,2},{3,19},{19,3},{4,20},{20... | collective-permute-start | bytes 786440 | tf_op jit(solution)/shard_map/ppermute | solution.py:30
  21.8 18.8 %collective-permute-start.6 = (bf16[256,512]{1,0:T(8,128)(2,1)S(1)}, bf16[256,512]{1,0:T(8,128)(2,1)S(1)}, u32[]{:S(2)}, u32[]{:S(2)}) collective-permute-start(bf16[256,512]{1,0:T(8,128)(2,1)S(1)} %collective-permute-done), channel_id=1, source_target_pairs={{10,10},{8,40},{14,78},{12,108},{2,130},{0,160},{4,196},{6,230},{3... | collective-permute-start | bytes 786440 | tf_op jit(solution)/shard_map/ppermute | solution.py:60
  23.7 16.9 %collective-permute-start.5 = (bf16[512,256]{1,0:T(8,128)(2,1)S(1)}, bf16[512,256]{1,0:T(8,128)(2,1)S(1)}, u32[]{:S(2)}, u32[]{:S(2)}) collective-permute-start(bf16[512,256]{1,0:T(8,128)(2,1)S(1)} %collective-permute-done.3.other), channel_id=1, source_target_pairs={{0,224},{32,0},{64,32},{96,64},{128,96},{160,128},{192,160},{224,1... | collective-permute-start | bytes 786440 | tf_op jit(solution)/shard_map/ppermute | solution.py:30
  23.8 19.9 %collective-permute-start.4 = (bf16[512,256]{1,0:T(8,128)(2,1)S(1)}, bf16[512,256]{1,0:T(8,128)(2,1)S(1)}, u32[]{:S(2)}, u32[]{:S(2)}) collective-permute-start(bf16[512,256]{1,0:T(8,128)(2,1)S(1)} %collective-permute-done.3.other), channel_id=1, source_target_pairs={{0,32},{32,64},{64,96},{96,128},{128,160},{160,192},{192,224},{224... | collective-permute-start | bytes 786440 | tf_op jit(solution)/shard_map/ppermute | solution.py:30
  40.6 6.7 %collective-permute-start.7 = (bf16[256,512]{1,0:T(8,128)(2,1)S(1)}, bf16[256,512]{1,0:T(8,128)(2,1)S(1)}, u32[]{:S(2)}, u32[]{:S(2)}) collective-permute-start(bf16[256,512]{1,0:T(8,128)(2,1)S(1)} %collective-permute-done.6), channel_id=1, source_target_pairs={{0,2},{2,0},{1,3},{3,1},{4,6},{6,4},{5,7},{7,5},{8,10},{10,8},{9,1... | collective-permute-start | bytes 786440 | tf_op jit(solution)/shard_map/ppermute | solution.py:30
  47.3 11.2 %collective-permute-start.9 = (bf16[1024,256]{1,0:T(8,128)(2,1)S(1)}, bf16[1024,256]{1,0:T(8,128)(2,1)S(1)}, u32[]{:S(2)}, u32[]{:S(2)}) collective-permute-start(bf16[1024,256]{1,0:T(8,128)(2,1)S(1)} %pad_maximum_fusion.up_1), channel_id=1, source_target_pairs={{0,32},{32,64},{64,96},{96,128},{128,160},{160,192},{192,224},{224... | collective-permute-start | bytes 1572872 | tf_op jit(solution)/shard_map/ppermute | solution.py:30
  47.4 11.1 %collective-permute-start.10 = (bf16[1024,256]{1,0:T(8,128)(2,1)S(1)}, bf16[1024,256]{1,0:T(8,128)(2,1)S(1)}, u32[]{:S(2)}, u32[]{:S(2)}) collective-permute-start(bf16[1024,256]{1,0:T(8,128)(2,1)S(1)} %pad_maximum_fusion.1.down_1), channel_id=1, source_target_pairs={{0,224},{32,0},{64,32},{96,64},{128,96},{160,128},{192,160},{224,1... | collective-permute-start | bytes 1572872 | tf_op jit(solution)/shard_map/ppermute | solution.py:30
  50.1 11.1 %collective-permute-start.8 = (bf16[512,512]{1,0:T(8,128)(2,1)S(1)}, bf16[512,512]{1,0:T(8,128)(2,1)S(1)}, u32[]{:S(2)}, u32[]{:S(2)}) collective-permute-start(bf16[512,512]{1,0:T(8,128)(2,1)S(1)} %pad_maximum_fusion.2.refs_0_), channel_id=1, source_target_pairs={{0,8},{4,12},{8,0},{12,4},{1,9},{5,13},{9,1},{13,5},{2,10},{6,14},... | collective-permute-start | bytes 1572872 | tf_op jit(solution)/shard_map/ppermute | solution.py:30
  50.1 25.9 %collective-permute-start.11 = (bf16[512,512]{1,0:T(8,128)(2,1)S(1)}, bf16[512,512]{1,0:T(8,128)(2,1)S(1)}, u32[]{:S(2)}, u32[]{:S(2)}) collective-permute-start(bf16[512,512]{1,0:T(8,128)(2,1)S(1)} %pad_maximum_fusion.2.refs_0_), channel_id=1, source_target_pairs={{0,4},{4,8},{8,12},{12,0},{1,5},{5,9},{9,13},{13,1},{2,6},{6,10},{... | collective-permute-start | bytes 1572872 | tf_op jit(solution)/shard_map/ppermute | solution.py:30
  50.1 26.8 %collective-permute-start.12 = (bf16[512,512]{1,0:T(8,128)(2,1)S(1)}, bf16[512,512]{1,0:T(8,128)(2,1)S(1)}, u32[]{:S(2)}, u32[]{:S(2)}) collective-permute-start(bf16[512,512]{1,0:T(8,128)(2,1)S(1)} %pad_maximum_fusion.2.refs_0_), channel_id=1, source_target_pairs={{0,12},{4,0},{8,4},{12,8},{1,13},{5,1},{9,5},{13,9},{2,14},{6,2},{... | collective-permute-start | bytes 1572872 | tf_op jit(solution)/shard_map/ppermute | solution.py:30
  58.5 18.3 %collective-permute-start.17 = (bf16[1024,256]{1,0:T(8,128)(2,1)S(1)}, bf16[1024,256]{1,0:T(8,128)(2,1)S(1)}, u32[]{:S(2)}, u32[]{:S(2)}) collective-permute-start(bf16[1024,256]{1,0:T(8,128)(2,1)S(1)} %collective-permute-done.9.up_2), channel_id=1, source_target_pairs={{0,32},{32,64},{64,96},{96,128},{128,160},{160,192},{192,224},{224... | collective-permute-start | bytes 1572872 | tf_op jit(solution)/shard_map/ppermute | solution.py:30
  58.5 18.9 %collective-permute-start.18 = (bf16[1024,256]{1,0:T(8,128)(2,1)S(1)}, bf16[1024,256]{1,0:T(8,128)(2,1)S(1)}, u32[]{:S(2)}, u32[]{:S(2)}) collective-permute-start(bf16[1024,256]{1,0:T(8,128)(2,1)S(1)} %collective-permute-done.10.down_2), channel_id=1, source_target_pairs={{0,224},{32,0},{64,32},{96,64},{128,96},{160,128},{192,160},{224,1... | collective-permute-start | bytes 1572872 | tf_op jit(solution)/shard_map/ppermute | solution.py:30
  61.2 16.3 %collective-permute-start.13 = (bf16[512,512]{1,0:T(8,128)(2,1)S(1)}, bf16[512,512]{1,0:T(8,128)(2,1)S(1)}, u32[]{:S(2)}, u32[]{:S(2)}) collective-permute-start(bf16[512,512]{1,0:T(8,128)(2,1)S(1)} %pad_maximum_fusion.2.refs_0_), channel_id=1, source_target_pairs={{0,1},{1,0},{2,3},{3,2},{4,5},{5,4},{6,7},{7,6},{8,9},{9,8},{10,11... | collective-permute-start | bytes 1572872 | tf_op jit(solution)/shard_map/ppermute | solution.py:30
  76.0 4.2 %collective-permute-start.16 = (bf16[512,512]{1,0:T(8,128)(2,1)S(1)}, bf16[512,512]{1,0:T(8,128)(2,1)S(1)}, u32[]{:S(2)}, u32[]{:S(2)}) collective-permute-start(bf16[512,512]{1,0:T(8,128)(2,1)S(1)} %collective-permute-done.8.refs_3_), channel_id=1, source_target_pairs={{0,1},{1,0},{2,3},{3,2},{4,5},{5,4},{6,7},{7,6},{8,9},{9,8},{10,11... | collective-permute-start | bytes 1572872 | tf_op jit(solution)/shard_map/ppermute | solution.py:30
  76.9 3.4 %collective-permute-start.14 = (bf16[512,512]{1,0:T(8,128)(2,1)S(1)}, bf16[512,512]{1,0:T(8,128)(2,1)S(1)}, u32[]{:S(2)}, u32[]{:S(2)}) collective-permute-start(bf16[512,512]{1,0:T(8,128)(2,1)S(1)} %collective-permute-done.11.refs_1_), channel_id=1, source_target_pairs={{0,1},{1,0},{2,3},{3,2},{4,5},{5,4},{6,7},{7,6},{8,9},{9,8},{10,11... | collective-permute-start | bytes 1572872 | tf_op jit(solution)/shard_map/ppermute | solution.py:30
  76.9 3.3 %collective-permute-start.15 = (bf16[512,512]{1,0:T(8,128)(2,1)S(1)}, bf16[512,512]{1,0:T(8,128)(2,1)S(1)}, u32[]{:S(2)}, u32[]{:S(2)}) collective-permute-start(bf16[512,512]{1,0:T(8,128)(2,1)S(1)} %collective-permute-done.12.refs_2_), channel_id=1, source_target_pairs={{0,1},{1,0},{2,3},{3,2},{4,5},{5,4},{6,7},{7,6},{8,9},{9,8},{10,11... | collective-permute-start | bytes 1572872 | tf_op jit(solution)/shard_map/ppermute | solution.py:30
  77.4 9.7 %collective-permute-start.19 = (bf16[512,256]{1,0:T(8,128)(2,1)S(1)}, bf16[512,256]{1,0:T(8,128)(2,1)S(1)}, u32[]{:S(2)}, u32[]{:S(2)}) collective-permute-start(bf16[512,256]{1,0:T(8,128)(2,1)S(1)} %slice.8), channel_id=1, source_target_pairs={{0,32},{32,64},{64,96},{96,128},{128,160},{160,192},{192,224},{224... | collective-permute-start | bytes 786440 | tf_op jit(solution)/shard_map/ppermute | solution.py:30
  77.5 9.6 %collective-permute-start.20 = (bf16[512,256]{1,0:T(8,128)(2,1)S(1)}, bf16[512,256]{1,0:T(8,128)(2,1)S(1)}, u32[]{:S(2)}, u32[]{:S(2)}) collective-permute-start(bf16[512,256]{1,0:T(8,128)(2,1)S(1)} %slice.9), channel_id=1, source_target_pairs={{0,224},{32,0},{64,32},{96,64},{128,96},{160,128},{192,160},{224,1... | collective-permute-start | bytes 786440 | tf_op jit(solution)/shard_map/ppermute | solution.py:30

commit v11 on v10

--- a/solution.py
+++ b/solution.py
@@ -146,12 +146,9 @@
     for dz, piece in ((-2, up_2), (-1, up_1), (1, down_1), (2, down_2)):
         raw[:, at_block(4 + 2 * dz + yl, rows)] = piece[:cols]
         raw[:, at_block(5 + 2 * dz - yl, rows)] = piece[cols:]
-    for i in range(NE):
+    for i in range(1, 10):
         e = (2 * z + i - 4) & (NE - 1)
-        if 1 <= i < 10:
-            out_ref[:, at_block(e, rows)] = filter_left(raw, i, e, meta_ref, tables_ref)
-        else:
-            out_ref[:, at_block(e, rows)] = jnp.zeros((cols, rows), BF16)
+        out_ref[:, (i + 1) * rows : (i + 2) * rows] = filter_left(raw, i, e, meta_ref, tables_ref)
 
 
 def right_kernel(meta_ref, tables_ref, *refs):
@@ -169,7 +166,7 @@
     for e in range(NE):
         table = tables_ref[table_of(e, meta_ref)]
         white = jnp.dot(table, raw[e * rows : (e + 2) * rows], preferred_element_type=F32)
-        out_ref[e * rows : (e + 1) * rows] = white.astype(BF16)
+        out_ref[at_block((e - 2 * z + 5) & (NE - 1), rows)] = white.astype(BF16)
 
 
 def most_kernel(meta_ref, tables_ref, left_in, right_ref, up_2, down_2, up_3, down_3, out_ref, left_ref, raw):
@@ -183,11 +180,13 @@
         raw[:, at_block(at + 1 - yl, rows)] = piece[cols:]
     for i, shift in ((1, 5), (2, 5), (4, -9), (5, -9)):
         e = (2 * z + i + shift) & (NE - 1)
-        left_ref[:, at_block(e, rows)] = filter_left(raw, i, e, meta_ref, tables_ref)
-    out_ref[...] = jnp.dot(left_ref[...], right_ref[...], preferred_element_type=F32)
-
-
-def last_kernel(scale, meta_ref, tables_ref, most_ref, right_ref, up_3, down_3, far_own, far_other, out_ref, raw, left, right):
+        at = (i + shift + 5) % NE * rows
+        left_ref[:, at : at + rows] = filter_left(raw, i, e, meta_ref, tables_ref)
+    depth = (NE - 3) * rows
+    out_ref[...] = jnp.dot(left_ref[:, :depth], right_ref[:depth], preferred_element_type=F32)
+
+
+def last_kernel(scale, meta_ref, tables_ref, most_ref, right_ref, up_3, down_3, far_own, far_other, out_ref, raw, left):
     cols, rows = far_own.shape
     z, yl = meta_ref[0], meta_ref[1]
     raw[:, :rows] = down_3[at_block(1 ^ yl, cols)]
@@ -197,8 +196,8 @@
     for i in range(1, 4):
         e = (2 * z + i + 7) & (NE - 1)
         left[:, (i - 1) * rows : i * rows] = filter_left(raw, i, e, meta_ref, tables_ref)
-        right[(i - 1) * rows : i * rows] = right_ref[at_block(e, rows)]
-    out_ref[...] = (most_ref[...] + jnp.dot(left[...], right[...], preferred_element_type=F32)) * scale
+    right = right_ref[(NE - 3) * rows :]
+    out_ref[...] = (most_ref[...] + jnp.dot(left[...], right, preferred_element_type=F32)) * scale
 
 
 def whitened(kernel, name, meta, tables, pieces, shape, raw_shape):
@@ -237,7 +236,7 @@
         out_shape=jax.ShapeDtypeStruct((cols, cols), F32),
         in_specs=[pl.BlockSpec(memory_space=pltpu.SMEM)] + [vmem] * (3 + len(pieces)),
         out_specs=vmem,
-        scratch_shapes=[pltpu.VMEM((cols, 4 * rows), BF16), pltpu.VMEM((cols, 3 * rows), BF16), pltpu.VMEM((3 * rows, cols), BF16)],
+        scratch_shapes=[pltpu.VMEM((cols, 4 * rows), BF16), pltpu.VMEM((cols, 3 * rows), BF16)],
         compiler_params=pltpu.CompilerParams(vmem_limit_bytes=16 * 1024 * 1024),
         name="product",
     )(meta, tables, most, right, *pieces)
@@ -269,12 +268,10 @@
     sync = lax.optimization_barrier
     here = in_plane(masked)
     other = around(own, "yl", NYL, 1)
-    up_own, down_own = up(own), down(own)
-    here, tables, up_own, down_own = sync((here, make_tables(meta, taps, rows), up_own, down_own))
+    here, tables = sync((here, make_tables(meta, taps, rows)))
     here = along_z(here)
-    up_other, down_other = up(other), down(other)
-    up_1 = jnp.concatenate([up_own, up_other], axis=0)
-    down_1 = jnp.concatenate([down_own, down_other], axis=0)
+    both = jnp.concatenate([own, other], axis=0)
+    up_1, down_1 = up(both), down(both)
     pair = jnp.concatenate([here, across(here)], axis=0)
     up_1, down_1, pair = sync((up_1, down_1, pair))
     up_2, down_2 = up(up_1), down(down_1)

time: 90 us -> 89.2 us (level)
  the two profiles are of different devices: /device:TPU:25 before, /device:TPU:18 now
where the time goes in v11:
time: 89.2 us; the launch traced here: 89 us
  starting transfers between devices  40.3 us (45%)
  waiting for transfers between devices  32.3 us (36%)
  Pallas kernels  12.4 us (14%)
  local copies, waits for them, and re-layouts  3.11 us (3%)
    ppermute x17, starting transfers between devices, around(): return lax.ppermute(block, axis, [(i, (i + step) % n) for i in range(n)])  30.2 us
    ppermute x17, waiting for transfers between devices, around(): return lax.ppermute(block, axis, [(i, (i + step) % n) for i in range(n)])  25.2 us
    ppermute x1, starting transfers between devices, along_z(): return lax.ppermute(block, ('z', 'x', 'yh'), route)  6.25 us
    pallas_call x2, Pallas kernels, whitened(): pl.pallas_call(kernel, out_shape=jax.ShapeDtypeStruct(shape, BF16), in_sp...  5.3 us
    ppermute x1, waiting for transfers between devices, in_plane(): return lax.ppermute(block, axes, route)  4.75 us
    ppermute x1, starting transfers between devices, in_plane(): return lax.ppermute(block, axes, route)  3.81 us
    pallas_call x1, Pallas kernels, most_of_product(): pl.pallas_call(most_kernel, out_shape=[jax.ShapeDtypeStruct((cols, cols),...  3.12 us
    pallas_call x1, Pallas kernels, product(): pl.pallas_call(functools.partial(last_kernel, scale), out_shape=jax.Shape...  2.63 us
  transfers between devices with their start and end apart: 19, of which 8 were waited for; matrix products, arithmetic and copies ran while one was open for 2% of the time, Pallas kernels for 11%

profile of v11, /device:TPU:18, one launch (start us, length us, event | category | flops | bytes accessed | tf_op | source)
XLA Modules:
  0.0 89.0 jit_solution(14023133468252839467)
XLA Ops:
  0.0 0.9 %copy-done = bf16[256,512]{1,0:T(8,128)(2,1)S(1)} copy-done((bf16[256,512]{1,0:T(8,128)(2,1)S(1)}, bf16[256,512]{1,0:T(8,128)(2,1)}, u32[]{:S(2)}) %copy-start) | copy-done | bytes 262168
  1.9 3.8 %collective-permute-start = (bf16[256,512]{1,0:T(8,128)(2,1)S(1)}, bf16[256,512]{1,0:T(8,128)(2,1)S(1)}, u32[]{:S(2)}, u32[]{:S(2)}) collective-permute-start(bf16[256,512]{1,0:T(8,128)(2,1)S(1)} %get-tuple-element.20), channel_id=1, source_target_pairs={{0,10},{1,26},{2,8},{3,24},{4,14},{5,30},{6,12},{7,28},{8,2},{9,18... | collective-permute-start | bytes 786440 | tf_op jit(solution)/shard_map/ppermute | solution.py:51
  7.8 0.7 concatenate.9.meta_ref
  8.5 1.1 %tables.1 = (bf16[4,256,512]{2,1,0:T(8,128)(2,1)S(1)}, bf16[4,512,256]{2,1,0:T(8,128)(2,1)S(1)}) custom-call(s32[71]{0:T(128)S(1)} %concatenate.9.meta_ref, bf16[1,256]{1,0:T(2,128)(2,1)S(1)} %broadcast_in_dim.3.taps_ref), custom_call_target="tpu_custom_call" | custom-call | tf_op jit(solution)/shard_map/tables/pallas_call | solution.py:87
  9.6 4.7 %collective-permute-done = bf16[256,512]{1,0:T(8,128)(2,1)S(1)} collective-permute-done((bf16[256,512]{1,0:T(8,128)(2,1)S(1)}, bf16[256,512]{1,0:T(8,128)(2,1)S(1)}, u32[]{:S(2)}, u32[]{:S(2)}) %collective-permute-start) | collective-permute-done | bytes 262176 | tf_op jit(solution)/shard_map/ppermute | solution.py:51
  14.3 6.2 %collective-permute-start.4 = (bf16[256,512]{1,0:T(8,128)(2,1)S(1)}, bf16[256,512]{1,0:T(8,128)(2,1)S(1)}, u32[]{:S(2)}, u32[]{:S(2)}) collective-permute-start(bf16[256,512]{1,0:T(8,128)(2,1)S(1)} %collective-permute-done), channel_id=1, source_target_pairs={{10,10},{8,40},{14,78},{12,108},{2,130},{0,160},{4,196},{6,230},{3... | collective-permute-start | bytes 786440 | tf_op jit(solution)/shard_map/ppermute | solution.py:60
  20.8 4.1 %collective-permute-start.3 = (bf16[1024,256]{1,0:T(8,128)(2,1)S(1)}, bf16[1024,256]{1,0:T(8,128)(2,1)S(1)}, u32[]{:S(2)}, u32[]{:S(2)}) collective-permute-start(bf16[1024,256]{1,0:T(8,128)(2,1)S(1)} %constant_dynamic-update-slice_fusion), channel_id=1, source_target_pairs={{0,224},{32,0},{64,32},{96,64},{128,96},{160,128},{192,160},{224,1... | collective-permute-start | bytes 1572872 | tf_op jit(solution)/shard_map/ppermute | solution.py:30
  24.9 2.4 %collective-permute-done.4 = bf16[256,512]{1,0:T(8,128)(2,1)S(1)} collective-permute-done((bf16[256,512]{1,0:T(8,128)(2,1)S(1)}, bf16[256,512]{1,0:T(8,128)(2,1)S(1)}, u32[]{:S(2)}, u32[]{:S(2)}) %collective-permute-start.4) | collective-permute-done | bytes 262176 | tf_op jit(solution)/shard_map/ppermute | solution.py:60
  27.3 3.3 %collective-permute-start.5 = (bf16[256,512]{1,0:T(8,128)(2,1)S(1)}, bf16[256,512]{1,0:T(8,128)(2,1)S(1)}, u32[]{:S(2)}, u32[]{:S(2)}) collective-permute-start(bf16[256,512]{1,0:T(8,128)(2,1)S(1)} %collective-permute-done.4), channel_id=1, source_target_pairs={{0,2},{2,0},{1,3},{3,1},{4,6},{6,4},{5,7},{7,5},{8,10},{10,8},{9,1... | collective-permute-start | bytes 786440 | tf_op jit(solution)/shard_map/ppermute | solution.py:30
  30.5 4.8 %collective-permute-done.5 = bf16[256,512]{1,0:T(8,128)(2,1)S(1)} collective-permute-done((bf16[256,512]{1,0:T(8,128)(2,1)S(1)}, bf16[256,512]{1,0:T(8,128)(2,1)S(1)}, u32[]{:S(2)}, u32[]{:S(2)}) %collective-permute-start.5) | collective-permute-done | bytes 262176 | tf_op jit(solution)/shard_map/ppermute | solution.py:30
  35.4 3.4 %collective-permute-done.2.up_1 = bf16[1024,256]{1,0:T(8,128)(2,1)S(1)} collective-permute-done((bf16[1024,256]{1,0:T(8,128)(2,1)S(1)}, bf16[1024,256]{1,0:T(8,128)(2,1)S(1)}, u32[]{:S(2)}, u32[]{:S(2)}) %collective-permute-start.2) | collective-permute-done | bytes 524320 | tf_op jit(solution)/shard_map/ppermute | solution.py:30
  38.8 1.4 %collective-permute-start.7 = (bf16[1024,256]{1,0:T(8,128)(2,1)S(1)}, bf16[1024,256]{1,0:T(8,128)(2,1)S(1)}, u32[]{:S(2)}, u32[]{:S(2)}) collective-permute-start(bf16[1024,256]{1,0:T(8,128)(2,1)S(1)} %collective-permute-done.2.up_1), channel_id=1, source_target_pairs={{0,32},{32,64},{64,96},{96,128},{128,160},{160,192},{192,224},{224... | collective-permute-start | bytes 1572872 | tf_op jit(solution)/shard_map/ppermute | solution.py:30
  40.2 1.8 %collective-permute-start.8 = (bf16[1024,256]{1,0:T(8,128)(2,1)S(1)}, bf16[1024,256]{1,0:T(8,128)(2,1)S(1)}, u32[]{:S(2)}, u32[]{:S(2)}) collective-permute-start(bf16[1024,256]{1,0:T(8,128)(2,1)S(1)} %collective-permute-done.3.down_1), channel_id=1, source_target_pairs={{0,224},{32,0},{64,32},{96,64},{128,96},{160,128},{192,160},{224,1... | collective-permute-start | bytes 1572872 | tf_op jit(solution)/shard_map/ppermute | solution.py:30
  42.1 3.7 %collective-permute-start.6 = (bf16[512,512]{1,0:T(8,128)(2,1)S(1)}, bf16[512,512]{1,0:T(8,128)(2,1)S(1)}, u32[]{:S(2)}, u32[]{:S(2)}) collective-permute-start(bf16[512,512]{1,0:T(8,128)(2,1)S(1)} %pad_maximum_fusion.refs_0_), channel_id=1, source_target_pairs={{0,8},{4,12},{8,0},{12,4},{1,9},{5,13},{9,1},{13,5},{2,10},{6,14},... | collective-permute-start | bytes 1572872 | tf_op jit(solution)/shard_map/ppermute | solution.py:30
  45.8 5.7 %collective-permute-start.9 = (bf16[512,512]{1,0:T(8,128)(2,1)S(1)}, bf16[512,512]{1,0:T(8,128)(2,1)S(1)}, u32[]{:S(2)}, u32[]{:S(2)}) collective-permute-start(bf16[512,512]{1,0:T(8,128)(2,1)S(1)} %pad_maximum_fusion.refs_0_), channel_id=1, source_target_pairs={{0,4},{4,8},{8,12},{12,0},{1,5},{5,9},{9,13},{13,1},{2,6},{6,10},{... | collective-permute-start | bytes 1572872 | tf_op jit(solution)/shard_map/ppermute | solution.py:30
  51.5 2.1 %collective-permute-start.10 = (bf16[512,512]{1,0:T(8,128)(2,1)S(1)}, bf16[512,512]{1,0:T(8,128)(2,1)S(1)}, u32[]{:S(2)}, u32[]{:S(2)}) collective-permute-start(bf16[512,512]{1,0:T(8,128)(2,1)S(1)} %pad_maximum_fusion.refs_0_), channel_id=1, source_target_pairs={{0,12},{4,0},{8,4},{12,8},{1,13},{5,1},{9,5},{13,9},{2,14},{6,2},{... | collective-permute-start | bytes 1572872 | tf_op jit(solution)/shard_map/ppermute | solution.py:30
  54.1 3.1 %collective-permute-start.16 = (bf16[1024,256]{1,0:T(8,128)(2,1)S(1)}, bf16[1024,256]{1,0:T(8,128)(2,1)S(1)}, u32[]{:S(2)}, u32[]{:S(2)}) collective-permute-start(bf16[1024,256]{1,0:T(8,128)(2,1)S(1)} %collective-permute-done.8.down_2), channel_id=1, source_target_pairs={{0,224},{32,0},{64,32},{96,64},{128,96},{160,128},{192,160},{224,1... | collective-permute-start | bytes 1572872 | tf_op jit(solution)/shard_map/ppermute | solution.py:30
  57.2 1.5 %collective-permute-done.6.refs_3_ = bf16[512,512]{1,0:T(8,128)(2,1)S(1)} collective-permute-done((bf16[512,512]{1,0:T(8,128)(2,1)S(1)}, bf16[512,512]{1,0:T(8,128)(2,1)S(1)}, u32[]{:S(2)}, u32[]{:S(2)}) %collective-permute-start.6) | collective-permute-done | bytes 524320 | tf_op jit(solution)/shard_map/ppermute | solution.py:30
  58.7 2.1 %left.1.left_in = bf16[512,4096]{1,0:T(8,128)(2,1)S(1)} custom-call(s32[71]{0:T(128)S(1)} %concatenate.9.meta_ref, bf16[4,512,256]{2,1,0:T(8,128)(2,1)S(1)} %get-tuple-element.23.tables_ref, bf16[512,256]{1,0:T(8,128)(2,1)S(1)} %get-tuple-element.24.own, bf16[512,256]{1,0:T(8,128)(2,1)S(1)} %collective-permute-done.1.other, ...), custom_call_target="tpu_custom_call" | custom-call | tf_op jit(solution)/shard_map/left/pallas_call | solution.py:205
  60.8 15.0 %collective-permute-done.9.refs_1_ = bf16[512,512]{1,0:T(8,128)(2,1)S(1)} collective-permute-done((bf16[512,512]{1,0:T(8,128)(2,1)S(1)}, bf16[512,512]{1,0:T(8,128)(2,1)S(1)}, u32[]{:S(2)}, u32[]{:S(2)}) %collective-permute-start.9) | collective-permute-done | bytes 524320 | tf_op jit(solution)/shard_map/ppermute | solution.py:30
  76.7 3.2 %collective-permute-start.18 = (bf16[512,256]{1,0:T(8,128)(2,1)S(1)}, bf16[512,256]{1,0:T(8,128)(2,1)S(1)}, u32[]{:S(2)}, u32[]{:S(2)}) collective-permute-start(bf16[512,256]{1,0:T(8,128)(2,1)S(1)} %slice.9), channel_id=1, source_target_pairs={{0,224},{32,0},{64,32},{96,64},{128,96},{160,128},{192,160},{224,1... | collective-permute-start | bytes 786440 | tf_op jit(solution)/shard_map/ppermute | solution.py:30
  79.9 3.2 %right.1.right_ref = bf16[4096,512]{1,0:T(8,128)(2,1)S(1)} custom-call(s32[71]{0:T(128)S(1)} %concatenate.9.meta_ref, bf16[4,256,512]{2,1,0:T(8,128)(2,1)S(1)} %get-tuple-element.30.tables_ref, bf16[512,512]{1,0:T(8,128)(2,1)S(1)} %pad_maximum_fusion.refs_0_, bf16[512,512]{1,0:T(8,128)(2,1)S(1)} %collective-permute-done.9.refs_1_, ...), custom_call_target="tpu_custom_call" | custom-call | tf_op jit(solution)/shard_map/right/pallas_call | solution.py:205
  83.1 3.1 %most.1 = (f32[512,512]{1,0:T(8,128)S(1)}, bf16[512,4096]{1,0:T(8,128)(2,1)S(1)}) custom-call(s32[71]{0:T(128)S(1)} %concatenate.9.meta_ref, bf16[4,512,256]{2,1,0:T(8,128)(2,1)S(1)} %get-tuple-element.23.tables_ref, bf16[512,4096]{1,0:T(8,128)(2,1)S(1)} %left.1.left_in, bf16[4096,512]{1,0:T(8,128)(2,1)S(1)} %right.1.right_ref, ...), custom_call_target="tpu_custom_call", output_to_operand_aliasing={{1}: (2, {})} | custom-call | tf_op jit(solution)/shard_map/most/pallas_call | solution.py:219
  86.4 2.6 %product.1 = f32[512,512]{1,0:T(8,128)} custom-call(s32[71]{0:T(128)S(1)} %concatenate.9.meta_ref, bf16[4,512,256]{2,1,0:T(8,128)(2,1)S(1)} %get-tuple-element.23.tables_ref, f32[512,512]{1,0:T(8,128)S(1)} %get-tuple-element.32.most_ref, bf16[4096,512]{1,0:T(8,128)(2,1)S(1)} %right.1.right_ref, bf16[1024,256]{1,0:T(8,128)(2,1)S(1)} %collective-permute-done.15.up_3, ...), custom_call_target="tpu_custom_call" | custom-call | tf_op jit(solution)/shard_map/product/pallas_call | solution.py:234
  (32 shorter events, 4.0 us)
Async XLA Ops:
  0.0 0.9 %copy-start = (bf16[256,512]{1,0:T(8,128)(2,1)S(1)}, bf16[256,512]{1,0:T(8,128)(2,1)}, u32[]{:S(2)}) copy-start(bf16[256,512]{1,0:T(8,128)(2,1)} %partials_ref.1) | copy-start | bytes 786436
  1.0 0.7 copy-start.1
  1.9 12.4 %collective-permute-start = (bf16[256,512]{1,0:T(8,128)(2,1)S(1)}, bf16[256,512]{1,0:T(8,128)(2,1)S(1)}, u32[]{:S(2)}, u32[]{:S(2)}) collective-permute-start(bf16[256,512]{1,0:T(8,128)(2,1)S(1)} %get-tuple-element.20), channel_id=1, source_target_pairs={{0,10},{1,26},{2,8},{3,24},{4,14},{5,30},{6,12},{7,28},{8,2},{9,18... | collective-permute-start | bytes 786440 | tf_op jit(solution)/shard_map/ppermute | solution.py:51
  5.7 14.9 %collective-permute-start.1 = (bf16[512,256]{1,0:T(8,128)(2,1)S(1)}, bf16[512,256]{1,0:T(8,128)(2,1)S(1)}, u32[]{:S(2)}, u32[]{:S(2)}) collective-permute-start(bf16[512,256]{1,0:T(8,128)(2,1)S(1)} %get-tuple-element.24.own), channel_id=1, source_target_pairs={{0,16},{16,0},{1,17},{17,1},{2,18},{18,2},{3,19},{19,3},{4,20},{20... | collective-permute-start | bytes 786440 | tf_op jit(solution)/shard_map/ppermute | solution.py:30
  14.3 12.9 %collective-permute-start.4 = (bf16[256,512]{1,0:T(8,128)(2,1)S(1)}, bf16[256,512]{1,0:T(8,128)(2,1)S(1)}, u32[]{:S(2)}, u32[]{:S(2)}) collective-permute-start(bf16[256,512]{1,0:T(8,128)(2,1)S(1)} %collective-permute-done), channel_id=1, source_target_pairs={{10,10},{8,40},{14,78},{12,108},{2,130},{0,160},{4,196},{6,230},{3... | collective-permute-start | bytes 786440 | tf_op jit(solution)/shard_map/ppermute | solution.py:60
  20.7 18.1 %collective-permute-start.2 = (bf16[1024,256]{1,0:T(8,128)(2,1)S(1)}, bf16[1024,256]{1,0:T(8,128)(2,1)S(1)}, u32[]{:S(2)}, u32[]{:S(2)}) collective-permute-start(bf16[1024,256]{1,0:T(8,128)(2,1)S(1)} %constant_dynamic-update-slice_fusion), channel_id=1, source_target_pairs={{0,32},{32,64},{64,96},{96,128},{128,160},{160,192},{192,224},{224... | collective-permute-start | bytes 1572872 | tf_op jit(solution)/shard_map/ppermute | solution.py:30
  20.8 18.1 %collective-permute-start.3 = (bf16[1024,256]{1,0:T(8,128)(2,1)S(1)}, bf16[1024,256]{1,0:T(8,128)(2,1)S(1)}, u32[]{:S(2)}, u32[]{:S(2)}) collective-permute-start(bf16[1024,256]{1,0:T(8,128)(2,1)S(1)} %constant_dynamic-update-slice_fusion), channel_id=1, source_target_pairs={{0,224},{32,0},{64,32},{96,64},{128,96},{160,128},{192,160},{224,1... | collective-permute-start | bytes 1572872 | tf_op jit(solution)/shard_map/ppermute | solution.py:30
  27.3 8.1 %collective-permute-start.5 = (bf16[256,512]{1,0:T(8,128)(2,1)S(1)}, bf16[256,512]{1,0:T(8,128)(2,1)S(1)}, u32[]{:S(2)}, u32[]{:S(2)}) collective-permute-start(bf16[256,512]{1,0:T(8,128)(2,1)S(1)} %collective-permute-done.4), channel_id=1, source_target_pairs={{0,2},{2,0},{1,3},{3,1},{4,6},{6,4},{5,7},{7,5},{8,10},{10,8},{9,1... | collective-permute-start | bytes 786440 | tf_op jit(solution)/shard_map/ppermute | solution.py:30
  38.8 15.1 %collective-permute-start.7 = (bf16[1024,256]{1,0:T(8,128)(2,1)S(1)}, bf16[1024,256]{1,0:T(8,128)(2,1)S(1)}, u32[]{:S(2)}, u32[]{:S(2)}) collective-permute-start(bf16[1024,256]{1,0:T(8,128)(2,1)S(1)} %collective-permute-done.2.up_1), channel_id=1, source_target_pairs={{0,32},{32,64},{64,96},{96,128},{128,160},{160,192},{192,224},{224... | collective-permute-start | bytes 1572872 | tf_op jit(solution)/shard_map/ppermute | solution.py:30
  40.2 13.9 %collective-permute-start.8 = (bf16[1024,256]{1,0:T(8,128)(2,1)S(1)}, bf16[1024,256]{1,0:T(8,128)(2,1)S(1)}, u32[]{:S(2)}, u32[]{:S(2)}) collective-permute-start(bf16[1024,256]{1,0:T(8,128)(2,1)S(1)} %collective-permute-done.3.down_1), channel_id=1, source_target_pairs={{0,224},{32,0},{64,32},{96,64},{128,96},{160,128},{192,160},{224,1... | collective-permute-start | bytes 1572872 | tf_op jit(solution)/shard_map/ppermute | solution.py:30
  42.1 16.6 %collective-permute-start.6 = (bf16[512,512]{1,0:T(8,128)(2,1)S(1)}, bf16[512,512]{1,0:T(8,128)(2,1)S(1)}, u32[]{:S(2)}, u32[]{:S(2)}) collective-permute-start(bf16[512,512]{1,0:T(8,128)(2,1)S(1)} %pad_maximum_fusion.refs_0_), channel_id=1, source_target_pairs={{0,8},{4,12},{8,0},{12,4},{1,9},{5,13},{9,1},{13,5},{2,10},{6,14},... | collective-permute-start | bytes 1572872 | tf_op jit(solution)/shard_map/ppermute | solution.py:30
  45.8 30.0 %collective-permute-start.9 = (bf16[512,512]{1,0:T(8,128)(2,1)S(1)}, bf16[512,512]{1,0:T(8,128)(2,1)S(1)}, u32[]{:S(2)}, u32[]{:S(2)}) collective-permute-start(bf16[512,512]{1,0:T(8,128)(2,1)S(1)} %pad_maximum_fusion.refs_0_), channel_id=1, source_target_pairs={{0,4},{4,8},{8,12},{12,0},{1,5},{5,9},{9,13},{13,1},{2,6},{6,10},{... | collective-permute-start | bytes 1572872 | tf_op jit(solution)/shard_map/ppermute | solution.py:30
  51.5 24.3 %collective-permute-start.10 = (bf16[512,512]{1,0:T(8,128)(2,1)S(1)}, bf16[512,512]{1,0:T(8,128)(2,1)S(1)}, u32[]{:S(2)}, u32[]{:S(2)}) collective-permute-start(bf16[512,512]{1,0:T(8,128)(2,1)S(1)} %pad_maximum_fusion.refs_0_), channel_id=1, source_target_pairs={{0,12},{4,0},{8,4},{12,8},{1,13},{5,1},{9,5},{13,9},{2,14},{6,2},{... | collective-permute-start | bytes 1572872 | tf_op jit(solution)/shard_map/ppermute | solution.py:30
  53.9 22.4 %collective-permute-start.15 = (bf16[1024,256]{1,0:T(8,128)(2,1)S(1)}, bf16[1024,256]{1,0:T(8,128)(2,1)S(1)}, u32[]{:S(2)}, u32[]{:S(2)}) collective-permute-start(bf16[1024,256]{1,0:T(8,128)(2,1)S(1)} %collective-permute-done.7.up_2), channel_id=1, source_target_pairs={{0,32},{32,64},{64,96},{96,128},{128,160},{160,192},{192,224},{224... | collective-permute-start | bytes 1572872 | tf_op jit(solution)/shard_map/ppermute | solution.py:30
  54.1 22.5 %collective-permute-start.16 = (bf16[1024,256]{1,0:T(8,128)(2,1)S(1)}, bf16[1024,256]{1,0:T(8,128)(2,1)S(1)}, u32[]{:S(2)}, u32[]{:S(2)}) collective-permute-start(bf16[1024,256]{1,0:T(8,128)(2,1)S(1)} %collective-permute-done.8.down_2), channel_id=1, source_target_pairs={{0,224},{32,0},{64,32},{96,64},{128,96},{160,128},{192,160},{224,1... | collective-permute-start | bytes 1572872 | tf_op jit(solution)/shard_map/ppermute | solution.py:30
  58.7 18.1 %collective-permute-start.11 = (bf16[512,512]{1,0:T(8,128)(2,1)S(1)}, bf16[512,512]{1,0:T(8,128)(2,1)S(1)}, u32[]{:S(2)}, u32[]{:S(2)}) collective-permute-start(bf16[512,512]{1,0:T(8,128)(2,1)S(1)} %pad_maximum_fusion.refs_0_), channel_id=1, source_target_pairs={{0,1},{1,0},{2,3},{3,2},{4,5},{5,4},{6,7},{7,6},{8,9},{9,8},{10,11... | collective-permute-start | bytes 1572872 | tf_op jit(solution)/shard_map/ppermute | solution.py:30
  75.8 4.2 %collective-permute-start.14 = (bf16[512,512]{1,0:T(8,128)(2,1)S(1)}, bf16[512,512]{1,0:T(8,128)(2,1)S(1)}, u32[]{:S(2)}, u32[]{:S(2)}) collective-permute-start(bf16[512,512]{1,0:T(8,128)(2,1)S(1)} %collective-permute-done.6.refs_3_), channel_id=1, source_target_pairs={{0,1},{1,0},{2,3},{3,2},{4,5},{5,4},{6,7},{7,6},{8,9},{9,8},{10,11... | collective-permute-start | bytes 1572872 | tf_op jit(solution)/shard_map/ppermute | solution.py:30
  75.8 4.2 %collective-permute-start.12 = (bf16[512,512]{1,0:T(8,128)(2,1)S(1)}, bf16[512,512]{1,0:T(8,128)(2,1)S(1)}, u32[]{:S(2)}, u32[]{:S(2)}) collective-permute-start(bf16[512,512]{1,0:T(8,128)(2,1)S(1)} %collective-permute-done.9.refs_1_), channel_id=1, source_target_pairs={{0,1},{1,0},{2,3},{3,2},{4,5},{5,4},{6,7},{7,6},{8,9},{9,8},{10,11... | collective-permute-start | bytes 1572872 | tf_op jit(solution)/shard_map/ppermute | solution.py:30
  76.3 3.7 %collective-permute-start.13 = (bf16[512,512]{1,0:T(8,128)(2,1)S(1)}, bf16[512,512]{1,0:T(8,128)(2,1)S(1)}, u32[]{:S(2)}, u32[]{:S(2)}) collective-permute-start(bf16[512,512]{1,0:T(8,128)(2,1)S(1)} %collective-permute-done.10.refs_2_), channel_id=1, source_target_pairs={{0,1},{1,0},{2,3},{3,2},{4,5},{5,4},{6,7},{7,6},{8,9},{9,8},{10,11... | collective-permute-start | bytes 1572872 | tf_op jit(solution)/shard_map/ppermute | solution.py:30
  76.6 9.7 %collective-permute-start.17 = (bf16[512,256]{1,0:T(8,128)(2,1)S(1)}, bf16[512,256]{1,0:T(8,128)(2,1)S(1)}, u32[]{:S(2)}, u32[]{:S(2)}) collective-permute-start(bf16[512,256]{1,0:T(8,128)(2,1)S(1)} %slice.8), channel_id=1, source_target_pairs={{0,32},{32,64},{64,96},{96,128},{128,160},{160,192},{192,224},{224... | collective-permute-start | bytes 786440 | tf_op jit(solution)/shard_map/ppermute | solution.py:30
  76.7 9.6 %collective-permute-start.18 = (bf16[512,256]{1,0:T(8,128)(2,1)S(1)}, bf16[512,256]{1,0:T(8,128)(2,1)S(1)}, u32[]{:S(2)}, u32[]{:S(2)}) collective-permute-start(bf16[512,256]{1,0:T(8,128)(2,1)S(1)} %slice.9), channel_id=1, source_target_pairs={{0,224},{32,0},{64,32},{96,64},{128,96},{160,128},{192,160},{224,1... | collective-permute-start | bytes 786440 | tf_op jit(solution)/shard_map/ppermute | solution.py:30

commit v12 on v11

--- a/solution.py
+++ b/solution.py
@@ -268,10 +268,13 @@
     sync = lax.optimization_barrier
     here = in_plane(masked)
     other = around(own, "yl", NYL, 1)
+    up_own, down_own = up(own), down(own)
     here, tables = sync((here, make_tables(meta, taps, rows)))
+    here, up_own, down_own = sync((here, up_own, down_own))
     here = along_z(here)
-    both = jnp.concatenate([own, other], axis=0)
-    up_1, down_1 = up(both), down(both)
+    up_other, down_other = up(other), down(other)
+    up_1 = jnp.concatenate([up_own, up_other], axis=0)
+    down_1 = jnp.concatenate([down_own, down_other], axis=0)
     pair = jnp.concatenate([here, across(here)], axis=0)
     up_1, down_1, pair = sync((up_1, down_1, pair))
     up_2, down_2 = up(up_1), down(down_1)

time: 89.2 us -> 88.7 us (level)
  the two profiles are of different devices: /device:TPU:18 before, /device:TPU:1 now
where the time goes in v12:
time: 88.7 us; the launch traced here: 88.5 us
  starting transfers between devices  53.5 us (60%)
  waiting for transfers between devices  18.5 us (21%)
  Pallas kernels  12.4 us (14%)
  local copies, waits for them, and re-layouts  3.07 us (3%)
    ppermute x19, starting transfers between devices, around(): return lax.ppermute(block, axis, [(i, (i + step) % n) for i in range(n)])  41.1 us
    ppermute x19, waiting for transfers between devices, around(): return lax.ppermute(block, axis, [(i, (i + step) % n) for i in range(n)])  15.5 us
    ppermute x1, starting transfers between devices, in_plane(): return lax.ppermute(block, axes, route)  8.49 us
    pallas_call x2, Pallas kernels, whitened(): pl.pallas_call(kernel, out_shape=jax.ShapeDtypeStruct(shape, BF16), in_sp...  5.3 us
    ppermute x1, starting transfers between devices, along_z(): return lax.ppermute(block, ('z', 'x', 'yh'), route)  3.94 us
    pallas_call x1, Pallas kernels, most_of_product(): pl.pallas_call(most_kernel, out_shape=[jax.ShapeDtypeStruct((cols, cols),...  3.12 us
    ppermute x1, waiting for transfers between devices, along_z(): return lax.ppermute(block, ('z', 'x', 'yh'), route)  3.07 us
    pallas_call x1, Pallas kernels, product(): pl.pallas_call(functools.partial(last_kernel, scale), out_shape=jax.Shape...  2.63 us
  transfers between devices with their start and end apart: 21, of which 7 were waited for; matrix products, arithmetic and copies ran while one was open for 2% of the time, Pallas kernels for 11%

profile of v12, /device:TPU:1, one launch (start us, length us, event | category | flops | bytes accessed | tf_op | source)
XLA Modules:
  0.0 88.5 jit_solution(7005769445886799008)
XLA Ops:
  0.0 0.9 %copy-done = bf16[256,512]{1,0:T(8,128)(2,1)S(1)} copy-done((bf16[256,512]{1,0:T(8,128)(2,1)S(1)}, bf16[256,512]{1,0:T(8,128)(2,1)}, u32[]{:S(2)}) %copy-start) | copy-done | bytes 262168
  1.9 8.5 %collective-permute-start = (bf16[256,512]{1,0:T(8,128)(2,1)S(1)}, bf16[256,512]{1,0:T(8,128)(2,1)S(1)}, u32[]{:S(2)}, u32[]{:S(2)}) collective-permute-start(bf16[256,512]{1,0:T(8,128)(2,1)S(1)} %get-tuple-element.23), channel_id=1, source_target_pairs={{0,10},{1,26},{2,8},{3,24},{4,14},{5,30},{6,12},{7,28},{8,2},{9,18... | collective-permute-start | bytes 786440 | tf_op jit(solution)/shard_map/ppermute | solution.py:51
  10.5 5.4 %collective-permute-start.2 = (bf16[512,256]{1,0:T(8,128)(2,1)S(1)}, bf16[512,256]{1,0:T(8,128)(2,1)S(1)}, u32[]{:S(2)}, u32[]{:S(2)}) collective-permute-start(bf16[512,256]{1,0:T(8,128)(2,1)S(1)} %get-tuple-element.28.own), channel_id=1, source_target_pairs={{0,224},{32,0},{64,32},{96,64},{128,96},{160,128},{192,160},{224,1... | collective-permute-start | bytes 786440 | tf_op jit(solution)/shard_map/ppermute | solution.py:30
  18.0 1.1 %tables.1 = (bf16[4,256,512]{2,1,0:T(8,128)(2,1)S(1)}, bf16[4,512,256]{2,1,0:T(8,128)(2,1)S(1)}) custom-call(s32[71]{0:T(128)S(1)} %concatenate.12.meta_ref, bf16[1,256]{1,0:T(2,128)(2,1)S(1)} %broadcast_in_dim.3.taps_ref), custom_call_target="tpu_custom_call" | custom-call | tf_op jit(solution)/shard_map/tables/pallas_call | solution.py:87
  19.1 2.9 %collective-permute-done.1 = bf16[512,256]{1,0:T(8,128)(2,1)S(1)} collective-permute-done((bf16[512,256]{1,0:T(8,128)(2,1)S(1)}, bf16[512,256]{1,0:T(8,128)(2,1)S(1)}, u32[]{:S(2)}, u32[]{:S(2)}) %collective-permute-start.1) | collective-permute-done | bytes 262176 | tf_op jit(solution)/shard_map/ppermute | solution.py:30
  22.0 3.9 %collective-permute-start.6 = (bf16[256,512]{1,0:T(8,128)(2,1)S(1)}, bf16[256,512]{1,0:T(8,128)(2,1)S(1)}, u32[]{:S(2)}, u32[]{:S(2)}) collective-permute-start(bf16[256,512]{1,0:T(8,128)(2,1)S(1)} %collective-permute-done), channel_id=1, source_target_pairs={{10,10},{8,40},{14,78},{12,108},{2,130},{0,160},{4,196},{6,230},{3... | collective-permute-start | bytes 786440 | tf_op jit(solution)/shard_map/ppermute | solution.py:60
  26.4 1.1 %collective-permute-start.4 = (bf16[512,256]{1,0:T(8,128)(2,1)S(1)}, bf16[512,256]{1,0:T(8,128)(2,1)S(1)}, u32[]{:S(2)}, u32[]{:S(2)}) collective-permute-start(bf16[512,256]{1,0:T(8,128)(2,1)S(1)} %collective-permute-done.3.other), channel_id=1, source_target_pairs={{0,32},{32,64},{64,96},{96,128},{128,160},{160,192},{192,224},{224... | collective-permute-start | bytes 786440 | tf_op jit(solution)/shard_map/ppermute | solution.py:30
  27.5 3.1 %collective-permute-done.6 = bf16[256,512]{1,0:T(8,128)(2,1)S(1)} collective-permute-done((bf16[256,512]{1,0:T(8,128)(2,1)S(1)}, bf16[256,512]{1,0:T(8,128)(2,1)S(1)}, u32[]{:S(2)}, u32[]{:S(2)}) %collective-permute-start.6) | collective-permute-done | bytes 262176 | tf_op jit(solution)/shard_map/ppermute | solution.py:60
  30.5 7.0 %collective-permute-start.7 = (bf16[256,512]{1,0:T(8,128)(2,1)S(1)}, bf16[256,512]{1,0:T(8,128)(2,1)S(1)}, u32[]{:S(2)}, u32[]{:S(2)}) collective-permute-start(bf16[256,512]{1,0:T(8,128)(2,1)S(1)} %collective-permute-done.6), channel_id=1, source_target_pairs={{0,2},{2,0},{1,3},{3,1},{4,6},{6,4},{5,7},{7,5},{8,10},{10,8},{9,1... | collective-permute-start | bytes 786440 | tf_op jit(solution)/shard_map/ppermute | solution.py:30
  37.7 3.6 %collective-permute-done.7 = bf16[256,512]{1,0:T(8,128)(2,1)S(1)} collective-permute-done((bf16[256,512]{1,0:T(8,128)(2,1)S(1)}, bf16[256,512]{1,0:T(8,128)(2,1)S(1)}, u32[]{:S(2)}, u32[]{:S(2)}) %collective-permute-start.7) | collective-permute-done | bytes 262176 | tf_op jit(solution)/shard_map/ppermute | solution.py:30
  41.4 2.7 %collective-permute-start.10 = (bf16[1024,256]{1,0:T(8,128)(2,1)S(1)}, bf16[1024,256]{1,0:T(8,128)(2,1)S(1)}, u32[]{:S(2)}, u32[]{:S(2)}) collective-permute-start(bf16[1024,256]{1,0:T(8,128)(2,1)S(1)} %pad_maximum_fusion.1.down_1), channel_id=1, source_target_pairs={{0,224},{32,0},{64,32},{96,64},{128,96},{160,128},{192,160},{224,1... | collective-permute-start | bytes 1572872 | tf_op jit(solution)/shard_map/ppermute | solution.py:30
  44.1 7.9 %collective-permute-start.8 = (bf16[512,512]{1,0:T(8,128)(2,1)S(1)}, bf16[512,512]{1,0:T(8,128)(2,1)S(1)}, u32[]{:S(2)}, u32[]{:S(2)}) collective-permute-start(bf16[512,512]{1,0:T(8,128)(2,1)S(1)} %pad_maximum_fusion.2.refs_0_), channel_id=1, source_target_pairs={{0,8},{4,12},{8,0},{12,4},{1,9},{5,13},{9,1},{13,5},{2,10},{6,14},... | collective-permute-start | bytes 1572872 | tf_op jit(solution)/shard_map/ppermute | solution.py:30
  52.0 2.7 %collective-permute-start.12 = (bf16[512,512]{1,0:T(8,128)(2,1)S(1)}, bf16[512,512]{1,0:T(8,128)(2,1)S(1)}, u32[]{:S(2)}, u32[]{:S(2)}) collective-permute-start(bf16[512,512]{1,0:T(8,128)(2,1)S(1)} %pad_maximum_fusion.2.refs_0_), channel_id=1, source_target_pairs={{0,12},{4,0},{8,4},{12,8},{1,13},{5,1},{9,5},{13,9},{2,14},{6,2},{... | collective-permute-start | bytes 1572872 | tf_op jit(solution)/shard_map/ppermute | solution.py:30
  54.7 5.6 %collective-permute-start.17 = (bf16[1024,256]{1,0:T(8,128)(2,1)S(1)}, bf16[1024,256]{1,0:T(8,128)(2,1)S(1)}, u32[]{:S(2)}, u32[]{:S(2)}) collective-permute-start(bf16[1024,256]{1,0:T(8,128)(2,1)S(1)} %collective-permute-done.9.up_2), channel_id=1, source_target_pairs={{0,32},{32,64},{64,96},{96,128},{128,160},{160,192},{192,224},{224... | collective-permute-start | bytes 1572872 | tf_op jit(solution)/shard_map/ppermute | solution.py:30
  60.3 0.7 collective-permute-done.10.down_2
  61.0 1.5 %collective-permute-done.8.refs_3_ = bf16[512,512]{1,0:T(8,128)(2,1)S(1)} collective-permute-done((bf16[512,512]{1,0:T(8,128)(2,1)S(1)}, bf16[512,512]{1,0:T(8,128)(2,1)S(1)}, u32[]{:S(2)}, u32[]{:S(2)}) %collective-permute-start.8) | collective-permute-done | bytes 524320 | tf_op jit(solution)/shard_map/ppermute | solution.py:30
  62.5 4.4 %collective-permute-start.13 = (bf16[512,512]{1,0:T(8,128)(2,1)S(1)}, bf16[512,512]{1,0:T(8,128)(2,1)S(1)}, u32[]{:S(2)}, u32[]{:S(2)}) collective-permute-start(bf16[512,512]{1,0:T(8,128)(2,1)S(1)} %pad_maximum_fusion.2.refs_0_), channel_id=1, source_target_pairs={{0,1},{1,0},{2,3},{3,2},{4,5},{5,4},{6,7},{7,6},{8,9},{9,8},{10,11... | collective-permute-start | bytes 1572872 | tf_op jit(solution)/shard_map/ppermute | solution.py:30
  66.9 2.1 %left.1.left_in = bf16[512,4096]{1,0:T(8,128)(2,1)S(1)} custom-call(s32[71]{0:T(128)S(1)} %concatenate.12.meta_ref, bf16[4,512,256]{2,1,0:T(8,128)(2,1)S(1)} %get-tuple-element.26.tables_ref, bf16[512,256]{1,0:T(8,128)(2,1)S(1)} %get-tuple-element.28.own, bf16[512,256]{1,0:T(8,128)(2,1)S(1)} %collective-permute-done.3.other, ...), custom_call_target="tpu_custom_call" | custom-call | tf_op jit(solution)/shard_map/left/pallas_call | solution.py:205
  69.0 6.6 %collective-permute-done.11.refs_1_ = bf16[512,512]{1,0:T(8,128)(2,1)S(1)} collective-permute-done((bf16[512,512]{1,0:T(8,128)(2,1)S(1)}, bf16[512,512]{1,0:T(8,128)(2,1)S(1)}, u32[]{:S(2)}, u32[]{:S(2)}) %collective-permute-start.11) | collective-permute-done | bytes 524320 | tf_op jit(solution)/shard_map/ppermute | solution.py:30
  76.7 1.0 %collective-permute-start.19 = (bf16[512,256]{1,0:T(8,128)(2,1)S(1)}, bf16[512,256]{1,0:T(8,128)(2,1)S(1)}, u32[]{:S(2)}, u32[]{:S(2)}) collective-permute-start(bf16[512,256]{1,0:T(8,128)(2,1)S(1)} %slice.8), channel_id=1, source_target_pairs={{0,32},{32,64},{64,96},{96,128},{128,160},{160,192},{192,224},{224... | collective-permute-start | bytes 786440 | tf_op jit(solution)/shard_map/ppermute | solution.py:30
  77.7 1.8 %collective-permute-start.20 = (bf16[512,256]{1,0:T(8,128)(2,1)S(1)}, bf16[512,256]{1,0:T(8,128)(2,1)S(1)}, u32[]{:S(2)}, u32[]{:S(2)}) collective-permute-start(bf16[512,256]{1,0:T(8,128)(2,1)S(1)} %slice.9), channel_id=1, source_target_pairs={{0,224},{32,0},{64,32},{96,64},{128,96},{160,128},{192,160},{224,1... | collective-permute-start | bytes 786440 | tf_op jit(solution)/shard_map/ppermute | solution.py:30
  79.5 3.2 %right.1.right_ref = bf16[4096,512]{1,0:T(8,128)(2,1)S(1)} custom-call(s32[71]{0:T(128)S(1)} %concatenate.12.meta_ref, bf16[4,256,512]{2,1,0:T(8,128)(2,1)S(1)} %get-tuple-element.36.tables_ref, bf16[512,512]{1,0:T(8,128)(2,1)S(1)} %pad_maximum_fusion.2.refs_0_, bf16[512,512]{1,0:T(8,128)(2,1)S(1)} %collective-permute-done.11.refs_1_, ...), custom_call_target="tpu_custom_call" | custom-call | tf_op jit(solution)/shard_map/right/pallas_call | solution.py:205
  82.7 3.1 %most.1 = (f32[512,512]{1,0:T(8,128)S(1)}, bf16[512,4096]{1,0:T(8,128)(2,1)S(1)}) custom-call(s32[71]{0:T(128)S(1)} %concatenate.12.meta_ref, bf16[4,512,256]{2,1,0:T(8,128)(2,1)S(1)} %get-tuple-element.26.tables_ref, bf16[512,4096]{1,0:T(8,128)(2,1)S(1)} %left.1.left_in, bf16[4096,512]{1,0:T(8,128)(2,1)S(1)} %right.1.right_ref, ...), custom_call_target="tpu_custom_call", output_to_operand_aliasing={{1}: (2, {})} | custom-call | tf_op jit(solution)/shard_map/most/pallas_call | solution.py:219
  85.8 2.6 %product.1 = f32[512,512]{1,0:T(8,128)} custom-call(s32[71]{0:T(128)S(1)} %concatenate.12.meta_ref, bf16[4,512,256]{2,1,0:T(8,128)(2,1)S(1)} %get-tuple-element.26.tables_ref, f32[512,512]{1,0:T(8,128)S(1)} %get-tuple-element.38.most_ref, bf16[4096,512]{1,0:T(8,128)(2,1)S(1)} %right.1.right_ref, bf16[1024,256]{1,0:T(8,128)(2,1)S(1)} %collective-permute-done.17.up_3, ...), custom_call_target="tpu_custom_call" | custom-call | tf_op jit(solution)/shard_map/product/pallas_call | solution.py:234
  (36 shorter events, 4.4 us)
Async XLA Ops:
  0.0 0.9 %copy-start = (bf16[256,512]{1,0:T(8,128)(2,1)S(1)}, bf16[256,512]{1,0:T(8,128)(2,1)}, u32[]{:S(2)}) copy-start(bf16[256,512]{1,0:T(8,128)(2,1)} %partials_ref.1) | copy-start | bytes 786436
  1.0 0.7 copy-start.1
  1.9 17.2 %collective-permute-start = (bf16[256,512]{1,0:T(8,128)(2,1)S(1)}, bf16[256,512]{1,0:T(8,128)(2,1)S(1)}, u32[]{:S(2)}, u32[]{:S(2)}) collective-permute-start(bf16[256,512]{1,0:T(8,128)(2,1)S(1)} %get-tuple-element.23), channel_id=1, source_target_pairs={{0,10},{1,26},{2,8},{3,24},{4,14},{5,30},{6,12},{7,28},{8,2},{9,18... | collective-permute-start | bytes 786440 | tf_op jit(solution)/shard_map/ppermute | solution.py:51
  10.4 11.5 %collective-permute-start.1 = (bf16[512,256]{1,0:T(8,128)(2,1)S(1)}, bf16[512,256]{1,0:T(8,128)(2,1)S(1)}, u32[]{:S(2)}, u32[]{:S(2)}) collective-permute-start(bf16[512,256]{1,0:T(8,128)(2,1)S(1)} %get-tuple-element.28.own), channel_id=1, source_target_pairs={{0,32},{32,64},{64,96},{96,128},{128,160},{160,192},{192,224},{224... | collective-permute-start | bytes 786440 | tf_op jit(solution)/shard_map/ppermute | solution.py:30
  10.5 11.4 %collective-permute-start.2 = (bf16[512,256]{1,0:T(8,128)(2,1)S(1)}, bf16[512,256]{1,0:T(8,128)(2,1)S(1)}, u32[]{:S(2)}, u32[]{:S(2)}) collective-permute-start(bf16[512,256]{1,0:T(8,128)(2,1)S(1)} %get-tuple-element.28.own), channel_id=1, source_target_pairs={{0,224},{32,0},{64,32},{96,64},{128,96},{160,128},{192,160},{224,1... | collective-permute-start | bytes 786440 | tf_op jit(solution)/shard_map/ppermute | solution.py:30
  15.9 10.0 %collective-permute-start.3 = (bf16[512,256]{1,0:T(8,128)(2,1)S(1)}, bf16[512,256]{1,0:T(8,128)(2,1)S(1)}, u32[]{:S(2)}, u32[]{:S(2)}) collective-permute-start(bf16[512,256]{1,0:T(8,128)(2,1)S(1)} %get-tuple-element.28.own), channel_id=1, source_target_pairs={{0,16},{16,0},{1,17},{17,1},{2,18},{18,2},{3,19},{19,3},{4,20},{20... | collective-permute-start | bytes 786440 | tf_op jit(solution)/shard_map/ppermute | solution.py:30
  22.0 8.6 %collective-permute-start.6 = (bf16[256,512]{1,0:T(8,128)(2,1)S(1)}, bf16[256,512]{1,0:T(8,128)(2,1)S(1)}, u32[]{:S(2)}, u32[]{:S(2)}) collective-permute-start(bf16[256,512]{1,0:T(8,128)(2,1)S(1)} %collective-permute-done), channel_id=1, source_target_pairs={{10,10},{8,40},{14,78},{12,108},{2,130},{0,160},{4,196},{6,230},{3... | collective-permute-start | bytes 786440 | tf_op jit(solution)/shard_map/ppermute | solution.py:60
  25.9 11.6 %collective-permute-start.5 = (bf16[512,256]{1,0:T(8,128)(2,1)S(1)}, bf16[512,256]{1,0:T(8,128)(2,1)S(1)}, u32[]{:S(2)}, u32[]{:S(2)}) collective-permute-start(bf16[512,256]{1,0:T(8,128)(2,1)S(1)} %collective-permute-done.3.other), channel_id=1, source_target_pairs={{0,224},{32,0},{64,32},{96,64},{128,96},{160,128},{192,160},{224,1... | collective-permute-start | bytes 786440 | tf_op jit(solution)/shard_map/ppermute | solution.py:30
  26.4 11.3 %collective-permute-start.4 = (bf16[512,256]{1,0:T(8,128)(2,1)S(1)}, bf16[512,256]{1,0:T(8,128)(2,1)S(1)}, u32[]{:S(2)}, u32[]{:S(2)}) collective-permute-start(bf16[512,256]{1,0:T(8,128)(2,1)S(1)} %collective-permute-done.3.other), channel_id=1, source_target_pairs={{0,32},{32,64},{64,96},{96,128},{128,160},{160,192},{192,224},{224... | collective-permute-start | bytes 786440 | tf_op jit(solution)/shard_map/ppermute | solution.py:30
  30.5 10.7 %collective-permute-start.7 = (bf16[256,512]{1,0:T(8,128)(2,1)S(1)}, bf16[256,512]{1,0:T(8,128)(2,1)S(1)}, u32[]{:S(2)}, u32[]{:S(2)}) collective-permute-start(bf16[256,512]{1,0:T(8,128)(2,1)S(1)} %collective-permute-done.6), channel_id=1, source_target_pairs={{0,2},{2,0},{1,3},{3,1},{4,6},{6,4},{5,7},{7,5},{8,10},{10,8},{9,1... | collective-permute-start | bytes 786440 | tf_op jit(solution)/shard_map/ppermute | solution.py:30
  41.3 13.4 %collective-permute-start.9 = (bf16[1024,256]{1,0:T(8,128)(2,1)S(1)}, bf16[1024,256]{1,0:T(8,128)(2,1)S(1)}, u32[]{:S(2)}, u32[]{:S(2)}) collective-permute-start(bf16[1024,256]{1,0:T(8,128)(2,1)S(1)} %pad_maximum_fusion.up_1), channel_id=1, source_target_pairs={{0,32},{32,64},{64,96},{96,128},{128,160},{160,192},{192,224},{224... | collective-permute-start | bytes 1572872 | tf_op jit(solution)/shard_map/ppermute | solution.py:30
  41.4 19.6 %collective-permute-start.10 = (bf16[1024,256]{1,0:T(8,128)(2,1)S(1)}, bf16[1024,256]{1,0:T(8,128)(2,1)S(1)}, u32[]{:S(2)}, u32[]{:S(2)}) collective-permute-start(bf16[1024,256]{1,0:T(8,128)(2,1)S(1)} %pad_maximum_fusion.1.down_1), channel_id=1, source_target_pairs={{0,224},{32,0},{64,32},{96,64},{128,96},{160,128},{192,160},{224,1... | collective-permute-start | bytes 1572872 | tf_op jit(solution)/shard_map/ppermute | solution.py:30
  44.1 18.5 %collective-permute-start.8 = (bf16[512,512]{1,0:T(8,128)(2,1)S(1)}, bf16[512,512]{1,0:T(8,128)(2,1)S(1)}, u32[]{:S(2)}, u32[]{:S(2)}) collective-permute-start(bf16[512,512]{1,0:T(8,128)(2,1)S(1)} %pad_maximum_fusion.2.refs_0_), channel_id=1, source_target_pairs={{0,8},{4,12},{8,0},{12,4},{1,9},{5,13},{9,1},{13,5},{2,10},{6,14},... | collective-permute-start | bytes 1572872 | tf_op jit(solution)/shard_map/ppermute | solution.py:30
  52.0 23.6 %collective-permute-start.11 = (bf16[512,512]{1,0:T(8,128)(2,1)S(1)}, bf16[512,512]{1,0:T(8,128)(2,1)S(1)}, u32[]{:S(2)}, u32[]{:S(2)}) collective-permute-start(bf16[512,512]{1,0:T(8,128)(2,1)S(1)} %pad_maximum_fusion.2.refs_0_), channel_id=1, source_target_pairs={{0,4},{4,8},{8,12},{12,0},{1,5},{5,9},{9,13},{13,1},{2,6},{6,10},{... | collective-permute-start | bytes 1572872 | tf_op jit(solution)/shard_map/ppermute | solution.py:30
  52.0 24.1 %collective-permute-start.12 = (bf16[512,512]{1,0:T(8,128)(2,1)S(1)}, bf16[512,512]{1,0:T(8,128)(2,1)S(1)}, u32[]{:S(2)}, u32[]{:S(2)}) collective-permute-start(bf16[512,512]{1,0:T(8,128)(2,1)S(1)} %pad_maximum_fusion.2.refs_0_), channel_id=1, source_target_pairs={{0,12},{4,0},{8,4},{12,8},{1,13},{5,1},{9,5},{13,9},{2,14},{6,2},{... | collective-permute-start | bytes 1572872 | tf_op jit(solution)/shard_map/ppermute | solution.py:30
  54.7 21.5 %collective-permute-start.17 = (bf16[1024,256]{1,0:T(8,128)(2,1)S(1)}, bf16[1024,256]{1,0:T(8,128)(2,1)S(1)}, u32[]{:S(2)}, u32[]{:S(2)}) collective-permute-start(bf16[1024,256]{1,0:T(8,128)(2,1)S(1)} %collective-permute-done.9.up_2), channel_id=1, source_target_pairs={{0,32},{32,64},{64,96},{96,128},{128,160},{160,192},{192,224},{224... | collective-permute-start | bytes 1572872 | tf_op jit(solution)/shard_map/ppermute | solution.py:30
  61.0 15.6 %collective-permute-start.18 = (bf16[1024,256]{1,0:T(8,128)(2,1)S(1)}, bf16[1024,256]{1,0:T(8,128)(2,1)S(1)}, u32[]{:S(2)}, u32[]{:S(2)}) collective-permute-start(bf16[1024,256]{1,0:T(8,128)(2,1)S(1)} %collective-permute-done.10.down_2), channel_id=1, source_target_pairs={{0,224},{32,0},{64,32},{96,64},{128,96},{160,128},{192,160},{224,1... | collective-permute-start | bytes 1572872 | tf_op jit(solution)/shard_map/ppermute | solution.py:30
  62.5 15.2 %collective-permute-start.13 = (bf16[512,512]{1,0:T(8,128)(2,1)S(1)}, bf16[512,512]{1,0:T(8,128)(2,1)S(1)}, u32[]{:S(2)}, u32[]{:S(2)}) collective-permute-start(bf16[512,512]{1,0:T(8,128)(2,1)S(1)} %pad_maximum_fusion.2.refs_0_), channel_id=1, source_target_pairs={{0,1},{1,0},{2,3},{3,2},{4,5},{5,4},{6,7},{7,6},{8,9},{9,8},{10,11... | collective-permute-start | bytes 1572872 | tf_op jit(solution)/shard_map/ppermute | solution.py:30
  75.6 3.8 %collective-permute-start.16 = (bf16[512,512]{1,0:T(8,128)(2,1)S(1)}, bf16[512,512]{1,0:T(8,128)(2,1)S(1)}, u32[]{:S(2)}, u32[]{:S(2)}) collective-permute-start(bf16[512,512]{1,0:T(8,128)(2,1)S(1)} %collective-permute-done.8.refs_3_), channel_id=1, source_target_pairs={{0,1},{1,0},{2,3},{3,2},{4,5},{5,4},{6,7},{7,6},{8,9},{9,8},{10,11... | collective-permute-start | bytes 1572872 | tf_op jit(solution)/shard_map/ppermute | solution.py:30
  76.1 3.4 %collective-permute-start.14 = (bf16[512,512]{1,0:T(8,128)(2,1)S(1)}, bf16[512,512]{1,0:T(8,128)(2,1)S(1)}, u32[]{:S(2)}, u32[]{:S(2)}) collective-permute-start(bf16[512,512]{1,0:T(8,128)(2,1)S(1)} %collective-permute-done.11.refs_1_), channel_id=1, source_target_pairs={{0,1},{1,0},{2,3},{3,2},{4,5},{5,4},{6,7},{7,6},{8,9},{9,8},{10,11... | collective-permute-start | bytes 1572872 | tf_op jit(solution)/shard_map/ppermute | solution.py:30
  76.1 3.3 %collective-permute-start.15 = (bf16[512,512]{1,0:T(8,128)(2,1)S(1)}, bf16[512,512]{1,0:T(8,128)(2,1)S(1)}, u32[]{:S(2)}, u32[]{:S(2)}) collective-permute-start(bf16[512,512]{1,0:T(8,128)(2,1)S(1)} %collective-permute-done.12.refs_2_), channel_id=1, source_target_pairs={{0,1},{1,0},{2,3},{3,2},{4,5},{5,4},{6,7},{7,6},{8,9},{9,8},{10,11... | collective-permute-start | bytes 1572872 | tf_op jit(solution)/shard_map/ppermute | solution.py:30
  76.7 9.2 %collective-permute-start.19 = (bf16[512,256]{1,0:T(8,128)(2,1)S(1)}, bf16[512,256]{1,0:T(8,128)(2,1)S(1)}, u32[]{:S(2)}, u32[]{:S(2)}) collective-permute-start(bf16[512,256]{1,0:T(8,128)(2,1)S(1)} %slice.8), channel_id=1, source_target_pairs={{0,32},{32,64},{64,96},{96,128},{128,160},{160,192},{192,224},{224... | collective-permute-start | bytes 786440 | tf_op jit(solution)/shard_map/ppermute | solution.py:30
  77.7 8.2 %collective-permute-start.20 = (bf16[512,256]{1,0:T(8,128)(2,1)S(1)}, bf16[512,256]{1,0:T(8,128)(2,1)S(1)}, u32[]{:S(2)}, u32[]{:S(2)}) collective-permute-start(bf16[512,256]{1,0:T(8,128)(2,1)S(1)} %slice.9), channel_id=1, source_target_pairs={{0,224},{32,0},{64,32},{96,64},{128,96},{160,128},{192,160},{224,1... | collective-permute-start | bytes 786440 | tf_op jit(solution)/shard_map/ppermute | solution.py:30

commit v13 on v12

--- a/solution.py
+++ b/solution.py
@@ -152,8 +152,8 @@
 
 
 def right_kernel(meta_ref, tables_ref, *refs):
-    pieces = refs[0:8]
-    out_ref, raw = refs[8:]
+    pieces = refs[0:10]
+    out_ref, raw = refs[10:]
     rows = tables_ref.shape[1]
     z, x, yh, core = [meta_ref[i] for i in (0, 2, 3, 4)]
     raw[:rows] = jnp.zeros((rows, raw.shape[1]), BF16)
@@ -162,7 +162,8 @@
             for dy in range(2):
                 line = NYH * ((x + DX[s]) & 3) + (yh ^ dy)
                 e = 2 * meta_ref[7 + NZ * z + line] + (core ^ q)
-                raw[at_block(e + 1, rows)] = pieces[4 * q + s][dy * rows : (dy + 1) * rows]
+                piece, at = (pieces[5 * q + s], dy * rows) if s < 3 else (pieces[5 * q + 3 + dy], 0)
+                raw[at_block(e + 1, rows)] = piece[at : at + rows]
     for e in range(NE):
         table = tables_ref[table_of(e, meta_ref)]
         white = jnp.dot(table, raw[e * rows : (e + 2) * rows], preferred_element_type=F32)
@@ -257,7 +258,9 @@
         return around(block, "z", NZ, -1)
 
     def along_x(block):
-        return [around(block, "x", NX, step) for step in (1, -1, 2)]
+        near = [around(block, "x", NX, step) for step in (1, -1)]
+        rows = block.shape[0] // 2
+        return near + [around(near[0][:rows], "x", NX, 1), around(near[1][rows:], "x", NX, -1)]
 
     def swapped(block):
         return around(block, "c", NC, 1)

time: 88.7 us -> 88.6 us (level)
  waiting for transfers between devices: 18.5 us -> 15.3 us
  starting transfers between devices: 53.5 us -> 56.6 us
    ppermute x19 -> x21, waiting for transfers between devices: 15.5 us -> 12.2 us  [around(): return lax.ppermute(block, axis, [(i, (i + step) % n) for i in range(n)])]
    ppermute x19 -> x21, starting transfers between devices: 41.1 us -> 44.2 us  [around(): return lax.ppermute(block, axis, [(i, (i + step) % n) for i in range(n)])]
  transfers between devices with their start and end apart: 21 -> 23, of which waited for: 7 -> 9; matrix products, arithmetic and copies ran while one was open for 2% -> 2% of each run, Pallas kernels for 11% -> 11%
where the time goes in v13:
time: 88.6 us; the launch traced here: 88.4 us
  starting transfers between devices  56.6 us (64%)
  waiting for transfers between devices  15.3 us (17%)
  Pallas kernels  12.4 us (14%)
  local copies, waits for them, and re-layouts  3.1 us (3%)
    ppermute x21, starting transfers between devices, around(): return lax.ppermute(block, axis, [(i, (i + step) % n) for i in range(n)])  44.2 us
    ppermute x21, waiting for transfers between devices, around(): return lax.ppermute(block, axis, [(i, (i + step) % n) for i in range(n)])  12.2 us
    ppermute x1, starting transfers between devices, in_plane(): return lax.ppermute(block, axes, route)  8.49 us
    pallas_call x2, Pallas kernels, whitened(): pl.pallas_call(kernel, out_shape=jax.ShapeDtypeStruct(shape, BF16), in_sp...  5.3 us
    ppermute x1, starting transfers between devices, along_z(): return lax.ppermute(block, ('z', 'x', 'yh'), route)  3.94 us
    pallas_call x1, Pallas kernels, most_of_product(): pl.pallas_call(most_kernel, out_shape=[jax.ShapeDtypeStruct((cols, cols),...  3.12 us
    ppermute x1, waiting for transfers between devices, along_z(): return lax.ppermute(block, ('z', 'x', 'yh'), route)  3.07 us
    pallas_call x1, Pallas kernels, product(): pl.pallas_call(functools.partial(last_kernel, scale), out_shape=jax.Shape...  2.63 us
  transfers between devices with their start and end apart: 23, of which 9 were waited for; matrix products, arithmetic and copies ran while one was open for 2% of the time, Pallas kernels for 11%

profile of v13, /device:TPU:1, one launch (start us, length us, event | category | flops | bytes accessed | tf_op | source)
XLA Modules:
  0.0 88.4 jit_solution(9949541589756904724)
XLA Ops:
  1.9 8.5 %collective-permute-start = (bf16[256,512]{1,0:T(8,128)(2,1)S(1)}, bf16[256,512]{1,0:T(8,128)(2,1)S(1)}, u32[]{:S(2)}, u32[]{:S(2)}) collective-permute-start(bf16[256,512]{1,0:T(8,128)(2,1)S(1)} %get-tuple-element.23), channel_id=1, source_target_pairs={{0,10},{1,26},{2,8},{3,24},{4,14},{5,30},{6,12},{7,28},{8,2},{9,18... | collective-permute-start | bytes 786440 | tf_op jit(solution)/shard_map/ppermute | solution.py:51
  10.5 5.4 %collective-permute-start.2 = (bf16[512,256]{1,0:T(8,128)(2,1)S(1)}, bf16[512,256]{1,0:T(8,128)(2,1)S(1)}, u32[]{:S(2)}, u32[]{:S(2)}) collective-permute-start(bf16[512,256]{1,0:T(8,128)(2,1)S(1)} %get-tuple-element.28.own), channel_id=1, source_target_pairs={{0,224},{32,0},{64,32},{96,64},{128,96},{160,128},{192,160},{224,1... | collective-permute-start | bytes 786440 | tf_op jit(solution)/shard_map/ppermute | solution.py:30
  18.0 1.1 %tables.1 = (bf16[4,256,512]{2,1,0:T(8,128)(2,1)S(1)}, bf16[4,512,256]{2,1,0:T(8,128)(2,1)S(1)}) custom-call(s32[71]{0:T(128)S(1)} %concatenate.12.meta_ref, bf16[1,256]{1,0:T(2,128)(2,1)S(1)} %broadcast_in_dim.3.taps_ref), custom_call_target="tpu_custom_call" | custom-call | tf_op jit(solution)/shard_map/tables/pallas_call | solution.py:87
  19.1 2.9 %collective-permute-done.1 = bf16[512,256]{1,0:T(8,128)(2,1)S(1)} collective-permute-done((bf16[512,256]{1,0:T(8,128)(2,1)S(1)}, bf16[512,256]{1,0:T(8,128)(2,1)S(1)}, u32[]{:S(2)}, u32[]{:S(2)}) %collective-permute-start.1) | collective-permute-done | bytes 262176 | tf_op jit(solution)/shard_map/ppermute | solution.py:30
  22.0 3.9 %collective-permute-start.6 = (bf16[256,512]{1,0:T(8,128)(2,1)S(1)}, bf16[256,512]{1,0:T(8,128)(2,1)S(1)}, u32[]{:S(2)}, u32[]{:S(2)}) collective-permute-start(bf16[256,512]{1,0:T(8,128)(2,1)S(1)} %collective-permute-done), channel_id=1, source_target_pairs={{10,10},{8,40},{14,78},{12,108},{2,130},{0,160},{4,196},{6,230},{3... | collective-permute-start | bytes 786440 | tf_op jit(solution)/shard_map/ppermute | solution.py:60
  26.4 1.1 %collective-permute-start.4 = (bf16[512,256]{1,0:T(8,128)(2,1)S(1)}, bf16[512,256]{1,0:T(8,128)(2,1)S(1)}, u32[]{:S(2)}, u32[]{:S(2)}) collective-permute-start(bf16[512,256]{1,0:T(8,128)(2,1)S(1)} %collective-permute-done.3.other), channel_id=1, source_target_pairs={{0,32},{32,64},{64,96},{96,128},{128,160},{160,192},{192,224},{224... | collective-permute-start | bytes 786440 | tf_op jit(solution)/shard_map/ppermute | solution.py:30
  27.5 3.1 %collective-permute-done.6 = bf16[256,512]{1,0:T(8,128)(2,1)S(1)} collective-permute-done((bf16[256,512]{1,0:T(8,128)(2,1)S(1)}, bf16[256,512]{1,0:T(8,128)(2,1)S(1)}, u32[]{:S(2)}, u32[]{:S(2)}) %collective-permute-start.6) | collective-permute-done | bytes 262176 | tf_op jit(solution)/shard_map/ppermute | solution.py:60
  30.5 7.0 %collective-permute-start.7 = (bf16[256,512]{1,0:T(8,128)(2,1)S(1)}, bf16[256,512]{1,0:T(8,128)(2,1)S(1)}, u32[]{:S(2)}, u32[]{:S(2)}) collective-permute-start(bf16[256,512]{1,0:T(8,128)(2,1)S(1)} %collective-permute-done.6), channel_id=1, source_target_pairs={{0,2},{2,0},{1,3},{3,1},{4,6},{6,4},{5,7},{7,5},{8,10},{10,8},{9,1... | collective-permute-start | bytes 786440 | tf_op jit(solution)/shard_map/ppermute | solution.py:30
  37.7 3.6 %collective-permute-done.7 = bf16[256,512]{1,0:T(8,128)(2,1)S(1)} collective-permute-done((bf16[256,512]{1,0:T(8,128)(2,1)S(1)}, bf16[256,512]{1,0:T(8,128)(2,1)S(1)}, u32[]{:S(2)}, u32[]{:S(2)}) %collective-permute-start.7) | collective-permute-done | bytes 262176 | tf_op jit(solution)/shard_map/ppermute | solution.py:30
  41.5 2.6 %collective-permute-start.11 = (bf16[1024,256]{1,0:T(8,128)(2,1)S(1)}, bf16[1024,256]{1,0:T(8,128)(2,1)S(1)}, u32[]{:S(2)}, u32[]{:S(2)}) collective-permute-start(bf16[1024,256]{1,0:T(8,128)(2,1)S(1)} %pad_maximum_fusion.1.down_1), channel_id=1, source_target_pairs={{0,224},{32,0},{64,32},{96,64},{128,96},{160,128},{192,160},{224,1... | collective-permute-start | bytes 1572872 | tf_op jit(solution)/shard_map/ppermute | solution.py:30
  44.1 2.7 %collective-permute-start.12 = (bf16[512,512]{1,0:T(8,128)(2,1)S(1)}, bf16[512,512]{1,0:T(8,128)(2,1)S(1)}, u32[]{:S(2)}, u32[]{:S(2)}) collective-permute-start(bf16[512,512]{1,0:T(8,128)(2,1)S(1)} %pad_maximum_fusion.2.refs_0_), channel_id=1, source_target_pairs={{0,12},{4,0},{8,4},{12,8},{1,13},{5,1},{9,5},{13,9},{2,14},{6,2},{... | collective-permute-start | bytes 1572872 | tf_op jit(solution)/shard_map/ppermute | solution.py:30
  46.7 3.9 %collective-permute-done.10.up_2 = bf16[1024,256]{1,0:T(8,128)(2,1)S(1)} collective-permute-done((bf16[1024,256]{1,0:T(8,128)(2,1)S(1)}, bf16[1024,256]{1,0:T(8,128)(2,1)S(1)}, u32[]{:S(2)}, u32[]{:S(2)}) %collective-permute-start.10) | collective-permute-done | bytes 524320 | tf_op jit(solution)/shard_map/ppermute | solution.py:30
  50.6 9.7 %collective-permute-start.19 = (bf16[1024,256]{1,0:T(8,128)(2,1)S(1)}, bf16[1024,256]{1,0:T(8,128)(2,1)S(1)}, u32[]{:S(2)}, u32[]{:S(2)}) collective-permute-start(bf16[1024,256]{1,0:T(8,128)(2,1)S(1)} %collective-permute-done.10.up_2), channel_id=1, source_target_pairs={{0,32},{32,64},{64,96},{96,128},{128,160},{160,192},{192,224},{224... | collective-permute-start | bytes 1572872 | tf_op jit(solution)/shard_map/ppermute | solution.py:30
  62.2 1.5 %collective-permute-start.13 = (bf16[256,512]{1,0:T(8,128)(2,1)S(1)}, bf16[256,512]{1,0:T(8,128)(2,1)S(1)}, u32[]{:S(2)}, u32[]{:S(2)}) collective-permute-start(bf16[256,512]{1,0:T(8,128)(2,1)S(1)} %slice.17), channel_id=1, source_target_pairs={{0,12},{4,0},{8,4},{12,8},{1,13},{5,1},{9,5},{13,9},{2,14},{6,2},{... | collective-permute-start | bytes 786440 | tf_op jit(solution)/shard_map/ppermute | solution.py:30
  63.6 2.5 %collective-permute-start.14 = (bf16[512,512]{1,0:T(8,128)(2,1)S(1)}, bf16[512,512]{1,0:T(8,128)(2,1)S(1)}, u32[]{:S(2)}, u32[]{:S(2)}) collective-permute-start(bf16[512,512]{1,0:T(8,128)(2,1)S(1)} %pad_maximum_fusion.2.refs_0_), channel_id=1, source_target_pairs={{0,1},{1,0},{2,3},{3,2},{4,5},{5,4},{6,7},{7,6},{8,9},{9,8},{10,11... | collective-permute-start | bytes 1572872 | tf_op jit(solution)/shard_map/ppermute | solution.py:30
  66.2 2.1 %left.1.left_in = bf16[512,4096]{1,0:T(8,128)(2,1)S(1)} custom-call(s32[71]{0:T(128)S(1)} %concatenate.12.meta_ref, bf16[4,512,256]{2,1,0:T(8,128)(2,1)S(1)} %get-tuple-element.26.tables_ref, bf16[512,256]{1,0:T(8,128)(2,1)S(1)} %get-tuple-element.28.own, bf16[512,256]{1,0:T(8,128)(2,1)S(1)} %collective-permute-done.3.other, ...), custom_call_target="tpu_custom_call" | custom-call | tf_op jit(solution)/shard_map/left/pallas_call | solution.py:206
  68.3 2.0 %collective-permute-start.15 = (bf16[512,512]{1,0:T(8,128)(2,1)S(1)}, bf16[512,512]{1,0:T(8,128)(2,1)S(1)}, u32[]{:S(2)}, u32[]{:S(2)}) collective-permute-start(bf16[512,512]{1,0:T(8,128)(2,1)S(1)} %collective-permute-done.8.refs_1_), channel_id=1, source_target_pairs={{0,1},{1,0},{2,3},{3,2},{4,5},{5,4},{6,7},{7,6},{8,9},{9,8},{10,11... | collective-permute-start | bytes 1572872 | tf_op jit(solution)/shard_map/ppermute | solution.py:30
  70.3 2.5 %collective-permute-start.16 = (bf16[512,512]{1,0:T(8,128)(2,1)S(1)}, bf16[512,512]{1,0:T(8,128)(2,1)S(1)}, u32[]{:S(2)}, u32[]{:S(2)}) collective-permute-start(bf16[512,512]{1,0:T(8,128)(2,1)S(1)} %collective-permute-done.12.refs_2_), channel_id=1, source_target_pairs={{0,1},{1,0},{2,3},{3,2},{4,5},{5,4},{6,7},{7,6},{8,9},{9,8},{10,11... | collective-permute-start | bytes 1572872 | tf_op jit(solution)/shard_map/ppermute | solution.py:30
  73.5 3.0 %collective-permute-start.18 = (bf16[256,512]{1,0:T(8,128)(2,1)S(1)}, bf16[256,512]{1,0:T(8,128)(2,1)S(1)}, u32[]{:S(2)}, u32[]{:S(2)}) collective-permute-start(bf16[256,512]{1,0:T(8,128)(2,1)S(1)} %collective-permute-done.13.refs_4_), channel_id=1, source_target_pairs={{0,1},{1,0},{2,3},{3,2},{4,5},{5,4},{6,7},{7,6},{8,9},{9,8},{10,11... | collective-permute-start | bytes 786440 | tf_op jit(solution)/shard_map/ppermute | solution.py:30
  76.5 1.5 %collective-permute-start.21 = (bf16[512,256]{1,0:T(8,128)(2,1)S(1)}, bf16[512,256]{1,0:T(8,128)(2,1)S(1)}, u32[]{:S(2)}, u32[]{:S(2)}) collective-permute-start(bf16[512,256]{1,0:T(8,128)(2,1)S(1)} %slice.18), channel_id=1, source_target_pairs={{0,32},{32,64},{64,96},{96,128},{128,160},{160,192},{192,224},{224... | collective-permute-start | bytes 786440 | tf_op jit(solution)/shard_map/ppermute | solution.py:30
  78.1 1.2 %collective-permute-start.22 = (bf16[512,256]{1,0:T(8,128)(2,1)S(1)}, bf16[512,256]{1,0:T(8,128)(2,1)S(1)}, u32[]{:S(2)}, u32[]{:S(2)}) collective-permute-start(bf16[512,256]{1,0:T(8,128)(2,1)S(1)} %slice.19), channel_id=1, source_target_pairs={{0,224},{32,0},{64,32},{96,64},{128,96},{160,128},{192,160},{224,1... | collective-permute-start | bytes 786440 | tf_op jit(solution)/shard_map/ppermute | solution.py:30
  79.3 3.2 %right.1.right_ref = bf16[4096,512]{1,0:T(8,128)(2,1)S(1)} custom-call(s32[71]{0:T(128)S(1)} %concatenate.12.meta_ref, bf16[4,256,512]{2,1,0:T(8,128)(2,1)S(1)} %get-tuple-element.36.tables_ref, bf16[512,512]{1,0:T(8,128)(2,1)S(1)} %pad_maximum_fusion.2.refs_0_, bf16[512,512]{1,0:T(8,128)(2,1)S(1)} %collective-permute-done.8.refs_1_, ...), custom_call_target="tpu_custom_call" | custom-call | tf_op jit(solution)/shard_map/right/pallas_call | solution.py:206
  82.5 3.1 %most.1 = (f32[512,512]{1,0:T(8,128)S(1)}, bf16[512,4096]{1,0:T(8,128)(2,1)S(1)}) custom-call(s32[71]{0:T(128)S(1)} %concatenate.12.meta_ref, bf16[4,512,256]{2,1,0:T(8,128)(2,1)S(1)} %get-tuple-element.26.tables_ref, bf16[512,4096]{1,0:T(8,128)(2,1)S(1)} %left.1.left_in, bf16[4096,512]{1,0:T(8,128)(2,1)S(1)} %right.1.right_ref, ...), custom_call_target="tpu_custom_call", output_to_operand_aliasing={{1}: (2, {})} | custom-call | tf_op jit(solution)/shard_map/most/pallas_call | solution.py:220
  85.8 2.6 %product.1 = f32[512,512]{1,0:T(8,128)} custom-call(s32[71]{0:T(128)S(1)} %concatenate.12.meta_ref, bf16[4,512,256]{2,1,0:T(8,128)(2,1)S(1)} %get-tuple-element.26.tables_ref, f32[512,512]{1,0:T(8,128)S(1)} %get-tuple-element.38.most_ref, bf16[4096,512]{1,0:T(8,128)(2,1)S(1)} %right.1.right_ref, bf16[1024,256]{1,0:T(8,128)(2,1)S(1)} %collective-permute-done.19.up_3, ...), custom_call_target="tpu_custom_call" | custom-call | tf_op jit(solution)/shard_map/product/pallas_call | solution.py:235
  (42 shorter events, 7.0 us)
Async XLA Ops:
  0.0 0.9 %copy-start = (bf16[256,512]{1,0:T(8,128)(2,1)S(1)}, bf16[256,512]{1,0:T(8,128)(2,1)}, u32[]{:S(2)}) copy-start(bf16[256,512]{1,0:T(8,128)(2,1)} %partials_ref.1) | copy-start | bytes 786436
  1.9 17.2 %collective-permute-start = (bf16[256,512]{1,0:T(8,128)(2,1)S(1)}, bf16[256,512]{1,0:T(8,128)(2,1)S(1)}, u32[]{:S(2)}, u32[]{:S(2)}) collective-permute-start(bf16[256,512]{1,0:T(8,128)(2,1)S(1)} %get-tuple-element.23), channel_id=1, source_target_pairs={{0,10},{1,26},{2,8},{3,24},{4,14},{5,30},{6,12},{7,28},{8,2},{9,18... | collective-permute-start | bytes 786440 | tf_op jit(solution)/shard_map/ppermute | solution.py:51
  10.4 11.5 %collective-permute-start.1 = (bf16[512,256]{1,0:T(8,128)(2,1)S(1)}, bf16[512,256]{1,0:T(8,128)(2,1)S(1)}, u32[]{:S(2)}, u32[]{:S(2)}) collective-permute-start(bf16[512,256]{1,0:T(8,128)(2,1)S(1)} %get-tuple-element.28.own), channel_id=1, source_target_pairs={{0,32},{32,64},{64,96},{96,128},{128,160},{160,192},{192,224},{224... | collective-permute-start | bytes 786440 | tf_op jit(solution)/shard_map/ppermute | solution.py:30
  10.5 11.4 %collective-permute-start.2 = (bf16[512,256]{1,0:T(8,128)(2,1)S(1)}, bf16[512,256]{1,0:T(8,128)(2,1)S(1)}, u32[]{:S(2)}, u32[]{:S(2)}) collective-permute-start(bf16[512,256]{1,0:T(8,128)(2,1)S(1)} %get-tuple-element.28.own), channel_id=1, source_target_pairs={{0,224},{32,0},{64,32},{96,64},{128,96},{160,128},{192,160},{224,1... | collective-permute-start | bytes 786440 | tf_op jit(solution)/shard_map/ppermute | solution.py:30
  15.9 10.0 %collective-permute-start.3 = (bf16[512,256]{1,0:T(8,128)(2,1)S(1)}, bf16[512,256]{1,0:T(8,128)(2,1)S(1)}, u32[]{:S(2)}, u32[]{:S(2)}) collective-permute-start(bf16[512,256]{1,0:T(8,128)(2,1)S(1)} %get-tuple-element.28.own), channel_id=1, source_target_pairs={{0,16},{16,0},{1,17},{17,1},{2,18},{18,2},{3,19},{19,3},{4,20},{20... | collective-permute-start | bytes 786440 | tf_op jit(solution)/shard_map/ppermute | solution.py:30
  22.0 8.6 %collective-permute-start.6 = (bf16[256,512]{1,0:T(8,128)(2,1)S(1)}, bf16[256,512]{1,0:T(8,128)(2,1)S(1)}, u32[]{:S(2)}, u32[]{:S(2)}) collective-permute-start(bf16[256,512]{1,0:T(8,128)(2,1)S(1)} %collective-permute-done), channel_id=1, source_target_pairs={{10,10},{8,40},{14,78},{12,108},{2,130},{0,160},{4,196},{6,230},{3... | collective-permute-start | bytes 786440 | tf_op jit(solution)/shard_map/ppermute | solution.py:60
  25.9 11.6 %collective-permute-start.5 = (bf16[512,256]{1,0:T(8,128)(2,1)S(1)}, bf16[512,256]{1,0:T(8,128)(2,1)S(1)}, u32[]{:S(2)}, u32[]{:S(2)}) collective-permute-start(bf16[512,256]{1,0:T(8,128)(2,1)S(1)} %collective-permute-done.3.other), channel_id=1, source_target_pairs={{0,224},{32,0},{64,32},{96,64},{128,96},{160,128},{192,160},{224,1... | collective-permute-start | bytes 786440 | tf_op jit(solution)/shard_map/ppermute | solution.py:30
  26.4 11.3 %collective-permute-start.4 = (bf16[512,256]{1,0:T(8,128)(2,1)S(1)}, bf16[512,256]{1,0:T(8,128)(2,1)S(1)}, u32[]{:S(2)}, u32[]{:S(2)}) collective-permute-start(bf16[512,256]{1,0:T(8,128)(2,1)S(1)} %collective-permute-done.3.other), channel_id=1, source_target_pairs={{0,32},{32,64},{64,96},{96,128},{128,160},{160,192},{192,224},{224... | collective-permute-start | bytes 786440 | tf_op jit(solution)/shard_map/ppermute | solution.py:30
  30.5 10.7 %collective-permute-start.7 = (bf16[256,512]{1,0:T(8,128)(2,1)S(1)}, bf16[256,512]{1,0:T(8,128)(2,1)S(1)}, u32[]{:S(2)}, u32[]{:S(2)}) collective-permute-start(bf16[256,512]{1,0:T(8,128)(2,1)S(1)} %collective-permute-done.6), channel_id=1, source_target_pairs={{0,2},{2,0},{1,3},{3,1},{4,6},{6,4},{5,7},{7,5},{8,10},{10,8},{9,1... | collective-permute-start | bytes 786440 | tf_op jit(solution)/shard_map/ppermute | solution.py:30
  41.3 9.3 %collective-permute-start.10 = (bf16[1024,256]{1,0:T(8,128)(2,1)S(1)}, bf16[1024,256]{1,0:T(8,128)(2,1)S(1)}, u32[]{:S(2)}, u32[]{:S(2)}) collective-permute-start(bf16[1024,256]{1,0:T(8,128)(2,1)S(1)} %pad_maximum_fusion.up_1), channel_id=1, source_target_pairs={{0,32},{32,64},{64,96},{96,128},{128,160},{160,192},{192,224},{224... | collective-permute-start | bytes 1572872 | tf_op jit(solution)/shard_map/ppermute | solution.py:30
  41.4 18.9 %collective-permute-start.8 = (bf16[512,512]{1,0:T(8,128)(2,1)S(1)}, bf16[512,512]{1,0:T(8,128)(2,1)S(1)}, u32[]{:S(2)}, u32[]{:S(2)}) collective-permute-start(bf16[512,512]{1,0:T(8,128)(2,1)S(1)} %pad_maximum_fusion.2.refs_0_), channel_id=1, source_target_pairs={{0,4},{4,8},{8,12},{12,0},{1,5},{5,9},{9,13},{13,1},{2,6},{6,10},{... | collective-permute-start | bytes 1572872 | tf_op jit(solution)/shard_map/ppermute | solution.py:30
  41.5 19.5 %collective-permute-start.11 = (bf16[1024,256]{1,0:T(8,128)(2,1)S(1)}, bf16[1024,256]{1,0:T(8,128)(2,1)S(1)}, u32[]{:S(2)}, u32[]{:S(2)}) collective-permute-start(bf16[1024,256]{1,0:T(8,128)(2,1)S(1)} %pad_maximum_fusion.1.down_1), channel_id=1, source_target_pairs={{0,224},{32,0},{64,32},{96,64},{128,96},{160,128},{192,160},{224,1... | collective-permute-start | bytes 1572872 | tf_op jit(solution)/shard_map/ppermute | solution.py:30
  44.1 18.1 %collective-permute-start.12 = (bf16[512,512]{1,0:T(8,128)(2,1)S(1)}, bf16[512,512]{1,0:T(8,128)(2,1)S(1)}, u32[]{:S(2)}, u32[]{:S(2)}) collective-permute-start(bf16[512,512]{1,0:T(8,128)(2,1)S(1)} %pad_maximum_fusion.2.refs_0_), channel_id=1, source_target_pairs={{0,12},{4,0},{8,4},{12,8},{1,13},{5,1},{9,5},{13,9},{2,14},{6,2},{... | collective-permute-start | bytes 1572872 | tf_op jit(solution)/shard_map/ppermute | solution.py:30
  50.6 22.2 %collective-permute-start.19 = (bf16[1024,256]{1,0:T(8,128)(2,1)S(1)}, bf16[1024,256]{1,0:T(8,128)(2,1)S(1)}, u32[]{:S(2)}, u32[]{:S(2)}) collective-permute-start(bf16[1024,256]{1,0:T(8,128)(2,1)S(1)} %collective-permute-done.10.up_2), channel_id=1, source_target_pairs={{0,32},{32,64},{64,96},{96,128},{128,160},{160,192},{192,224},{224... | collective-permute-start | bytes 1572872 | tf_op jit(solution)/shard_map/ppermute | solution.py:30
  60.3 8.0 %collective-permute-start.9 = (bf16[256,512]{1,0:T(8,128)(2,1)S(1)}, bf16[256,512]{1,0:T(8,128)(2,1)S(1)}, u32[]{:S(2)}, u32[]{:S(2)}) collective-permute-start(bf16[256,512]{1,0:T(8,128)(2,1)S(1)} %slice.16), channel_id=1, source_target_pairs={{0,4},{4,8},{8,12},{12,0},{1,5},{5,9},{9,13},{13,1},{2,6},{6,10},{... | collective-permute-start | bytes 786440 | tf_op jit(solution)/shard_map/ppermute | solution.py:30
  61.0 12.5 %collective-permute-start.20 = (bf16[1024,256]{1,0:T(8,128)(2,1)S(1)}, bf16[1024,256]{1,0:T(8,128)(2,1)S(1)}, u32[]{:S(2)}, u32[]{:S(2)}) collective-permute-start(bf16[1024,256]{1,0:T(8,128)(2,1)S(1)} %collective-permute-done.11.down_2), channel_id=1, source_target_pairs={{0,224},{32,0},{64,32},{96,64},{128,96},{160,128},{192,160},{224,1... | collective-permute-start | bytes 1572872 | tf_op jit(solution)/shard_map/ppermute | solution.py:30
  62.2 8.1 %collective-permute-start.13 = (bf16[256,512]{1,0:T(8,128)(2,1)S(1)}, bf16[256,512]{1,0:T(8,128)(2,1)S(1)}, u32[]{:S(2)}, u32[]{:S(2)}) collective-permute-start(bf16[256,512]{1,0:T(8,128)(2,1)S(1)} %slice.17), channel_id=1, source_target_pairs={{0,12},{4,0},{8,4},{12,8},{1,13},{5,1},{9,5},{13,9},{2,14},{6,2},{... | collective-permute-start | bytes 786440 | tf_op jit(solution)/shard_map/ppermute | solution.py:30
  63.6 12.9 %collective-permute-start.14 = (bf16[512,512]{1,0:T(8,128)(2,1)S(1)}, bf16[512,512]{1,0:T(8,128)(2,1)S(1)}, u32[]{:S(2)}, u32[]{:S(2)}) collective-permute-start(bf16[512,512]{1,0:T(8,128)(2,1)S(1)} %pad_maximum_fusion.2.refs_0_), channel_id=1, source_target_pairs={{0,1},{1,0},{2,3},{3,2},{4,5},{5,4},{6,7},{7,6},{8,9},{9,8},{10,11... | collective-permute-start | bytes 1572872 | tf_op jit(solution)/shard_map/ppermute | solution.py:30
  68.3 11.0 %collective-permute-start.15 = (bf16[512,512]{1,0:T(8,128)(2,1)S(1)}, bf16[512,512]{1,0:T(8,128)(2,1)S(1)}, u32[]{:S(2)}, u32[]{:S(2)}) collective-permute-start(bf16[512,512]{1,0:T(8,128)(2,1)S(1)} %collective-permute-done.8.refs_1_), channel_id=1, source_target_pairs={{0,1},{1,0},{2,3},{3,2},{4,5},{5,4},{6,7},{7,6},{8,9},{9,8},{10,11... | collective-permute-start | bytes 1572872 | tf_op jit(solution)/shard_map/ppermute | solution.py:30
  70.3 9.0 %collective-permute-start.16 = (bf16[512,512]{1,0:T(8,128)(2,1)S(1)}, bf16[512,512]{1,0:T(8,128)(2,1)S(1)}, u32[]{:S(2)}, u32[]{:S(2)}) collective-permute-start(bf16[512,512]{1,0:T(8,128)(2,1)S(1)} %collective-permute-done.12.refs_2_), channel_id=1, source_target_pairs={{0,1},{1,0},{2,3},{3,2},{4,5},{5,4},{6,7},{7,6},{8,9},{9,8},{10,11... | collective-permute-start | bytes 1572872 | tf_op jit(solution)/shard_map/ppermute | solution.py:30
  72.8 5.3 %collective-permute-start.17 = (bf16[256,512]{1,0:T(8,128)(2,1)S(1)}, bf16[256,512]{1,0:T(8,128)(2,1)S(1)}, u32[]{:S(2)}, u32[]{:S(2)}) collective-permute-start(bf16[256,512]{1,0:T(8,128)(2,1)S(1)} %collective-permute-done.9.refs_3_), channel_id=1, source_target_pairs={{0,1},{1,0},{2,3},{3,2},{4,5},{5,4},{6,7},{7,6},{8,9},{9,8},{10,11... | collective-permute-start | bytes 786440 | tf_op jit(solution)/shard_map/ppermute | solution.py:30
  73.5 5.8 %collective-permute-start.18 = (bf16[256,512]{1,0:T(8,128)(2,1)S(1)}, bf16[256,512]{1,0:T(8,128)(2,1)S(1)}, u32[]{:S(2)}, u32[]{:S(2)}) collective-permute-start(bf16[256,512]{1,0:T(8,128)(2,1)S(1)} %collective-permute-done.13.refs_4_), channel_id=1, source_target_pairs={{0,1},{1,0},{2,3},{3,2},{4,5},{5,4},{6,7},{7,6},{8,9},{9,8},{10,11... | collective-permute-start | bytes 786440 | tf_op jit(solution)/shard_map/ppermute | solution.py:30
  76.5 9.2 %collective-permute-start.21 = (bf16[512,256]{1,0:T(8,128)(2,1)S(1)}, bf16[512,256]{1,0:T(8,128)(2,1)S(1)}, u32[]{:S(2)}, u32[]{:S(2)}) collective-permute-start(bf16[512,256]{1,0:T(8,128)(2,1)S(1)} %slice.18), channel_id=1, source_target_pairs={{0,32},{32,64},{64,96},{96,128},{128,160},{160,192},{192,224},{224... | collective-permute-start | bytes 786440 | tf_op jit(solution)/shard_map/ppermute | solution.py:30
  78.1 7.7 %collective-permute-start.22 = (bf16[512,256]{1,0:T(8,128)(2,1)S(1)}, bf16[512,256]{1,0:T(8,128)(2,1)S(1)}, u32[]{:S(2)}, u32[]{:S(2)}) collective-permute-start(bf16[512,256]{1,0:T(8,128)(2,1)S(1)} %slice.19), channel_id=1, source_target_pairs={{0,224},{32,0},{64,32},{96,64},{128,96},{160,128},{192,160},{224,1... | collective-permute-start | bytes 786440 | tf_op jit(solution)/shard_map/ppermute | solution.py:30
  (1 other events, 0.7 us)

commit v14 on v13

--- a/solution.py
+++ b/solution.py
@@ -272,9 +272,9 @@
     here = in_plane(masked)
     other = around(own, "yl", NYL, 1)
     up_own, down_own = up(own), down(own)
-    here, tables = sync((here, make_tables(meta, taps, rows)))
-    here, up_own, down_own = sync((here, up_own, down_own))
+    here, other, tables = sync((here, other, make_tables(meta, taps, rows)))
     here = along_z(here)
+    up_own, down_own, here = sync((up_own, down_own, here))
     up_other, down_other = up(other), down(other)
     up_1 = jnp.concatenate([up_own, up_other], axis=0)
     down_1 = jnp.concatenate([down_own, down_other], axis=0)

time: 88.6 us -> 86.1 us (0.972)
  waiting for transfers between devices: 15.3 us -> 12.3 us
    ppermute x21, waiting for transfers between devices: 12.2 us -> 9.41 us  [around(): return lax.ppermute(block, axis, [(i, (i + step) % n) for i in range(n)])]
    ppermute x21, starting transfers between devices: 44.2 us -> 46.2 us  [around(): return lax.ppermute(block, axis, [(i, (i + step) % n) for i in range(n)])]
    ppermute x1, starting transfers between devices: 8.49 us -> 7.1 us  [in_plane(): return lax.ppermute(block, axes, route)]
  transfers between devices with their start and end apart: 23 -> 23, of which waited for: 9 -> 6; matrix products, arithmetic and copies ran while one was open for 2% -> 2% of each run, Pallas kernels for 11% -> 11%
where the time goes in v14:
time: 86.1 us; the launch traced here: 85.9 us
  starting transfers between devices  57.2 us (66%)
  Pallas kernels  12.4 us (14%)
  waiting for transfers between devices  12.3 us (14%)
  local copies, waits for them, and re-layouts  3.1 us (4%)
    ppermute x21, starting transfers between devices, around(): return lax.ppermute(block, axis, [(i, (i + step) % n) for i in range(n)])  46.2 us
    ppermute x21, waiting for transfers between devices, around(): return lax.ppermute(block, axis, [(i, (i + step) % n) for i in range(n)])  9.41 us
    ppermute x1, starting transfers between devices, in_plane(): return lax.ppermute(block, axes, route)  7.1 us
    pallas_call x2, Pallas kernels, whitened(): pl.pallas_call(kernel, out_shape=jax.ShapeDtypeStruct(shape, BF16), in_sp...  5.3 us
    ppermute x1, starting transfers between devices, along_z(): return lax.ppermute(block, ('z', 'x', 'yh'), route)  3.89 us
    pallas_call x1, Pallas kernels, most_of_product(): pl.pallas_call(most_kernel, out_shape=[jax.ShapeDtypeStruct((cols, cols),...  3.12 us
    ppermute x1, waiting for transfers between devices, along_z(): return lax.ppermute(block, ('z', 'x', 'yh'), route)  2.85 us
    pallas_call x1, Pallas kernels, product(): pl.pallas_call(functools.partial(last_kernel, scale), out_shape=jax.Shape...  2.63 us
  transfers between devices with their start and end apart: 23, of which 6 were waited for; matrix products, arithmetic and copies ran while one was open for 2% of the time, Pallas kernels for 11%

profile of v14, /device:TPU:1, one launch (start us, length us, event | category | flops | bytes accessed | tf_op | source)
XLA Modules:
  0.0 85.9 jit_solution(16562036857320645959)
XLA Ops:
  1.9 2.2 %collective-permute-start.1 = (bf16[512,256]{1,0:T(8,128)(2,1)S(1)}, bf16[512,256]{1,0:T(8,128)(2,1)S(1)}, u32[]{:S(2)}, u32[]{:S(2)}) collective-permute-start(bf16[512,256]{1,0:T(8,128)(2,1)S(1)} %get-tuple-element.25.own), channel_id=1, source_target_pairs={{0,16},{16,0},{1,17},{17,1},{2,18},{18,2},{3,19},{19,3},{4,20},{20... | collective-permute-start | bytes 786440 | tf_op jit(solution)/shard_map/ppermute | solution.py:30
  4.1 7.1 %collective-permute-start = (bf16[256,512]{1,0:T(8,128)(2,1)S(1)}, bf16[256,512]{1,0:T(8,128)(2,1)S(1)}, u32[]{:S(2)}, u32[]{:S(2)}) collective-permute-start(bf16[256,512]{1,0:T(8,128)(2,1)S(1)} %get-tuple-element.24), channel_id=1, source_target_pairs={{0,10},{1,26},{2,8},{3,24},{4,14},{5,30},{6,12},{7,28},{8,2},{9,18... | collective-permute-start | bytes 786440 | tf_op jit(solution)/shard_map/ppermute | solution.py:51
  11.3 5.4 %collective-permute-start.3 = (bf16[512,256]{1,0:T(8,128)(2,1)S(1)}, bf16[512,256]{1,0:T(8,128)(2,1)S(1)}, u32[]{:S(2)}, u32[]{:S(2)}) collective-permute-start(bf16[512,256]{1,0:T(8,128)(2,1)S(1)} %get-tuple-element.25.own), channel_id=1, source_target_pairs={{0,224},{32,0},{64,32},{96,64},{128,96},{160,128},{192,160},{224,1... | collective-permute-start | bytes 786440 | tf_op jit(solution)/shard_map/ppermute | solution.py:30
  18.8 1.1 %tables.1 = (bf16[4,256,512]{2,1,0:T(8,128)(2,1)S(1)}, bf16[4,512,256]{2,1,0:T(8,128)(2,1)S(1)}) custom-call(s32[71]{0:T(128)S(1)} %concatenate.12.meta_ref, bf16[1,256]{1,0:T(2,128)(2,1)S(1)} %broadcast_in_dim.3.taps_ref), custom_call_target="tpu_custom_call" | custom-call | tf_op jit(solution)/shard_map/tables/pallas_call | solution.py:87
  19.9 3.9 %collective-permute-start.4 = (bf16[256,512]{1,0:T(8,128)(2,1)S(1)}, bf16[256,512]{1,0:T(8,128)(2,1)S(1)}, u32[]{:S(2)}, u32[]{:S(2)}) collective-permute-start(bf16[256,512]{1,0:T(8,128)(2,1)S(1)} %collective-permute-done), channel_id=1, source_target_pairs={{10,10},{8,40},{14,78},{12,108},{2,130},{0,160},{4,196},{6,230},{3... | collective-permute-start | bytes 786440 | tf_op jit(solution)/shard_map/ppermute | solution.py:60
  25.4 2.9 %collective-permute-done.4 = bf16[256,512]{1,0:T(8,128)(2,1)S(1)} collective-permute-done((bf16[256,512]{1,0:T(8,128)(2,1)S(1)}, bf16[256,512]{1,0:T(8,128)(2,1)S(1)}, u32[]{:S(2)}, u32[]{:S(2)}) %collective-permute-start.4) | collective-permute-done | bytes 262176 | tf_op jit(solution)/shard_map/ppermute | solution.py:60
  28.2 5.8 %collective-permute-start.7 = (bf16[256,512]{1,0:T(8,128)(2,1)S(1)}, bf16[256,512]{1,0:T(8,128)(2,1)S(1)}, u32[]{:S(2)}, u32[]{:S(2)}) collective-permute-start(bf16[256,512]{1,0:T(8,128)(2,1)S(1)} %collective-permute-done.4), channel_id=1, source_target_pairs={{0,2},{2,0},{1,3},{3,1},{4,6},{6,4},{5,7},{7,5},{8,10},{10,8},{9,1... | collective-permute-start | bytes 786440 | tf_op jit(solution)/shard_map/ppermute | solution.py:30
  34.0 1.6 %collective-permute-done.5 = bf16[512,256]{1,0:T(8,128)(2,1)S(1)} collective-permute-done((bf16[512,256]{1,0:T(8,128)(2,1)S(1)}, bf16[512,256]{1,0:T(8,128)(2,1)S(1)}, u32[]{:S(2)}, u32[]{:S(2)}) %collective-permute-start.5) | collective-permute-done | bytes 262176 | tf_op jit(solution)/shard_map/ppermute | solution.py:30
  35.7 2.1 %collective-permute-done.7 = bf16[256,512]{1,0:T(8,128)(2,1)S(1)} collective-permute-done((bf16[256,512]{1,0:T(8,128)(2,1)S(1)}, bf16[256,512]{1,0:T(8,128)(2,1)S(1)}, u32[]{:S(2)}, u32[]{:S(2)}) %collective-permute-start.7) | collective-permute-done | bytes 262176 | tf_op jit(solution)/shard_map/ppermute | solution.py:30
  39.0 1.9 %collective-permute-start.11 = (bf16[1024,256]{1,0:T(8,128)(2,1)S(1)}, bf16[1024,256]{1,0:T(8,128)(2,1)S(1)}, u32[]{:S(2)}, u32[]{:S(2)}) collective-permute-start(bf16[1024,256]{1,0:T(8,128)(2,1)S(1)} %pad_maximum_fusion.1.down_1), channel_id=1, source_target_pairs={{0,224},{32,0},{64,32},{96,64},{128,96},{160,128},{192,160},{224,1... | collective-permute-start | bytes 1572872 | tf_op jit(solution)/shard_map/ppermute | solution.py:30
  41.0 2.2 %collective-permute-start.12 = (bf16[512,512]{1,0:T(8,128)(2,1)S(1)}, bf16[512,512]{1,0:T(8,128)(2,1)S(1)}, u32[]{:S(2)}, u32[]{:S(2)}) collective-permute-start(bf16[512,512]{1,0:T(8,128)(2,1)S(1)} %pad_maximum_fusion.2.refs_0_), channel_id=1, source_target_pairs={{0,12},{4,0},{8,4},{12,8},{1,13},{5,1},{9,5},{13,9},{2,14},{6,2},{... | collective-permute-start | bytes 1572872 | tf_op jit(solution)/shard_map/ppermute | solution.py:30
  43.2 4.9 %collective-permute-done.10.up_2 = bf16[1024,256]{1,0:T(8,128)(2,1)S(1)} collective-permute-done((bf16[1024,256]{1,0:T(8,128)(2,1)S(1)}, bf16[1024,256]{1,0:T(8,128)(2,1)S(1)}, u32[]{:S(2)}, u32[]{:S(2)}) %collective-permute-start.10) | collective-permute-done | bytes 524320 | tf_op jit(solution)/shard_map/ppermute | solution.py:30
  48.1 9.7 %collective-permute-start.19 = (bf16[1024,256]{1,0:T(8,128)(2,1)S(1)}, bf16[1024,256]{1,0:T(8,128)(2,1)S(1)}, u32[]{:S(2)}, u32[]{:S(2)}) collective-permute-start(bf16[1024,256]{1,0:T(8,128)(2,1)S(1)} %collective-permute-done.10.up_2), channel_id=1, source_target_pairs={{0,32},{32,64},{64,96},{96,128},{128,160},{160,192},{192,224},{224... | collective-permute-start | bytes 1572872 | tf_op jit(solution)/shard_map/ppermute | solution.py:30
  58.6 2.6 %collective-permute-start.13 = (bf16[256,512]{1,0:T(8,128)(2,1)S(1)}, bf16[256,512]{1,0:T(8,128)(2,1)S(1)}, u32[]{:S(2)}, u32[]{:S(2)}) collective-permute-start(bf16[256,512]{1,0:T(8,128)(2,1)S(1)} %slice.17), channel_id=1, source_target_pairs={{0,12},{4,0},{8,4},{12,8},{1,13},{5,1},{9,5},{13,9},{2,14},{6,2},{... | collective-permute-start | bytes 786440 | tf_op jit(solution)/shard_map/ppermute | solution.py:30
  61.2 3.8 %collective-permute-start.14 = (bf16[512,512]{1,0:T(8,128)(2,1)S(1)}, bf16[512,512]{1,0:T(8,128)(2,1)S(1)}, u32[]{:S(2)}, u32[]{:S(2)}) collective-permute-start(bf16[512,512]{1,0:T(8,128)(2,1)S(1)} %pad_maximum_fusion.2.refs_0_), channel_id=1, source_target_pairs={{0,1},{1,0},{2,3},{3,2},{4,5},{5,4},{6,7},{7,6},{8,9},{9,8},{10,11... | collective-permute-start | bytes 1572872 | tf_op jit(solution)/shard_map/ppermute | solution.py:30
  65.0 2.1 %left.1.left_in = bf16[512,4096]{1,0:T(8,128)(2,1)S(1)} custom-call(s32[71]{0:T(128)S(1)} %concatenate.12.meta_ref, bf16[4,512,256]{2,1,0:T(8,128)(2,1)S(1)} %get-tuple-element.28.tables_ref, bf16[512,256]{1,0:T(8,128)(2,1)S(1)} %get-tuple-element.25.own, bf16[512,256]{1,0:T(8,128)(2,1)S(1)} %collective-permute-done.1.other, ...), custom_call_target="tpu_custom_call" | custom-call | tf_op jit(solution)/shard_map/left/pallas_call | solution.py:206
  67.9 1.0 %collective-permute-start.16 = (bf16[512,512]{1,0:T(8,128)(2,1)S(1)}, bf16[512,512]{1,0:T(8,128)(2,1)S(1)}, u32[]{:S(2)}, u32[]{:S(2)}) collective-permute-start(bf16[512,512]{1,0:T(8,128)(2,1)S(1)} %collective-permute-done.12.refs_2_), channel_id=1, source_target_pairs={{0,1},{1,0},{2,3},{3,2},{4,5},{5,4},{6,7},{7,6},{8,9},{9,8},{10,11... | collective-permute-start | bytes 1572872 | tf_op jit(solution)/shard_map/ppermute | solution.py:30
  68.9 2.3 %collective-permute-start.17 = (bf16[256,512]{1,0:T(8,128)(2,1)S(1)}, bf16[256,512]{1,0:T(8,128)(2,1)S(1)}, u32[]{:S(2)}, u32[]{:S(2)}) collective-permute-start(bf16[256,512]{1,0:T(8,128)(2,1)S(1)} %collective-permute-done.9.refs_3_), channel_id=1, source_target_pairs={{0,1},{1,0},{2,3},{3,2},{4,5},{5,4},{6,7},{7,6},{8,9},{9,8},{10,11... | collective-permute-start | bytes 786440 | tf_op jit(solution)/shard_map/ppermute | solution.py:30
  71.3 2.8 %collective-permute-start.18 = (bf16[256,512]{1,0:T(8,128)(2,1)S(1)}, bf16[256,512]{1,0:T(8,128)(2,1)S(1)}, u32[]{:S(2)}, u32[]{:S(2)}) collective-permute-start(bf16[256,512]{1,0:T(8,128)(2,1)S(1)} %collective-permute-done.13.refs_4_), channel_id=1, source_target_pairs={{0,1},{1,0},{2,3},{3,2},{4,5},{5,4},{6,7},{7,6},{8,9},{9,8},{10,11... | collective-permute-start | bytes 786440 | tf_op jit(solution)/shard_map/ppermute | solution.py:30
  74.1 1.5 %collective-permute-start.21 = (bf16[512,256]{1,0:T(8,128)(2,1)S(1)}, bf16[512,256]{1,0:T(8,128)(2,1)S(1)}, u32[]{:S(2)}, u32[]{:S(2)}) collective-permute-start(bf16[512,256]{1,0:T(8,128)(2,1)S(1)} %slice.18), channel_id=1, source_target_pairs={{0,32},{32,64},{64,96},{96,128},{128,160},{160,192},{192,224},{224... | collective-permute-start | bytes 786440 | tf_op jit(solution)/shard_map/ppermute | solution.py:30
  75.6 1.2 %collective-permute-start.22 = (bf16[512,256]{1,0:T(8,128)(2,1)S(1)}, bf16[512,256]{1,0:T(8,128)(2,1)S(1)}, u32[]{:S(2)}, u32[]{:S(2)}) collective-permute-start(bf16[512,256]{1,0:T(8,128)(2,1)S(1)} %slice.19), channel_id=1, source_target_pairs={{0,224},{32,0},{64,32},{96,64},{128,96},{160,128},{192,160},{224,1... | collective-permute-start | bytes 786440 | tf_op jit(solution)/shard_map/ppermute | solution.py:30
  76.8 3.2 %right.1.right_ref = bf16[4096,512]{1,0:T(8,128)(2,1)S(1)} custom-call(s32[71]{0:T(128)S(1)} %concatenate.12.meta_ref, bf16[4,256,512]{2,1,0:T(8,128)(2,1)S(1)} %get-tuple-element.38.tables_ref, bf16[512,512]{1,0:T(8,128)(2,1)S(1)} %pad_maximum_fusion.2.refs_0_, bf16[512,512]{1,0:T(8,128)(2,1)S(1)} %collective-permute-done.8.refs_1_, ...), custom_call_target="tpu_custom_call" | custom-call | tf_op jit(solution)/shard_map/right/pallas_call | solution.py:206
  80.0 3.1 %most.1 = (f32[512,512]{1,0:T(8,128)S(1)}, bf16[512,4096]{1,0:T(8,128)(2,1)S(1)}) custom-call(s32[71]{0:T(128)S(1)} %concatenate.12.meta_ref, bf16[4,512,256]{2,1,0:T(8,128)(2,1)S(1)} %get-tuple-element.28.tables_ref, bf16[512,4096]{1,0:T(8,128)(2,1)S(1)} %left.1.left_in, bf16[4096,512]{1,0:T(8,128)(2,1)S(1)} %right.1.right_ref, ...), custom_call_target="tpu_custom_call", output_to_operand_aliasing={{1}: (2, {})} | custom-call | tf_op jit(solution)/shard_map/most/pallas_call | solution.py:220
  83.3 2.6 %product.1 = f32[512,512]{1,0:T(8,128)} custom-call(s32[71]{0:T(128)S(1)} %concatenate.12.meta_ref, bf16[4,512,256]{2,1,0:T(8,128)(2,1)S(1)} %get-tuple-element.28.tables_ref, f32[512,512]{1,0:T(8,128)S(1)} %get-tuple-element.40.most_ref, bf16[4096,512]{1,0:T(8,128)(2,1)S(1)} %right.1.right_ref, bf16[1024,256]{1,0:T(8,128)(2,1)S(1)} %collective-permute-done.19.up_3, ...), custom_call_target="tpu_custom_call" | custom-call | tf_op jit(solution)/shard_map/product/pallas_call | solution.py:235
  (42 shorter events, 8.0 us)
Async XLA Ops:
  0.0 0.9 %copy-start = (bf16[256,512]{1,0:T(8,128)(2,1)S(1)}, bf16[256,512]{1,0:T(8,128)(2,1)}, u32[]{:S(2)}) copy-start(bf16[256,512]{1,0:T(8,128)(2,1)} %partials_ref.1) | copy-start | bytes 786436
  1.9 18.0 %collective-permute-start.1 = (bf16[512,256]{1,0:T(8,128)(2,1)S(1)}, bf16[512,256]{1,0:T(8,128)(2,1)S(1)}, u32[]{:S(2)}, u32[]{:S(2)}) collective-permute-start(bf16[512,256]{1,0:T(8,128)(2,1)S(1)} %get-tuple-element.25.own), channel_id=1, source_target_pairs={{0,16},{16,0},{1,17},{17,1},{2,18},{18,2},{3,19},{19,3},{4,20},{20... | collective-permute-start | bytes 786440 | tf_op jit(solution)/shard_map/ppermute | solution.py:30
  4.1 15.8 %collective-permute-start = (bf16[256,512]{1,0:T(8,128)(2,1)S(1)}, bf16[256,512]{1,0:T(8,128)(2,1)S(1)}, u32[]{:S(2)}, u32[]{:S(2)}) collective-permute-start(bf16[256,512]{1,0:T(8,128)(2,1)S(1)} %get-tuple-element.24), channel_id=1, source_target_pairs={{0,10},{1,26},{2,8},{3,24},{4,14},{5,30},{6,12},{7,28},{8,2},{9,18... | collective-permute-start | bytes 786440 | tf_op jit(solution)/shard_map/ppermute | solution.py:51
  11.2 14.1 %collective-permute-start.2 = (bf16[512,256]{1,0:T(8,128)(2,1)S(1)}, bf16[512,256]{1,0:T(8,128)(2,1)S(1)}, u32[]{:S(2)}, u32[]{:S(2)}) collective-permute-start(bf16[512,256]{1,0:T(8,128)(2,1)S(1)} %get-tuple-element.25.own), channel_id=1, source_target_pairs={{0,32},{32,64},{64,96},{96,128},{128,160},{160,192},{192,224},{224... | collective-permute-start | bytes 786440 | tf_op jit(solution)/shard_map/ppermute | solution.py:30
  11.3 14.0 %collective-permute-start.3 = (bf16[512,256]{1,0:T(8,128)(2,1)S(1)}, bf16[512,256]{1,0:T(8,128)(2,1)S(1)}, u32[]{:S(2)}, u32[]{:S(2)}) collective-permute-start(bf16[512,256]{1,0:T(8,128)(2,1)S(1)} %get-tuple-element.25.own), channel_id=1, source_target_pairs={{0,224},{32,0},{64,32},{96,64},{128,96},{160,128},{192,160},{224,1... | collective-permute-start | bytes 786440 | tf_op jit(solution)/shard_map/ppermute | solution.py:30
  19.9 8.3 %collective-permute-start.4 = (bf16[256,512]{1,0:T(8,128)(2,1)S(1)}, bf16[256,512]{1,0:T(8,128)(2,1)S(1)}, u32[]{:S(2)}, u32[]{:S(2)}) collective-permute-start(bf16[256,512]{1,0:T(8,128)(2,1)S(1)} %collective-permute-done), channel_id=1, source_target_pairs={{10,10},{8,40},{14,78},{12,108},{2,130},{0,160},{4,196},{6,230},{3... | collective-permute-start | bytes 786440 | tf_op jit(solution)/shard_map/ppermute | solution.py:60
  23.8 10.2 %collective-permute-start.6 = (bf16[512,256]{1,0:T(8,128)(2,1)S(1)}, bf16[512,256]{1,0:T(8,128)(2,1)S(1)}, u32[]{:S(2)}, u32[]{:S(2)}) collective-permute-start(bf16[512,256]{1,0:T(8,128)(2,1)S(1)} %collective-permute-done.1.other), channel_id=1, source_target_pairs={{0,224},{32,0},{64,32},{96,64},{128,96},{160,128},{192,160},{224,1... | collective-permute-start | bytes 786440 | tf_op jit(solution)/shard_map/ppermute | solution.py:30
  24.4 11.3 %collective-permute-start.5 = (bf16[512,256]{1,0:T(8,128)(2,1)S(1)}, bf16[512,256]{1,0:T(8,128)(2,1)S(1)}, u32[]{:S(2)}, u32[]{:S(2)}) collective-permute-start(bf16[512,256]{1,0:T(8,128)(2,1)S(1)} %collective-permute-done.1.other), channel_id=1, source_target_pairs={{0,32},{32,64},{64,96},{96,128},{128,160},{160,192},{192,224},{224... | collective-permute-start | bytes 786440 | tf_op jit(solution)/shard_map/ppermute | solution.py:30
  28.2 9.5 %collective-permute-start.7 = (bf16[256,512]{1,0:T(8,128)(2,1)S(1)}, bf16[256,512]{1,0:T(8,128)(2,1)S(1)}, u32[]{:S(2)}, u32[]{:S(2)}) collective-permute-start(bf16[256,512]{1,0:T(8,128)(2,1)S(1)} %collective-permute-done.4), channel_id=1, source_target_pairs={{0,2},{2,0},{1,3},{3,1},{4,6},{6,4},{5,7},{7,5},{8,10},{10,8},{9,1... | collective-permute-start | bytes 786440 | tf_op jit(solution)/shard_map/ppermute | solution.py:30
  37.8 10.4 %collective-permute-start.10 = (bf16[1024,256]{1,0:T(8,128)(2,1)S(1)}, bf16[1024,256]{1,0:T(8,128)(2,1)S(1)}, u32[]{:S(2)}, u32[]{:S(2)}) collective-permute-start(bf16[1024,256]{1,0:T(8,128)(2,1)S(1)} %pad_maximum_fusion.up_1), channel_id=1, source_target_pairs={{0,32},{32,64},{64,96},{96,128},{128,160},{160,192},{192,224},{224... | collective-permute-start | bytes 1572872 | tf_op jit(solution)/shard_map/ppermute | solution.py:30
  38.0 19.8 %collective-permute-start.8 = (bf16[512,512]{1,0:T(8,128)(2,1)S(1)}, bf16[512,512]{1,0:T(8,128)(2,1)S(1)}, u32[]{:S(2)}, u32[]{:S(2)}) collective-permute-start(bf16[512,512]{1,0:T(8,128)(2,1)S(1)} %pad_maximum_fusion.2.refs_0_), channel_id=1, source_target_pairs={{0,4},{4,8},{8,12},{12,0},{1,5},{5,9},{9,13},{13,1},{2,6},{6,10},{... | collective-permute-start | bytes 1572872 | tf_op jit(solution)/shard_map/ppermute | solution.py:30
  39.0 19.5 %collective-permute-start.11 = (bf16[1024,256]{1,0:T(8,128)(2,1)S(1)}, bf16[1024,256]{1,0:T(8,128)(2,1)S(1)}, u32[]{:S(2)}, u32[]{:S(2)}) collective-permute-start(bf16[1024,256]{1,0:T(8,128)(2,1)S(1)} %pad_maximum_fusion.1.down_1), channel_id=1, source_target_pairs={{0,224},{32,0},{64,32},{96,64},{128,96},{160,128},{192,160},{224,1... | collective-permute-start | bytes 1572872 | tf_op jit(solution)/shard_map/ppermute | solution.py:30
  41.0 17.6 %collective-permute-start.12 = (bf16[512,512]{1,0:T(8,128)(2,1)S(1)}, bf16[512,512]{1,0:T(8,128)(2,1)S(1)}, u32[]{:S(2)}, u32[]{:S(2)}) collective-permute-start(bf16[512,512]{1,0:T(8,128)(2,1)S(1)} %pad_maximum_fusion.2.refs_0_), channel_id=1, source_target_pairs={{0,12},{4,0},{8,4},{12,8},{1,13},{5,1},{9,5},{13,9},{2,14},{6,2},{... | collective-permute-start | bytes 1572872 | tf_op jit(solution)/shard_map/ppermute | solution.py:30
  48.1 20.8 %collective-permute-start.19 = (bf16[1024,256]{1,0:T(8,128)(2,1)S(1)}, bf16[1024,256]{1,0:T(8,128)(2,1)S(1)}, u32[]{:S(2)}, u32[]{:S(2)}) collective-permute-start(bf16[1024,256]{1,0:T(8,128)(2,1)S(1)} %collective-permute-done.10.up_2), channel_id=1, source_target_pairs={{0,32},{32,64},{64,96},{96,128},{128,160},{160,192},{192,224},{224... | collective-permute-start | bytes 1572872 | tf_op jit(solution)/shard_map/ppermute | solution.py:30
  57.8 9.3 %collective-permute-start.9 = (bf16[256,512]{1,0:T(8,128)(2,1)S(1)}, bf16[256,512]{1,0:T(8,128)(2,1)S(1)}, u32[]{:S(2)}, u32[]{:S(2)}) collective-permute-start(bf16[256,512]{1,0:T(8,128)(2,1)S(1)} %slice.16), channel_id=1, source_target_pairs={{0,4},{4,8},{8,12},{12,0},{1,5},{5,9},{9,13},{13,1},{2,6},{6,10},{... | collective-permute-start | bytes 786440 | tf_op jit(solution)/shard_map/ppermute | solution.py:30
  58.6 12.7 %collective-permute-start.20 = (bf16[1024,256]{1,0:T(8,128)(2,1)S(1)}, bf16[1024,256]{1,0:T(8,128)(2,1)S(1)}, u32[]{:S(2)}, u32[]{:S(2)}) collective-permute-start(bf16[1024,256]{1,0:T(8,128)(2,1)S(1)} %collective-permute-done.11.down_2), channel_id=1, source_target_pairs={{0,224},{32,0},{64,32},{96,64},{128,96},{160,128},{192,160},{224,1... | collective-permute-start | bytes 1572872 | tf_op jit(solution)/shard_map/ppermute | solution.py:30
  58.6 9.3 %collective-permute-start.13 = (bf16[256,512]{1,0:T(8,128)(2,1)S(1)}, bf16[256,512]{1,0:T(8,128)(2,1)S(1)}, u32[]{:S(2)}, u32[]{:S(2)}) collective-permute-start(bf16[256,512]{1,0:T(8,128)(2,1)S(1)} %slice.17), channel_id=1, source_target_pairs={{0,12},{4,0},{8,4},{12,8},{1,13},{5,1},{9,5},{13,9},{2,14},{6,2},{... | collective-permute-start | bytes 786440 | tf_op jit(solution)/shard_map/ppermute | solution.py:30
  61.2 12.8 %collective-permute-start.14 = (bf16[512,512]{1,0:T(8,128)(2,1)S(1)}, bf16[512,512]{1,0:T(8,128)(2,1)S(1)}, u32[]{:S(2)}, u32[]{:S(2)}) collective-permute-start(bf16[512,512]{1,0:T(8,128)(2,1)S(1)} %pad_maximum_fusion.2.refs_0_), channel_id=1, source_target_pairs={{0,1},{1,0},{2,3},{3,2},{4,5},{5,4},{6,7},{7,6},{8,9},{9,8},{10,11... | collective-permute-start | bytes 1572872 | tf_op jit(solution)/shard_map/ppermute | solution.py:30
  67.2 9.7 %collective-permute-start.15 = (bf16[512,512]{1,0:T(8,128)(2,1)S(1)}, bf16[512,512]{1,0:T(8,128)(2,1)S(1)}, u32[]{:S(2)}, u32[]{:S(2)}) collective-permute-start(bf16[512,512]{1,0:T(8,128)(2,1)S(1)} %collective-permute-done.8.refs_1_), channel_id=1, source_target_pairs={{0,1},{1,0},{2,3},{3,2},{4,5},{5,4},{6,7},{7,6},{8,9},{9,8},{10,11... | collective-permute-start | bytes 1572872 | tf_op jit(solution)/shard_map/ppermute | solution.py:30
  67.9 8.9 %collective-permute-start.16 = (bf16[512,512]{1,0:T(8,128)(2,1)S(1)}, bf16[512,512]{1,0:T(8,128)(2,1)S(1)}, u32[]{:S(2)}, u32[]{:S(2)}) collective-permute-start(bf16[512,512]{1,0:T(8,128)(2,1)S(1)} %collective-permute-done.12.refs_2_), channel_id=1, source_target_pairs={{0,1},{1,0},{2,3},{3,2},{4,5},{5,4},{6,7},{7,6},{8,9},{9,8},{10,11... | collective-permute-start | bytes 1572872 | tf_op jit(solution)/shard_map/ppermute | solution.py:30
  68.9 6.7 %collective-permute-start.17 = (bf16[256,512]{1,0:T(8,128)(2,1)S(1)}, bf16[256,512]{1,0:T(8,128)(2,1)S(1)}, u32[]{:S(2)}, u32[]{:S(2)}) collective-permute-start(bf16[256,512]{1,0:T(8,128)(2,1)S(1)} %collective-permute-done.9.refs_3_), channel_id=1, source_target_pairs={{0,1},{1,0},{2,3},{3,2},{4,5},{5,4},{6,7},{7,6},{8,9},{9,8},{10,11... | collective-permute-start | bytes 786440 | tf_op jit(solution)/shard_map/ppermute | solution.py:30
  71.3 5.6 %collective-permute-start.18 = (bf16[256,512]{1,0:T(8,128)(2,1)S(1)}, bf16[256,512]{1,0:T(8,128)(2,1)S(1)}, u32[]{:S(2)}, u32[]{:S(2)}) collective-permute-start(bf16[256,512]{1,0:T(8,128)(2,1)S(1)} %collective-permute-done.13.refs_4_), channel_id=1, source_target_pairs={{0,1},{1,0},{2,3},{3,2},{4,5},{5,4},{6,7},{7,6},{8,9},{9,8},{10,11... | collective-permute-start | bytes 786440 | tf_op jit(solution)/shard_map/ppermute | solution.py:30
  74.1 9.2 %collective-permute-start.21 = (bf16[512,256]{1,0:T(8,128)(2,1)S(1)}, bf16[512,256]{1,0:T(8,128)(2,1)S(1)}, u32[]{:S(2)}, u32[]{:S(2)}) collective-permute-start(bf16[512,256]{1,0:T(8,128)(2,1)S(1)} %slice.18), channel_id=1, source_target_pairs={{0,32},{32,64},{64,96},{96,128},{128,160},{160,192},{192,224},{224... | collective-permute-start | bytes 786440 | tf_op jit(solution)/shard_map/ppermute | solution.py:30
  75.6 7.7 %collective-permute-start.22 = (bf16[512,256]{1,0:T(8,128)(2,1)S(1)}, bf16[512,256]{1,0:T(8,128)(2,1)S(1)}, u32[]{:S(2)}, u32[]{:S(2)}) collective-permute-start(bf16[512,256]{1,0:T(8,128)(2,1)S(1)} %slice.19), channel_id=1, source_target_pairs={{0,224},{32,0},{64,32},{96,64},{128,96},{160,128},{192,160},{224,1... | collective-permute-start | bytes 786440 | tf_op jit(solution)/shard_map/ppermute | solution.py:30
  (1 other events, 0.7 us)

commit v15 on v12

--- a/solution.py
+++ b/solution.py
@@ -269,9 +269,9 @@
     here = in_plane(masked)
     other = around(own, "yl", NYL, 1)
     up_own, down_own = up(own), down(own)
-    here, tables = sync((here, make_tables(meta, taps, rows)))
-    here, up_own, down_own = sync((here, up_own, down_own))
+    here, other, tables = sync((here, other, make_tables(meta, taps, rows)))
     here = along_z(here)
+    up_own, down_own, here = sync((up_own, down_own, here))
     up_other, down_other = up(other), down(other)
     up_1 = jnp.concatenate([up_own, up_other], axis=0)
     down_1 = jnp.concatenate([down_own, down_other], axis=0)

time: 88.7 us -> 85.9 us (0.968)
  waiting for transfers between devices: 18.5 us -> 11.1 us
  starting transfers between devices: 53.5 us -> 58.2 us
    ppermute x19, waiting for transfers between devices: 15.5 us -> 8.28 us  [around(): return lax.ppermute(block, axis, [(i, (i + step) % n) for i in range(n)])]
    ppermute x19, starting transfers between devices: 41.1 us -> 47.2 us  [around(): return lax.ppermute(block, axis, [(i, (i + step) % n) for i in range(n)])]
    ppermute x1, starting transfers between devices: 8.49 us -> 7.1 us  [in_plane(): return lax.ppermute(block, axes, route)]
where the time goes in v15:
time: 85.9 us; the launch traced here: 85.7 us
  starting transfers between devices  58.2 us (68%)
  Pallas kernels  12.4 us (14%)
  waiting for transfers between devices  11.1 us (13%)
  local copies, waits for them, and re-layouts  3.07 us (4%)
    ppermute x19, starting transfers between devices, around(): return lax.ppermute(block, axis, [(i, (i + step) % n) for i in range(n)])  47.2 us
    ppermute x19, waiting for transfers between devices, around(): return lax.ppermute(block, axis, [(i, (i + step) % n) for i in range(n)])  8.28 us
    ppermute x1, starting transfers between devices, in_plane(): return lax.ppermute(block, axes, route)  7.1 us
    pallas_call x2, Pallas kernels, whitened(): pl.pallas_call(kernel, out_shape=jax.ShapeDtypeStruct(shape, BF16), in_sp...  5.3 us
    ppermute x1, starting transfers between devices, along_z(): return lax.ppermute(block, ('z', 'x', 'yh'), route)  3.89 us
    pallas_call x1, Pallas kernels, most_of_product(): pl.pallas_call(most_kernel, out_shape=[jax.ShapeDtypeStruct((cols, cols),...  3.12 us
    ppermute x1, waiting for transfers between devices, along_z(): return lax.ppermute(block, ('z', 'x', 'yh'), route)  2.85 us
    pallas_call x1, Pallas kernels, product(): pl.pallas_call(functools.partial(last_kernel, scale), out_shape=jax.Shape...  2.63 us
  transfers between devices with their start and end apart: 21, of which 7 were waited for; matrix products, arithmetic and copies ran while one was open for 2% of the time, Pallas kernels for 11%

profile of v15, /device:TPU:1, one launch (start us, length us, event | category | flops | bytes accessed | tf_op | source)
XLA Modules:
  0.0 85.7 jit_solution(2194787646798765625)
XLA Ops:
  0.0 0.9 %copy-done = bf16[256,512]{1,0:T(8,128)(2,1)S(1)} copy-done((bf16[256,512]{1,0:T(8,128)(2,1)S(1)}, bf16[256,512]{1,0:T(8,128)(2,1)}, u32[]{:S(2)}) %copy-start) | copy-done | bytes 262168
  1.9 2.2 %collective-permute-start.1 = (bf16[512,256]{1,0:T(8,128)(2,1)S(1)}, bf16[512,256]{1,0:T(8,128)(2,1)S(1)}, u32[]{:S(2)}, u32[]{:S(2)}) collective-permute-start(bf16[512,256]{1,0:T(8,128)(2,1)S(1)} %get-tuple-element.25.own), channel_id=1, source_target_pairs={{0,16},{16,0},{1,17},{17,1},{2,18},{18,2},{3,19},{19,3},{4,20},{20... | collective-permute-start | bytes 786440 | tf_op jit(solution)/shard_map/ppermute | solution.py:30
  4.1 7.1 %collective-permute-start = (bf16[256,512]{1,0:T(8,128)(2,1)S(1)}, bf16[256,512]{1,0:T(8,128)(2,1)S(1)}, u32[]{:S(2)}, u32[]{:S(2)}) collective-permute-start(bf16[256,512]{1,0:T(8,128)(2,1)S(1)} %get-tuple-element.24), channel_id=1, source_target_pairs={{0,10},{1,26},{2,8},{3,24},{4,14},{5,30},{6,12},{7,28},{8,2},{9,18... | collective-permute-start | bytes 786440 | tf_op jit(solution)/shard_map/ppermute | solution.py:51
  11.3 5.4 %collective-permute-start.3 = (bf16[512,256]{1,0:T(8,128)(2,1)S(1)}, bf16[512,256]{1,0:T(8,128)(2,1)S(1)}, u32[]{:S(2)}, u32[]{:S(2)}) collective-permute-start(bf16[512,256]{1,0:T(8,128)(2,1)S(1)} %get-tuple-element.25.own), channel_id=1, source_target_pairs={{0,224},{32,0},{64,32},{96,64},{128,96},{160,128},{192,160},{224,1... | collective-permute-start | bytes 786440 | tf_op jit(solution)/shard_map/ppermute | solution.py:30
  18.8 1.1 %tables.1 = (bf16[4,256,512]{2,1,0:T(8,128)(2,1)S(1)}, bf16[4,512,256]{2,1,0:T(8,128)(2,1)S(1)}) custom-call(s32[71]{0:T(128)S(1)} %concatenate.12.meta_ref, bf16[1,256]{1,0:T(2,128)(2,1)S(1)} %broadcast_in_dim.3.taps_ref), custom_call_target="tpu_custom_call" | custom-call | tf_op jit(solution)/shard_map/tables/pallas_call | solution.py:87
  19.9 3.9 %collective-permute-start.4 = (bf16[256,512]{1,0:T(8,128)(2,1)S(1)}, bf16[256,512]{1,0:T(8,128)(2,1)S(1)}, u32[]{:S(2)}, u32[]{:S(2)}) collective-permute-start(bf16[256,512]{1,0:T(8,128)(2,1)S(1)} %collective-permute-done), channel_id=1, source_target_pairs={{10,10},{8,40},{14,78},{12,108},{2,130},{0,160},{4,196},{6,230},{3... | collective-permute-start | bytes 786440 | tf_op jit(solution)/shard_map/ppermute | solution.py:60
  24.4 1.0 %collective-permute-start.5 = (bf16[512,256]{1,0:T(8,128)(2,1)S(1)}, bf16[512,256]{1,0:T(8,128)(2,1)S(1)}, u32[]{:S(2)}, u32[]{:S(2)}) collective-permute-start(bf16[512,256]{1,0:T(8,128)(2,1)S(1)} %collective-permute-done.1.other), channel_id=1, source_target_pairs={{0,32},{32,64},{64,96},{96,128},{128,160},{160,192},{192,224},{224... | collective-permute-start | bytes 786440 | tf_op jit(solution)/shard_map/ppermute | solution.py:30
  25.4 2.9 %collective-permute-done.4 = bf16[256,512]{1,0:T(8,128)(2,1)S(1)} collective-permute-done((bf16[256,512]{1,0:T(8,128)(2,1)S(1)}, bf16[256,512]{1,0:T(8,128)(2,1)S(1)}, u32[]{:S(2)}, u32[]{:S(2)}) %collective-permute-start.4) | collective-permute-done | bytes 262176 | tf_op jit(solution)/shard_map/ppermute | solution.py:60
  28.2 5.8 %collective-permute-start.7 = (bf16[256,512]{1,0:T(8,128)(2,1)S(1)}, bf16[256,512]{1,0:T(8,128)(2,1)S(1)}, u32[]{:S(2)}, u32[]{:S(2)}) collective-permute-start(bf16[256,512]{1,0:T(8,128)(2,1)S(1)} %collective-permute-done.4), channel_id=1, source_target_pairs={{0,2},{2,0},{1,3},{3,1},{4,6},{6,4},{5,7},{7,5},{8,10},{10,8},{9,1... | collective-permute-start | bytes 786440 | tf_op jit(solution)/shard_map/ppermute | solution.py:30
  34.0 1.6 %collective-permute-done.5 = bf16[512,256]{1,0:T(8,128)(2,1)S(1)} collective-permute-done((bf16[512,256]{1,0:T(8,128)(2,1)S(1)}, bf16[512,256]{1,0:T(8,128)(2,1)S(1)}, u32[]{:S(2)}, u32[]{:S(2)}) %collective-permute-start.5) | collective-permute-done | bytes 262176 | tf_op jit(solution)/shard_map/ppermute | solution.py:30
  35.7 2.1 %collective-permute-done.7 = bf16[256,512]{1,0:T(8,128)(2,1)S(1)} collective-permute-done((bf16[256,512]{1,0:T(8,128)(2,1)S(1)}, bf16[256,512]{1,0:T(8,128)(2,1)S(1)}, u32[]{:S(2)}, u32[]{:S(2)}) %collective-permute-start.7) | collective-permute-done | bytes 262176 | tf_op jit(solution)/shard_map/ppermute | solution.py:30
  38.0 2.5 %collective-permute-start.10 = (bf16[1024,256]{1,0:T(8,128)(2,1)S(1)}, bf16[1024,256]{1,0:T(8,128)(2,1)S(1)}, u32[]{:S(2)}, u32[]{:S(2)}) collective-permute-start(bf16[1024,256]{1,0:T(8,128)(2,1)S(1)} %pad_maximum_fusion.1.down_1), channel_id=1, source_target_pairs={{0,224},{32,0},{64,32},{96,64},{128,96},{160,128},{192,160},{224,1... | collective-permute-start | bytes 1572872 | tf_op jit(solution)/shard_map/ppermute | solution.py:30
  40.5 6.8 %collective-permute-start.8 = (bf16[512,512]{1,0:T(8,128)(2,1)S(1)}, bf16[512,512]{1,0:T(8,128)(2,1)S(1)}, u32[]{:S(2)}, u32[]{:S(2)}) collective-permute-start(bf16[512,512]{1,0:T(8,128)(2,1)S(1)} %pad_maximum_fusion.2.refs_0_), channel_id=1, source_target_pairs={{0,8},{4,12},{8,0},{12,4},{1,9},{5,13},{9,1},{13,5},{2,10},{6,14},... | collective-permute-start | bytes 1572872 | tf_op jit(solution)/shard_map/ppermute | solution.py:30
  47.3 2.7 %collective-permute-start.12 = (bf16[512,512]{1,0:T(8,128)(2,1)S(1)}, bf16[512,512]{1,0:T(8,128)(2,1)S(1)}, u32[]{:S(2)}, u32[]{:S(2)}) collective-permute-start(bf16[512,512]{1,0:T(8,128)(2,1)S(1)} %pad_maximum_fusion.2.refs_0_), channel_id=1, source_target_pairs={{0,12},{4,0},{8,4},{12,8},{1,13},{5,1},{9,5},{13,9},{2,14},{6,2},{... | collective-permute-start | bytes 1572872 | tf_op jit(solution)/shard_map/ppermute | solution.py:30
  50.0 7.8 %collective-permute-start.17 = (bf16[1024,256]{1,0:T(8,128)(2,1)S(1)}, bf16[1024,256]{1,0:T(8,128)(2,1)S(1)}, u32[]{:S(2)}, u32[]{:S(2)}) collective-permute-start(bf16[1024,256]{1,0:T(8,128)(2,1)S(1)} %collective-permute-done.9.up_2), channel_id=1, source_target_pairs={{0,32},{32,64},{64,96},{96,128},{128,160},{160,192},{192,224},{224... | collective-permute-start | bytes 1572872 | tf_op jit(solution)/shard_map/ppermute | solution.py:30
  57.8 0.7 collective-permute-done.10.down_2
  58.6 6.4 %collective-permute-start.13 = (bf16[512,512]{1,0:T(8,128)(2,1)S(1)}, bf16[512,512]{1,0:T(8,128)(2,1)S(1)}, u32[]{:S(2)}, u32[]{:S(2)}) collective-permute-start(bf16[512,512]{1,0:T(8,128)(2,1)S(1)} %pad_maximum_fusion.2.refs_0_), channel_id=1, source_target_pairs={{0,1},{1,0},{2,3},{3,2},{4,5},{5,4},{6,7},{7,6},{8,9},{9,8},{10,11... | collective-permute-start | bytes 1572872 | tf_op jit(solution)/shard_map/ppermute | solution.py:30
  65.0 2.1 %left.1.left_in = bf16[512,4096]{1,0:T(8,128)(2,1)S(1)} custom-call(s32[71]{0:T(128)S(1)} %concatenate.12.meta_ref, bf16[4,512,256]{2,1,0:T(8,128)(2,1)S(1)} %get-tuple-element.28.tables_ref, bf16[512,256]{1,0:T(8,128)(2,1)S(1)} %get-tuple-element.25.own, bf16[512,256]{1,0:T(8,128)(2,1)S(1)} %collective-permute-done.1.other, ...), custom_call_target="tpu_custom_call" | custom-call | tf_op jit(solution)/shard_map/left/pallas_call | solution.py:205
  67.1 3.2 %collective-permute-done.11.refs_1_ = bf16[512,512]{1,0:T(8,128)(2,1)S(1)} collective-permute-done((bf16[512,512]{1,0:T(8,128)(2,1)S(1)}, bf16[512,512]{1,0:T(8,128)(2,1)S(1)}, u32[]{:S(2)}, u32[]{:S(2)}) %collective-permute-start.11) | collective-permute-done | bytes 524320 | tf_op jit(solution)/shard_map/ppermute | solution.py:30
  70.3 1.2 %collective-permute-start.16 = (bf16[512,512]{1,0:T(8,128)(2,1)S(1)}, bf16[512,512]{1,0:T(8,128)(2,1)S(1)}, u32[]{:S(2)}, u32[]{:S(2)}) collective-permute-start(bf16[512,512]{1,0:T(8,128)(2,1)S(1)} %collective-permute-done.8.refs_3_), channel_id=1, source_target_pairs={{0,1},{1,0},{2,3},{3,2},{4,5},{5,4},{6,7},{7,6},{8,9},{9,8},{10,11... | collective-permute-start | bytes 1572872 | tf_op jit(solution)/shard_map/ppermute | solution.py:30
  72.0 3.5 %collective-permute-start.19 = (bf16[512,256]{1,0:T(8,128)(2,1)S(1)}, bf16[512,256]{1,0:T(8,128)(2,1)S(1)}, u32[]{:S(2)}, u32[]{:S(2)}) collective-permute-start(bf16[512,256]{1,0:T(8,128)(2,1)S(1)} %slice.8), channel_id=1, source_target_pairs={{0,32},{32,64},{64,96},{96,128},{128,160},{160,192},{192,224},{224... | collective-permute-start | bytes 786440 | tf_op jit(solution)/shard_map/ppermute | solution.py:30
  76.1 3.2 %right.1.right_ref = bf16[4096,512]{1,0:T(8,128)(2,1)S(1)} custom-call(s32[71]{0:T(128)S(1)} %concatenate.12.meta_ref, bf16[4,256,512]{2,1,0:T(8,128)(2,1)S(1)} %get-tuple-element.38.tables_ref, bf16[512,512]{1,0:T(8,128)(2,1)S(1)} %pad_maximum_fusion.2.refs_0_, bf16[512,512]{1,0:T(8,128)(2,1)S(1)} %collective-permute-done.11.refs_1_, ...), custom_call_target="tpu_custom_call" | custom-call | tf_op jit(solution)/shard_map/right/pallas_call | solution.py:205
  79.3 3.1 %most.1 = (f32[512,512]{1,0:T(8,128)S(1)}, bf16[512,4096]{1,0:T(8,128)(2,1)S(1)}) custom-call(s32[71]{0:T(128)S(1)} %concatenate.12.meta_ref, bf16[4,512,256]{2,1,0:T(8,128)(2,1)S(1)} %get-tuple-element.28.tables_ref, bf16[512,4096]{1,0:T(8,128)(2,1)S(1)} %left.1.left_in, bf16[4096,512]{1,0:T(8,128)(2,1)S(1)} %right.1.right_ref, ...), custom_call_target="tpu_custom_call", output_to_operand_aliasing={{1}: (2, {})} | custom-call | tf_op jit(solution)/shard_map/most/pallas_call | solution.py:219
  83.1 2.6 %product.1 = f32[512,512]{1,0:T(8,128)} custom-call(s32[71]{0:T(128)S(1)} %concatenate.12.meta_ref, bf16[4,512,256]{2,1,0:T(8,128)(2,1)S(1)} %get-tuple-element.28.tables_ref, f32[512,512]{1,0:T(8,128)S(1)} %get-tuple-element.40.most_ref, bf16[4096,512]{1,0:T(8,128)(2,1)S(1)} %right.1.right_ref, bf16[1024,256]{1,0:T(8,128)(2,1)S(1)} %collective-permute-done.17.up_3, ...), custom_call_target="tpu_custom_call" | custom-call | tf_op jit(solution)/shard_map/product/pallas_call | solution.py:234
  (36 shorter events, 5.1 us)
Async XLA Ops:
  0.0 0.9 %copy-start = (bf16[256,512]{1,0:T(8,128)(2,1)S(1)}, bf16[256,512]{1,0:T(8,128)(2,1)}, u32[]{:S(2)}) copy-start(bf16[256,512]{1,0:T(8,128)(2,1)} %partials_ref.1) | copy-start | bytes 786436
  1.0 0.7 copy-start.1
  1.9 18.0 %collective-permute-start.1 = (bf16[512,256]{1,0:T(8,128)(2,1)S(1)}, bf16[512,256]{1,0:T(8,128)(2,1)S(1)}, u32[]{:S(2)}, u32[]{:S(2)}) collective-permute-start(bf16[512,256]{1,0:T(8,128)(2,1)S(1)} %get-tuple-element.25.own), channel_id=1, source_target_pairs={{0,16},{16,0},{1,17},{17,1},{2,18},{18,2},{3,19},{19,3},{4,20},{20... | collective-permute-start | bytes 786440 | tf_op jit(solution)/shard_map/ppermute | solution.py:30
  4.1 15.8 %collective-permute-start = (bf16[256,512]{1,0:T(8,128)(2,1)S(1)}, bf16[256,512]{1,0:T(8,128)(2,1)S(1)}, u32[]{:S(2)}, u32[]{:S(2)}) collective-permute-start(bf16[256,512]{1,0:T(8,128)(2,1)S(1)} %get-tuple-element.24), channel_id=1, source_target_pairs={{0,10},{1,26},{2,8},{3,24},{4,14},{5,30},{6,12},{7,28},{8,2},{9,18... | collective-permute-start | bytes 786440 | tf_op jit(solution)/shard_map/ppermute | solution.py:51
  11.2 14.1 %collective-permute-start.2 = (bf16[512,256]{1,0:T(8,128)(2,1)S(1)}, bf16[512,256]{1,0:T(8,128)(2,1)S(1)}, u32[]{:S(2)}, u32[]{:S(2)}) collective-permute-start(bf16[512,256]{1,0:T(8,128)(2,1)S(1)} %get-tuple-element.25.own), channel_id=1, source_target_pairs={{0,32},{32,64},{64,96},{96,128},{128,160},{160,192},{192,224},{224... | collective-permute-start | bytes 786440 | tf_op jit(solution)/shard_map/ppermute | solution.py:30
  11.3 14.0 %collective-permute-start.3 = (bf16[512,256]{1,0:T(8,128)(2,1)S(1)}, bf16[512,256]{1,0:T(8,128)(2,1)S(1)}, u32[]{:S(2)}, u32[]{:S(2)}) collective-permute-start(bf16[512,256]{1,0:T(8,128)(2,1)S(1)} %get-tuple-element.25.own), channel_id=1, source_target_pairs={{0,224},{32,0},{64,32},{96,64},{128,96},{160,128},{192,160},{224,1... | collective-permute-start | bytes 786440 | tf_op jit(solution)/shard_map/ppermute | solution.py:30
  19.9 8.3 %collective-permute-start.4 = (bf16[256,512]{1,0:T(8,128)(2,1)S(1)}, bf16[256,512]{1,0:T(8,128)(2,1)S(1)}, u32[]{:S(2)}, u32[]{:S(2)}) collective-permute-start(bf16[256,512]{1,0:T(8,128)(2,1)S(1)} %collective-permute-done), channel_id=1, source_target_pairs={{10,10},{8,40},{14,78},{12,108},{2,130},{0,160},{4,196},{6,230},{3... | collective-permute-start | bytes 786440 | tf_op jit(solution)/shard_map/ppermute | solution.py:60
  23.8 10.2 %collective-permute-start.6 = (bf16[512,256]{1,0:T(8,128)(2,1)S(1)}, bf16[512,256]{1,0:T(8,128)(2,1)S(1)}, u32[]{:S(2)}, u32[]{:S(2)}) collective-permute-start(bf16[512,256]{1,0:T(8,128)(2,1)S(1)} %collective-permute-done.1.other), channel_id=1, source_target_pairs={{0,224},{32,0},{64,32},{96,64},{128,96},{160,128},{192,160},{224,1... | collective-permute-start | bytes 786440 | tf_op jit(solution)/shard_map/ppermute | solution.py:30
  24.4 11.3 %collective-permute-start.5 = (bf16[512,256]{1,0:T(8,128)(2,1)S(1)}, bf16[512,256]{1,0:T(8,128)(2,1)S(1)}, u32[]{:S(2)}, u32[]{:S(2)}) collective-permute-start(bf16[512,256]{1,0:T(8,128)(2,1)S(1)} %collective-permute-done.1.other), channel_id=1, source_target_pairs={{0,32},{32,64},{64,96},{96,128},{128,160},{160,192},{192,224},{224... | collective-permute-start | bytes 786440 | tf_op jit(solution)/shard_map/ppermute | solution.py:30
  28.2 9.5 %collective-permute-start.7 = (bf16[256,512]{1,0:T(8,128)(2,1)S(1)}, bf16[256,512]{1,0:T(8,128)(2,1)S(1)}, u32[]{:S(2)}, u32[]{:S(2)}) collective-permute-start(bf16[256,512]{1,0:T(8,128)(2,1)S(1)} %collective-permute-done.4), channel_id=1, source_target_pairs={{0,2},{2,0},{1,3},{3,1},{4,6},{6,4},{5,7},{7,5},{8,10},{10,8},{9,1... | collective-permute-start | bytes 786440 | tf_op jit(solution)/shard_map/ppermute | solution.py:30
  37.8 12.3 %collective-permute-start.9 = (bf16[1024,256]{1,0:T(8,128)(2,1)S(1)}, bf16[1024,256]{1,0:T(8,128)(2,1)S(1)}, u32[]{:S(2)}, u32[]{:S(2)}) collective-permute-start(bf16[1024,256]{1,0:T(8,128)(2,1)S(1)} %pad_maximum_fusion.up_1), channel_id=1, source_target_pairs={{0,32},{32,64},{64,96},{96,128},{128,160},{160,192},{192,224},{224... | collective-permute-start | bytes 1572872 | tf_op jit(solution)/shard_map/ppermute | solution.py:30
  38.0 20.6 %collective-permute-start.10 = (bf16[1024,256]{1,0:T(8,128)(2,1)S(1)}, bf16[1024,256]{1,0:T(8,128)(2,1)S(1)}, u32[]{:S(2)}, u32[]{:S(2)}) collective-permute-start(bf16[1024,256]{1,0:T(8,128)(2,1)S(1)} %pad_maximum_fusion.1.down_1), channel_id=1, source_target_pairs={{0,224},{32,0},{64,32},{96,64},{128,96},{160,128},{192,160},{224,1... | collective-permute-start | bytes 1572872 | tf_op jit(solution)/shard_map/ppermute | solution.py:30
  40.5 18.0 %collective-permute-start.8 = (bf16[512,512]{1,0:T(8,128)(2,1)S(1)}, bf16[512,512]{1,0:T(8,128)(2,1)S(1)}, u32[]{:S(2)}, u32[]{:S(2)}) collective-permute-start(bf16[512,512]{1,0:T(8,128)(2,1)S(1)} %pad_maximum_fusion.2.refs_0_), channel_id=1, source_target_pairs={{0,8},{4,12},{8,0},{12,4},{1,9},{5,13},{9,1},{13,5},{2,10},{6,14},... | collective-permute-start | bytes 1572872 | tf_op jit(solution)/shard_map/ppermute | solution.py:30
  47.3 22.9 %collective-permute-start.11 = (bf16[512,512]{1,0:T(8,128)(2,1)S(1)}, bf16[512,512]{1,0:T(8,128)(2,1)S(1)}, u32[]{:S(2)}, u32[]{:S(2)}) collective-permute-start(bf16[512,512]{1,0:T(8,128)(2,1)S(1)} %pad_maximum_fusion.2.refs_0_), channel_id=1, source_target_pairs={{0,4},{4,8},{8,12},{12,0},{1,5},{5,9},{9,13},{13,1},{2,6},{6,10},{... | collective-permute-start | bytes 1572872 | tf_op jit(solution)/shard_map/ppermute | solution.py:30
  47.3 24.1 %collective-permute-start.12 = (bf16[512,512]{1,0:T(8,128)(2,1)S(1)}, bf16[512,512]{1,0:T(8,128)(2,1)S(1)}, u32[]{:S(2)}, u32[]{:S(2)}) collective-permute-start(bf16[512,512]{1,0:T(8,128)(2,1)S(1)} %pad_maximum_fusion.2.refs_0_), channel_id=1, source_target_pairs={{0,12},{4,0},{8,4},{12,8},{1,13},{5,1},{9,5},{13,9},{2,14},{6,2},{... | collective-permute-start | bytes 1572872 | tf_op jit(solution)/shard_map/ppermute | solution.py:30
  50.0 21.4 %collective-permute-start.17 = (bf16[1024,256]{1,0:T(8,128)(2,1)S(1)}, bf16[1024,256]{1,0:T(8,128)(2,1)S(1)}, u32[]{:S(2)}, u32[]{:S(2)}) collective-permute-start(bf16[1024,256]{1,0:T(8,128)(2,1)S(1)} %collective-permute-done.9.up_2), channel_id=1, source_target_pairs={{0,32},{32,64},{64,96},{96,128},{128,160},{160,192},{192,224},{224... | collective-permute-start | bytes 1572872 | tf_op jit(solution)/shard_map/ppermute | solution.py:30
  58.6 13.4 %collective-permute-start.18 = (bf16[1024,256]{1,0:T(8,128)(2,1)S(1)}, bf16[1024,256]{1,0:T(8,128)(2,1)S(1)}, u32[]{:S(2)}, u32[]{:S(2)}) collective-permute-start(bf16[1024,256]{1,0:T(8,128)(2,1)S(1)} %collective-permute-done.10.down_2), channel_id=1, source_target_pairs={{0,224},{32,0},{64,32},{96,64},{128,96},{160,128},{192,160},{224,1... | collective-permute-start | bytes 1572872 | tf_op jit(solution)/shard_map/ppermute | solution.py:30
  58.6 17.0 %collective-permute-start.13 = (bf16[512,512]{1,0:T(8,128)(2,1)S(1)}, bf16[512,512]{1,0:T(8,128)(2,1)S(1)}, u32[]{:S(2)}, u32[]{:S(2)}) collective-permute-start(bf16[512,512]{1,0:T(8,128)(2,1)S(1)} %pad_maximum_fusion.2.refs_0_), channel_id=1, source_target_pairs={{0,1},{1,0},{2,3},{3,2},{4,5},{5,4},{6,7},{7,6},{8,9},{9,8},{10,11... | collective-permute-start | bytes 1572872 | tf_op jit(solution)/shard_map/ppermute | solution.py:30
  70.3 5.8 %collective-permute-start.16 = (bf16[512,512]{1,0:T(8,128)(2,1)S(1)}, bf16[512,512]{1,0:T(8,128)(2,1)S(1)}, u32[]{:S(2)}, u32[]{:S(2)}) collective-permute-start(bf16[512,512]{1,0:T(8,128)(2,1)S(1)} %collective-permute-done.8.refs_3_), channel_id=1, source_target_pairs={{0,1},{1,0},{2,3},{3,2},{4,5},{5,4},{6,7},{7,6},{8,9},{9,8},{10,11... | collective-permute-start | bytes 1572872 | tf_op jit(solution)/shard_map/ppermute | solution.py:30
  71.5 4.6 %collective-permute-start.14 = (bf16[512,512]{1,0:T(8,128)(2,1)S(1)}, bf16[512,512]{1,0:T(8,128)(2,1)S(1)}, u32[]{:S(2)}, u32[]{:S(2)}) collective-permute-start(bf16[512,512]{1,0:T(8,128)(2,1)S(1)} %collective-permute-done.11.refs_1_), channel_id=1, source_target_pairs={{0,1},{1,0},{2,3},{3,2},{4,5},{5,4},{6,7},{7,6},{8,9},{9,8},{10,11... | collective-permute-start | bytes 1572872 | tf_op jit(solution)/shard_map/ppermute | solution.py:30
  71.5 4.6 %collective-permute-start.15 = (bf16[512,512]{1,0:T(8,128)(2,1)S(1)}, bf16[512,512]{1,0:T(8,128)(2,1)S(1)}, u32[]{:S(2)}, u32[]{:S(2)}) collective-permute-start(bf16[512,512]{1,0:T(8,128)(2,1)S(1)} %collective-permute-done.12.refs_2_), channel_id=1, source_target_pairs={{0,1},{1,0},{2,3},{3,2},{4,5},{5,4},{6,7},{7,6},{8,9},{9,8},{10,11... | collective-permute-start | bytes 1572872 | tf_op jit(solution)/shard_map/ppermute | solution.py:30
  72.0 10.5 %collective-permute-start.19 = (bf16[512,256]{1,0:T(8,128)(2,1)S(1)}, bf16[512,256]{1,0:T(8,128)(2,1)S(1)}, u32[]{:S(2)}, u32[]{:S(2)}) collective-permute-start(bf16[512,256]{1,0:T(8,128)(2,1)S(1)} %slice.8), channel_id=1, source_target_pairs={{0,32},{32,64},{64,96},{96,128},{128,160},{160,192},{192,224},{224... | collective-permute-start | bytes 786440 | tf_op jit(solution)/shard_map/ppermute | solution.py:30
  75.5 7.5 %collective-permute-start.20 = (bf16[512,256]{1,0:T(8,128)(2,1)S(1)}, bf16[512,256]{1,0:T(8,128)(2,1)S(1)}, u32[]{:S(2)}, u32[]{:S(2)}) collective-permute-start(bf16[512,256]{1,0:T(8,128)(2,1)S(1)} %slice.9), channel_id=1, source_target_pairs={{0,224},{32,0},{64,32},{96,64},{128,96},{160,128},{192,160},{224,1... | collective-permute-start | bytes 786440 | tf_op jit(solution)/shard_map/ppermute | solution.py:30
